TPU v7x, 128 devices: a whole 4x4x4 slice. The times are simulated.
128 devices in a mesh: gx: 8 (over y, core), gy: 4 (over z), gz: 4 (over x).
Axes of the slice: x: 4, y: 4, z: 4, core: 2. Of those that a mesh axis runs over, the one named last changes fastest.
Arguments:
- right_side: float32 [128, 64, 1024], P('gx', 'gy', 'gz'), may hold values from -8 to 8
- conductance: float32 [3, 128, 64, 1024], P(None, 'gx', 'gy', 'gz'), may hold values from 0.2 to 5
- storage: float32 [128, 64, 1024], P('gx', 'gy', 'gz'), may hold values from 0.05 to 0.8
- dirichlet: int32 [128, 64, 1024], P('gx', 'gy', 'gz'), may hold values 0 or 1
- basis: float32 [16, 128, 64, 1024], P(None, 'gx', 'gy', 'gz'), may hold values from -2 to 2
- coarse_inverse: float32 [2048, 2048], P(('gx', 'gy', 'gz')), may hold values from 0 to 2, as said below
Outputs:
- solution_field: float32 [128, 64, 1024], P('gx', 'gy', 'gz')
- residual: float32 [128, 64, 1024], P('gx', 'gy', 'gz')
Inputs may be any that keep to these rules, and one draw needn't show every extreme that they name: `coarse_inverse`: symmetric positive definite.
All inputs are finite; a program needn't handle non-finite values. No bound on the sum of `dirichlet` on one device may be relied on, other than what follows from the above.
Results may differ from a plain program's by a relative error of at most 0.0003.
Values sent between devices are 32-bit elements; how exact they have to be, the bound alone decides.
A program may use at most 128 MiB of HBM per device.

v0:
```python
import functools

import jax
import jax.numpy as jnp
from jax import lax
from jax.experimental import pallas as pl
from jax.experimental.pallas import tpu as pltpu
from jax.sharding import PartitionSpec as P

MESH_ID = pl.DeviceIdType.MESH

SWEEPS = 4
ITERS = 2


RELAX = 2.0 / 3.0


def padded(value, sides, width):
    for axis, dim in sides:
        count, length = (lax.axis_size(axis), value.shape[dim])
        up = [(i, (i + 1) % count) for i in range(count - 1)]
        down = [(j, i) for i, j in up]
        last = lax.slice_in_dim(value, length - width, length, axis=dim)
        leading = lax.slice_in_dim(value, 0, width, axis=dim)
        before = lax.ppermute(last, axis, up)
        after = lax.ppermute(leading, axis, down)
        value = jnp.concatenate([before, value, after], axis=dim)
    return value


def pad_cond(cond):
    return jnp.pad(cond, ((0, 0), (1, 1), (1, 1), (1, 1)))


def stencil(padded_free, padded_cond, field, storage, free):
    middle = padded_free[1:-1, 1:-1, 1:-1]
    total = storage * middle
    total = (
        total
        + padded_cond[0, 1:-1, 1:-1, 1:-1] * (middle - padded_free[2:, 1:-1, 1:-1])
        + padded_cond[0, :-2, 1:-1, 1:-1] * (middle - padded_free[:-2, 1:-1, 1:-1])
    )
    total = (
        total
        + padded_cond[1, 1:-1, 1:-1, 1:-1] * (middle - padded_free[1:-1, 2:, 1:-1])
        + padded_cond[1, 1:-1, :-2, 1:-1] * (middle - padded_free[1:-1, :-2, 1:-1])
    )
    total = (
        total
        + padded_cond[2, 1:-1, 1:-1, 1:-1] * (middle - padded_free[1:-1, 1:-1, 2:])
        + padded_cond[2, 1:-1, 1:-1, :-2] * (middle - padded_free[1:-1, 1:-1, :-2])
    )
    return free * total + (1.0 - free) * field


def diagonal_of(padded_cond, storage, free):
    total = storage + padded_cond[0, 1:-1, 1:-1, 1:-1] + padded_cond[0, :-2, 1:-1, 1:-1]
    total = total + padded_cond[1, 1:-1, 1:-1, 1:-1] + padded_cond[1, 1:-1, :-2, 1:-1]
    total = total + padded_cond[2, 1:-1, 1:-1, 1:-1] + padded_cond[2, 1:-1, 1:-1, :-2]
    return free * total + (1.0 - free)


def jacobi(rhs_box, padded_cond, diagonal, storage_box, free_box):
    guess = jnp.zeros_like(rhs_box)
    for sweep in range(SWEEPS):
        image = stencil(jnp.pad(free_box * guess, 1), padded_cond, guess, storage_box, free_box)
        guess = guess + RELAX * (rhs_box - image) / diagonal
    return guess


def project(basis, field):
    return jnp.sum(basis * field[None], axis=(1, 2, 3))


def expand(basis, weights, field):
    return jnp.sum(weights[:, None, None, None] * basis, axis=0)


LANES = 128


def faces(field):
    pieces = []
    for dim, axis in enumerate(("gx", "gy", "gz")):
        count, length = (lax.axis_size(axis), field.shape[dim])
        up = [(i, i + 1) for i in range(count - 1)]
        down = [(j, i) for i, j in up]
        before = lax.ppermute(lax.slice_in_dim(field, length - 1, length, axis=dim), axis, up)
        after = lax.ppermute(lax.slice_in_dim(field, 0, 1, axis=dim), axis, down)
        pieces.append((before, after))
    result = field
    for dim in range(3):
        before, after = pieces[dim]
        widths = [(1, 1) if d < dim else (0, 0) for d in range(3)]
        result = jnp.concatenate([jnp.pad(before, widths), result, jnp.pad(after, widths)], axis=dim)
    return result


def residual_rim(field):
    return padded(field, (("gx", 0), ("gy", 1), ("gz", 2)), 2)


def gather_kernel(sizes, row_ref, out_ref, held, local_sem, send1, recv1, send2, recv2):
    nx, ny, nz = sizes
    plane = ny * nz
    a = lax.axis_index("gx")
    b = lax.axis_index("gy")
    c = lax.axis_index("gz")
    me = (a * ny + b) * nz + c

    def in_plane(k):
        return (a, lax.rem(b + k // nz, ny), lax.rem(c + k % nz, nz))

    def along_x(k):
        return (lax.rem(a + k, nx), b, c)

    peers = [in_plane(k) for k in range(1, plane)] + [along_x(k) for k in range(1, nx)]
    barrier = pltpu.get_barrier_semaphore()
    for peer in peers:
        pl.semaphore_signal(barrier, inc=1, device_id=peer, device_id_type=MESH_ID)
    pl.semaphore_wait(barrier, len(peers))

    own = pltpu.make_async_copy(row_ref, held.at[pl.ds(me, 1)], local_sem.at[0])
    own.start()
    sent = []

    def stage(src_of, first_of, count, size, toward, send, recv):
        for k in range(1, size):
            copy = pltpu.make_async_remote_copy(
                src_ref=src_of(0),
                dst_ref=held.at[pl.ds(first_of(0), count)],
                send_sem=send.at[k],
                recv_sem=recv.at[k],
                device_id=toward(k),
                device_id_type=MESH_ID,
            )
            copy.start()
            sent.append(copy)
        for k in range(1, size):
            pltpu.make_async_remote_copy(
                src_ref=src_of(k),
                dst_ref=held.at[pl.ds(first_of(k), count)],
                send_sem=send.at[k],
                recv_sem=recv.at[k],
                device_id=toward(size - k),
                device_id_type=MESH_ID,
            ).wait_recv()

    def p_first(k):
        return (a * ny + lax.rem(b + ny - k // nz, ny)) * nz + lax.rem(c + nz - k % nz, nz)

    stage(lambda k: row_ref, p_first, 1, plane, in_plane, send1, recv1)
    own.wait()
    x_first = lambda k: lax.rem(a + nx - k, nx) * plane
    stage(lambda k: held.at[pl.ds(x_first(k), plane)], x_first, plane, nx, along_x, send2, recv2)
    for copy in sent:
        copy.wait_send()
    final = pltpu.make_async_copy(held, out_ref, local_sem.at[1])
    final.start()
    final.wait()


def gather_rows(row):
    sizes = (lax.axis_size("gx"), lax.axis_size("gy"), lax.axis_size("gz"))
    count = sizes[0] * sizes[1] * sizes[2]
    tile = row[:, None, :]
    rows = pl.pallas_call(
        functools.partial(gather_kernel, sizes),
        out_shape=jax.ShapeDtypeStruct((count, 1, LANES), jnp.float32),
        in_specs=[pl.BlockSpec(memory_space=pltpu.VMEM)],
        out_specs=pl.BlockSpec(memory_space=pltpu.VMEM),
        scratch_shapes=[
            pltpu.VMEM((count, 1, LANES), jnp.float32),
            pltpu.SemaphoreType.DMA((2,)),
            pltpu.SemaphoreType.DMA((sizes[1] * sizes[2],)),
            pltpu.SemaphoreType.DMA((sizes[1] * sizes[2],)),
            pltpu.SemaphoreType.DMA((sizes[0],)),
            pltpu.SemaphoreType.DMA((sizes[0],)),
        ],
        compiler_params=pltpu.CompilerParams(collective_id=0, has_side_effects=True),
    )(tile)
    return rows[:, 0, :]


def pack(coarse, scalars):
    vecs = coarse.shape[0]
    row = jnp.zeros((LANES,), jnp.float32)
    row = row.at[:vecs].set(coarse)
    if scalars:
        row = row.at[vecs:vecs + len(scalars)].set(jnp.stack(scalars))
    return row[None]


def unpack(rows, vecs, count):
    coarse = rows[:, :vecs].reshape(-1)
    sums = jnp.sum(rows[:, vecs:vecs + count], axis=0)
    return coarse, [sums[i] for i in range(count)]


def shards(right_side, conductance, storage, dirichlet, basis, coarse_inverse):
    vecs = basis.shape[0]
    sides = (("gx", 0), ("gy", 1), ("gz", 2))
    free = 1.0 - dirichlet.astype(jnp.float32)
    stacked = jnp.concatenate([conductance, storage[None], free[None], right_side[None]], axis=0)
    wide = padded(stacked, (("gx", 1), ("gy", 2), ("gz", 3)), 3)
    cond_wide = wide[:3]
    free_wide = wide[4]
    storage_wide = wide[3]
    cond_box = wide[:3, 1:-1, 1:-1, 1:-1]
    storage_box = wide[3, 1:-1, 1:-1, 1:-1]
    free_box = wide[4, 1:-1, 1:-1, 1:-1]
    rhs_box0 = wide[5, 1:-1, 1:-1, 1:-1]
    box_cond = pad_cond(cond_box)
    box_diag = diagonal_of(box_cond, storage_box, free_box)
    cond_face = wide[:3, 2:-2, 2:-2, 2:-2]
    free_face = wide[4, 2:-2, 2:-2, 2:-2]

    def schwarz(rhs_box):
        return jacobi(rhs_box, box_cond, box_diag, storage_box, free_box)[2:-2, 2:-2, 2:-2]

    def precondition(rhs_box, residual, coarse_all):
        weights = jnp.dot(coarse_inverse, coarse_all, precision=lax.Precision.HIGHEST)
        return schwarz(rhs_box) + expand(basis, weights, residual)

    residual0 = right_side
    coarse0 = project(basis, residual0)
    coarse0_all, _ = unpack(gather_rows(pack(coarse0, [])), vecs, 0)
    z0 = precondition(rhs_box0, residual0, coarse0_all)
    near0 = padded(z0, sides, 3)
    inner = (slice(1, -1),) * 3
    image0_box = stencil(free_wide * near0, cond_wide, near0[inner], storage_wide[inner], free_wide[inner])
    image0 = image0_box[2:-2, 2:-2, 2:-2]
    coarse_img = project(basis, image0)
    rows = gather_rows(pack(coarse_img, [jnp.sum(residual0 * z0), jnp.sum(z0 * image0)]))
    coarse_img_all, (rz0, curve0) = unpack(rows, vecs, 2)
    alpha0 = rz0 / curve0
    solution1 = alpha0 * z0
    rhs_box1 = rhs_box0 - alpha0 * image0_box
    residual1 = rhs_box1[2:-2, 2:-2, 2:-2]
    coarse1_all = coarse0_all - alpha0 * coarse_img_all
    z1 = precondition(rhs_box1, residual1, coarse1_all)
    near1 = faces(z1)
    image_z1 = stencil(free_face * near1, cond_face, z1, storage, free)
    local = [
        jnp.sum(residual1 * z1),
        jnp.sum(z1 * image_z1),
        jnp.sum(z1 * image0),
        jnp.sum(z0 * image_z1),
    ]
    _, (rz1, zz, cross_a, cross_b) = unpack(gather_rows(pack(jnp.zeros((0,), jnp.float32), local)), 0, 4)
    beta = rz1 / rz0
    direction1 = z1 + beta * z0
    image1 = image_z1 + beta * image0
    curve1 = zz + beta * (cross_a + cross_b) + beta * beta * curve0
    alpha1 = rz1 / curve1
    solution2 = solution1 + alpha1 * direction1
    residual2 = residual1 - alpha1 * image1
    return (solution2, residual2)


def solution(mesh):
    placed = (
        P("gx", "gy", "gz"),
        P(None, "gx", "gy", "gz"),
        P("gx", "gy", "gz"),
        P("gx", "gy", "gz"),
        P(None, "gx", "gy", "gz"),
        P(("gx", "gy", "gz"), None),
    )
    return jax.shard_map(
        shards,
        mesh=mesh,
        in_specs=placed,
        out_specs=(P("gx", "gy", "gz"), P("gx", "gy", "gz")),
        check_vma=False,
    )
```

profile of v0, /device:TPU:1, one launch (start us, length us, event | category | flops | bytes accessed | tf_op | source)
XLA Modules:
  0.0 205.3 jit_solution(6385358298605831411)
XLA Ops:
  3.3 3.3 %collective-permute-start.1 = (f32[6,3,16,256]{3,2,1,0:T(8,128)S(1)}, f32[6,3,16,256]{3,2,1,0:T(8,128)S(1)}, u32[]{:S(2)}, u32[]{:S(2)}) collective-permute-start(f32[6,3,16,256]{3,2,1,0:T(8,128)S(1)} %get-tuple-element.84), channel_id=1, source_target_pairs={{16,0},{32,16},{48,32},{64,48},{80,64},{96,80},{112,96},{17,1},{33... | collective-permute-start | bytes 884744 | tf_op jit(solution)/shard_map/ppermute | solution.py:27
  6.6 3.2 %collective-permute-start = (f32[6,3,16,256]{3,2,1,0:T(8,128)S(1)}, f32[6,3,16,256]{3,2,1,0:T(8,128)S(1)}, u32[]{:S(2)}, u32[]{:S(2)}) collective-permute-start(f32[6,3,16,256]{3,2,1,0:T(8,128)S(1)} %get-tuple-element.83), channel_id=1, source_target_pairs={{0,16},{16,32},{32,48},{48,64},{64,80},{80,96},{96,112},{1,17},{17... | collective-permute-start | bytes 884744 | tf_op jit(solution)/shard_map/ppermute | solution.py:26
  9.8 2.5 %collective-permute-done.1 = f32[6,3,16,256]{3,2,1,0:T(8,128)S(1)} collective-permute-done((f32[6,3,16,256]{3,2,1,0:T(8,128)S(1)}, f32[6,3,16,256]{3,2,1,0:T(8,128)S(1)}, u32[]{:S(2)}, u32[]{:S(2)}) %collective-permute-start.1) | collective-permute-done | bytes 294944 | tf_op jit(solution)/shard_map/ppermute | solution.py:27
  17.5 4.9 %collective-permute-start.2 = (f32[6,22,3,256]{3,1,2,0:T(8,128)}, f32[6,22,3,256]{3,1,2,0:T(8,128)}, u32[]{:S(2)}, u32[]{:S(2)}) collective-permute-start(f32[6,22,3,256]{3,1,2,0:T(8,128)} %copy.25), channel_id=1, source_target_pairs={{0,4},{4,8},{8,12},{1,5},{5,9},{9,13},{2,6},{6,10},{10,14},{3,7},{... | collective-permute-start | bytes 1216520 | tf_op jit(solution)/shard_map/ppermute | solution.py:26
  23.6 18.6 %shard_map.77 = f32[128,1,128]{2,1,0:T(1,128)} custom-call(f32[1,1,128]{2,1,0:T(1,128)} %scatter.14.row_ref), custom_call_target="tpu_custom_call" | custom-call | tf_op jit(solution)/shard_map/pallas_call | solution.py:168
  48.5 2.4 %copy.30 = f32[6,22,22,3]{2,1,3,0:T(8,128)S(1)} copy(f32[6,22,22,3]{3,2,1,0:T(8,128)} %get-tuple-element.80) | data formatting | bytes 69696 | tf_op jit(solution)/shard_map/slice | solution.py:25
  53.8 4.7 %collective-permute-start.4 = (f32[6,22,22,3]{2,1,3,0:T(8,128)}, f32[6,22,22,3]{2,1,3,0:T(8,128)}, u32[]{:S(2)}, u32[]{:S(2)}) collective-permute-start(f32[6,22,22,3]{2,1,3,0:T(8,128)} %copy.29), channel_id=1, source_target_pairs={{0,1},{1,2},{2,3},{4,5},{5,6},{6,7},{8,9},{9,10},{10,11},{12,13},{... | collective-permute-start | bytes 104552 | tf_op jit(solution)/shard_map/ppermute | solution.py:26
  58.5 3.5 %multiply_reduce_fusion.2 = f32[16,16,256]{2,1,0:T(8,128)} fusion(f32[16,16,16,256]{3,2,1,0:T(8,128)} %param.18, f32[16]{0:T(128)S(1)} %convolution_bitcast_fusion.1), kind=kLoop, calls=%fused_computation.4 | loop fusion | flops 2031616 | bytes 4456512 | tf_op jit(solution)/shard_map/reduce_sum | solution.py:77
  61.9 3.0 %copy.32 = f32[6,22,22,3]{3,2,1,0:T(8,128)} copy(f32[6,22,22,3]{2,1,3,0:T(8,128)} %collective-permute-done.5) | data formatting | bytes 69696 | tf_op jit(solution)/shard_map/ppermute | solution.py:27
  65.0 1.9 copy.31
  66.8 9.6 %pad_maximum_fusion = f32[6,22,22,262]{3,2,1,0:T(8,128)S(1)} fusion(f32[6,22,22,3]{3,2,1,0:T(8,128)} %copy.32, f32[6,22,3,256]{3,2,1,0:T(4,128)} %copy-done.20, f32[6,3,16,256]{3,2,1,0:T(8,128)} %copy-done.26, f32[1,16,16,256]{3,2,1,0:T(8,128)S(1)} %bitcast.309, f32[1,16,16,256]{3,2,1,0:T(8,128)S(1)} %fusion.203, f32[1,16,16,256]{3,2,1,0:T(8,128)S(1)} %bitcast.314, ...), kind=kLoop, calls=%fused_computation | loop fusion | flops 6847632 | bytes 6086784 | tf_op jit(solution)/shard_map/concatenate | solution.py:28
  78.1 2.4 %fusion.204 = (f32[20,20,260]{2,1,0:T(8,128)S(1)}, f32[20,20,260]{2,1,0:T(8,128)S(1)}, f32[20,20,260]{2,1,0:T(8,128)S(1)}, f32[20,20,260]{2,1,0:T(8,128)S(1)}) fusion(f32[6,22,22,262]{3,2,1,0:T(8,128)S(1)} %pad_maximum_fusion, f32[20,20,260]{2,1,0:T(8,128)S(1)} %broadcast_multiply_fusion, f32[3,20,20,260]{3,2,1,0:T(8,128)S(1)} %slice.610), kind=kLoop, calls=%fused_computation.339 | loop fusion | flops 3640000 | bytes 5824000 | tf_op jit(solution)/shard_map/mul | solution.py:67
  80.6 2.3 %fusion.210 = (f32[20,20,260]{2,1,0:T(8,128)S(1)}, f32[20,20,260]{2,1,0:T(8,128)S(1)}) fusion(f32[6,22,22,262]{3,2,1,0:T(8,128)S(1)} %pad_maximum_fusion, f32[20,20,260]{2,1,0:T(8,128)S(1)} %get-tuple-element.73, f32[20,20,260]{2,1,0:T(8,128)S(1)} %get-tuple-element.71, f32[3,20,20,260]{3,2,1,0:T(8,128)S(1)} %slice.610, f32[20,20,260]{2,1,0:T(8,128)S(1)} %get-tuple-element.72), kind=kLoop, calls=%fused_computation.354 | loop fusion | flops 3224000 | bytes 5824000 | tf_op jit(solution)/shard_map/mul | solution.py:67
  82.8 2.1 %fusion.209 = (f32[20,20,260]{2,1,0:T(8,128)S(1)}, f32[20,20,260]{2,1,0:T(8,128)S(1)}) fusion(f32[6,22,22,262]{3,2,1,0:T(8,128)S(1)} %pad_maximum_fusion, f32[20,20,260]{2,1,0:T(8,128)S(1)} %get-tuple-element.70, f32[20,20,260]{2,1,0:T(8,128)S(1)} %get-tuple-element.73, f32[20,20,260]{2,1,0:T(8,128)S(1)} %get-tuple-element.69, f32[3,20,20,260]{3,2,1,0:T(8,128)S(1)} %slice.610), kind=kLoop, calls=%fused_computation.353 | loop fusion | flops 2912000 | bytes 5824000 | tf_op jit(solution)/shard_map/mul | solution.py:67
  87.1 2.9 %collective-permute-start.7 = (f32[3,16,256]{2,1,0:T(8,128)S(1)}, f32[3,16,256]{2,1,0:T(8,128)S(1)}, u32[]{:S(2)}, u32[]{:S(2)}) collective-permute-start(f32[3,16,256]{2,1,0:T(8,128)S(1)} %get-tuple-element.97), channel_id=1, source_target_pairs={{16,0},{32,16},{48,32},{64,48},{80,64},{96,80},{112,96},{17,1},{33... | collective-permute-start | bytes 147464 | tf_op jit(solution)/shard_map/ppermute | solution.py:27
  90.0 2.9 %collective-permute-start.6 = (f32[3,16,256]{2,1,0:T(8,128)S(1)}, f32[3,16,256]{2,1,0:T(8,128)S(1)}, u32[]{:S(2)}, u32[]{:S(2)}) collective-permute-start(f32[3,16,256]{2,1,0:T(8,128)S(1)} %get-tuple-element.96), channel_id=1, source_target_pairs={{0,16},{16,32},{32,48},{48,64},{64,80},{80,96},{96,112},{1,17},{17... | collective-permute-start | bytes 147464 | tf_op jit(solution)/shard_map/ppermute | solution.py:26
  95.8 4.6 %collective-permute-start.8 = (f32[22,3,256]{2,1,0:T(4,128)}, f32[22,3,256]{2,1,0:T(4,128)}, u32[]{:S(2)}, u32[]{:S(2)}) collective-permute-start(f32[22,3,256]{2,1,0:T(4,128)} %get-tuple-element.88), channel_id=1, source_target_pairs={{0,4},{4,8},{8,12},{1,5},{5,9},{9,13},{2,6},{6,10},{10,14},{3,7},{... | collective-permute-start | bytes 202760 | tf_op jit(solution)/shard_map/ppermute | solution.py:26
  105.0 4.0 %collective-permute-start.10 = (f32[22,22,3]{2,1,0:T(8,128)S(1)}, f32[22,22,3]{2,1,0:T(8,128)S(1)}, u32[]{:S(2)}, u32[]{:S(2)}) collective-permute-start(f32[22,22,3]{2,1,0:T(8,128)S(1)} %get-tuple-element.86), channel_id=1, source_target_pairs={{0,1},{1,2},{2,3},{4,5},{5,6},{6,7},{8,9},{9,10},{10,11},{12,13},{... | collective-permute-start | bytes 17432 | tf_op jit(solution)/shard_map/ppermute | solution.py:26
  110.5 2.8 %collective-permute-done.11 = f32[22,22,3]{2,1,0:T(8,128)S(1)} collective-permute-done((f32[22,22,3]{2,1,0:T(8,128)S(1)}, f32[22,22,3]{2,1,0:T(8,128)S(1)}, u32[]{:S(2)}, u32[]{:S(2)}) %collective-permute-start.11) | collective-permute-done | bytes 5840 | tf_op jit(solution)/shard_map/ppermute | solution.py:27
  115.7 3.0 %fusion.159 = f32[20,20,260]{2,1,0:T(8,128)S(1)} fusion(f32[22,22,262]{2,1,0:T(8,128)S(1)} %get-tuple-element.66, f32[22,22,262]{2,1,0:T(8,128)S(1)} %get-tuple-element.65, f32[6,22,22,262]{3,2,1,0:T(8,128)S(1)} %copy-done.2, f32[22,22,262]{2,1,0:T(8,128)S(1)} %get-tuple-element.75, f32[22,22,262]{2,1,0:T(8,128)S(1)} %get-tuple-element.74), kind=kLoop, calls=%fused_computation.219 | loop fusion | flops 2392000 | bytes 7072000 | tf_op jit(solution)/shard_map/add | solution.py:54
  122.1 16.6 %shard_map.78 = f32[128,1,128]{2,1,0:T(1,128)} custom-call(f32[1,1,128]{2,1,0:T(1,128)} %copy-done.37), custom_call_target="tpu_custom_call" | custom-call | tf_op jit(solution)/shard_map/pallas_call | solution.py:168
  142.4 3.6 %fusion.205 = (f32[20,20,260]{2,1,0:T(8,128)}, f32[20,20,260]{2,1,0:T(8,128)}) fusion(f32[20,20,260]{2,1,0:T(8,128)} %copy-done.6, f32[20,20,260]{2,1,0:T(8,128)} %copy-done.18, f32[6,22,22,262]{3,2,1,0:T(8,128)} %copy-done.1, f32[20,20,260]{2,1,0:T(8,128)} %copy-done.24, f32[]{:T(128)S(6)} %div.37), kind=kLoop, calls=%fused_computation.340 | loop fusion | flops 624000 | bytes 2912004 | tf_op jit(solution)/shard_map/mul | solution.py:67
  146.4 3.0 %multiply_reduce_fusion = f32[16,16,256]{2,1,0:T(8,128)S(1)} fusion(f32[16,16,16,256]{3,2,1,0:T(8,128)} %param.18, f32[16]{0:T(128)S(1)} %convolution_bitcast_fusion), kind=kLoop, calls=%fused_computation.2 | loop fusion | flops 2031616 | bytes 4456512 | tf_op jit(solution)/shard_map/reduce_sum | solution.py:77
  149.5 4.0 %fusion.208 = (f32[20,20,260]{2,1,0:T(8,128)S(1)}, f32[20,20,260]{2,1,0:T(8,128)S(1)}) fusion(f32[6,22,22,262]{3,2,1,0:T(8,128)} %copy-done.1, f32[20,20,260]{2,1,0:T(8,128)S(1)} %copy-done.7, f32[20,20,260]{2,1,0:T(8,128)S(1)} %copy-done.17, f32[20,20,260]{2,1,0:T(8,128)S(1)} %copy-done.30, f32[3,20,20,260]{3,2,1,0:T(8,128)S(1)} %slice.610, ...), kind=kLoop, calls=%fused_computation.352 | loop fusion | flops 3224000 | bytes 5824000 | tf_op jit(solution)/shard_map/mul | solution.py:67
  153.5 1.8 fusion.207
  161.9 4.0 %collective-permute-start.13 = (f32[16,1,256]{2,1,0:T(1,128)S(1)}, f32[16,1,256]{2,1,0:T(1,128)S(1)}, u32[]{:S(2)}, u32[]{:S(2)}) collective-permute-start(f32[16,1,256]{2,1,0:T(1,128)S(1)} %get-tuple-element.94), channel_id=1, source_target_pairs={{0,4},{4,8},{8,12},{1,5},{5,9},{9,13},{2,6},{6,10},{10,14},{3,7},{... | collective-permute-start | bytes 49160 | tf_op jit(solution)/shard_map/ppermute | solution.py:89
  165.9 4.0 %collective-permute-start.12 = (f32[16,16,1]{2,1,0:T(8,128)S(1)}, f32[16,16,1]{2,1,0:T(8,128)S(1)}, u32[]{:S(2)}, u32[]{:S(2)}) collective-permute-start(f32[16,16,1]{2,1,0:T(8,128)S(1)} %get-tuple-element.92), channel_id=1, source_target_pairs={{0,1},{1,2},{2,3},{4,5},{5,6},{6,7},{8,9},{9,10},{10,11},{12,13},{... | collective-permute-start | bytes 3080 | tf_op jit(solution)/shard_map/ppermute | solution.py:89
  169.9 3.4 %collective-permute-start.15 = (f32[1,16,256]{2,1,0:T(8,128)S(1)}, f32[1,16,256]{2,1,0:T(8,128)S(1)}, u32[]{:S(2)}, u32[]{:S(2)}) collective-permute-start(f32[1,16,256]{2,1,0:T(8,128)S(1)} %get-tuple-element.91), channel_id=1, source_target_pairs={{16,0},{32,16},{48,32},{64,48},{80,64},{96,80},{112,96},{17,1},{33... | collective-permute-start | bytes 49160 | tf_op jit(solution)/shard_map/ppermute | solution.py:90
  173.3 2.5 %collective-permute-start.14 = (f32[1,16,256]{2,1,0:T(8,128)S(1)}, f32[1,16,256]{2,1,0:T(8,128)S(1)}, u32[]{:S(2)}, u32[]{:S(2)}) collective-permute-start(f32[1,16,256]{2,1,0:T(8,128)S(1)} %get-tuple-element.90), channel_id=1, source_target_pairs={{0,16},{16,32},{32,48},{48,64},{64,80},{80,96},{96,112},{1,17},{17... | collective-permute-start | bytes 49160 | tf_op jit(solution)/shard_map/ppermute | solution.py:89
  179.0 2.7 %maximum_bitcast_fusion.1 = f32[1,1,4]{2,1,0:T(1,128)S(1)} fusion(f32[1]{0:T(128)} %bitcast.39, f32[1]{0:T(128)} %bitcast.38, f32[1]{0:T(128)} %bitcast.37, f32[1]{0:T(128)} %bitcast.29), kind=kLoop, calls=%fused_computation.348 | loop fusion | flops 12 | bytes 32 | tf_op jit(solution)/shard_map/broadcast_in_dim;broadcast_in_dim | solution.py:167
  182.1 15.0 %shard_map.79 = f32[128,1,128]{2,1,0:T(1,128)} custom-call(f32[1,1,128]{2,1,0:T(1,128)} %scatter.19.row_ref), custom_call_target="tpu_custom_call" | custom-call | tf_op jit(solution)/shard_map/pallas_call | solution.py:168
  203.3 2.1 %multiply_subtract_fusion.1 = (f32[16,16,256]{2,1,0:T(8,128)}, f32[16,16,256]{2,1,0:T(8,128)}) fusion(f32[16,16,256]{2,1,0:T(8,128)S(1)} %get-tuple-element.58, f32[20,20,260]{2,1,0:T(8,128)} %get-tuple-element.64, f32[]{:T(128)S(6)} %div.42, f32[]{:T(128)S(6)} %div.43, f32[20,20,260]{2,1,0:T(8,128)S(1)} %copy-done.25, f32[16,16,256]{2,1,0:T(8,128)S(1)} %fusion.197, ...), kind=kLoop, calls=%fused_computation.329 | loop fusion | flops 589824 | bytes 1835020 | tf_op jit(solution)/shard_map/sub | solution.py:258
  (151 shorter events, 50.7 us)
Async XLA Ops:
  0.6 42.5 %copy-start = (f32[16,2048]{1,0:T(8,128)S(1)}, f32[16,2048]{1,0:T(8,128)}, u32[]{:S(2)}) copy-start(f32[16,2048]{1,0:T(8,128)} %param.19) | copy-start | bytes 393220
  0.6 21.8 %copy-start.10 = (f32[16,16,256]{2,1,0:T(8,128)S(1)}, f32[16,16,256]{2,1,0:T(8,128)}, u32[]{:S(2)}) copy-start(f32[16,16,256]{2,1,0:T(8,128)} %param.14) | copy-start | bytes 786436
  0.7 21.8 %copy-start.3 = (f32[16,16,16,256]{3,2,1,0:T(8,128)S(1)}, f32[16,16,16,256]{3,2,1,0:T(8,128)}, u32[]{:S(2)}) copy-start(f32[16,16,16,256]{3,2,1,0:T(8,128)} %param.18) | copy-start | bytes 12582916
  1.8 65.0 %copy-start.13 = (f32[1,16,16,256]{3,2,1,0:T(8,128)}, f32[1,16,16,256]{3,2,1,0:T(8,128)S(1)}, u32[]{:S(2)}) copy-start(f32[1,16,16,256]{3,2,1,0:T(8,128)S(1)} %fusion.203) | copy-start | bytes 786436
  3.3 9.0 %collective-permute-start.1 = (f32[6,3,16,256]{3,2,1,0:T(8,128)S(1)}, f32[6,3,16,256]{3,2,1,0:T(8,128)S(1)}, u32[]{:S(2)}, u32[]{:S(2)}) collective-permute-start(f32[6,3,16,256]{3,2,1,0:T(8,128)S(1)} %get-tuple-element.84), channel_id=1, source_target_pairs={{16,0},{32,16},{48,32},{64,48},{80,64},{96,80},{112,96},{17,1},{33... | collective-permute-start | bytes 884744 | tf_op jit(solution)/shard_map/ppermute | solution.py:27
  6.6 6.8 %collective-permute-start = (f32[6,3,16,256]{3,2,1,0:T(8,128)S(1)}, f32[6,3,16,256]{3,2,1,0:T(8,128)S(1)}, u32[]{:S(2)}, u32[]{:S(2)}) collective-permute-start(f32[6,3,16,256]{3,2,1,0:T(8,128)S(1)} %get-tuple-element.83), channel_id=1, source_target_pairs={{0,16},{16,32},{32,48},{48,64},{64,80},{80,96},{96,112},{1,17},{17... | collective-permute-start | bytes 884744 | tf_op jit(solution)/shard_map/ppermute | solution.py:26
  12.3 32.7 %copy-start.26 = (f32[6,3,16,256]{3,2,1,0:T(8,128)}, f32[6,3,16,256]{3,2,1,0:T(8,128)S(1)}, u32[]{:S(2)}) copy-start(f32[6,3,16,256]{3,2,1,0:T(8,128)S(1)} %collective-permute-done.1) | copy-start | bytes 884740
  13.5 31.6 %copy-start.28 = (f32[6,3,16,256]{3,2,1,0:T(8,128)}, f32[6,3,16,256]{3,2,1,0:T(8,128)S(1)}, u32[]{:S(2)}) copy-start(f32[6,3,16,256]{3,2,1,0:T(8,128)S(1)} %collective-permute-done) | copy-start | bytes 884740
  15.2 30.8 %copy-start.5 = (f32[3,16,16,256]{3,2,1,0:T(8,128)S(1)}, f32[3,16,16,256]{3,2,1,0:T(8,128)}, u32[]{:S(2)}) copy-start(f32[3,16,16,256]{3,2,1,0:T(8,128)} %param.15) | copy-start | bytes 2359300
  15.2 30.8 %copy-start.15 = (f32[16,16,256]{2,1,0:T(8,128)S(1)}, f32[16,16,256]{2,1,0:T(8,128)}, u32[]{:S(2)}) copy-start(f32[16,16,256]{2,1,0:T(8,128)} %param.16) | copy-start | bytes 786436
  15.3 28.0 %collective-permute-start.3 = (f32[6,22,3,256]{3,1,2,0:T(8,128)S(1)}, f32[6,22,3,256]{3,1,2,0:T(8,128)S(1)}, u32[]{:S(2)}, u32[]{:S(2)}) collective-permute-start(f32[6,22,3,256]{3,1,2,0:T(8,128)S(1)} %copy.26), channel_id=1, source_target_pairs={{4,0},{8,4},{12,8},{5,1},{9,5},{13,9},{6,2},{10,6},{14,10},{7,3},{... | collective-permute-start | bytes 1216520 | tf_op jit(solution)/shard_map/ppermute | solution.py:27
  17.5 26.1 %collective-permute-start.2 = (f32[6,22,3,256]{3,1,2,0:T(8,128)}, f32[6,22,3,256]{3,1,2,0:T(8,128)}, u32[]{:S(2)}, u32[]{:S(2)}) collective-permute-start(f32[6,22,3,256]{3,1,2,0:T(8,128)} %copy.25), channel_id=1, source_target_pairs={{0,4},{4,8},{8,12},{1,5},{5,9},{9,13},{2,6},{6,10},{10,14},{3,7},{... | collective-permute-start | bytes 1216520 | tf_op jit(solution)/shard_map/ppermute | solution.py:26
  50.8 11.1 %collective-permute-start.5 = (f32[6,22,22,3]{2,1,3,0:T(8,128)S(1)}, f32[6,22,22,3]{2,1,3,0:T(8,128)}, u32[]{:S(2)}, u32[]{:S(2)}) collective-permute-start(f32[6,22,22,3]{2,1,3,0:T(8,128)S(1)} %copy.30), channel_id=1, source_target_pairs={{1,0},{2,1},{3,2},{5,4},{6,5},{7,6},{9,8},{10,9},{11,10},{13,12},{... | collective-permute-start | bytes 104552 | tf_op jit(solution)/shard_map/ppermute | solution.py:27
  53.8 11.2 %collective-permute-start.4 = (f32[6,22,22,3]{2,1,3,0:T(8,128)}, f32[6,22,22,3]{2,1,3,0:T(8,128)}, u32[]{:S(2)}, u32[]{:S(2)}) collective-permute-start(f32[6,22,22,3]{2,1,3,0:T(8,128)} %copy.29), channel_id=1, source_target_pairs={{0,1},{1,2},{2,3},{4,5},{5,6},{6,7},{8,9},{9,10},{10,11},{12,13},{... | collective-permute-start | bytes 104552 | tf_op jit(solution)/shard_map/ppermute | solution.py:26
  87.1 5.8 %collective-permute-start.7 = (f32[3,16,256]{2,1,0:T(8,128)S(1)}, f32[3,16,256]{2,1,0:T(8,128)S(1)}, u32[]{:S(2)}, u32[]{:S(2)}) collective-permute-start(f32[3,16,256]{2,1,0:T(8,128)S(1)} %get-tuple-element.97), channel_id=1, source_target_pairs={{16,0},{32,16},{48,32},{64,48},{80,64},{96,80},{112,96},{17,1},{33... | collective-permute-start | bytes 147464 | tf_op jit(solution)/shard_map/ppermute | solution.py:27
  90.0 3.9 %collective-permute-start.6 = (f32[3,16,256]{2,1,0:T(8,128)S(1)}, f32[3,16,256]{2,1,0:T(8,128)S(1)}, u32[]{:S(2)}, u32[]{:S(2)}) collective-permute-start(f32[3,16,256]{2,1,0:T(8,128)S(1)} %get-tuple-element.96), channel_id=1, source_target_pairs={{0,16},{16,32},{32,48},{48,64},{64,80},{80,96},{96,112},{1,17},{17... | collective-permute-start | bytes 147464 | tf_op jit(solution)/shard_map/ppermute | solution.py:26
  94.5 6.6 %collective-permute-start.9 = (f32[22,3,256]{2,1,0:T(4,128)}, f32[22,3,256]{2,1,0:T(4,128)}, u32[]{:S(2)}, u32[]{:S(2)}) collective-permute-start(f32[22,3,256]{2,1,0:T(4,128)} %get-tuple-element.89), channel_id=1, source_target_pairs={{4,0},{8,4},{12,8},{5,1},{9,5},{13,9},{6,2},{10,6},{14,10},{7,3},{... | collective-permute-start | bytes 202760 | tf_op jit(solution)/shard_map/ppermute | solution.py:27
  95.8 6.6 %collective-permute-start.8 = (f32[22,3,256]{2,1,0:T(4,128)}, f32[22,3,256]{2,1,0:T(4,128)}, u32[]{:S(2)}, u32[]{:S(2)}) collective-permute-start(f32[22,3,256]{2,1,0:T(4,128)} %get-tuple-element.88), channel_id=1, source_target_pairs={{0,4},{4,8},{8,12},{1,5},{5,9},{9,13},{2,6},{6,10},{10,14},{3,7},{... | collective-permute-start | bytes 202760 | tf_op jit(solution)/shard_map/ppermute | solution.py:26
  103.7 9.6 %collective-permute-start.11 = (f32[22,22,3]{2,1,0:T(8,128)S(1)}, f32[22,22,3]{2,1,0:T(8,128)S(1)}, u32[]{:S(2)}, u32[]{:S(2)}) collective-permute-start(f32[22,22,3]{2,1,0:T(8,128)S(1)} %get-tuple-element.87), channel_id=1, source_target_pairs={{1,0},{2,1},{3,2},{5,4},{6,5},{7,6},{9,8},{10,9},{11,10},{13,12},{... | collective-permute-start | bytes 17432 | tf_op jit(solution)/shard_map/ppermute | solution.py:27
  105.0 9.2 %collective-permute-start.10 = (f32[22,22,3]{2,1,0:T(8,128)S(1)}, f32[22,22,3]{2,1,0:T(8,128)S(1)}, u32[]{:S(2)}, u32[]{:S(2)}) collective-permute-start(f32[22,22,3]{2,1,0:T(8,128)S(1)} %get-tuple-element.86), channel_id=1, source_target_pairs={{0,1},{1,2},{2,3},{4,5},{5,6},{6,7},{8,9},{9,10},{10,11},{12,13},{... | collective-permute-start | bytes 17432 | tf_op jit(solution)/shard_map/ppermute | solution.py:26
  119.5 26.6 %copy-start.36 = (f32[2048]{0:T(1024)S(1)}, f32[2048]{0:T(1024)}, u32[]{:S(2)}) copy-start(f32[2048]{0:T(1024)} %reshape.101) | copy-start | bytes 24580
  155.4 20.4 %copy-start.14 = (f32[1,16,16,256]{3,2,1,0:T(8,128)S(1)}, f32[1,16,16,256]{3,2,1,0:T(8,128)}, u32[]{:S(2)}) copy-start(f32[1,16,16,256]{3,2,1,0:T(8,128)} %copy-done.13) | copy-start | bytes 786436
  155.4 20.4 %copy-start.16 = (f32[16,16,256]{2,1,0:T(8,128)S(1)}, f32[16,16,256]{2,1,0:T(8,128)}, u32[]{:S(2)}) copy-start(f32[16,16,256]{2,1,0:T(8,128)} %param.16) | copy-start | bytes 786436
  158.9 18.5 %copy-start.9 = (f32[6,22,22,3]{3,2,1,0:T(8,128)S(1)}, f32[6,22,22,3]{3,2,1,0:T(8,128)}, u32[]{:S(2)}) copy-start(f32[6,22,22,3]{3,2,1,0:T(8,128)} %copy-done.8) | copy-start | bytes 104548
  158.9 18.5 %copy-start.12 = (f32[16,16,256]{2,1,0:T(8,128)S(1)}, f32[16,16,256]{2,1,0:T(8,128)}, u32[]{:S(2)}) copy-start(f32[16,16,256]{2,1,0:T(8,128)} %param.14) | copy-start | bytes 786436
  158.9 18.5 %copy-start.21 = (f32[6,22,3,256]{3,2,1,0:T(4,128)S(1)}, f32[6,22,3,256]{3,2,1,0:T(4,128)}, u32[]{:S(2)}) copy-start(f32[6,22,3,256]{3,2,1,0:T(4,128)} %copy-done.20) | copy-start | bytes 1216516
  159.0 14.3 %collective-permute-start.17 = (f32[16,16,1]{2,1,0:T(8,128)S(1)}, f32[16,16,1]{2,1,0:T(8,128)S(1)}, u32[]{:S(2)}, u32[]{:S(2)}) collective-permute-start(f32[16,16,1]{2,1,0:T(8,128)S(1)} %get-tuple-element.93), channel_id=1, source_target_pairs={{1,0},{2,1},{3,2},{5,4},{6,5},{7,6},{9,8},{10,9},{11,10},{13,12},{... | collective-permute-start | bytes 3080 | tf_op jit(solution)/shard_map/ppermute | solution.py:90
  160.6 16.1 %collective-permute-start.16 = (f32[16,1,256]{2,1,0:T(1,128)S(1)}, f32[16,1,256]{2,1,0:T(1,128)S(1)}, u32[]{:S(2)}, u32[]{:S(2)}) collective-permute-start(f32[16,1,256]{2,1,0:T(1,128)S(1)} %get-tuple-element.95), channel_id=1, source_target_pairs={{4,0},{8,4},{12,8},{5,1},{9,5},{13,9},{6,2},{10,6},{14,10},{7,3},{... | collective-permute-start | bytes 49160 | tf_op jit(solution)/shard_map/ppermute | solution.py:90
  161.9 14.8 %collective-permute-start.13 = (f32[16,1,256]{2,1,0:T(1,128)S(1)}, f32[16,1,256]{2,1,0:T(1,128)S(1)}, u32[]{:S(2)}, u32[]{:S(2)}) collective-permute-start(f32[16,1,256]{2,1,0:T(1,128)S(1)} %get-tuple-element.94), channel_id=1, source_target_pairs={{0,4},{4,8},{8,12},{1,5},{5,9},{9,13},{2,6},{6,10},{10,14},{3,7},{... | collective-permute-start | bytes 49160 | tf_op jit(solution)/shard_map/ppermute | solution.py:89
  165.9 10.8 %collective-permute-start.12 = (f32[16,16,1]{2,1,0:T(8,128)S(1)}, f32[16,16,1]{2,1,0:T(8,128)S(1)}, u32[]{:S(2)}, u32[]{:S(2)}) collective-permute-start(f32[16,16,1]{2,1,0:T(8,128)S(1)} %get-tuple-element.92), channel_id=1, source_target_pairs={{0,1},{1,2},{2,3},{4,5},{5,6},{6,7},{8,9},{9,10},{10,11},{12,13},{... | collective-permute-start | bytes 3080 | tf_op jit(solution)/shard_map/ppermute | solution.py:89
  169.9 6.8 %collective-permute-start.15 = (f32[1,16,256]{2,1,0:T(8,128)S(1)}, f32[1,16,256]{2,1,0:T(8,128)S(1)}, u32[]{:S(2)}, u32[]{:S(2)}) collective-permute-start(f32[1,16,256]{2,1,0:T(8,128)S(1)} %get-tuple-element.91), channel_id=1, source_target_pairs={{16,0},{32,16},{48,32},{64,48},{80,64},{96,80},{112,96},{17,1},{33... | collective-permute-start | bytes 49160 | tf_op jit(solution)/shard_map/ppermute | solution.py:90
  173.3 3.4 %collective-permute-start.14 = (f32[1,16,256]{2,1,0:T(8,128)S(1)}, f32[1,16,256]{2,1,0:T(8,128)S(1)}, u32[]{:S(2)}, u32[]{:S(2)}) collective-permute-start(f32[1,16,256]{2,1,0:T(8,128)S(1)} %get-tuple-element.90), channel_id=1, source_target_pairs={{0,16},{16,32},{32,48},{48,64},{64,80},{80,96},{96,112},{1,17},{17... | collective-permute-start | bytes 49160 | tf_op jit(solution)/shard_map/ppermute | solution.py:89
  (26 other events, 199.8 us)
where the time goes:
time: 207 us; the launch traced here: 205 us
  other arithmetic  63.2 us (31%)
  starting transfers between devices  52.5 us (25%)
  Pallas kernels  50.2 us (24%)
  local copies, waits for them, and re-layouts  22 us (11%)
  waiting for transfers between devices  9.51 us (5%)
  between operations  7.5 us (4%)
    pallas_call x3, Pallas kernels, gather_rows(): pl.pallas_call(functools.partial(gather_kernel, sizes), out_shape=jax.Sha...  50.2 us
    ppermute x6, starting transfers between devices, padded(): before = lax.ppermute(last, axis, up)  24.3 us
    mul x7, other arithmetic, jacobi(): free_box * guess  16.5 us
    concatenate x3, other arithmetic, padded(): value = jnp.concatenate([before, value, after], axis=dim)  11.6 us
    ppermute x6, starting transfers between devices, padded(): after = lax.ppermute(leading, axis, down)  11.5 us
    ppermute x3, starting transfers between devices, faces(): lax.ppermute(lax.slice_in_dim(field, length - 1, length, axis=dim), axis,...  10.4 us
    reduce_sum x2, other arithmetic, expand(): return jnp.sum(weights[:, None, None, None] * basis, axis=0)  6.5 us
    ppermute x3, starting transfers between devices, faces(): after = lax.ppermute(lax.slice_in_dim(field, 0, 1, axis=dim), axis, down)  6.27 us
  transfers between devices with their start and end apart: 18, of which 6 were waited for; matrix products, arithmetic and copies ran while one was open for 7% of the time, Pallas kernels for 9%

commit v1 on v0

--- a/solution.py
+++ b/solution.py
@@ -203,7 +203,7 @@
     sides = (("gx", 0), ("gy", 1), ("gz", 2))
     free = 1.0 - dirichlet.astype(jnp.float32)
     stacked = jnp.concatenate([conductance, storage[None], free[None], right_side[None]], axis=0)
-    wide = padded(stacked, (("gx", 1), ("gy", 2), ("gz", 3)), 3)
+    wide = padded(stacked, (("gz", 3), ("gx", 1), ("gy", 2)), 3)
     cond_wide = wide[:3]
     free_wide = wide[4]
     storage_wide = wide[3]
@@ -227,7 +227,7 @@
     coarse0 = project(basis, residual0)
     coarse0_all, _ = unpack(gather_rows(pack(coarse0, [])), vecs, 0)
     z0 = precondition(rhs_box0, residual0, coarse0_all)
-    near0 = padded(z0, sides, 3)
+    near0 = padded(z0, (("gz", 2), ("gx", 0), ("gy", 1)), 3)
     inner = (slice(1, -1),) * 3
     image0_box = stencil(free_wide * near0, cond_wide, near0[inner], storage_wide[inner], free_wide[inner])
     image0 = image0_box[2:-2, 2:-2, 2:-2]

time: 207 us -> 206 us (level)
  Pallas kernels: 50.2 us -> 55.8 us
  other arithmetic: 63.2 us -> 58.9 us
  local copies, waits for them, and re-layouts: 22 us -> 17.7 us
    pallas_call x3, Pallas kernels: 50.2 us -> 55.8 us  [gather_rows(): pl.pallas_call(functools.partial(gather_kernel, sizes), out_shape=jax.Sha...]
    concatenate x3 -> x2, other arithmetic: 11.6 us -> 7.68 us  [padded(): value = jnp.concatenate([before, value, after], axis=dim)]
    slice x5 -> x3, local copies, waits for them, and re-layouts: 4.32 us -> 0.65 us  [padded(): last = lax.slice_in_dim(value, length - width, length, axis=dim)]
    unnamed x80 -> x90, local copies, waits for them, and re-layouts: 1.55 us -> 4.58 us
    slice x2 -> x1, local copies, waits for them, and re-layouts: 2.44 us -> 0.01 us  [faces(): after = lax.ppermute(lax.slice_in_dim(field, 0, 1, axis=dim), axis, down)]
  transfers between devices with their start and end apart: 18 -> 18, of which waited for: 6 -> 7; matrix products, arithmetic and copies ran while one was open for 7% -> 6% of each run, Pallas kernels for 9% -> 12%
where the time goes in v1:
time: 206 us; the launch traced here: 204 us
  other arithmetic  58.9 us (29%)
  Pallas kernels  55.8 us (27%)
  starting transfers between devices  53.8 us (26%)
  local copies, waits for them, and re-layouts  17.7 us (9%)
  waiting for transfers between devices  10.1 us (5%)
  between operations  7.54 us (4%)
    pallas_call x3, Pallas kernels, gather_rows(): pl.pallas_call(functools.partial(gather_kernel, sizes), out_shape=jax.Sha...  55.8 us
    ppermute x6, starting transfers between devices, padded(): before = lax.ppermute(last, axis, up)  24.9 us
    mul x7, other arithmetic, jacobi(): free_box * guess  16.7 us
    ppermute x6, starting transfers between devices, padded(): after = lax.ppermute(leading, axis, down)  12.3 us
    ppermute x3, starting transfers between devices, faces(): lax.ppermute(lax.slice_in_dim(field, length - 1, length, axis=dim), axis,...  10.4 us
    concatenate x2, other arithmetic, padded(): value = jnp.concatenate([before, value, after], axis=dim)  7.68 us
    ppermute x3, starting transfers between devices, faces(): after = lax.ppermute(lax.slice_in_dim(field, 0, 1, axis=dim), axis, down)  6.27 us
    reduce_sum x2, other arithmetic, expand(): return jnp.sum(weights[:, None, None, None] * basis, axis=0)  5.87 us
  transfers between devices with their start and end apart: 18, of which 7 were waited for; matrix products, arithmetic and copies ran while one was open for 6% of the time, Pallas kernels for 12%

profile of v1, /device:TPU:1, one launch (start us, length us, event | category | flops | bytes accessed | tf_op | source)
XLA Modules:
  0.0 204.2 jit_solution(12210041817960153564)
XLA Ops:
  6.2 5.3 %collective-permute-start = (f32[6,16,16,3]{2,1,3,0:T(8,128)S(1)}, f32[6,16,16,3]{2,1,3,0:T(8,128)}, u32[]{:S(2)}, u32[]{:S(2)}) collective-permute-start(f32[6,16,16,3]{2,1,3,0:T(8,128)S(1)} %copy.62), channel_id=1, source_target_pairs={{0,1},{1,2},{2,3},{4,5},{5,6},{6,7},{8,9},{9,10},{10,11},{12,13},{... | collective-permute-start | bytes 55304 | tf_op jit(solution)/shard_map/ppermute | solution.py:26
  14.8 3.9 %collective-permute-start.3 = (f32[6,3,16,262]{3,2,1,0:T(8,128)S(1)}, f32[6,3,16,262]{3,2,1,0:T(8,128)S(1)}, u32[]{:S(2)}, u32[]{:S(2)}) collective-permute-start(f32[6,3,16,262]{3,2,1,0:T(8,128)S(1)} %get-tuple-element.82), channel_id=1, source_target_pairs={{16,0},{32,16},{48,32},{64,48},{80,64},{96,80},{112,96},{17,1},{33... | collective-permute-start | bytes 905480 | tf_op jit(solution)/shard_map/ppermute | solution.py:27
  18.7 3.3 %collective-permute-start.2 = (f32[6,3,16,262]{3,2,1,0:T(8,128)S(1)}, f32[6,3,16,262]{3,2,1,0:T(8,128)S(1)}, u32[]{:S(2)}, u32[]{:S(2)}) collective-permute-start(f32[6,3,16,262]{3,2,1,0:T(8,128)S(1)} %get-tuple-element.81), channel_id=1, source_target_pairs={{0,16},{16,32},{32,48},{48,64},{64,80},{80,96},{96,112},{1,17},{17... | collective-permute-start | bytes 905480 | tf_op jit(solution)/shard_map/ppermute | solution.py:26
  22.0 4.0 %collective-permute-done.3 = f32[6,3,16,262]{3,2,1,0:T(8,128)S(1)} collective-permute-done((f32[6,3,16,262]{3,2,1,0:T(8,128)S(1)}, f32[6,3,16,262]{3,2,1,0:T(8,128)S(1)}, u32[]{:S(2)}, u32[]{:S(2)}) %collective-permute-start.3) | collective-permute-done | bytes 301856 | tf_op jit(solution)/shard_map/ppermute | solution.py:27
  27.2 2.2 %pad_maximum_fusion.2 = f32[6,22,16,262]{3,2,1,0:T(8,128)S(1)} fusion(f32[6,3,16,262]{3,2,1,0:T(8,128)S(1)} %collective-permute-done.3, f32[6,16,16,3]{3,2,1,0:T(8,128)S(1)} %copy.47, f32[1,16,16,256]{3,2,1,0:T(8,128)S(1)} %bitcast.308, f32[1,16,16,256]{3,2,1,0:T(8,128)S(1)} %fusion.203, f32[1,16,16,256]{3,2,1,0:T(8,128)S(1)} %bitcast.313, ...), kind=kLoop, calls=%fused_computation.6 | loop fusion | flops 3873408 | bytes 4426752 | tf_op jit(solution)/shard_map/concatenate | solution.py:28
  33.0 5.0 %collective-permute-start.4 = (f32[6,22,3,262]{3,1,2,0:T(8,128)}, f32[6,22,3,262]{3,1,2,0:T(8,128)}, u32[]{:S(2)}, u32[]{:S(2)}) collective-permute-start(f32[6,22,3,262]{3,1,2,0:T(8,128)} %copy.64), channel_id=1, source_target_pairs={{0,4},{4,8},{8,12},{1,5},{5,9},{9,13},{2,6},{6,10},{10,14},{3,7},{... | collective-permute-start | bytes 1245032 | tf_op jit(solution)/shard_map/ppermute | solution.py:26
  39.1 24.0 %shard_map.77 = f32[128,1,128]{2,1,0:T(1,128)} custom-call(f32[1,1,128]{2,1,0:T(1,128)} %scatter.14.row_ref), custom_call_target="tpu_custom_call" | custom-call | tf_op jit(solution)/shard_map/pallas_call | solution.py:168
  64.2 2.8 %multiply_reduce_fusion.2 = f32[16,16,256]{2,1,0:T(8,128)S(1)} fusion(f32[16,16,16,256]{3,2,1,0:T(8,128)} %param.18, f32[16]{0:T(128)S(1)} %convolution_bitcast_fusion.1), kind=kLoop, calls=%fused_computation.4 | loop fusion | flops 2031616 | bytes 4456512 | tf_op jit(solution)/shard_map/reduce_sum | solution.py:77
  69.7 5.5 %pad_maximum_fusion = f32[6,22,22,262]{3,2,1,0:T(8,128)S(1)} fusion(f32[6,22,3,262]{3,2,1,0:T(4,128)S(1)} %copy.51, f32[6,3,16,262]{3,2,1,0:T(8,128)S(1)} %copy-done.27, f32[6,16,16,3]{3,2,1,0:T(8,128)S(1)} %copy.47, f32[1,16,16,256]{3,2,1,0:T(8,128)S(1)} %bitcast.309, f32[1,16,16,256]{3,2,1,0:T(8,128)S(1)} %fusion.203, f32[1,16,16,256]{3,2,1,0:T(8,128)S(1)} %bitcast.314, ...), kind=kLoop, calls=%fused_computation | loop fusion | flops 6847632 | bytes 6086784 | tf_op jit(solution)/shard_map/concatenate | solution.py:28
  76.9 2.4 %fusion.204 = (f32[20,20,260]{2,1,0:T(8,128)S(1)}, f32[20,20,260]{2,1,0:T(8,128)S(1)}, f32[20,20,260]{2,1,0:T(8,128)S(1)}, f32[20,20,260]{2,1,0:T(8,128)S(1)}) fusion(f32[6,22,22,262]{3,2,1,0:T(8,128)S(1)} %pad_maximum_fusion, f32[20,20,260]{2,1,0:T(8,128)S(1)} %broadcast_multiply_fusion, f32[3,20,20,260]{3,2,1,0:T(8,128)S(1)} %slice.612), kind=kLoop, calls=%fused_computation.335 | loop fusion | flops 3640000 | bytes 5824000 | tf_op jit(solution)/shard_map/mul | solution.py:67
  79.4 2.5 %fusion.210 = (f32[20,20,260]{2,1,0:T(8,128)S(1)}, f32[20,20,260]{2,1,0:T(8,128)S(1)}) fusion(f32[6,22,22,262]{3,2,1,0:T(8,128)S(1)} %pad_maximum_fusion, f32[20,20,260]{2,1,0:T(8,128)S(1)} %get-tuple-element.73, f32[20,20,260]{2,1,0:T(8,128)S(1)} %get-tuple-element.71, f32[3,20,20,260]{3,2,1,0:T(8,128)S(1)} %slice.612, f32[20,20,260]{2,1,0:T(8,128)S(1)} %get-tuple-element.72), kind=kLoop, calls=%fused_computation.355 | loop fusion | flops 3224000 | bytes 5824000 | tf_op jit(solution)/shard_map/mul | solution.py:67
  81.9 2.1 %fusion.209 = (f32[20,20,260]{2,1,0:T(8,128)S(1)}, f32[20,20,260]{2,1,0:T(8,128)S(1)}) fusion(f32[6,22,22,262]{3,2,1,0:T(8,128)S(1)} %pad_maximum_fusion, f32[20,20,260]{2,1,0:T(8,128)S(1)} %get-tuple-element.70, f32[20,20,260]{2,1,0:T(8,128)S(1)} %get-tuple-element.73, f32[20,20,260]{2,1,0:T(8,128)S(1)} %get-tuple-element.69, f32[3,20,20,260]{3,2,1,0:T(8,128)S(1)} %slice.612), kind=kLoop, calls=%fused_computation.354 | loop fusion | flops 2912000 | bytes 5824000 | tf_op jit(solution)/shard_map/mul | solution.py:67
  87.5 4.8 %collective-permute-start.6 = (f32[16,16,3]{2,1,0:T(8,128)S(1)}, f32[16,16,3]{2,1,0:T(8,128)S(1)}, u32[]{:S(2)}, u32[]{:S(2)}) collective-permute-start(f32[16,16,3]{2,1,0:T(8,128)S(1)} %get-tuple-element.96), channel_id=1, source_target_pairs={{0,1},{1,2},{2,3},{4,5},{5,6},{6,7},{8,9},{9,10},{10,11},{12,13},{... | collective-permute-start | bytes 9224 | tf_op jit(solution)/shard_map/ppermute | solution.py:26
  92.4 1.6 collective-permute-done.7
  96.2 3.1 %collective-permute-start.9 = (f32[3,16,262]{2,1,0:T(8,128)}, f32[3,16,262]{2,1,0:T(8,128)}, u32[]{:S(2)}, u32[]{:S(2)}) collective-permute-start(f32[3,16,262]{2,1,0:T(8,128)} %get-tuple-element.89), channel_id=1, source_target_pairs={{16,0},{32,16},{48,32},{64,48},{80,64},{96,80},{112,96},{17,1},{33... | collective-permute-start | bytes 150920 | tf_op jit(solution)/shard_map/ppermute | solution.py:27
  99.4 2.4 %collective-permute-start.8 = (f32[3,16,262]{2,1,0:T(8,128)}, f32[3,16,262]{2,1,0:T(8,128)}, u32[]{:S(2)}, u32[]{:S(2)}) collective-permute-start(f32[3,16,262]{2,1,0:T(8,128)} %get-tuple-element.88), channel_id=1, source_target_pairs={{0,16},{16,32},{32,48},{48,64},{64,80},{80,96},{96,112},{1,17},{17... | collective-permute-start | bytes 150920 | tf_op jit(solution)/shard_map/ppermute | solution.py:26
  106.4 4.0 %collective-permute-start.10 = (f32[22,3,262]{2,0,1:T(8,128)S(1)}, f32[22,3,262]{2,0,1:T(8,128)S(1)}, u32[]{:S(2)}, u32[]{:S(2)}) collective-permute-start(f32[22,3,262]{2,0,1:T(8,128)S(1)} %copy.66), channel_id=1, source_target_pairs={{0,4},{4,8},{8,12},{1,5},{5,9},{9,13},{2,6},{6,10},{10,14},{3,7},{... | collective-permute-start | bytes 207512 | tf_op jit(solution)/shard_map/ppermute | solution.py:26
  114.1 3.0 %fusion.159 = f32[20,20,260]{2,1,0:T(8,128)S(1)} fusion(f32[22,22,262]{2,1,0:T(8,128)S(1)} %get-tuple-element.66, f32[22,22,262]{2,1,0:T(8,128)S(1)} %get-tuple-element.65, f32[6,22,22,262]{3,2,1,0:T(8,128)S(1)} %copy-done.2, f32[22,22,262]{2,1,0:T(8,128)S(1)} %get-tuple-element.75, f32[22,22,262]{2,1,0:T(8,128)S(1)} %get-tuple-element.74), kind=kLoop, calls=%fused_computation.220 | loop fusion | flops 2392000 | bytes 7072000 | tf_op jit(solution)/shard_map/add | solution.py:54
  120.7 17.5 %shard_map.78 = f32[128,1,128]{2,1,0:T(1,128)} custom-call(f32[1,1,128]{2,1,0:T(1,128)} %copy-done.38), custom_call_target="tpu_custom_call" | custom-call | tf_op jit(solution)/shard_map/pallas_call | solution.py:168
  142.0 3.6 %fusion.205 = (f32[20,20,260]{2,1,0:T(8,128)}, f32[20,20,260]{2,1,0:T(8,128)}) fusion(f32[20,20,260]{2,1,0:T(8,128)} %copy-done.6, f32[20,20,260]{2,1,0:T(8,128)} %copy-done.20, f32[6,22,22,262]{3,2,1,0:T(8,128)} %copy-done.1, f32[20,20,260]{2,1,0:T(8,128)} %copy-done.24, f32[]{:T(128)S(6)} %div.37), kind=kLoop, calls=%fused_computation.336 | loop fusion | flops 624000 | bytes 2912004 | tf_op jit(solution)/shard_map/mul | solution.py:67
  145.9 3.0 %multiply_reduce_fusion = f32[16,16,256]{2,1,0:T(8,128)S(1)} fusion(f32[16,16,16,256]{3,2,1,0:T(8,128)} %param.18, f32[16]{0:T(128)S(1)} %convolution_bitcast_fusion), kind=kLoop, calls=%fused_computation.2 | loop fusion | flops 2031616 | bytes 4456512 | tf_op jit(solution)/shard_map/reduce_sum | solution.py:77
  149.0 4.0 %fusion.208 = (f32[20,20,260]{2,1,0:T(8,128)S(1)}, f32[20,20,260]{2,1,0:T(8,128)S(1)}) fusion(f32[6,22,22,262]{3,2,1,0:T(8,128)} %copy-done.1, f32[20,20,260]{2,1,0:T(8,128)S(1)} %copy-done.7, f32[20,20,260]{2,1,0:T(8,128)S(1)} %copy-done.19, f32[20,20,260]{2,1,0:T(8,128)S(1)} %copy-done.32, f32[3,20,20,260]{3,2,1,0:T(8,128)S(1)} %slice.612, ...), kind=kLoop, calls=%fused_computation.353 | loop fusion | flops 3224000 | bytes 5824000 | tf_op jit(solution)/shard_map/mul | solution.py:67
  153.1 1.8 fusion.207
  156.5 1.8 fusion.197
  161.4 4.0 %collective-permute-start.13 = (f32[16,1,256]{2,0,1:T(8,128)S(1)}, f32[16,1,256]{2,0,1:T(8,128)S(1)}, u32[]{:S(2)}, u32[]{:S(2)}) collective-permute-start(f32[16,1,256]{2,0,1:T(8,128)S(1)} %copy.56), channel_id=1, source_target_pairs={{0,4},{4,8},{8,12},{1,5},{5,9},{9,13},{2,6},{6,10},{10,14},{3,7},{... | collective-permute-start | bytes 49160 | tf_op jit(solution)/shard_map/ppermute | solution.py:89
  165.4 4.0 %collective-permute-start.12 = (f32[16,16,1]{2,1,0:T(8,128)S(1)}, f32[16,16,1]{2,1,0:T(8,128)S(1)}, u32[]{:S(2)}, u32[]{:S(2)}) collective-permute-start(f32[16,16,1]{2,1,0:T(8,128)S(1)} %get-tuple-element.92), channel_id=1, source_target_pairs={{0,1},{1,2},{2,3},{4,5},{5,6},{6,7},{8,9},{9,10},{10,11},{12,13},{... | collective-permute-start | bytes 3080 | tf_op jit(solution)/shard_map/ppermute | solution.py:89
  169.4 3.4 %collective-permute-start.15 = (f32[1,16,256]{2,1,0:T(8,128)S(1)}, f32[1,16,256]{2,1,0:T(8,128)S(1)}, u32[]{:S(2)}, u32[]{:S(2)}) collective-permute-start(f32[1,16,256]{2,1,0:T(8,128)S(1)} %get-tuple-element.91), channel_id=1, source_target_pairs={{16,0},{32,16},{48,32},{64,48},{80,64},{96,80},{112,96},{17,1},{33... | collective-permute-start | bytes 49160 | tf_op jit(solution)/shard_map/ppermute | solution.py:90
  172.9 2.4 %collective-permute-start.14 = (f32[1,16,256]{2,1,0:T(8,128)S(1)}, f32[1,16,256]{2,1,0:T(8,128)S(1)}, u32[]{:S(2)}, u32[]{:S(2)}) collective-permute-start(f32[1,16,256]{2,1,0:T(8,128)S(1)} %get-tuple-element.90), channel_id=1, source_target_pairs={{0,16},{16,32},{32,48},{48,64},{64,80},{80,96},{96,112},{1,17},{17... | collective-permute-start | bytes 49160 | tf_op jit(solution)/shard_map/ppermute | solution.py:89
  177.0 1.7 multiply_reduce_fusion.7
  178.6 2.6 %maximum_bitcast_fusion.1 = f32[1,1,4]{2,1,0:T(1,128)S(1)} fusion(f32[1]{0:T(128)} %bitcast.39, f32[1]{0:T(128)} %bitcast.38, f32[1]{0:T(128)} %bitcast.37, f32[1]{0:T(128)} %bitcast.29), kind=kLoop, calls=%fused_computation.349 | loop fusion | flops 12 | bytes 32 | tf_op jit(solution)/shard_map/broadcast_in_dim;broadcast_in_dim | solution.py:167
  181.8 14.3 %shard_map.79 = f32[128,1,128]{2,1,0:T(1,128)} custom-call(f32[1,1,128]{2,1,0:T(1,128)} %scatter.19.row_ref), custom_call_target="tpu_custom_call" | custom-call | tf_op jit(solution)/shard_map/pallas_call | solution.py:168
  202.2 2.1 %multiply_subtract_fusion.1 = (f32[16,16,256]{2,1,0:T(8,128)}, f32[16,16,256]{2,1,0:T(8,128)}) fusion(f32[16,16,256]{2,1,0:T(8,128)S(1)} %get-tuple-element.58, f32[20,20,260]{2,1,0:T(8,128)} %get-tuple-element.64, f32[]{:T(128)S(6)} %div.42, f32[]{:T(128)S(6)} %div.43, f32[20,20,260]{2,1,0:T(8,128)S(1)} %copy-done.25, f32[16,16,256]{2,1,0:T(8,128)S(1)} %fusion.197, ...), kind=kLoop, calls=%fused_computation.325 | loop fusion | flops 589824 | bytes 1835020 | tf_op jit(solution)/shard_map/sub | solution.py:258
  (161 shorter events, 48.5 us)
Async XLA Ops:
  0.6 63.3 %copy-start = (f32[16,2048]{1,0:T(8,128)S(1)}, f32[16,2048]{1,0:T(8,128)}, u32[]{:S(2)}) copy-start(f32[16,2048]{1,0:T(8,128)} %param.19) | copy-start | bytes 393220
  1.7 68.0 %copy-start.17 = (f32[1,16,16,256]{3,2,1,0:T(8,128)}, f32[1,16,16,256]{3,2,1,0:T(8,128)S(1)}, u32[]{:S(2)}) copy-start(f32[1,16,16,256]{3,2,1,0:T(8,128)S(1)} %fusion.203) | copy-start | bytes 786436
  4.2 7.2 %collective-permute-start.1 = (f32[6,16,16,3]{2,1,3,0:T(8,128)S(1)}, f32[6,16,16,3]{2,1,3,0:T(8,128)S(1)}, u32[]{:S(2)}, u32[]{:S(2)}) collective-permute-start(f32[6,16,16,3]{2,1,3,0:T(8,128)S(1)} %copy.63), channel_id=1, source_target_pairs={{1,0},{2,1},{3,2},{5,4},{6,5},{7,6},{9,8},{10,9},{11,10},{13,12},{... | collective-permute-start | bytes 55304 | tf_op jit(solution)/shard_map/ppermute | solution.py:27
  6.2 6.7 %collective-permute-start = (f32[6,16,16,3]{2,1,3,0:T(8,128)S(1)}, f32[6,16,16,3]{2,1,3,0:T(8,128)}, u32[]{:S(2)}, u32[]{:S(2)}) collective-permute-start(f32[6,16,16,3]{2,1,3,0:T(8,128)S(1)} %copy.62), channel_id=1, source_target_pairs={{0,1},{1,2},{2,3},{4,5},{5,6},{6,7},{8,9},{9,10},{10,11},{12,13},{... | collective-permute-start | bytes 55304 | tf_op jit(solution)/shard_map/ppermute | solution.py:26
  12.1 57.6 %copy-start.8 = (f32[6,16,16,3]{3,2,1,0:T(8,128)}, f32[6,16,16,3]{3,2,1,0:T(8,128)S(1)}, u32[]{:S(2)}) copy-start(f32[6,16,16,3]{3,2,1,0:T(8,128)S(1)} %copy.47) | copy-start | bytes 55300
  14.4 55.3 %copy-start.10 = (f32[6,16,16,3]{3,2,1,0:T(8,128)}, f32[6,16,16,3]{3,2,1,0:T(8,128)S(1)}, u32[]{:S(2)}) copy-start(f32[6,16,16,3]{3,2,1,0:T(8,128)S(1)} %copy.46) | copy-start | bytes 55300
  14.8 11.3 %collective-permute-start.3 = (f32[6,3,16,262]{3,2,1,0:T(8,128)S(1)}, f32[6,3,16,262]{3,2,1,0:T(8,128)S(1)}, u32[]{:S(2)}, u32[]{:S(2)}) collective-permute-start(f32[6,3,16,262]{3,2,1,0:T(8,128)S(1)} %get-tuple-element.82), channel_id=1, source_target_pairs={{16,0},{32,16},{48,32},{64,48},{80,64},{96,80},{112,96},{17,1},{33... | collective-permute-start | bytes 905480 | tf_op jit(solution)/shard_map/ppermute | solution.py:27
  18.7 8.6 %collective-permute-start.2 = (f32[6,3,16,262]{3,2,1,0:T(8,128)S(1)}, f32[6,3,16,262]{3,2,1,0:T(8,128)S(1)}, u32[]{:S(2)}, u32[]{:S(2)}) collective-permute-start(f32[6,3,16,262]{3,2,1,0:T(8,128)S(1)} %get-tuple-element.81), channel_id=1, source_target_pairs={{0,16},{16,32},{32,48},{48,64},{64,80},{80,96},{96,112},{1,17},{17... | collective-permute-start | bytes 905480 | tf_op jit(solution)/shard_map/ppermute | solution.py:26
  30.6 36.4 %collective-permute-start.5 = (f32[6,22,3,262]{3,1,2,0:T(8,128)}, f32[6,22,3,262]{3,1,2,0:T(8,128)}, u32[]{:S(2)}, u32[]{:S(2)}) collective-permute-start(f32[6,22,3,262]{3,1,2,0:T(8,128)} %copy.65), channel_id=1, source_target_pairs={{4,0},{8,4},{12,8},{5,1},{9,5},{13,9},{6,2},{10,6},{14,10},{7,3},{... | collective-permute-start | bytes 1245032 | tf_op jit(solution)/shard_map/ppermute | solution.py:27
  33.0 35.4 %collective-permute-start.4 = (f32[6,22,3,262]{3,1,2,0:T(8,128)}, f32[6,22,3,262]{3,1,2,0:T(8,128)}, u32[]{:S(2)}, u32[]{:S(2)}) collective-permute-start(f32[6,22,3,262]{3,1,2,0:T(8,128)} %copy.64), channel_id=1, source_target_pairs={{0,4},{4,8},{8,12},{1,5},{5,9},{9,13},{2,6},{6,10},{10,14},{3,7},{... | collective-permute-start | bytes 1245032 | tf_op jit(solution)/shard_map/ppermute | solution.py:26
  86.2 7.7 %collective-permute-start.7 = (f32[16,16,3]{2,1,0:T(8,128)S(1)}, f32[16,16,3]{2,1,0:T(8,128)S(1)}, u32[]{:S(2)}, u32[]{:S(2)}) collective-permute-start(f32[16,16,3]{2,1,0:T(8,128)S(1)} %get-tuple-element.97), channel_id=1, source_target_pairs={{1,0},{2,1},{3,2},{5,4},{6,5},{7,6},{9,8},{10,9},{11,10},{13,12},{... | collective-permute-start | bytes 9224 | tf_op jit(solution)/shard_map/ppermute | solution.py:27
  87.5 7.3 %collective-permute-start.6 = (f32[16,16,3]{2,1,0:T(8,128)S(1)}, f32[16,16,3]{2,1,0:T(8,128)S(1)}, u32[]{:S(2)}, u32[]{:S(2)}) collective-permute-start(f32[16,16,3]{2,1,0:T(8,128)S(1)} %get-tuple-element.96), channel_id=1, source_target_pairs={{0,1},{1,2},{2,3},{4,5},{5,6},{6,7},{8,9},{9,10},{10,11},{12,13},{... | collective-permute-start | bytes 9224 | tf_op jit(solution)/shard_map/ppermute | solution.py:26
  96.2 6.5 %collective-permute-start.9 = (f32[3,16,262]{2,1,0:T(8,128)}, f32[3,16,262]{2,1,0:T(8,128)}, u32[]{:S(2)}, u32[]{:S(2)}) collective-permute-start(f32[3,16,262]{2,1,0:T(8,128)} %get-tuple-element.89), channel_id=1, source_target_pairs={{16,0},{32,16},{48,32},{64,48},{80,64},{96,80},{112,96},{17,1},{33... | collective-permute-start | bytes 150920 | tf_op jit(solution)/shard_map/ppermute | solution.py:27
  99.4 4.1 %collective-permute-start.8 = (f32[3,16,262]{2,1,0:T(8,128)}, f32[3,16,262]{2,1,0:T(8,128)}, u32[]{:S(2)}, u32[]{:S(2)}) collective-permute-start(f32[3,16,262]{2,1,0:T(8,128)} %get-tuple-element.88), channel_id=1, source_target_pairs={{0,16},{16,32},{32,48},{48,64},{64,80},{80,96},{96,112},{1,17},{17... | collective-permute-start | bytes 150920 | tf_op jit(solution)/shard_map/ppermute | solution.py:26
  105.0 6.8 %collective-permute-start.11 = (f32[22,3,262]{2,0,1:T(8,128)S(1)}, f32[22,3,262]{2,0,1:T(8,128)S(1)}, u32[]{:S(2)}, u32[]{:S(2)}) collective-permute-start(f32[22,3,262]{2,0,1:T(8,128)S(1)} %copy.67), channel_id=1, source_target_pairs={{4,0},{8,4},{12,8},{5,1},{9,5},{13,9},{6,2},{10,6},{14,10},{7,3},{... | collective-permute-start | bytes 207512 | tf_op jit(solution)/shard_map/ppermute | solution.py:27
  106.4 6.4 %collective-permute-start.10 = (f32[22,3,262]{2,0,1:T(8,128)S(1)}, f32[22,3,262]{2,0,1:T(8,128)S(1)}, u32[]{:S(2)}, u32[]{:S(2)}) collective-permute-start(f32[22,3,262]{2,0,1:T(8,128)S(1)} %copy.66), channel_id=1, source_target_pairs={{0,4},{4,8},{8,12},{1,5},{5,9},{9,13},{2,6},{6,10},{10,14},{3,7},{... | collective-permute-start | bytes 207512 | tf_op jit(solution)/shard_map/ppermute | solution.py:26
  154.9 20.4 %copy-start.16 = (f32[16,16,256]{2,1,0:T(8,128)S(1)}, f32[16,16,256]{2,1,0:T(8,128)}, u32[]{:S(2)}) copy-start(f32[16,16,256]{2,1,0:T(8,128)} %param.16) | copy-start | bytes 786436
  154.9 20.4 %copy-start.18 = (f32[1,16,16,256]{3,2,1,0:T(8,128)S(1)}, f32[1,16,16,256]{3,2,1,0:T(8,128)}, u32[]{:S(2)}) copy-start(f32[1,16,16,256]{3,2,1,0:T(8,128)} %copy-done.17) | copy-start | bytes 786436
  158.4 18.5 %copy-start.9 = (f32[6,16,16,3]{3,2,1,0:T(8,128)S(1)}, f32[6,16,16,3]{3,2,1,0:T(8,128)}, u32[]{:S(2)}) copy-start(f32[6,16,16,3]{3,2,1,0:T(8,128)} %copy-done.8) | copy-start | bytes 55300
  158.4 18.5 %copy-start.11 = (f32[6,16,16,3]{3,2,1,0:T(8,128)S(1)}, f32[6,16,16,3]{3,2,1,0:T(8,128)}, u32[]{:S(2)}) copy-start(f32[6,16,16,3]{3,2,1,0:T(8,128)} %copy-done.10) | copy-start | bytes 55300
  158.4 18.5 %copy-start.14 = (f32[16,16,256]{2,1,0:T(8,128)S(1)}, f32[16,16,256]{2,1,0:T(8,128)}, u32[]{:S(2)}) copy-start(f32[16,16,256]{2,1,0:T(8,128)} %param.14) | copy-start | bytes 786436
  158.5 18.5 %copy-start.23 = (f32[6,22,3,262]{3,2,1,0:T(4,128)S(1)}, f32[6,22,3,262]{3,2,1,0:T(4,128)}, u32[]{:S(2)}) copy-start(f32[6,22,3,262]{3,2,1,0:T(4,128)} %copy-done.22) | copy-start | bytes 1245028
  158.5 18.5 %copy-start.25 = (f32[20,20,260]{2,1,0:T(8,128)S(1)}, f32[20,20,260]{2,1,0:T(8,128)}, u32[]{:S(2)}) copy-start(f32[20,20,260]{2,1,0:T(8,128)} %copy-done.24) | copy-start | bytes 1248004
  158.5 18.5 %copy-start.28 = (f32[6,3,16,262]{3,2,1,0:T(8,128)S(1)}, f32[6,3,16,262]{3,2,1,0:T(8,128)}, u32[]{:S(2)}) copy-start(f32[6,3,16,262]{3,2,1,0:T(8,128)} %copy-done.26) | copy-start | bytes 905476
  158.5 18.5 %copy-start.31 = (f32[6,3,16,262]{3,2,1,0:T(8,128)S(1)}, f32[6,3,16,262]{3,2,1,0:T(8,128)}, u32[]{:S(2)}) copy-start(f32[6,3,16,262]{3,2,1,0:T(8,128)} %copy-done.29) | copy-start | bytes 905476
  158.5 18.5 %copy-start.37 = (s32[16,16,256]{2,1,0:T(8,128)S(1)}, s32[16,16,256]{2,1,0:T(8,128)}, u32[]{:S(2)}) copy-start(s32[16,16,256]{2,1,0:T(8,128)} %param.17) | copy-start | bytes 786436
  158.5 14.3 %collective-permute-start.16 = (f32[16,1,256]{2,0,1:T(8,128)S(1)}, f32[16,1,256]{2,0,1:T(8,128)S(1)}, u32[]{:S(2)}, u32[]{:S(2)}) collective-permute-start(f32[16,1,256]{2,0,1:T(8,128)S(1)} %copy.57), channel_id=1, source_target_pairs={{4,0},{8,4},{12,8},{5,1},{9,5},{13,9},{6,2},{10,6},{14,10},{7,3},{... | collective-permute-start | bytes 49160 | tf_op jit(solution)/shard_map/ppermute | solution.py:90
  160.1 16.1 %collective-permute-start.17 = (f32[16,16,1]{2,1,0:T(8,128)S(1)}, f32[16,16,1]{2,1,0:T(8,128)S(1)}, u32[]{:S(2)}, u32[]{:S(2)}) collective-permute-start(f32[16,16,1]{2,1,0:T(8,128)S(1)} %get-tuple-element.93), channel_id=1, source_target_pairs={{1,0},{2,1},{3,2},{5,4},{6,5},{7,6},{9,8},{10,9},{11,10},{13,12},{... | collective-permute-start | bytes 3080 | tf_op jit(solution)/shard_map/ppermute | solution.py:90
  161.4 14.8 %collective-permute-start.13 = (f32[16,1,256]{2,0,1:T(8,128)S(1)}, f32[16,1,256]{2,0,1:T(8,128)S(1)}, u32[]{:S(2)}, u32[]{:S(2)}) collective-permute-start(f32[16,1,256]{2,0,1:T(8,128)S(1)} %copy.56), channel_id=1, source_target_pairs={{0,4},{4,8},{8,12},{1,5},{5,9},{9,13},{2,6},{6,10},{10,14},{3,7},{... | collective-permute-start | bytes 49160 | tf_op jit(solution)/shard_map/ppermute | solution.py:89
  165.4 10.8 %collective-permute-start.12 = (f32[16,16,1]{2,1,0:T(8,128)S(1)}, f32[16,16,1]{2,1,0:T(8,128)S(1)}, u32[]{:S(2)}, u32[]{:S(2)}) collective-permute-start(f32[16,16,1]{2,1,0:T(8,128)S(1)} %get-tuple-element.92), channel_id=1, source_target_pairs={{0,1},{1,2},{2,3},{4,5},{5,6},{6,7},{8,9},{9,10},{10,11},{12,13},{... | collective-permute-start | bytes 3080 | tf_op jit(solution)/shard_map/ppermute | solution.py:89
  169.4 6.8 %collective-permute-start.15 = (f32[1,16,256]{2,1,0:T(8,128)S(1)}, f32[1,16,256]{2,1,0:T(8,128)S(1)}, u32[]{:S(2)}, u32[]{:S(2)}) collective-permute-start(f32[1,16,256]{2,1,0:T(8,128)S(1)} %get-tuple-element.91), channel_id=1, source_target_pairs={{16,0},{32,16},{48,32},{64,48},{80,64},{96,80},{112,96},{17,1},{33... | collective-permute-start | bytes 49160 | tf_op jit(solution)/shard_map/ppermute | solution.py:90
  172.9 3.4 %collective-permute-start.14 = (f32[1,16,256]{2,1,0:T(8,128)S(1)}, f32[1,16,256]{2,1,0:T(8,128)S(1)}, u32[]{:S(2)}, u32[]{:S(2)}) collective-permute-start(f32[1,16,256]{2,1,0:T(8,128)S(1)} %get-tuple-element.90), channel_id=1, source_target_pairs={{0,16},{16,32},{32,48},{48,64},{64,80},{80,96},{96,112},{1,17},{17... | collective-permute-start | bytes 49160 | tf_op jit(solution)/shard_map/ppermute | solution.py:89
  (27 other events, 152.2 us)

commit v2 on v1

--- a/solution.py
+++ b/solution.py
@@ -80,20 +80,84 @@
 LANES = 128
 
 
+def face_kernel(sizes, ins_outs_held, *refs):
+    count = 6
+    ins, outs, held = refs[:count], refs[count:2 * count], refs[2 * count:3 * count]
+    send_sem, recv_sem, local_sem = refs[3 * count:]
+    here = [lax.axis_index(name) for name in ("gx", "gy", "gz")]
+
+    def toward(dim, step):
+        return tuple(lax.rem(i + step + n, n) if d == dim else i for d, (i, n) in enumerate(zip(here, sizes)))
+
+    barrier = pltpu.get_barrier_semaphore()
+    for dim in range(3):
+        for step in (-1, 1):
+            pl.semaphore_signal(barrier, inc=1, device_id=toward(dim, step), device_id_type=MESH_ID)
+    pl.semaphore_wait(barrier, count)
+    sent = []
+    for dim in range(3):
+        for side, step in ((0, -1), (1, 1)):
+            i = 2 * dim + side
+            j = 2 * dim + 1 - side
+            copy = pltpu.make_async_remote_copy(
+                src_ref=ins[i],
+                dst_ref=held[j],
+                send_sem=send_sem.at[i],
+                recv_sem=recv_sem.at[j],
+                device_id=toward(dim, step),
+                device_id_type=MESH_ID,
+            )
+            copy.start()
+            sent.append(copy)
+    for dim in range(3):
+        for side, step in ((0, -1), (1, 1)):
+            j = 2 * dim + side
+            i = 2 * dim + 1 - side
+            pltpu.make_async_remote_copy(
+                src_ref=ins[i],
+                dst_ref=held[j],
+                send_sem=send_sem.at[i],
+                recv_sem=recv_sem.at[j],
+                device_id=toward(dim, step),
+                device_id_type=MESH_ID,
+            ).wait_recv()
+    for copy in sent:
+        copy.wait_send()
+    local = []
+    for j in range(count):
+        copy = pltpu.make_async_copy(held[j], outs[j], local_sem.at[j])
+        copy.start()
+        local.append(copy)
+    for copy in local:
+        copy.wait()
+
+
 def faces(field):
-    pieces = []
-    for dim, axis in enumerate(("gx", "gy", "gz")):
-        count, length = (lax.axis_size(axis), field.shape[dim])
-        up = [(i, i + 1) for i in range(count - 1)]
-        down = [(j, i) for i, j in up]
-        before = lax.ppermute(lax.slice_in_dim(field, length - 1, length, axis=dim), axis, up)
-        after = lax.ppermute(lax.slice_in_dim(field, 0, 1, axis=dim), axis, down)
-        pieces.append((before, after))
+    names = ("gx", "gy", "gz")
+    sizes = tuple(lax.axis_size(name) for name in names)
+    here = [lax.axis_index(name) for name in names]
+    slabs = []
+    for dim in range(3):
+        length = field.shape[dim]
+        slabs.append(lax.slice_in_dim(field, 0, 1, axis=dim))
+        slabs.append(lax.slice_in_dim(field, length - 1, length, axis=dim))
+    spec = pl.BlockSpec(memory_space=pltpu.VMEM)
+    got = pl.pallas_call(
+        functools.partial(face_kernel, sizes, None),
+        out_shape=[jax.ShapeDtypeStruct(s.shape, s.dtype) for s in slabs],
+        in_specs=[spec] * 6,
+        out_specs=[spec] * 6,
+        scratch_shapes=[pltpu.VMEM(s.shape, s.dtype) for s in slabs] + [pltpu.SemaphoreType.DMA((6,))] * 3,
+        compiler_params=pltpu.CompilerParams(collective_id=1, has_side_effects=True),
+    )(*slabs)
     result = field
     for dim in range(3):
-        before, after = pieces[dim]
+        below = jnp.where(here[dim] > 0, got[2 * dim], 0.0)
+        above = jnp.where(here[dim] < sizes[dim] - 1, got[2 * dim + 1], 0.0)
         widths = [(1, 1) if d < dim else (0, 0) for d in range(3)]
-        result = jnp.concatenate([jnp.pad(before, widths), result, jnp.pad(after, widths)], axis=dim)
+        below = jnp.pad(below, widths)
+        above = jnp.pad(above, widths)
+        result = jnp.concatenate([below, result, above], axis=dim)
     return result
 
 

time: 206 us -> 211 us (1.024)
  starting transfers between devices: 53.8 us -> 37.3 us
  other arithmetic: 58.9 us -> 69.1 us
  Pallas kernels: 55.8 us -> 64.1 us
  local copies, waits for them, and re-layouts: 17.7 us -> 22.3 us
    ppermute x6 -> x0, starting transfers between devices: 16.6 us -> none  [the longest x3 10.4 us: faces(): lax.ppermute(lax.slice_in_dim(field, length - 1, length, axis=dim), axis,...]
    pallas_call x0 -> x1, Pallas kernels: none -> 7.42 us  [faces(): pl.pallas_call(functools.partial(face_kernel, sizes, None), out_shape=[ja...]
    slice x5, local copies, waits for them, and re-layouts: 0.13 us -> 4.78 us  [the longest x2 2.7 us: padded(): leading = lax.slice_in_dim(value, 0, width, axis=dim)]
    unnamed x90 -> x80, local copies, waits for them, and re-layouts: 4.58 us -> 0.71 us
    slice x3 -> x5, local copies, waits for them, and re-layouts: 0.65 us -> 4.49 us  [padded(): last = lax.slice_in_dim(value, length - width, length, axis=dim)]
    select_n x0 -> x3, other arithmetic: none -> 2.45 us  [faces(): above = jnp.where(here[dim] < sizes[dim] - 1, got[2 * dim + 1], 0.0)]
    reduce_sum x1, other arithmetic: 1.65 us -> 3.92 us  [shards(): jnp.sum(residual1 * z1)]
    concatenate x2, other arithmetic: 2.38 us -> 4.64 us  [shards(): jnp.concatenate([conductance, storage[None], free[None], right_side[None]...]
  transfers between devices with their start and end apart: 18 -> 12, of which waited for: 7 -> 6; matrix products, arithmetic and copies ran while one was open for 6% -> 7% of each run, Pallas kernels for 12% -> 11%
where the time goes in v2:
time: 211 us; the launch traced here: 209 us
  other arithmetic  69.1 us (33%)
  Pallas kernels  64.1 us (30%)
  starting transfers between devices  37.3 us (18%)
  local copies, waits for them, and re-layouts  22.3 us (11%)
  waiting for transfers between devices  8.93 us (4%)
  between operations  7.19 us (3%)
    pallas_call x3, Pallas kernels, gather_rows(): pl.pallas_call(functools.partial(gather_kernel, sizes), out_shape=jax.Sha...  56.7 us
    ppermute x6, starting transfers between devices, padded(): before = lax.ppermute(last, axis, up)  24.9 us
    mul x7, other arithmetic, jacobi(): free_box * guess  16.9 us
    ppermute x6, starting transfers between devices, padded(): after = lax.ppermute(leading, axis, down)  12.4 us
    concatenate x2, other arithmetic, padded(): value = jnp.concatenate([before, value, after], axis=dim)  7.68 us
    pallas_call x1, Pallas kernels, faces(): pl.pallas_call(functools.partial(face_kernel, sizes, None), out_shape=[ja...  7.42 us
    reduce_sum x2, other arithmetic, expand(): return jnp.sum(weights[:, None, None, None] * basis, axis=0)  5.87 us
    ppermute x6, waiting for transfers between devices, padded(): after = lax.ppermute(leading, axis, down)  5.64 us
  transfers between devices with their start and end apart: 12, of which 6 were waited for; matrix products, arithmetic and copies ran while one was open for 7% of the time, Pallas kernels for 11%

profile of v2, /device:TPU:1, one launch (start us, length us, event | category | flops | bytes accessed | tf_op | source)
XLA Modules:
  0.0 209.3 jit_solution(11567718629929736147)
XLA Ops:
  4.6 1.8 copy.9
  7.7 1.8 copy.8
  9.5 5.2 %collective-permute-start = (f32[6,16,16,3]{2,1,3,0:T(8,128)S(1)}, f32[6,16,16,3]{2,1,3,0:T(8,128)}, u32[]{:S(2)}, u32[]{:S(2)}) collective-permute-start(f32[6,16,16,3]{2,1,3,0:T(8,128)S(1)} %copy.8), channel_id=1, source_target_pairs={{0,1},{1,2},{2,3},{4,5},{5,6},{6,7},{8,9},{9,10},{10,11},{12,13},{... | collective-permute-start | bytes 55304 | tf_op jit(solution)/shard_map/ppermute | solution.py:26
  18.2 3.9 %collective-permute-start.3 = (f32[6,3,16,262]{3,2,1,0:T(8,128)S(1)}, f32[6,3,16,262]{3,2,1,0:T(8,128)S(1)}, u32[]{:S(2)}, u32[]{:S(2)}) collective-permute-start(f32[6,3,16,262]{3,2,1,0:T(8,128)S(1)} %get-tuple-element.92), channel_id=1, source_target_pairs={{16,0},{32,16},{48,32},{64,48},{80,64},{96,80},{112,96},{17,1},{33... | collective-permute-start | bytes 905480 | tf_op jit(solution)/shard_map/ppermute | solution.py:27
  22.0 3.3 %collective-permute-start.2 = (f32[6,3,16,262]{3,2,1,0:T(8,128)S(1)}, f32[6,3,16,262]{3,2,1,0:T(8,128)S(1)}, u32[]{:S(2)}, u32[]{:S(2)}) collective-permute-start(f32[6,3,16,262]{3,2,1,0:T(8,128)S(1)} %get-tuple-element.91), channel_id=1, source_target_pairs={{0,16},{16,32},{32,48},{48,64},{64,80},{80,96},{96,112},{1,17},{17... | collective-permute-start | bytes 905480 | tf_op jit(solution)/shard_map/ppermute | solution.py:26
  25.4 4.0 %collective-permute-done.3 = f32[6,3,16,262]{3,2,1,0:T(8,128)S(1)} collective-permute-done((f32[6,3,16,262]{3,2,1,0:T(8,128)S(1)}, f32[6,3,16,262]{3,2,1,0:T(8,128)S(1)}, u32[]{:S(2)}, u32[]{:S(2)}) %collective-permute-start.3) | collective-permute-done | bytes 301856 | tf_op jit(solution)/shard_map/ppermute | solution.py:27
  30.6 2.2 %pad_maximum_fusion.2 = f32[6,22,16,262]{3,2,1,0:T(8,128)S(1)} fusion(f32[6,3,16,262]{3,2,1,0:T(8,128)S(1)} %collective-permute-done.3, f32[6,16,16,3]{3,2,1,0:T(8,128)S(1)} %copy.11, f32[1,16,16,256]{3,2,1,0:T(8,128)S(1)} %bitcast.310, f32[1,16,16,256]{3,2,1,0:T(8,128)S(1)} %fusion.203, f32[1,16,16,256]{3,2,1,0:T(8,128)S(1)} %bitcast.315, ...), kind=kLoop, calls=%fused_computation.6 | loop fusion | flops 3873408 | bytes 4426752 | tf_op jit(solution)/shard_map/concatenate | solution.py:28
  36.4 5.0 %collective-permute-start.4 = (f32[6,22,3,262]{3,1,2,0:T(8,128)}, f32[6,22,3,262]{3,1,2,0:T(8,128)}, u32[]{:S(2)}, u32[]{:S(2)}) collective-permute-start(f32[6,22,3,262]{3,1,2,0:T(8,128)} %copy.12), channel_id=1, source_target_pairs={{0,4},{4,8},{8,12},{1,5},{5,9},{9,13},{2,6},{6,10},{10,14},{3,7},{... | collective-permute-start | bytes 1245032 | tf_op jit(solution)/shard_map/ppermute | solution.py:26
  42.5 24.0 %shard_map.77 = f32[128,1,128]{2,1,0:T(1,128)} custom-call(f32[1,1,128]{2,1,0:T(1,128)} %scatter.14.row_ref), custom_call_target="tpu_custom_call" | custom-call | tf_op jit(solution)/shard_map/pallas_call | solution.py:232
  67.6 2.8 %multiply_reduce_fusion.2 = f32[16,16,256]{2,1,0:T(8,128)S(1)} fusion(f32[16,16,16,256]{3,2,1,0:T(8,128)} %param.18, f32[16]{0:T(128)S(1)} %convolution_bitcast_fusion.1), kind=kLoop, calls=%fused_computation.4 | loop fusion | flops 2031616 | bytes 4456512 | tf_op jit(solution)/shard_map/reduce_sum | solution.py:77
  73.1 5.5 %pad_maximum_fusion = f32[6,22,22,262]{3,2,1,0:T(8,128)S(1)} fusion(f32[6,22,3,262]{3,2,1,0:T(4,128)S(1)} %copy.15, f32[6,3,16,262]{3,2,1,0:T(8,128)S(1)} %copy-done.27, f32[6,16,16,3]{3,2,1,0:T(8,128)S(1)} %copy.11, f32[1,16,16,256]{3,2,1,0:T(8,128)S(1)} %bitcast.311, f32[1,16,16,256]{3,2,1,0:T(8,128)S(1)} %fusion.203, f32[1,16,16,256]{3,2,1,0:T(8,128)S(1)} %bitcast.316, ...), kind=kLoop, calls=%fused_computation | loop fusion | flops 6847632 | bytes 6086784 | tf_op jit(solution)/shard_map/concatenate | solution.py:28
  80.3 2.4 %fusion.204 = (f32[20,20,260]{2,1,0:T(8,128)S(1)}, f32[20,20,260]{2,1,0:T(8,128)S(1)}, f32[20,20,260]{2,1,0:T(8,128)S(1)}, f32[20,20,260]{2,1,0:T(8,128)S(1)}) fusion(f32[6,22,22,262]{3,2,1,0:T(8,128)S(1)} %pad_maximum_fusion, f32[20,20,260]{2,1,0:T(8,128)S(1)} %broadcast_multiply_fusion, f32[3,20,20,260]{3,2,1,0:T(8,128)S(1)} %slice.612), kind=kLoop, calls=%fused_computation.335 | loop fusion | flops 3640000 | bytes 5824000 | tf_op jit(solution)/shard_map/mul | solution.py:67
  82.8 2.5 %fusion.210 = (f32[20,20,260]{2,1,0:T(8,128)S(1)}, f32[20,20,260]{2,1,0:T(8,128)S(1)}) fusion(f32[6,22,22,262]{3,2,1,0:T(8,128)S(1)} %pad_maximum_fusion, f32[20,20,260]{2,1,0:T(8,128)S(1)} %get-tuple-element.83, f32[20,20,260]{2,1,0:T(8,128)S(1)} %get-tuple-element.81, f32[3,20,20,260]{3,2,1,0:T(8,128)S(1)} %slice.612, f32[20,20,260]{2,1,0:T(8,128)S(1)} %get-tuple-element.82), kind=kLoop, calls=%fused_computation.361 | loop fusion | flops 3224000 | bytes 5824000 | tf_op jit(solution)/shard_map/mul | solution.py:67
  85.3 2.1 fusion.209
  90.9 4.8 %collective-permute-start.6 = (f32[16,16,3]{2,1,0:T(8,128)S(1)}, f32[16,16,3]{2,1,0:T(8,128)S(1)}, u32[]{:S(2)}, u32[]{:S(2)}) collective-permute-start(f32[16,16,3]{2,1,0:T(8,128)S(1)} %get-tuple-element.106), channel_id=1, source_target_pairs={{0,1},{1,2},{2,3},{4,5},{5,6},{6,7},{8,9},{9,10},{10,11},{12,13},{... | collective-permute-start | bytes 9224 | tf_op jit(solution)/shard_map/ppermute | solution.py:26
  99.0 3.1 %collective-permute-start.9 = (f32[3,16,262]{2,1,0:T(8,128)}, f32[3,16,262]{2,1,0:T(8,128)}, u32[]{:S(2)}, u32[]{:S(2)}) collective-permute-start(f32[3,16,262]{2,1,0:T(8,128)} %get-tuple-element.99), channel_id=1, source_target_pairs={{16,0},{32,16},{48,32},{64,48},{80,64},{96,80},{112,96},{17,1},{33... | collective-permute-start | bytes 150920 | tf_op jit(solution)/shard_map/ppermute | solution.py:27
  102.2 2.4 %collective-permute-start.8 = (f32[3,16,262]{2,1,0:T(8,128)}, f32[3,16,262]{2,1,0:T(8,128)}, u32[]{:S(2)}, u32[]{:S(2)}) collective-permute-start(f32[3,16,262]{2,1,0:T(8,128)} %get-tuple-element.98), channel_id=1, source_target_pairs={{0,16},{16,32},{32,48},{48,64},{64,80},{80,96},{96,112},{1,17},{17... | collective-permute-start | bytes 150920 | tf_op jit(solution)/shard_map/ppermute | solution.py:26
  104.6 3.1 %pad_maximum_fusion.1 = f32[6,22,19,262]{3,2,1,0:T(8,128)} fusion(f32[1,16,16,256]{3,2,1,0:T(8,128)S(1)} %copy-done.18, f32[1,16,16,256]{3,2,1,0:T(8,128)S(1)} %bitcast.317, f32[3,16,16,256]{3,2,1,0:T(8,128)S(1)} %copy-done.5), kind=kLoop, calls=%fused_computation.1 | loop fusion | flops 1314192 | bytes 3939104 | tf_op jit(solution)/shard_map/concatenate | solution.py:269
  111.5 4.0 %collective-permute-start.10 = (f32[22,3,262]{2,1,0:T(4,128)S(1)}, f32[22,3,262]{2,1,0:T(4,128)S(1)}, u32[]{:S(2)}, u32[]{:S(2)}) collective-permute-start(f32[22,3,262]{2,1,0:T(4,128)S(1)} %get-tuple-element.96), channel_id=1, source_target_pairs={{0,4},{4,8},{8,12},{1,5},{5,9},{9,13},{2,6},{6,10},{10,14},{3,7},{... | collective-permute-start | bytes 207512 | tf_op jit(solution)/shard_map/ppermute | solution.py:26
  119.0 3.0 %fusion.159 = f32[20,20,260]{2,1,0:T(8,128)S(1)} fusion(f32[22,22,262]{2,1,0:T(8,128)S(1)} %get-tuple-element.76, f32[22,22,262]{2,1,0:T(8,128)S(1)} %get-tuple-element.75, f32[6,22,22,262]{3,2,1,0:T(8,128)S(1)} %bitcast.305, f32[22,22,262]{2,1,0:T(8,128)S(1)} %get-tuple-element.85, f32[22,22,262]{2,1,0:T(8,128)S(1)} %get-tuple-element.84), kind=kLoop, calls=%fused_computation.220 | loop fusion | flops 2392000 | bytes 7072000 | tf_op jit(solution)/shard_map/add | solution.py:54
  125.5 17.3 %shard_map.78 = f32[128,1,128]{2,1,0:T(1,128)} custom-call(f32[1,1,128]{2,1,0:T(1,128)} %copy-done.35), custom_call_target="tpu_custom_call" | custom-call | tf_op jit(solution)/shard_map/pallas_call | solution.py:232
  146.6 3.6 %fusion.205 = (f32[20,20,260]{2,1,0:T(8,128)}, f32[20,20,260]{2,1,0:T(8,128)}) fusion(f32[20,20,260]{2,1,0:T(8,128)} %copy-done.7, f32[20,20,260]{2,1,0:T(8,128)} %copy-done.21, f32[6,22,22,262]{3,2,1,0:T(8,128)} %copy-done.1, f32[20,20,260]{2,1,0:T(8,128)} %copy-done.25, f32[]{:T(128)S(6)} %div.37), kind=kLoop, calls=%fused_computation.336 | loop fusion | flops 624000 | bytes 2912004 | tf_op jit(solution)/shard_map/mul | solution.py:67
  150.5 3.0 %multiply_reduce_fusion = f32[16,16,256]{2,1,0:T(8,128)S(1)} fusion(f32[16,16,16,256]{3,2,1,0:T(8,128)} %param.18, f32[16]{0:T(128)S(1)} %convolution_bitcast_fusion), kind=kLoop, calls=%fused_computation.2 | loop fusion | flops 2031616 | bytes 4456512 | tf_op jit(solution)/shard_map/reduce_sum | solution.py:77
  153.6 4.2 %fusion.208 = (f32[20,20,260]{2,1,0:T(8,128)S(1)}, f32[20,20,260]{2,1,0:T(8,128)S(1)}) fusion(f32[6,22,22,262]{3,2,1,0:T(8,128)} %copy-done.1, f32[20,20,260]{2,1,0:T(8,128)} %copy-done.7, f32[20,20,260]{2,1,0:T(8,128)S(1)} %copy-done.20, f32[20,20,260]{2,1,0:T(8,128)S(1)} %copy-done.30, f32[3,20,20,260]{3,2,1,0:T(8,128)S(1)} %slice.612, ...), kind=kLoop, calls=%fused_computation.359 | loop fusion | flops 3224000 | bytes 5824000 | tf_op jit(solution)/shard_map/mul | solution.py:67
  157.9 1.8 fusion.207
  161.4 2.0 fusion.197
  165.4 7.4 %shard_map.79 = (f32[1,16,256]{2,1,0:T(8,128)}, f32[1,16,256]{2,1,0:T(8,128)}, f32[16,1,256]{2,1,0:T(1,128)}, f32[16,1,256]{2,1,0:T(1,128)}, f32[16,16,1]{2,1,0:T(8,128)}, /*index=5*/f32[16,16,1]{2,1,0:T(8,128)}) custom-call(f32[1,16,256]{2,1,0:T(8,128)} %get-tuple-element.105.refs_0_, f32[1,16,256]{2,1,0:T(8,128)} %get-tuple-element.104.refs_1_, ...), custom_call_target="tpu_custom_call" | custom-call | tf_op jit(solution)/shard_map/pallas_call | solution.py:145
  175.3 1.7 fusion.173
  177.1 3.9 %multiply_reduce_fusion.7 = (f32[]{:T(128)}, f32[]{:T(128)}, f32[]{:T(128)}, f32[]{:T(128)}, f32[16,16,256]{2,1,0:T(8,128)}) fusion(f32[16,16,256]{2,1,0:T(8,128)} %copy-done.24, f32[20,20,260]{2,1,0:T(8,128)} %get-tuple-element.74, f32[20,20,260]{2,1,0:T(8,128)} %copy-done.25, f32[16,16,256]{2,1,0:T(8,128)S(1)} %fusion.201, ...), kind=kLoop, calls=%fused_computation.330 | loop fusion | flops 3211260 | bytes 8882992 | tf_op jit(solution)/shard_map/reduce_sum | solution.py:310
  181.0 2.5 %maximum_bitcast_fusion.1 = f32[1,1,4]{2,1,0:T(1,128)S(1)} fusion(f32[1]{0:T(128)} %bitcast.39, f32[1]{0:T(128)} %bitcast.38, f32[1]{0:T(128)} %bitcast.37, f32[1]{0:T(128)} %bitcast.29), kind=kLoop, calls=%fused_computation.355 | loop fusion | flops 12 | bytes 32 | tf_op jit(solution)/shard_map/broadcast_in_dim;broadcast_in_dim | solution.py:231
  184.0 15.4 %shard_map.80 = f32[128,1,128]{2,1,0:T(1,128)} custom-call(f32[1,1,128]{2,1,0:T(1,128)} %scatter.19.row_ref), custom_call_target="tpu_custom_call" | custom-call | tf_op jit(solution)/shard_map/pallas_call | solution.py:232
  207.0 2.2 %multiply_subtract_fusion.1 = f32[16,16,256]{2,1,0:T(8,128)} fusion(f32[16,16,256]{2,1,0:T(8,128)} %get-tuple-element.68, f32[20,20,260]{2,1,0:T(8,128)} %get-tuple-element.74, f32[]{:T(128)S(6)} %div.42, f32[]{:T(128)S(6)} %div.43, f32[20,20,260]{2,1,0:T(8,128)} %copy-done.25), kind=kLoop, calls=%fused_computation.325 | loop fusion | flops 262144 | bytes 1048584 | tf_op jit(solution)/shard_map/sub | solution.py:322
  (145 shorter events, 49.8 us)
Async XLA Ops:
  0.6 66.7 %copy-start = (f32[16,2048]{1,0:T(8,128)S(1)}, f32[16,2048]{1,0:T(8,128)}, u32[]{:S(2)}) copy-start(f32[16,2048]{1,0:T(8,128)} %param.19) | copy-start | bytes 393220
  1.7 71.4 %copy-start.17 = (f32[1,16,16,256]{3,2,1,0:T(8,128)}, f32[1,16,16,256]{3,2,1,0:T(8,128)S(1)}, u32[]{:S(2)}) copy-start(f32[1,16,16,256]{3,2,1,0:T(8,128)S(1)} %fusion.203) | copy-start | bytes 786436
  3.2 14.6 %copy-start.4 = (f32[3,16,16,256]{3,2,1,0:T(8,128)S(1)}, f32[3,16,16,256]{3,2,1,0:T(8,128)}, u32[]{:S(2)}) copy-start(f32[3,16,16,256]{3,2,1,0:T(8,128)} %param.15) | copy-start | bytes 2359300
  3.2 14.6 %copy-start.13 = (f32[16,16,256]{2,1,0:T(8,128)S(1)}, f32[16,16,256]{2,1,0:T(8,128)}, u32[]{:S(2)}) copy-start(f32[16,16,256]{2,1,0:T(8,128)} %param.14) | copy-start | bytes 786436
  3.2 14.5 %copy-start.14 = (f32[16,16,256]{2,1,0:T(8,128)S(1)}, f32[16,16,256]{2,1,0:T(8,128)}, u32[]{:S(2)}) copy-start(f32[16,16,256]{2,1,0:T(8,128)} %param.16) | copy-start | bytes 786436
  6.4 8.4 %collective-permute-start.1 = (f32[6,16,16,3]{2,1,3,0:T(8,128)S(1)}, f32[6,16,16,3]{2,1,3,0:T(8,128)S(1)}, u32[]{:S(2)}, u32[]{:S(2)}) collective-permute-start(f32[6,16,16,3]{2,1,3,0:T(8,128)S(1)} %copy.9), channel_id=1, source_target_pairs={{1,0},{2,1},{3,2},{5,4},{6,5},{7,6},{9,8},{10,9},{11,10},{13,12},{... | collective-permute-start | bytes 55304 | tf_op jit(solution)/shard_map/ppermute | solution.py:27
  9.5 6.7 %collective-permute-start = (f32[6,16,16,3]{2,1,3,0:T(8,128)S(1)}, f32[6,16,16,3]{2,1,3,0:T(8,128)}, u32[]{:S(2)}, u32[]{:S(2)}) collective-permute-start(f32[6,16,16,3]{2,1,3,0:T(8,128)S(1)} %copy.8), channel_id=1, source_target_pairs={{0,1},{1,2},{2,3},{4,5},{5,6},{6,7},{8,9},{9,10},{10,11},{12,13},{... | collective-permute-start | bytes 55304 | tf_op jit(solution)/shard_map/ppermute | solution.py:26
  15.4 57.7 %copy-start.9 = (f32[6,16,16,3]{3,2,1,0:T(8,128)}, f32[6,16,16,3]{3,2,1,0:T(8,128)S(1)}, u32[]{:S(2)}) copy-start(f32[6,16,16,3]{3,2,1,0:T(8,128)S(1)} %copy.11) | copy-start | bytes 55300
  17.8 55.3 %copy-start.11 = (f32[6,16,16,3]{3,2,1,0:T(8,128)}, f32[6,16,16,3]{3,2,1,0:T(8,128)S(1)}, u32[]{:S(2)}) copy-start(f32[6,16,16,3]{3,2,1,0:T(8,128)S(1)} %copy.10) | copy-start | bytes 55300
  18.2 11.3 %collective-permute-start.3 = (f32[6,3,16,262]{3,2,1,0:T(8,128)S(1)}, f32[6,3,16,262]{3,2,1,0:T(8,128)S(1)}, u32[]{:S(2)}, u32[]{:S(2)}) collective-permute-start(f32[6,3,16,262]{3,2,1,0:T(8,128)S(1)} %get-tuple-element.92), channel_id=1, source_target_pairs={{16,0},{32,16},{48,32},{64,48},{80,64},{96,80},{112,96},{17,1},{33... | collective-permute-start | bytes 905480 | tf_op jit(solution)/shard_map/ppermute | solution.py:27
  22.0 8.6 %collective-permute-start.2 = (f32[6,3,16,262]{3,2,1,0:T(8,128)S(1)}, f32[6,3,16,262]{3,2,1,0:T(8,128)S(1)}, u32[]{:S(2)}, u32[]{:S(2)}) collective-permute-start(f32[6,3,16,262]{3,2,1,0:T(8,128)S(1)} %get-tuple-element.91), channel_id=1, source_target_pairs={{0,16},{16,32},{32,48},{48,64},{64,80},{80,96},{96,112},{1,17},{17... | collective-permute-start | bytes 905480 | tf_op jit(solution)/shard_map/ppermute | solution.py:26
  32.8 8.6 %copy-start.2 = (f32[16,16,16,256]{3,2,1,0:T(8,128)S(1)}, f32[16,16,16,256]{3,2,1,0:T(8,128)}, u32[]{:S(2)}) copy-start(f32[16,16,16,256]{3,2,1,0:T(8,128)} %param.18) | copy-start | bytes 12582916
  34.0 36.4 %collective-permute-start.5 = (f32[6,22,3,262]{3,1,2,0:T(8,128)}, f32[6,22,3,262]{3,1,2,0:T(8,128)}, u32[]{:S(2)}, u32[]{:S(2)}) collective-permute-start(f32[6,22,3,262]{3,1,2,0:T(8,128)} %copy.13), channel_id=1, source_target_pairs={{4,0},{8,4},{12,8},{5,1},{9,5},{13,9},{6,2},{10,6},{14,10},{7,3},{... | collective-permute-start | bytes 1245032 | tf_op jit(solution)/shard_map/ppermute | solution.py:27
  36.4 35.4 %collective-permute-start.4 = (f32[6,22,3,262]{3,1,2,0:T(8,128)}, f32[6,22,3,262]{3,1,2,0:T(8,128)}, u32[]{:S(2)}, u32[]{:S(2)}) collective-permute-start(f32[6,22,3,262]{3,1,2,0:T(8,128)} %copy.12), channel_id=1, source_target_pairs={{0,4},{4,8},{8,12},{1,5},{5,9},{9,13},{2,6},{6,10},{10,14},{3,7},{... | collective-permute-start | bytes 1245032 | tf_op jit(solution)/shard_map/ppermute | solution.py:26
  78.6 8.7 %copy-start.1 = (f32[6,22,22,262]{3,2,1,0:T(8,128)}, f32[6,22,22,262]{3,2,1,0:T(8,128)S(1)}, u32[]{:S(2)}) copy-start(f32[6,22,22,262]{3,2,1,0:T(8,128)S(1)} %pad_maximum_fusion) | copy-start | bytes 9130180
  79.2 9.8 %copy-start.31 = (f32[20,20,260]{2,1,0:T(8,128)}, f32[20,20,260]{2,1,0:T(8,128)S(1)}, u32[]{:S(2)}) copy-start(f32[20,20,260]{2,1,0:T(8,128)S(1)} %get-tuple-element.86) | copy-start | bytes 1248004
  87.3 17.3 %copy-start.5 = (f32[3,16,16,256]{3,2,1,0:T(8,128)S(1)}, f32[3,16,16,256]{3,2,1,0:T(8,128)}, u32[]{:S(2)}) copy-start(f32[3,16,16,256]{3,2,1,0:T(8,128)} %param.15) | copy-start | bytes 2359300
  87.4 17.3 %copy-start.15 = (f32[16,16,256]{2,1,0:T(8,128)S(1)}, f32[16,16,256]{2,1,0:T(8,128)}, u32[]{:S(2)}) copy-start(f32[16,16,256]{2,1,0:T(8,128)} %param.16) | copy-start | bytes 786436
  87.4 17.3 %copy-start.18 = (f32[1,16,16,256]{3,2,1,0:T(8,128)S(1)}, f32[1,16,16,256]{3,2,1,0:T(8,128)}, u32[]{:S(2)}) copy-start(f32[1,16,16,256]{3,2,1,0:T(8,128)} %copy-done.17) | copy-start | bytes 786436
  89.6 7.7 %collective-permute-start.7 = (f32[16,16,3]{2,1,0:T(8,128)S(1)}, f32[16,16,3]{2,1,0:T(8,128)S(1)}, u32[]{:S(2)}, u32[]{:S(2)}) collective-permute-start(f32[16,16,3]{2,1,0:T(8,128)S(1)} %get-tuple-element.107), channel_id=1, source_target_pairs={{1,0},{2,1},{3,2},{5,4},{6,5},{7,6},{9,8},{10,9},{11,10},{13,12},{... | collective-permute-start | bytes 9224 | tf_op jit(solution)/shard_map/ppermute | solution.py:27
  90.9 7.3 %collective-permute-start.6 = (f32[16,16,3]{2,1,0:T(8,128)S(1)}, f32[16,16,3]{2,1,0:T(8,128)S(1)}, u32[]{:S(2)}, u32[]{:S(2)}) collective-permute-start(f32[16,16,3]{2,1,0:T(8,128)S(1)} %get-tuple-element.106), channel_id=1, source_target_pairs={{0,1},{1,2},{2,3},{4,5},{5,6},{6,7},{8,9},{9,10},{10,11},{12,13},{... | collective-permute-start | bytes 9224 | tf_op jit(solution)/shard_map/ppermute | solution.py:26
  99.0 9.7 %collective-permute-start.9 = (f32[3,16,262]{2,1,0:T(8,128)}, f32[3,16,262]{2,1,0:T(8,128)}, u32[]{:S(2)}, u32[]{:S(2)}) collective-permute-start(f32[3,16,262]{2,1,0:T(8,128)} %get-tuple-element.99), channel_id=1, source_target_pairs={{16,0},{32,16},{48,32},{64,48},{80,64},{96,80},{112,96},{17,1},{33... | collective-permute-start | bytes 150920 | tf_op jit(solution)/shard_map/ppermute | solution.py:27
  102.2 6.6 %collective-permute-start.8 = (f32[3,16,262]{2,1,0:T(8,128)}, f32[3,16,262]{2,1,0:T(8,128)}, u32[]{:S(2)}, u32[]{:S(2)}) collective-permute-start(f32[3,16,262]{2,1,0:T(8,128)} %get-tuple-element.98), channel_id=1, source_target_pairs={{0,16},{16,32},{32,48},{48,64},{64,80},{80,96},{96,112},{1,17},{17... | collective-permute-start | bytes 150920 | tf_op jit(solution)/shard_map/ppermute | solution.py:26
  104.6 14.4 %slice-start = ((s8[4866048]{0:T(1024)(128)(4,1)}), s8[671744]{0:T(1024)(128)(4,1)S(1)}, s32[]{:S(2)}) async-start(s8[4866048]{0:T(1024)(128)(4,1)} %bitcast.304), calls=%async_computation | async-start | bytes 1343488
  108.7 10.3 %slice-start.1 = ((s8[4866048]{0:T(1024)(128)(4,1)}), s8[4194304]{0:T(1024)(128)(4,1)S(1)}, s32[]{:S(2)}) async-start(s8[4866048]{0:T(1024)(128)(4,1)} %bitcast.304), calls=%async_computation.1 | async-start | bytes 8388608
  110.1 6.9 %collective-permute-start.11 = (f32[22,3,262]{2,1,0:T(4,128)S(1)}, f32[22,3,262]{2,1,0:T(4,128)S(1)}, u32[]{:S(2)}, u32[]{:S(2)}) collective-permute-start(f32[22,3,262]{2,1,0:T(4,128)S(1)} %get-tuple-element.97), channel_id=1, source_target_pairs={{4,0},{8,4},{12,8},{5,1},{9,5},{13,9},{6,2},{10,6},{14,10},{7,3},{... | collective-permute-start | bytes 207512 | tf_op jit(solution)/shard_map/ppermute | solution.py:27
  111.5 6.0 %collective-permute-start.10 = (f32[22,3,262]{2,1,0:T(4,128)S(1)}, f32[22,3,262]{2,1,0:T(4,128)S(1)}, u32[]{:S(2)}, u32[]{:S(2)}) collective-permute-start(f32[22,3,262]{2,1,0:T(4,128)S(1)} %get-tuple-element.96), channel_id=1, source_target_pairs={{0,4},{4,8},{8,12},{1,5},{5,9},{9,13},{2,6},{6,10},{10,14},{3,7},{... | collective-permute-start | bytes 207512 | tf_op jit(solution)/shard_map/ppermute | solution.py:26
  161.3 15.7 %copy-start.6 = (f32[3,16,16,256]{3,2,1,0:T(8,128)S(1)}, f32[3,16,16,256]{3,2,1,0:T(8,128)}, u32[]{:S(2)}) copy-start(f32[3,16,16,256]{3,2,1,0:T(8,128)} %param.15) | copy-start | bytes 2359300
  161.3 15.7 %copy-start.10 = (f32[6,16,16,3]{3,2,1,0:T(8,128)S(1)}, f32[6,16,16,3]{3,2,1,0:T(8,128)}, u32[]{:S(2)}) copy-start(f32[6,16,16,3]{3,2,1,0:T(8,128)} %copy-done.9) | copy-start | bytes 55300
  161.3 15.7 %copy-start.12 = (f32[6,16,16,3]{3,2,1,0:T(8,128)S(1)}, f32[6,16,16,3]{3,2,1,0:T(8,128)}, u32[]{:S(2)}) copy-start(f32[6,16,16,3]{3,2,1,0:T(8,128)} %copy-done.11) | copy-start | bytes 55300
  161.3 15.7 %copy-start.16 = (f32[16,16,256]{2,1,0:T(8,128)S(1)}, f32[16,16,256]{2,1,0:T(8,128)}, u32[]{:S(2)}) copy-start(f32[16,16,256]{2,1,0:T(8,128)} %param.16) | copy-start | bytes 786436
  161.4 15.7 %copy-start.19 = (f32[1,16,16,256]{3,2,1,0:T(8,128)S(1)}, f32[1,16,16,256]{3,2,1,0:T(8,128)}, u32[]{:S(2)}) copy-start(f32[1,16,16,256]{3,2,1,0:T(8,128)} %copy-done.17) | copy-start | bytes 786436
  (20 other events, 81.8 us)

commit v3 on v1

--- a/solution.py
+++ b/solution.py
@@ -203,6 +203,11 @@
     sides = (("gx", 0), ("gy", 1), ("gz", 2))
     free = 1.0 - dirichlet.astype(jnp.float32)
     stacked = jnp.concatenate([conductance, storage[None], free[None], right_side[None]], axis=0)
+    residual0 = right_side
+    coarse0 = project(basis, residual0)
+    rows0 = gather_rows(pack(coarse0, []))
+    rows0, stacked = lax.optimization_barrier((rows0, stacked))
+    coarse0_all, _ = unpack(rows0, vecs, 0)
     wide = padded(stacked, (("gz", 3), ("gx", 1), ("gy", 2)), 3)
     cond_wide = wide[:3]
     free_wide = wide[4]
@@ -223,9 +228,6 @@
         weights = jnp.dot(coarse_inverse, coarse_all, precision=lax.Precision.HIGHEST)
         return schwarz(rhs_box) + expand(basis, weights, residual)
 
-    residual0 = right_side
-    coarse0 = project(basis, residual0)
-    coarse0_all, _ = unpack(gather_rows(pack(coarse0, [])), vecs, 0)
     z0 = precondition(rhs_box0, residual0, coarse0_all)
     near0 = padded(z0, (("gz", 2), ("gx", 0), ("gy", 1)), 3)
     inner = (slice(1, -1),) * 3

time: 206 us -> 213 us (1.034)
  waiting for transfers between devices: 10.1 us -> 20.4 us
  local copies, waits for them, and re-layouts: 17.7 us -> 22.8 us
  other arithmetic: 58.9 us -> 54.3 us
  Pallas kernels: 55.8 us -> 52.7 us
    optimization_barrier x0 -> x1, local copies, waits for them, and re-layouts: none -> 8.74 us  [shards(): rows0, stacked = lax.optimization_barrier((rows0, stacked))]
    ppermute x6, waiting for transfers between devices: 5.64 us -> 11.9 us  [padded(): after = lax.ppermute(leading, axis, down)]
    concatenate x2 -> x1, other arithmetic: 7.68 us -> 2.05 us  [padded(): value = jnp.concatenate([before, value, after], axis=dim)]
    pallas_call x3, Pallas kernels: 55.8 us -> 52.7 us  [gather_rows(): pl.pallas_call(functools.partial(gather_kernel, sizes), out_shape=jax.Sha...]
    ppermute x6, starting transfers between devices: 24.9 us -> 27.1 us  [padded(): before = lax.ppermute(last, axis, up)]
    concatenate x2 -> x1, other arithmetic: 2.38 us -> 0.2 us  [shards(): jnp.concatenate([conductance, storage[None], free[None], right_side[None]...]
    reduce_sum x2, other arithmetic: 1.07 us -> 3.23 us  [project(): return jnp.sum(basis * field[None], axis=(1, 2, 3))]
    unnamed x90 -> x82, local copies, waits for them, and re-layouts: 4.58 us -> 3.25 us
  transfers between devices with their start and end apart: 18 -> 18, of which waited for: 7 -> 12; matrix products, arithmetic and copies ran while one was open for 6% -> 4% of each run, Pallas kernels for 12% -> 0%
where the time goes in v3:
time: 213 us; the launch traced here: 211 us
  other arithmetic  54.3 us (25%)
  starting transfers between devices  53.8 us (25%)
  Pallas kernels  52.7 us (25%)
  local copies, waits for them, and re-layouts  22.8 us (11%)
  waiting for transfers between devices  20.4 us (10%)
  between operations  7.16 us (3%)
    pallas_call x3, Pallas kernels, gather_rows(): pl.pallas_call(functools.partial(gather_kernel, sizes), out_shape=jax.Sha...  52.7 us
    ppermute x6, starting transfers between devices, padded(): before = lax.ppermute(last, axis, up)  27.1 us
    mul x7, other arithmetic, jacobi(): free_box * guess  17.1 us
    ppermute x6, waiting for transfers between devices, padded(): after = lax.ppermute(leading, axis, down)  11.9 us
    ppermute x3, starting transfers between devices, faces(): lax.ppermute(lax.slice_in_dim(field, length - 1, length, axis=dim), axis,...  10.7 us
    ppermute x6, starting transfers between devices, padded(): after = lax.ppermute(leading, axis, down)  10.5 us
    optimization_barrier x1, local copies, waits for them, and re-layouts, shards(): rows0, stacked = lax.optimization_barrier((rows0, stacked))  8.74 us
    reduce_sum x2, other arithmetic, expand(): return jnp.sum(weights[:, None, None, None] * basis, axis=0)  5.87 us
  transfers between devices with their start and end apart: 18, of which 12 were waited for; matrix products, arithmetic and copies ran while one was open for 4% of the time, Pallas kernels for 0%

profile of v3, /device:TPU:1, one launch (start us, length us, event | category | flops | bytes accessed | tf_op | source)
XLA Modules:
  0.0 211.5 jit_solution(14572019292319704847)
XLA Ops:
  0.7 2.8 %multiply_reduce_fusion.3 = f32[16]{0:T(128)S(1)} fusion(f32[16,16,16,256]{3,2,1,0:T(8,128)} %param.18, f32[16,16,256]{2,1,0:T(8,128)} %param.14), kind=kLoop, calls=%fused_computation.4 | loop fusion | flops 2097136 | bytes 4456512 | tf_op jit(solution)/shard_map/reduce_sum | solution.py:73
  4.0 18.1 %shard_map.77 = f32[128,1,128]{2,1,0:T(1,128)} custom-call(f32[1,1,128]{2,1,0:T(1,128)} %scatter.14.row_ref), custom_call_target="tpu_custom_call" | custom-call | tf_op jit(solution)/shard_map/pallas_call | solution.py:168
  22.4 8.7 %copy.41 = f32[6,16,16,256]{2,1,3,0:T(8,128)} copy(f32[6,16,16,256]{3,2,1,0:T(8,128)S(1)} %pad_maximum_fusion.1) | data formatting | bytes 3145728 | tf_op jit(solution)/shard_map/optimization_barrier | solution.py:209
  33.4 4.0 %collective-permute-start = (f32[6,16,16,3]{2,1,3,0:T(8,128)S(1)}, f32[6,16,16,3]{2,1,3,0:T(8,128)S(1)}, u32[]{:S(2)}, u32[]{:S(2)}) collective-permute-start(f32[6,16,16,3]{2,1,3,0:T(8,128)S(1)} %get-tuple-element.78), channel_id=1, source_target_pairs={{0,1},{1,2},{2,3},{4,5},{5,6},{6,7},{8,9},{9,10},{10,11},{12,13},{... | collective-permute-start | bytes 55304 | tf_op jit(solution)/shard_map/ppermute | solution.py:26
  40.9 3.5 %collective-permute-start.3 = (f32[6,3,16,262]{3,2,1,0:T(8,128)S(1)}, f32[6,3,16,262]{3,2,1,0:T(8,128)S(1)}, u32[]{:S(2)}, u32[]{:S(2)}) collective-permute-start(f32[6,3,16,262]{3,2,1,0:T(8,128)S(1)} %get-tuple-element.88), channel_id=1, source_target_pairs={{16,0},{32,16},{48,32},{64,48},{80,64},{96,80},{112,96},{17,1},{33... | collective-permute-start | bytes 905480 | tf_op jit(solution)/shard_map/ppermute | solution.py:27
  44.4 2.2 %collective-permute-start.2 = (f32[6,3,16,262]{3,2,1,0:T(8,128)S(1)}, f32[6,3,16,262]{3,2,1,0:T(8,128)S(1)}, u32[]{:S(2)}, u32[]{:S(2)}) collective-permute-start(f32[6,3,16,262]{3,2,1,0:T(8,128)S(1)} %get-tuple-element.87), channel_id=1, source_target_pairs={{0,16},{16,32},{32,48},{48,64},{64,80},{80,96},{96,112},{1,17},{17... | collective-permute-start | bytes 905480 | tf_op jit(solution)/shard_map/ppermute | solution.py:26
  46.7 3.9 %collective-permute-done.3 = f32[6,3,16,262]{3,2,1,0:T(8,128)S(1)} collective-permute-done((f32[6,3,16,262]{3,2,1,0:T(8,128)S(1)}, f32[6,3,16,262]{3,2,1,0:T(8,128)S(1)}, u32[]{:S(2)}, u32[]{:S(2)}) %collective-permute-start.3) | collective-permute-done | bytes 301856 | tf_op jit(solution)/shard_map/ppermute | solution.py:27
  55.9 4.8 %collective-permute-start.4 = (f32[6,22,3,262]{3,1,2,0:T(8,128)}, f32[6,22,3,262]{3,1,2,0:T(8,128)}, u32[]{:S(2)}, u32[]{:S(2)}) collective-permute-start(f32[6,22,3,262]{3,1,2,0:T(8,128)} %copy.59), channel_id=1, source_target_pairs={{0,4},{4,8},{8,12},{1,5},{5,9},{9,13},{2,6},{6,10},{10,14},{3,7},{... | collective-permute-start | bytes 1245032 | tf_op jit(solution)/shard_map/ppermute | solution.py:26
  61.1 2.8 %multiply_reduce_fusion.2 = f32[16,16,256]{2,1,0:T(8,128)S(1)} fusion(f32[16,16,16,256]{3,2,1,0:T(8,128)} %param.18, f32[16]{0:T(128)S(1)} %convolution_bitcast_fusion.1), kind=kLoop, calls=%fused_computation.3 | loop fusion | flops 2031616 | bytes 4456512 | tf_op jit(solution)/shard_map/reduce_sum | solution.py:77
  63.9 5.6 %collective-permute-done.5 = f32[6,22,3,262]{3,1,2,0:T(8,128)} collective-permute-done((f32[6,22,3,262]{3,1,2,0:T(8,128)}, f32[6,22,3,262]{3,1,2,0:T(8,128)}, u32[]{:S(2)}, u32[]{:S(2)}) %collective-permute-start.5) | collective-permute-done | bytes 415040 | tf_op jit(solution)/shard_map/ppermute | solution.py:27
  73.5 2.1 pad_maximum_fusion
  77.3 2.4 %fusion.204 = (f32[20,20,260]{2,1,0:T(8,128)S(1)}, f32[20,20,260]{2,1,0:T(8,128)S(1)}, f32[20,20,260]{2,1,0:T(8,128)S(1)}, f32[20,20,260]{2,1,0:T(8,128)S(1)}) fusion(f32[6,22,22,262]{3,2,1,0:T(8,128)S(1)} %pad_maximum_fusion, f32[20,20,260]{2,1,0:T(8,128)S(1)} %broadcast_multiply_fusion, f32[3,20,20,260]{3,2,1,0:T(8,128)S(1)} %slice.607), kind=kLoop, calls=%fused_computation.328 | loop fusion | flops 3640000 | bytes 5824000 | tf_op jit(solution)/shard_map/mul | solution.py:67
  79.7 2.3 %fusion.210 = (f32[20,20,260]{2,1,0:T(8,128)S(1)}, f32[20,20,260]{2,1,0:T(8,128)S(1)}) fusion(f32[6,22,22,262]{3,2,1,0:T(8,128)S(1)} %pad_maximum_fusion, f32[20,20,260]{2,1,0:T(8,128)S(1)} %get-tuple-element.77, f32[20,20,260]{2,1,0:T(8,128)S(1)} %get-tuple-element.75, f32[3,20,20,260]{3,2,1,0:T(8,128)S(1)} %slice.607, f32[20,20,260]{2,1,0:T(8,128)S(1)} %get-tuple-element.76), kind=kLoop, calls=%fused_computation.348 | loop fusion | flops 3224000 | bytes 5824000 | tf_op jit(solution)/shard_map/mul | solution.py:67
  82.0 2.0 fusion.209
  87.6 4.7 %collective-permute-start.6 = (f32[16,16,3]{2,1,0:T(8,128)S(1)}, f32[16,16,3]{2,1,0:T(8,128)S(1)}, u32[]{:S(2)}, u32[]{:S(2)}) collective-permute-start(f32[16,16,3]{2,1,0:T(8,128)S(1)} %get-tuple-element.100), channel_id=1, source_target_pairs={{0,1},{1,2},{2,3},{4,5},{5,6},{6,7},{8,9},{9,10},{10,11},{12,13},{... | collective-permute-start | bytes 9224 | tf_op jit(solution)/shard_map/ppermute | solution.py:26
  97.6 6.4 %collective-permute-start.8 = (f32[3,16,262]{2,1,0:T(8,128)}, f32[3,16,262]{2,1,0:T(8,128)}, u32[]{:S(2)}, u32[]{:S(2)}) collective-permute-start(f32[3,16,262]{2,1,0:T(8,128)} %get-tuple-element.92), channel_id=1, source_target_pairs={{0,16},{16,32},{32,48},{48,64},{64,80},{80,96},{96,112},{1,17},{17... | collective-permute-start | bytes 150920 | tf_op jit(solution)/shard_map/ppermute | solution.py:26
  108.2 5.0 %collective-permute-start.10 = (f32[22,3,262]{2,0,1:T(8,128)S(1)}, f32[22,3,262]{2,0,1:T(8,128)S(1)}, u32[]{:S(2)}, u32[]{:S(2)}) collective-permute-start(f32[22,3,262]{2,0,1:T(8,128)S(1)} %copy.61), channel_id=1, source_target_pairs={{0,4},{4,8},{8,12},{1,5},{5,9},{9,13},{2,6},{6,10},{10,14},{3,7},{... | collective-permute-start | bytes 207512 | tf_op jit(solution)/shard_map/ppermute | solution.py:26
  116.1 3.0 %fusion.159 = f32[20,20,260]{2,1,0:T(8,128)S(1)} fusion(f32[22,22,262]{2,1,0:T(8,128)S(1)} %get-tuple-element.70, f32[22,22,262]{2,1,0:T(8,128)S(1)} %get-tuple-element.69, f32[6,22,22,262]{3,2,1,0:T(8,128)S(1)} %copy-done.2, f32[22,22,262]{2,1,0:T(8,128)S(1)} %get-tuple-element.81, f32[22,22,262]{2,1,0:T(8,128)S(1)} %get-tuple-element.80), kind=kLoop, calls=%fused_computation.223 | loop fusion | flops 2392000 | bytes 7072000 | tf_op jit(solution)/shard_map/add | solution.py:54
  122.4 19.3 %shard_map.78 = f32[128,1,128]{2,1,0:T(1,128)} custom-call(f32[1,1,128]{2,1,0:T(1,128)} %copy-done.35), custom_call_target="tpu_custom_call" | custom-call | tf_op jit(solution)/shard_map/pallas_call | solution.py:168
  145.4 3.4 %fusion.205 = (f32[20,20,260]{2,1,0:T(8,128)}, f32[20,20,260]{2,1,0:T(8,128)}) fusion(f32[20,20,260]{2,1,0:T(8,128)S(1)} %get-tuple-element.77, f32[20,20,260]{2,1,0:T(8,128)} %copy-done.11, f32[6,22,22,262]{3,2,1,0:T(8,128)} %copy-done.1, f32[20,20,260]{2,1,0:T(8,128)} %copy-done.15, f32[]{:T(128)S(6)} %div.37), kind=kLoop, calls=%fused_computation.329 | loop fusion | flops 624000 | bytes 2912004 | tf_op jit(solution)/shard_map/mul | solution.py:67
  149.1 3.0 %multiply_reduce_fusion = f32[16,16,256]{2,1,0:T(8,128)S(1)} fusion(f32[16,16,16,256]{3,2,1,0:T(8,128)} %param.18, f32[16]{0:T(128)S(1)} %convolution_bitcast_fusion), kind=kLoop, calls=%fused_computation.1 | loop fusion | flops 2031616 | bytes 4456512 | tf_op jit(solution)/shard_map/reduce_sum | solution.py:77
  152.1 4.0 %fusion.208 = (f32[20,20,260]{2,1,0:T(8,128)S(1)}, f32[20,20,260]{2,1,0:T(8,128)S(1)}) fusion(f32[6,22,22,262]{3,2,1,0:T(8,128)} %copy-done.1, f32[20,20,260]{2,1,0:T(8,128)S(1)} %get-tuple-element.77, f32[20,20,260]{2,1,0:T(8,128)S(1)} %copy-done.10, f32[20,20,260]{2,1,0:T(8,128)S(1)} %copy-done.22, f32[3,20,20,260]{3,2,1,0:T(8,128)S(1)} %slice.607, ...), kind=kLoop, calls=%fused_computation.346 | loop fusion | flops 3224000 | bytes 5824000 | tf_op jit(solution)/shard_map/mul | solution.py:67
  156.2 2.7 %fusion.207 = (f32[20,20,260]{2,1,0:T(8,128)S(1)}, f32[20,20,260]{2,1,0:T(8,128)}) fusion(f32[6,22,22,262]{3,2,1,0:T(8,128)S(1)} %bitcast.305, f32[20,20,260]{2,1,0:T(8,128)S(1)} %get-tuple-element.66, f32[20,20,260]{2,1,0:T(8,128)S(1)} %get-tuple-element.77, f32[20,20,260]{2,1,0:T(8,128)S(1)} %copy-done.10, f32[20,20,260]{2,1,0:T(8,128)S(1)} %get-tuple-element.65, ...), kind=kLoop, calls=%fused_computation.345 | loop fusion | flops 2912000 | bytes 5824000 | tf_op jit(solution)/shard_map/mul | solution.py:67
  160.5 2.0 fusion.197
  163.9 4.0 %collective-permute-start.13 = (f32[16,1,256]{2,0,1:T(8,128)S(1)}, f32[16,1,256]{2,0,1:T(8,128)S(1)}, u32[]{:S(2)}, u32[]{:S(2)}) collective-permute-start(f32[16,1,256]{2,0,1:T(8,128)S(1)} %copy.53), channel_id=1, source_target_pairs={{0,4},{4,8},{8,12},{1,5},{5,9},{9,13},{2,6},{6,10},{10,14},{3,7},{... | collective-permute-start | bytes 49160 | tf_op jit(solution)/shard_map/ppermute | solution.py:89
  167.9 2.9 %collective-permute-start.15 = (f32[1,16,256]{2,1,0:T(8,128)S(1)}, f32[1,16,256]{2,1,0:T(8,128)S(1)}, u32[]{:S(2)}, u32[]{:S(2)}) collective-permute-start(f32[1,16,256]{2,1,0:T(8,128)S(1)} %get-tuple-element.95), channel_id=1, source_target_pairs={{16,0},{32,16},{48,32},{64,48},{80,64},{96,80},{112,96},{17,1},{33... | collective-permute-start | bytes 49160 | tf_op jit(solution)/shard_map/ppermute | solution.py:90
  170.8 2.7 %collective-permute-start.14 = (f32[1,16,256]{2,1,0:T(8,128)S(1)}, f32[1,16,256]{2,1,0:T(8,128)S(1)}, u32[]{:S(2)}, u32[]{:S(2)}) collective-permute-start(f32[1,16,256]{2,1,0:T(8,128)S(1)} %get-tuple-element.94), channel_id=1, source_target_pairs={{0,16},{16,32},{32,48},{48,64},{64,80},{80,96},{96,112},{1,17},{17... | collective-permute-start | bytes 49160 | tf_op jit(solution)/shard_map/ppermute | solution.py:89
  174.9 4.0 %collective-permute-start.12 = (f32[16,16,1]{2,1,0:T(8,128)S(1)}, f32[16,16,1]{2,1,0:T(8,128)S(1)}, u32[]{:S(2)}, u32[]{:S(2)}) collective-permute-start(f32[16,16,1]{2,1,0:T(8,128)S(1)} %get-tuple-element.96), channel_id=1, source_target_pairs={{0,1},{1,2},{2,3},{4,5},{5,6},{6,7},{8,9},{9,10},{10,11},{12,13},{... | collective-permute-start | bytes 3080 | tf_op jit(solution)/shard_map/ppermute | solution.py:89
  182.5 2.6 %multiply_reduce_fusion.7 = (f32[]{:T(128)}, f32[]{:T(128)}, f32[]{:T(128)}, f32[]{:T(128)}, f32[16,16,256]{2,1,0:T(8,128)S(1)}) fusion(f32[16,16,256]{2,1,0:T(8,128)S(1)} %fusion.197, f32[20,20,260]{2,1,0:T(8,128)S(1)} %copy-done.10, f32[20,20,260]{2,1,0:T(8,128)} %copy-done.15, f32[16,16,256]{2,1,0:T(8,128)S(1)} %fusion.201, ...), kind=kLoop, calls=%fused_computation.323 | loop fusion | flops 2752508 | bytes 9297936 | tf_op jit(solution)/shard_map/reduce_sum | solution.py:248
  185.1 2.5 %maximum_bitcast_fusion.1 = f32[1,1,4]{2,1,0:T(1,128)S(1)} fusion(f32[1]{0:T(128)} %bitcast.39, f32[1]{0:T(128)} %bitcast.38, f32[1]{0:T(128)} %bitcast.37, f32[1]{0:T(128)} %bitcast.29), kind=kLoop, calls=%fused_computation.342 | loop fusion | flops 12 | bytes 32 | tf_op jit(solution)/shard_map/broadcast_in_dim;broadcast_in_dim | solution.py:167
  188.1 15.3 %shard_map.79 = f32[128,1,128]{2,1,0:T(1,128)} custom-call(f32[1,1,128]{2,1,0:T(1,128)} %scatter.19.row_ref), custom_call_target="tpu_custom_call" | custom-call | tf_op jit(solution)/shard_map/pallas_call | solution.py:168
  209.2 2.2 %multiply_subtract_fusion.1 = (f32[16,16,256]{2,1,0:T(8,128)}, f32[16,16,256]{2,1,0:T(8,128)}) fusion(f32[16,16,256]{2,1,0:T(8,128)S(1)} %get-tuple-element.62, f32[20,20,260]{2,1,0:T(8,128)} %get-tuple-element.68, f32[]{:T(128)S(6)} %div.42, f32[]{:T(128)S(6)} %div.43, f32[20,20,260]{2,1,0:T(8,128)} %copy-done.15, f32[16,16,256]{2,1,0:T(8,128)S(1)} %fusion.197, ...), kind=kLoop, calls=%fused_computation.318 | loop fusion | flops 589824 | bytes 1835020 | tf_op jit(solution)/shard_map/sub | solution.py:260
  (152 shorter events, 49.5 us)
Async XLA Ops:
  0.6 60.2 %copy-start = (f32[16,2048]{1,0:T(8,128)S(1)}, f32[16,2048]{1,0:T(8,128)}, u32[]{:S(2)}) copy-start(f32[16,2048]{1,0:T(8,128)} %param.19) | copy-start | bytes 393220
  0.6 21.5 %copy-start.23 = (f32[16,16,256]{2,1,0:T(8,128)S(1)}, f32[16,16,256]{2,1,0:T(8,128)}, u32[]{:S(2)}) copy-start(f32[16,16,256]{2,1,0:T(8,128)} %param.14) | copy-start | bytes 786436
  0.7 21.5 %copy-start.29 = (f32[16,16,256]{2,1,0:T(8,128)S(1)}, f32[16,16,256]{2,1,0:T(8,128)}, u32[]{:S(2)}) copy-start(f32[16,16,256]{2,1,0:T(8,128)} %param.16) | copy-start | bytes 786436
  22.4 51.1 %copy-start.4 = (f32[6,16,16,256]{3,2,1,0:T(8,128)}, f32[6,16,16,256]{3,2,1,0:T(8,128)S(1)}, u32[]{:S(2)}) copy-start(f32[6,16,16,256]{3,2,1,0:T(8,128)S(1)} %pad_maximum_fusion.1) | copy-start | bytes 4718596
  32.1 6.9 %collective-permute-start.1 = (f32[6,16,16,3]{2,1,3,0:T(8,128)S(1)}, f32[6,16,16,3]{2,1,3,0:T(8,128)S(1)}, u32[]{:S(2)}, u32[]{:S(2)}) collective-permute-start(f32[6,16,16,3]{2,1,3,0:T(8,128)S(1)} %get-tuple-element.79), channel_id=1, source_target_pairs={{1,0},{2,1},{3,2},{5,4},{6,5},{7,6},{9,8},{10,9},{11,10},{13,12},{... | collective-permute-start | bytes 55304 | tf_op jit(solution)/shard_map/ppermute | solution.py:27
  33.4 6.5 %collective-permute-start = (f32[6,16,16,3]{2,1,3,0:T(8,128)S(1)}, f32[6,16,16,3]{2,1,3,0:T(8,128)S(1)}, u32[]{:S(2)}, u32[]{:S(2)}) collective-permute-start(f32[6,16,16,3]{2,1,3,0:T(8,128)S(1)} %get-tuple-element.78), channel_id=1, source_target_pairs={{0,1},{1,2},{2,3},{4,5},{5,6},{6,7},{8,9},{9,10},{10,11},{12,13},{... | collective-permute-start | bytes 55304 | tf_op jit(solution)/shard_map/ppermute | solution.py:26
  39.7 33.8 %copy-start.6 = (f32[6,16,16,3]{3,2,1,0:T(8,128)}, f32[6,16,16,3]{3,2,1,0:T(8,128)S(1)}, u32[]{:S(2)}) copy-start(f32[6,16,16,3]{3,2,1,0:T(8,128)S(1)} %copy.44) | copy-start | bytes 55300
  40.6 32.9 %copy-start.8 = (f32[6,16,16,3]{3,2,1,0:T(8,128)}, f32[6,16,16,3]{3,2,1,0:T(8,128)S(1)}, u32[]{:S(2)}) copy-start(f32[6,16,16,3]{3,2,1,0:T(8,128)S(1)} %copy.43) | copy-start | bytes 55300
  40.9 9.6 %collective-permute-start.3 = (f32[6,3,16,262]{3,2,1,0:T(8,128)S(1)}, f32[6,3,16,262]{3,2,1,0:T(8,128)S(1)}, u32[]{:S(2)}, u32[]{:S(2)}) collective-permute-start(f32[6,3,16,262]{3,2,1,0:T(8,128)S(1)} %get-tuple-element.88), channel_id=1, source_target_pairs={{16,0},{32,16},{48,32},{64,48},{80,64},{96,80},{112,96},{17,1},{33... | collective-permute-start | bytes 905480 | tf_op jit(solution)/shard_map/ppermute | solution.py:27
  44.4 7.5 %collective-permute-start.2 = (f32[6,3,16,262]{3,2,1,0:T(8,128)S(1)}, f32[6,3,16,262]{3,2,1,0:T(8,128)S(1)}, u32[]{:S(2)}, u32[]{:S(2)}) collective-permute-start(f32[6,3,16,262]{3,2,1,0:T(8,128)S(1)} %get-tuple-element.87), channel_id=1, source_target_pairs={{0,16},{16,32},{32,48},{48,64},{64,80},{80,96},{96,112},{1,17},{17... | collective-permute-start | bytes 905480 | tf_op jit(solution)/shard_map/ppermute | solution.py:26
  53.7 15.8 %collective-permute-start.5 = (f32[6,22,3,262]{3,1,2,0:T(8,128)}, f32[6,22,3,262]{3,1,2,0:T(8,128)}, u32[]{:S(2)}, u32[]{:S(2)}) collective-permute-start(f32[6,22,3,262]{3,1,2,0:T(8,128)} %copy.60), channel_id=1, source_target_pairs={{4,0},{8,4},{12,8},{5,1},{9,5},{13,9},{6,2},{10,6},{14,10},{7,3},{... | collective-permute-start | bytes 1245032 | tf_op jit(solution)/shard_map/ppermute | solution.py:27
  55.9 16.2 %collective-permute-start.4 = (f32[6,22,3,262]{3,1,2,0:T(8,128)}, f32[6,22,3,262]{3,1,2,0:T(8,128)}, u32[]{:S(2)}, u32[]{:S(2)}) collective-permute-start(f32[6,22,3,262]{3,1,2,0:T(8,128)} %copy.59), channel_id=1, source_target_pairs={{0,4},{4,8},{8,12},{1,5},{5,9},{9,13},{2,6},{6,10},{10,14},{3,7},{... | collective-permute-start | bytes 1245032 | tf_op jit(solution)/shard_map/ppermute | solution.py:26
  86.3 6.5 %collective-permute-start.7 = (f32[16,16,3]{2,1,0:T(8,128)S(1)}, f32[16,16,3]{2,1,0:T(8,128)S(1)}, u32[]{:S(2)}, u32[]{:S(2)}) collective-permute-start(f32[16,16,3]{2,1,0:T(8,128)S(1)} %get-tuple-element.101), channel_id=1, source_target_pairs={{1,0},{2,1},{3,2},{5,4},{6,5},{7,6},{9,8},{10,9},{11,10},{13,12},{... | collective-permute-start | bytes 9224 | tf_op jit(solution)/shard_map/ppermute | solution.py:27
  87.6 6.7 %collective-permute-start.6 = (f32[16,16,3]{2,1,0:T(8,128)S(1)}, f32[16,16,3]{2,1,0:T(8,128)S(1)}, u32[]{:S(2)}, u32[]{:S(2)}) collective-permute-start(f32[16,16,3]{2,1,0:T(8,128)S(1)} %get-tuple-element.100), channel_id=1, source_target_pairs={{0,1},{1,2},{2,3},{4,5},{5,6},{6,7},{8,9},{9,10},{10,11},{12,13},{... | collective-permute-start | bytes 9224 | tf_op jit(solution)/shard_map/ppermute | solution.py:26
  95.7 8.7 %collective-permute-start.9 = (f32[3,16,262]{2,1,0:T(8,128)}, f32[3,16,262]{2,1,0:T(8,128)}, u32[]{:S(2)}, u32[]{:S(2)}) collective-permute-start(f32[3,16,262]{2,1,0:T(8,128)} %get-tuple-element.93), channel_id=1, source_target_pairs={{16,0},{32,16},{48,32},{64,48},{80,64},{96,80},{112,96},{17,1},{33... | collective-permute-start | bytes 150920 | tf_op jit(solution)/shard_map/ppermute | solution.py:27
  97.6 8.1 %collective-permute-start.8 = (f32[3,16,262]{2,1,0:T(8,128)}, f32[3,16,262]{2,1,0:T(8,128)}, u32[]{:S(2)}, u32[]{:S(2)}) collective-permute-start(f32[3,16,262]{2,1,0:T(8,128)} %get-tuple-element.92), channel_id=1, source_target_pairs={{0,16},{16,32},{32,48},{48,64},{64,80},{80,96},{96,112},{1,17},{17... | collective-permute-start | bytes 150920 | tf_op jit(solution)/shard_map/ppermute | solution.py:26
  106.9 7.8 %collective-permute-start.11 = (f32[22,3,262]{2,0,1:T(8,128)S(1)}, f32[22,3,262]{2,0,1:T(8,128)S(1)}, u32[]{:S(2)}, u32[]{:S(2)}) collective-permute-start(f32[22,3,262]{2,0,1:T(8,128)S(1)} %copy.62), channel_id=1, source_target_pairs={{4,0},{8,4},{12,8},{5,1},{9,5},{13,9},{6,2},{10,6},{14,10},{7,3},{... | collective-permute-start | bytes 207512 | tf_op jit(solution)/shard_map/ppermute | solution.py:27
  108.2 6.5 %collective-permute-start.10 = (f32[22,3,262]{2,0,1:T(8,128)S(1)}, f32[22,3,262]{2,0,1:T(8,128)S(1)}, u32[]{:S(2)}, u32[]{:S(2)}) collective-permute-start(f32[22,3,262]{2,0,1:T(8,128)S(1)} %copy.61), channel_id=1, source_target_pairs={{0,4},{4,8},{8,12},{1,5},{5,9},{9,13},{2,6},{6,10},{10,14},{3,7},{... | collective-permute-start | bytes 207512 | tf_op jit(solution)/shard_map/ppermute | solution.py:26
  158.9 23.6 %copy-start.5 = (f32[6,16,16,256]{3,2,1,0:T(8,128)S(1)}, f32[6,16,16,256]{3,2,1,0:T(8,128)}, u32[]{:S(2)}) copy-start(f32[6,16,16,256]{3,2,1,0:T(8,128)} %copy-done.4) | copy-start | bytes 4718596
  158.9 23.6 %copy-start.7 = (f32[6,16,16,3]{3,2,1,0:T(8,128)S(1)}, f32[6,16,16,3]{3,2,1,0:T(8,128)}, u32[]{:S(2)}) copy-start(f32[6,16,16,3]{3,2,1,0:T(8,128)} %copy-done.6) | copy-start | bytes 55300
  158.9 23.6 %copy-start.9 = (f32[6,16,16,3]{3,2,1,0:T(8,128)S(1)}, f32[6,16,16,3]{3,2,1,0:T(8,128)}, u32[]{:S(2)}) copy-start(f32[6,16,16,3]{3,2,1,0:T(8,128)} %copy-done.8) | copy-start | bytes 55300
  158.9 23.6 %copy-start.14 = (f32[6,22,3,262]{3,2,1,0:T(4,128)S(1)}, f32[6,22,3,262]{3,2,1,0:T(4,128)}, u32[]{:S(2)}) copy-start(f32[6,22,3,262]{3,2,1,0:T(4,128)} %copy-done.13) | copy-start | bytes 1245028
  158.9 23.6 %copy-start.18 = (f32[6,3,16,262]{3,2,1,0:T(8,128)S(1)}, f32[6,3,16,262]{3,2,1,0:T(8,128)}, u32[]{:S(2)}) copy-start(f32[6,3,16,262]{3,2,1,0:T(8,128)} %copy-done.16) | copy-start | bytes 905476
  158.9 23.6 %copy-start.21 = (f32[6,3,16,262]{3,2,1,0:T(8,128)S(1)}, f32[6,3,16,262]{3,2,1,0:T(8,128)}, u32[]{:S(2)}) copy-start(f32[6,3,16,262]{3,2,1,0:T(8,128)} %copy-done.19) | copy-start | bytes 905476
  158.9 23.6 %copy-start.30 = (f32[16,16,256]{2,1,0:T(8,128)S(1)}, f32[16,16,256]{2,1,0:T(8,128)}, u32[]{:S(2)}) copy-start(f32[16,16,256]{2,1,0:T(8,128)} %param.16) | copy-start | bytes 786436
  158.9 23.6 %copy-start.32 = (s32[16,16,256]{2,1,0:T(8,128)S(1)}, s32[16,16,256]{2,1,0:T(8,128)}, u32[]{:S(2)}) copy-start(s32[16,16,256]{2,1,0:T(8,128)} %param.17) | copy-start | bytes 786436
  162.6 12.3 %collective-permute-start.16 = (f32[16,1,256]{2,0,1:T(8,128)S(1)}, f32[16,1,256]{2,0,1:T(8,128)S(1)}, u32[]{:S(2)}, u32[]{:S(2)}) collective-permute-start(f32[16,1,256]{2,0,1:T(8,128)S(1)} %copy.54), channel_id=1, source_target_pairs={{4,0},{8,4},{12,8},{5,1},{9,5},{13,9},{6,2},{10,6},{14,10},{7,3},{... | collective-permute-start | bytes 49160 | tf_op jit(solution)/shard_map/ppermute | solution.py:90
  163.9 15.0 %collective-permute-start.13 = (f32[16,1,256]{2,0,1:T(8,128)S(1)}, f32[16,1,256]{2,0,1:T(8,128)S(1)}, u32[]{:S(2)}, u32[]{:S(2)}) collective-permute-start(f32[16,1,256]{2,0,1:T(8,128)S(1)} %copy.53), channel_id=1, source_target_pairs={{0,4},{4,8},{8,12},{1,5},{5,9},{9,13},{2,6},{6,10},{10,14},{3,7},{... | collective-permute-start | bytes 49160 | tf_op jit(solution)/shard_map/ppermute | solution.py:89
  167.9 13.9 %collective-permute-start.15 = (f32[1,16,256]{2,1,0:T(8,128)S(1)}, f32[1,16,256]{2,1,0:T(8,128)S(1)}, u32[]{:S(2)}, u32[]{:S(2)}) collective-permute-start(f32[1,16,256]{2,1,0:T(8,128)S(1)} %get-tuple-element.95), channel_id=1, source_target_pairs={{16,0},{32,16},{48,32},{64,48},{80,64},{96,80},{112,96},{17,1},{33... | collective-permute-start | bytes 49160 | tf_op jit(solution)/shard_map/ppermute | solution.py:90
  170.8 11.0 %collective-permute-start.14 = (f32[1,16,256]{2,1,0:T(8,128)S(1)}, f32[1,16,256]{2,1,0:T(8,128)S(1)}, u32[]{:S(2)}, u32[]{:S(2)}) collective-permute-start(f32[1,16,256]{2,1,0:T(8,128)S(1)} %get-tuple-element.94), channel_id=1, source_target_pairs={{0,16},{16,32},{32,48},{48,64},{64,80},{80,96},{96,112},{1,17},{17... | collective-permute-start | bytes 49160 | tf_op jit(solution)/shard_map/ppermute | solution.py:89
  173.6 7.2 %collective-permute-start.17 = (f32[16,16,1]{2,1,0:T(8,128)S(1)}, f32[16,16,1]{2,1,0:T(8,128)S(1)}, u32[]{:S(2)}, u32[]{:S(2)}) collective-permute-start(f32[16,16,1]{2,1,0:T(8,128)S(1)} %get-tuple-element.97), channel_id=1, source_target_pairs={{1,0},{2,1},{3,2},{5,4},{6,5},{7,6},{9,8},{10,9},{11,10},{13,12},{... | collective-permute-start | bytes 3080 | tf_op jit(solution)/shard_map/ppermute | solution.py:90
  174.9 6.9 %collective-permute-start.12 = (f32[16,16,1]{2,1,0:T(8,128)S(1)}, f32[16,16,1]{2,1,0:T(8,128)S(1)}, u32[]{:S(2)}, u32[]{:S(2)}) collective-permute-start(f32[16,16,1]{2,1,0:T(8,128)S(1)} %get-tuple-element.96), channel_id=1, source_target_pairs={{0,1},{1,2},{2,3},{4,5},{5,6},{6,7},{8,9},{9,10},{10,11},{12,13},{... | collective-permute-start | bytes 3080 | tf_op jit(solution)/shard_map/ppermute | solution.py:89
  (24 other events, 173.7 us)

commit v4 on v1

--- a/solution.py
+++ b/solution.py
@@ -62,8 +62,8 @@
 
 
 def jacobi(rhs_box, padded_cond, diagonal, storage_box, free_box):
-    guess = jnp.zeros_like(rhs_box)
-    for sweep in range(SWEEPS):
+    guess = RELAX * rhs_box / diagonal
+    for sweep in range(1, SWEEPS):
         image = stencil(jnp.pad(free_box * guess, 1), padded_cond, guess, storage_box, free_box)
         guess = guess + RELAX * (rhs_box - image) / diagonal
     return guess

time: 206 us -> 208 us (level)
  waiting for transfers between devices: 10.1 us -> 24.7 us
  starting transfers between devices: 53.8 us -> 45.5 us
  Pallas kernels: 55.8 us -> 51.3 us
    ppermute x6, waiting for transfers between devices: 5.64 us -> 17.5 us  [padded(): after = lax.ppermute(leading, axis, down)]
    pallas_call x3, Pallas kernels: 55.8 us -> 51.3 us  [gather_rows(): pl.pallas_call(functools.partial(gather_kernel, sizes), out_shape=jax.Sha...]
    ppermute x6, starting transfers between devices: 12.3 us -> 9.6 us  [padded(): after = lax.ppermute(leading, axis, down)]
    ppermute x3, waiting for transfers between devices: 0.01 us -> 2.17 us  [faces(): after = lax.ppermute(lax.slice_in_dim(field, 0, 1, axis=dim), axis, down)]
    mul x7 -> x6, other arithmetic: 16.7 us -> 15.3 us  [jacobi(): free_box * guess]
    unnamed x90 -> x88, local copies, waits for them, and re-layouts: 4.58 us -> 4.55 us
  transfers between devices with their start and end apart: 18 -> 18, of which waited for: 7 -> 9; matrix products, arithmetic and copies ran while one was open for 6% -> 6% of each run, Pallas kernels for 12% -> 11%
where the time goes in v4:
time: 208 us; the launch traced here: 206 us
  other arithmetic  59 us (28%)
  Pallas kernels  51.3 us (25%)
  starting transfers between devices  45.5 us (22%)
  waiting for transfers between devices  24.7 us (12%)
  local copies, waits for them, and re-layouts  18 us (9%)
  between operations  7.35 us (4%)
    pallas_call x3, Pallas kernels, gather_rows(): pl.pallas_call(functools.partial(gather_kernel, sizes), out_shape=jax.Sha...  51.3 us
    ppermute x6, starting transfers between devices, padded(): before = lax.ppermute(last, axis, up)  23.1 us
    ppermute x6, waiting for transfers between devices, padded(): after = lax.ppermute(leading, axis, down)  17.5 us
    mul x6, other arithmetic, jacobi(): free_box * guess  15.3 us
    ppermute x6, starting transfers between devices, padded(): after = lax.ppermute(leading, axis, down)  9.6 us
    ppermute x3, starting transfers between devices, faces(): lax.ppermute(lax.slice_in_dim(field, length - 1, length, axis=dim), axis,...  8.36 us
    concatenate x2, other arithmetic, padded(): value = jnp.concatenate([before, value, after], axis=dim)  7.86 us
    reduce_sum x2, other arithmetic, expand(): return jnp.sum(weights[:, None, None, None] * basis, axis=0)  5.73 us
  transfers between devices with their start and end apart: 18, of which 9 were waited for; matrix products, arithmetic and copies ran while one was open for 6% of the time, Pallas kernels for 11%

profile of v4, /device:TPU:1, one launch (start us, length us, event | category | flops | bytes accessed | tf_op | source)
XLA Modules:
  0.0 206.2 jit_solution(15636734490776304563)
XLA Ops:
  4.2 4.0 %collective-permute-start = (f32[6,16,16,3]{2,1,3,0:T(8,128)S(1)}, f32[6,16,16,3]{2,1,3,0:T(8,128)S(1)}, u32[]{:S(2)}, u32[]{:S(2)}) collective-permute-start(f32[6,16,16,3]{2,1,3,0:T(8,128)S(1)} %copy.62), channel_id=1, source_target_pairs={{0,1},{1,2},{2,3},{4,5},{5,6},{6,7},{8,9},{9,10},{10,11},{12,13},{... | collective-permute-start | bytes 55304 | tf_op jit(solution)/shard_map/ppermute | solution.py:26
  11.3 3.9 %collective-permute-done.1 = f32[6,16,16,3]{2,1,3,0:T(8,128)} collective-permute-done((f32[6,16,16,3]{2,1,3,0:T(8,128)S(1)}, f32[6,16,16,3]{2,1,3,0:T(8,128)}, u32[]{:S(2)}, u32[]{:S(2)}) %collective-permute-start.1) | collective-permute-done | bytes 18464 | tf_op jit(solution)/shard_map/ppermute | solution.py:27
  17.2 5.0 %collective-permute-start.2 = (f32[6,3,16,262]{3,2,1,0:T(8,128)S(1)}, f32[6,3,16,262]{3,2,1,0:T(8,128)S(1)}, u32[]{:S(2)}, u32[]{:S(2)}) collective-permute-start(f32[6,3,16,262]{3,2,1,0:T(8,128)S(1)} %get-tuple-element.80), channel_id=1, source_target_pairs={{0,16},{16,32},{32,48},{48,64},{64,80},{80,96},{96,112},{1,17},{17... | collective-permute-start | bytes 905480 | tf_op jit(solution)/shard_map/ppermute | solution.py:26
  24.1 3.3 %collective-permute-done.2 = f32[6,3,16,262]{3,2,1,0:T(8,128)S(1)} collective-permute-done((f32[6,3,16,262]{3,2,1,0:T(8,128)S(1)}, f32[6,3,16,262]{3,2,1,0:T(8,128)S(1)}, u32[]{:S(2)}, u32[]{:S(2)}) %collective-permute-start.2) | collective-permute-done | bytes 301856 | tf_op jit(solution)/shard_map/ppermute | solution.py:26
  27.4 4.4 %collective-permute-done.3 = f32[6,3,16,262]{3,2,1,0:T(8,128)S(1)} collective-permute-done((f32[6,3,16,262]{3,2,1,0:T(8,128)S(1)}, f32[6,3,16,262]{3,2,1,0:T(8,128)S(1)}, u32[]{:S(2)}, u32[]{:S(2)}) %collective-permute-start.3) | collective-permute-done | bytes 301856 | tf_op jit(solution)/shard_map/ppermute | solution.py:27
  31.8 2.2 %pad_maximum_fusion.2 = f32[6,22,16,262]{3,2,1,0:T(8,128)S(1)} fusion(f32[6,3,16,262]{3,2,1,0:T(8,128)S(1)} %collective-permute-done.3, f32[6,16,16,3]{3,2,1,0:T(8,128)S(1)} %copy.47, f32[1,16,16,256]{3,2,1,0:T(8,128)S(1)} %bitcast.282, f32[1,16,16,256]{3,2,1,0:T(8,128)S(1)} %fusion.185, f32[1,16,16,256]{3,2,1,0:T(8,128)S(1)} %bitcast.287, ...), kind=kLoop, calls=%fused_computation.6 | loop fusion | flops 3873408 | bytes 4426752 | tf_op jit(solution)/shard_map/concatenate | solution.py:28
  35.2 4.5 %collective-permute-start.4 = (f32[6,22,3,262]{3,1,2,0:T(8,128)}, f32[6,22,3,262]{3,1,2,0:T(8,128)}, u32[]{:S(2)}, u32[]{:S(2)}) collective-permute-start(f32[6,22,3,262]{3,1,2,0:T(8,128)} %copy.64), channel_id=1, source_target_pairs={{0,4},{4,8},{8,12},{1,5},{5,9},{9,13},{2,6},{6,10},{10,14},{3,7},{... | collective-permute-start | bytes 1245032 | tf_op jit(solution)/shard_map/ppermute | solution.py:26
  42.9 22.1 %shard_map.77 = f32[128,1,128]{2,1,0:T(1,128)} custom-call(f32[1,1,128]{2,1,0:T(1,128)} %scatter.14.row_ref), custom_call_target="tpu_custom_call" | custom-call | tf_op jit(solution)/shard_map/pallas_call | solution.py:168
  66.2 2.8 %multiply_reduce_fusion.2 = f32[16,16,256]{2,1,0:T(8,128)S(1)} fusion(f32[16,16,16,256]{3,2,1,0:T(8,128)} %param.18, f32[16]{0:T(128)S(1)} %convolution_bitcast_fusion.1), kind=kLoop, calls=%fused_computation.4 | loop fusion | flops 2031616 | bytes 4456512 | tf_op jit(solution)/shard_map/reduce_sum | solution.py:77
  72.0 5.7 %pad_maximum_fusion = f32[6,22,22,262]{3,2,1,0:T(8,128)S(1)} fusion(f32[6,22,3,262]{3,2,1,0:T(4,128)S(1)} %copy.51, f32[6,3,16,262]{3,2,1,0:T(8,128)S(1)} %copy-done.29, f32[6,16,16,3]{3,2,1,0:T(8,128)S(1)} %copy.47, f32[1,16,16,256]{3,2,1,0:T(8,128)S(1)} %bitcast.283, f32[1,16,16,256]{3,2,1,0:T(8,128)S(1)} %fusion.185, f32[1,16,16,256]{3,2,1,0:T(8,128)S(1)} %bitcast.288, ...), kind=kLoop, calls=%fused_computation | loop fusion | flops 6847632 | bytes 6086784 | tf_op jit(solution)/shard_map/concatenate | solution.py:28
  87.1 3.1 %collective-permute-start.6 = (f32[16,16,3]{2,1,0:T(8,128)S(1)}, f32[16,16,3]{2,1,0:T(8,128)S(1)}, u32[]{:S(2)}, u32[]{:S(2)}) collective-permute-start(f32[16,16,3]{2,1,0:T(8,128)S(1)} %get-tuple-element.95), channel_id=1, source_target_pairs={{0,1},{1,2},{2,3},{4,5},{5,6},{6,7},{8,9},{9,10},{10,11},{12,13},{... | collective-permute-start | bytes 9224 | tf_op jit(solution)/shard_map/ppermute | solution.py:26
  92.7 3.8 %collective-permute-done.7 = f32[16,16,3]{2,1,0:T(8,128)S(1)} collective-permute-done((f32[16,16,3]{2,1,0:T(8,128)S(1)}, f32[16,16,3]{2,1,0:T(8,128)S(1)}, u32[]{:S(2)}, u32[]{:S(2)}) %collective-permute-start.7) | collective-permute-done | bytes 3104 | tf_op jit(solution)/shard_map/ppermute | solution.py:27
  97.9 2.8 %collective-permute-start.8 = (f32[3,16,262]{2,1,0:T(8,128)}, f32[3,16,262]{2,1,0:T(8,128)}, u32[]{:S(2)}, u32[]{:S(2)}) collective-permute-start(f32[3,16,262]{2,1,0:T(8,128)} %get-tuple-element.87), channel_id=1, source_target_pairs={{0,16},{16,32},{32,48},{48,64},{64,80},{80,96},{96,112},{1,17},{17... | collective-permute-start | bytes 150920 | tf_op jit(solution)/shard_map/ppermute | solution.py:26
  100.8 2.5 %collective-permute-start.9 = (f32[3,16,262]{2,1,0:T(8,128)}, f32[3,16,262]{2,1,0:T(8,128)}, u32[]{:S(2)}, u32[]{:S(2)}) collective-permute-start(f32[3,16,262]{2,1,0:T(8,128)} %get-tuple-element.88), channel_id=1, source_target_pairs={{16,0},{32,16},{48,32},{64,48},{80,64},{96,80},{112,96},{17,1},{33... | collective-permute-start | bytes 150920 | tf_op jit(solution)/shard_map/ppermute | solution.py:27
  104.2 2.5 %collective-permute-done.9 = f32[3,16,262]{2,1,0:T(8,128)} collective-permute-done((f32[3,16,262]{2,1,0:T(8,128)}, f32[3,16,262]{2,1,0:T(8,128)}, u32[]{:S(2)}, u32[]{:S(2)}) %collective-permute-start.9) | collective-permute-done | bytes 50336 | tf_op jit(solution)/shard_map/ppermute | solution.py:27
  107.9 3.7 %collective-permute-start.10 = (f32[22,3,262]{2,0,1:T(8,128)S(1)}, f32[22,3,262]{2,0,1:T(8,128)S(1)}, u32[]{:S(2)}, u32[]{:S(2)}) collective-permute-start(f32[22,3,262]{2,0,1:T(8,128)S(1)} %copy.66), channel_id=1, source_target_pairs={{0,4},{4,8},{8,12},{1,5},{5,9},{9,13},{2,6},{6,10},{10,14},{3,7},{... | collective-permute-start | bytes 207512 | tf_op jit(solution)/shard_map/ppermute | solution.py:26
  114.5 2.9 %collective-permute-done.11 = f32[22,3,262]{2,0,1:T(8,128)S(1)} collective-permute-done((f32[22,3,262]{2,0,1:T(8,128)S(1)}, f32[22,3,262]{2,0,1:T(8,128)S(1)}, u32[]{:S(2)}, u32[]{:S(2)}) %collective-permute-start.11) | collective-permute-done | bytes 69200 | tf_op jit(solution)/shard_map/ppermute | solution.py:27
  118.7 3.0 %fusion.139 = f32[20,20,260]{2,1,0:T(8,128)S(1)} fusion(f32[22,22,262]{2,1,0:T(8,128)S(1)} %get-tuple-element.66, f32[22,22,262]{2,1,0:T(8,128)S(1)} %get-tuple-element.65, f32[6,22,22,262]{3,2,1,0:T(8,128)S(1)} %copy-done.2, f32[22,22,262]{2,1,0:T(8,128)S(1)} %get-tuple-element.74, f32[22,22,262]{2,1,0:T(8,128)S(1)} %get-tuple-element.73), kind=kLoop, calls=%fused_computation.194 | loop fusion | flops 2392000 | bytes 7072000 | tf_op jit(solution)/shard_map/add | solution.py:54
  125.1 13.5 %shard_map.78 = f32[128,1,128]{2,1,0:T(1,128)} custom-call(f32[1,1,128]{2,1,0:T(1,128)} %copy-done.37), custom_call_target="tpu_custom_call" | custom-call | tf_op jit(solution)/shard_map/pallas_call | solution.py:168
  141.6 2.5 %fusion.156 = (f32[20,20,260]{2,1,0:T(8,128)S(1)}, f32[20,20,260]{2,1,0:T(8,128)S(1)}) fusion(f32[20,20,260]{2,1,0:T(8,128)} %copy-done.6, f32[6,22,22,262]{3,2,1,0:T(8,128)} %copy-done.1, f32[20,20,260]{2,1,0:T(8,128)} %copy-done.23, f32[]{:T(128)S(6)} %div.37), kind=kLoop, calls=%fused_computation.239 | loop fusion | flops 520000 | bytes 2496004 | tf_op jit(solution)/shard_map/mul | solution.py:67
  144.1 4.4 %fusion.188 = (f32[20,20,260]{2,1,0:T(8,128)S(1)}, f32[20,20,260]{2,1,0:T(8,128)S(1)}) fusion(f32[6,22,22,262]{3,2,1,0:T(8,128)} %copy-done.1, f32[20,20,260]{2,1,0:T(8,128)} %copy-done.6, f32[20,20,260]{2,1,0:T(8,128)S(1)} %get-tuple-element.64, f32[20,20,260]{2,1,0:T(8,128)S(1)} %get-tuple-element.63, f32[3,20,20,260]{3,2,1,0:T(8,128)S(1)} %slice.568), kind=kLoop, calls=%fused_computation.326 | loop fusion | flops 3120000 | bytes 5408000 | tf_op jit(solution)/shard_map/mul | solution.py:67
  148.6 2.7 %fusion.187 = (f32[20,20,260]{2,1,0:T(8,128)S(1)}, f32[20,20,260]{2,1,0:T(8,128)}) fusion(f32[6,22,22,262]{3,2,1,0:T(8,128)S(1)} %bitcast.279, f32[20,20,260]{2,1,0:T(8,128)S(1)} %get-tuple-element.62, f32[20,20,260]{2,1,0:T(8,128)S(1)} %copy-done.7, f32[20,20,260]{2,1,0:T(8,128)S(1)} %get-tuple-element.64, f32[20,20,260]{2,1,0:T(8,128)S(1)} %get-tuple-element.61, ...), kind=kLoop, calls=%fused_computation.325 | loop fusion | flops 2912000 | bytes 5824000 | tf_op jit(solution)/shard_map/mul | solution.py:67
  151.3 2.4 %fusion.125 = f32[20,20,260]{2,1,0:T(8,128)} fusion(f32[20,20,260]{2,1,0:T(8,128)S(1)} %get-tuple-element.59, f32[6,22,22,262]{3,2,1,0:T(8,128)S(1)} %bitcast.279, f32[3,20,20,260]{3,2,1,0:T(8,128)S(1)} %slice.568), kind=kLoop, calls=%fused_computation.179 | loop fusion | flops 1976000 | bytes 3744000 | tf_op jit(solution)/shard_map/add | solution.py:50
  154.0 2.9 %multiply_reduce_fusion = f32[16,16,256]{2,1,0:T(8,128)S(1)} fusion(f32[16,16,16,256]{3,2,1,0:T(8,128)} %param.18, f32[16]{0:T(128)S(1)} %convolution_bitcast_fusion), kind=kLoop, calls=%fused_computation.2 | loop fusion | flops 2031616 | bytes 4456512 | tf_op jit(solution)/shard_map/reduce_sum | solution.py:77
  156.9 2.3 %fusion.179 = f32[16,16,256]{2,1,0:T(8,128)S(1)} fusion(f32[16,16,256]{2,1,0:T(8,128)S(1)} %multiply_reduce_fusion, f32[20,20,260]{2,1,0:T(8,128)} %fusion.125, f32[20,20,260]{2,1,0:T(8,128)} %get-tuple-element.60, f32[20,20,260]{2,1,0:T(8,128)} %copy-done.6, f32[20,20,260]{2,1,0:T(8,128)} %copy-done.32, f32[20,20,260]{2,1,0:T(8,128)} %copy-done.31, ...), kind=kLoop, calls=%fused_computation.292 | loop fusion | flops 524288 | bytes 2097152 | tf_op jit(solution)/shard_map/add | solution.py:224
  159.4 2.6 %collective-permute-start.13 = (f32[16,1,256]{2,0,1:T(8,128)S(1)}, f32[16,1,256]{2,0,1:T(8,128)S(1)}, u32[]{:S(2)}, u32[]{:S(2)}) collective-permute-start(f32[16,1,256]{2,0,1:T(8,128)S(1)} %copy.56), channel_id=1, source_target_pairs={{0,4},{4,8},{8,12},{1,5},{5,9},{9,13},{2,6},{6,10},{10,14},{3,7},{... | collective-permute-start | bytes 49160 | tf_op jit(solution)/shard_map/ppermute | solution.py:89
  162.0 2.5 %collective-permute-start.12 = (f32[16,16,1]{2,1,0:T(8,128)S(1)}, f32[16,16,1]{2,1,0:T(8,128)S(1)}, u32[]{:S(2)}, u32[]{:S(2)}) collective-permute-start(f32[16,16,1]{2,1,0:T(8,128)S(1)} %get-tuple-element.91), channel_id=1, source_target_pairs={{0,1},{1,2},{2,3},{4,5},{5,6},{6,7},{8,9},{9,10},{10,11},{12,13},{... | collective-permute-start | bytes 3080 | tf_op jit(solution)/shard_map/ppermute | solution.py:89
  167.1 3.3 %collective-permute-start.14 = (f32[1,16,256]{2,1,0:T(8,128)S(1)}, f32[1,16,256]{2,1,0:T(8,128)S(1)}, u32[]{:S(2)}, u32[]{:S(2)}) collective-permute-start(f32[1,16,256]{2,1,0:T(8,128)S(1)} %get-tuple-element.89), channel_id=1, source_target_pairs={{0,16},{16,32},{32,48},{48,64},{64,80},{80,96},{96,112},{1,17},{17... | collective-permute-start | bytes 49160 | tf_op jit(solution)/shard_map/ppermute | solution.py:89
  173.3 2.2 %collective-permute-done.15 = f32[1,16,256]{2,1,0:T(8,128)S(1)} collective-permute-done((f32[1,16,256]{2,1,0:T(8,128)S(1)}, f32[1,16,256]{2,1,0:T(8,128)S(1)}, u32[]{:S(2)}, u32[]{:S(2)}) %collective-permute-start.15) | collective-permute-done | bytes 16416 | tf_op jit(solution)/shard_map/ppermute | solution.py:90
  177.2 2.3 %multiply_reduce_fusion.7 = (f32[]{:T(128)}, f32[]{:T(128)}, f32[]{:T(128)}, f32[]{:T(128)}, f32[16,16,256]{2,1,0:T(8,128)}) fusion(f32[16,16,256]{2,1,0:T(8,128)S(1)} %fusion.179, f32[20,20,260]{2,1,0:T(8,128)S(1)} %copy-done.20, f32[20,20,260]{2,1,0:T(8,128)S(1)} %copy-done.24, f32[16,16,256]{2,1,0:T(8,128)S(1)} %fusion.183, ...), kind=kLoop, calls=%fused_computation.305 | loop fusion | flops 3211260 | bytes 9560080 | tf_op jit(solution)/shard_map/reduce_sum | solution.py:246
  179.5 2.5 %maximum_bitcast_fusion.1 = f32[1,1,4]{2,1,0:T(1,128)S(1)} fusion(f32[1]{0:T(128)} %bitcast.39, f32[1]{0:T(128)} %bitcast.38, f32[1]{0:T(128)} %bitcast.37, f32[1]{0:T(128)} %bitcast.29), kind=kLoop, calls=%fused_computation.322 | loop fusion | flops 12 | bytes 32 | tf_op jit(solution)/shard_map/broadcast_in_dim;broadcast_in_dim | solution.py:167
  182.6 15.8 %shard_map.79 = f32[128,1,128]{2,1,0:T(1,128)} custom-call(f32[1,1,128]{2,1,0:T(1,128)} %scatter.19.row_ref), custom_call_target="tpu_custom_call" | custom-call | tf_op jit(solution)/shard_map/pallas_call | solution.py:168
  (158 shorter events, 54.9 us)
Async XLA Ops:
  0.6 65.3 %copy-start = (f32[16,2048]{1,0:T(8,128)S(1)}, f32[16,2048]{1,0:T(8,128)}, u32[]{:S(2)}) copy-start(f32[16,2048]{1,0:T(8,128)} %param.19) | copy-start | bytes 393220
  1.7 70.3 %copy-start.17 = (f32[1,16,16,256]{3,2,1,0:T(8,128)}, f32[1,16,16,256]{3,2,1,0:T(8,128)S(1)}, u32[]{:S(2)}) copy-start(f32[1,16,16,256]{3,2,1,0:T(8,128)S(1)} %fusion.185) | copy-start | bytes 786436
  4.2 6.5 %collective-permute-start = (f32[6,16,16,3]{2,1,3,0:T(8,128)S(1)}, f32[6,16,16,3]{2,1,3,0:T(8,128)S(1)}, u32[]{:S(2)}, u32[]{:S(2)}) collective-permute-start(f32[6,16,16,3]{2,1,3,0:T(8,128)S(1)} %copy.62), channel_id=1, source_target_pairs={{0,1},{1,2},{2,3},{4,5},{5,6},{6,7},{8,9},{9,10},{10,11},{12,13},{... | collective-permute-start | bytes 55304 | tf_op jit(solution)/shard_map/ppermute | solution.py:26
  8.8 6.4 %collective-permute-start.1 = (f32[6,16,16,3]{2,1,3,0:T(8,128)S(1)}, f32[6,16,16,3]{2,1,3,0:T(8,128)}, u32[]{:S(2)}, u32[]{:S(2)}) collective-permute-start(f32[6,16,16,3]{2,1,3,0:T(8,128)S(1)} %copy.63), channel_id=1, source_target_pairs={{1,0},{2,1},{3,2},{5,4},{6,5},{7,6},{9,8},{10,9},{11,10},{13,12},{... | collective-permute-start | bytes 55304 | tf_op jit(solution)/shard_map/ppermute | solution.py:27
  11.3 60.7 %copy-start.8 = (f32[6,16,16,3]{3,2,1,0:T(8,128)}, f32[6,16,16,3]{3,2,1,0:T(8,128)S(1)}, u32[]{:S(2)}) copy-start(f32[6,16,16,3]{3,2,1,0:T(8,128)S(1)} %copy.46) | copy-start | bytes 55300
  16.8 55.2 %copy-start.10 = (f32[6,16,16,3]{3,2,1,0:T(8,128)}, f32[6,16,16,3]{3,2,1,0:T(8,128)S(1)}, u32[]{:S(2)}) copy-start(f32[6,16,16,3]{3,2,1,0:T(8,128)S(1)} %copy.47) | copy-start | bytes 55300
  17.2 10.2 %collective-permute-start.2 = (f32[6,3,16,262]{3,2,1,0:T(8,128)S(1)}, f32[6,3,16,262]{3,2,1,0:T(8,128)S(1)}, u32[]{:S(2)}, u32[]{:S(2)}) collective-permute-start(f32[6,3,16,262]{3,2,1,0:T(8,128)S(1)} %get-tuple-element.80), channel_id=1, source_target_pairs={{0,16},{16,32},{32,48},{48,64},{64,80},{80,96},{96,112},{1,17},{17... | collective-permute-start | bytes 905480 | tf_op jit(solution)/shard_map/ppermute | solution.py:26
  22.1 9.6 %collective-permute-start.3 = (f32[6,3,16,262]{3,2,1,0:T(8,128)S(1)}, f32[6,3,16,262]{3,2,1,0:T(8,128)S(1)}, u32[]{:S(2)}, u32[]{:S(2)}) collective-permute-start(f32[6,3,16,262]{3,2,1,0:T(8,128)S(1)} %get-tuple-element.81), channel_id=1, source_target_pairs={{16,0},{32,16},{48,32},{64,48},{80,64},{96,80},{112,96},{17,1},{33... | collective-permute-start | bytes 905480 | tf_op jit(solution)/shard_map/ppermute | solution.py:27
  35.2 33.9 %collective-permute-start.4 = (f32[6,22,3,262]{3,1,2,0:T(8,128)}, f32[6,22,3,262]{3,1,2,0:T(8,128)}, u32[]{:S(2)}, u32[]{:S(2)}) collective-permute-start(f32[6,22,3,262]{3,1,2,0:T(8,128)} %copy.64), channel_id=1, source_target_pairs={{0,4},{4,8},{8,12},{1,5},{5,9},{9,13},{2,6},{6,10},{10,14},{3,7},{... | collective-permute-start | bytes 1245032 | tf_op jit(solution)/shard_map/ppermute | solution.py:26
  40.6 29.8 %collective-permute-start.5 = (f32[6,22,3,262]{3,1,2,0:T(8,128)}, f32[6,22,3,262]{3,1,2,0:T(8,128)}, u32[]{:S(2)}, u32[]{:S(2)}) collective-permute-start(f32[6,22,3,262]{3,1,2,0:T(8,128)} %copy.65), channel_id=1, source_target_pairs={{4,0},{8,4},{12,8},{5,1},{9,5},{13,9},{6,2},{10,6},{14,10},{7,3},{... | collective-permute-start | bytes 1245032 | tf_op jit(solution)/shard_map/ppermute | solution.py:27
  87.1 5.6 %collective-permute-start.6 = (f32[16,16,3]{2,1,0:T(8,128)S(1)}, f32[16,16,3]{2,1,0:T(8,128)S(1)}, u32[]{:S(2)}, u32[]{:S(2)}) collective-permute-start(f32[16,16,3]{2,1,0:T(8,128)S(1)} %get-tuple-element.95), channel_id=1, source_target_pairs={{0,1},{1,2},{2,3},{4,5},{5,6},{6,7},{8,9},{9,10},{10,11},{12,13},{... | collective-permute-start | bytes 9224 | tf_op jit(solution)/shard_map/ppermute | solution.py:26
  90.2 6.3 %collective-permute-start.7 = (f32[16,16,3]{2,1,0:T(8,128)S(1)}, f32[16,16,3]{2,1,0:T(8,128)S(1)}, u32[]{:S(2)}, u32[]{:S(2)}) collective-permute-start(f32[16,16,3]{2,1,0:T(8,128)S(1)} %get-tuple-element.96), channel_id=1, source_target_pairs={{1,0},{2,1},{3,2},{5,4},{6,5},{7,6},{9,8},{10,9},{11,10},{13,12},{... | collective-permute-start | bytes 9224 | tf_op jit(solution)/shard_map/ppermute | solution.py:27
  97.9 6.3 %collective-permute-start.8 = (f32[3,16,262]{2,1,0:T(8,128)}, f32[3,16,262]{2,1,0:T(8,128)}, u32[]{:S(2)}, u32[]{:S(2)}) collective-permute-start(f32[3,16,262]{2,1,0:T(8,128)} %get-tuple-element.87), channel_id=1, source_target_pairs={{0,16},{16,32},{32,48},{48,64},{64,80},{80,96},{96,112},{1,17},{17... | collective-permute-start | bytes 150920 | tf_op jit(solution)/shard_map/ppermute | solution.py:26
  100.8 6.0 %collective-permute-start.9 = (f32[3,16,262]{2,1,0:T(8,128)}, f32[3,16,262]{2,1,0:T(8,128)}, u32[]{:S(2)}, u32[]{:S(2)}) collective-permute-start(f32[3,16,262]{2,1,0:T(8,128)} %get-tuple-element.88), channel_id=1, source_target_pairs={{16,0},{32,16},{48,32},{64,48},{80,64},{96,80},{112,96},{17,1},{33... | collective-permute-start | bytes 150920 | tf_op jit(solution)/shard_map/ppermute | solution.py:27
  107.9 6.5 %collective-permute-start.10 = (f32[22,3,262]{2,0,1:T(8,128)S(1)}, f32[22,3,262]{2,0,1:T(8,128)S(1)}, u32[]{:S(2)}, u32[]{:S(2)}) collective-permute-start(f32[22,3,262]{2,0,1:T(8,128)S(1)} %copy.66), channel_id=1, source_target_pairs={{0,4},{4,8},{8,12},{1,5},{5,9},{9,13},{2,6},{6,10},{10,14},{3,7},{... | collective-permute-start | bytes 207512 | tf_op jit(solution)/shard_map/ppermute | solution.py:26
  111.6 5.7 %collective-permute-start.11 = (f32[22,3,262]{2,0,1:T(8,128)S(1)}, f32[22,3,262]{2,0,1:T(8,128)S(1)}, u32[]{:S(2)}, u32[]{:S(2)}) collective-permute-start(f32[22,3,262]{2,0,1:T(8,128)S(1)} %copy.67), channel_id=1, source_target_pairs={{4,0},{8,4},{12,8},{5,1},{9,5},{13,9},{6,2},{10,6},{14,10},{7,3},{... | collective-permute-start | bytes 207512 | tf_op jit(solution)/shard_map/ppermute | solution.py:27
  153.7 18.7 %copy-start.16 = (f32[16,16,256]{2,1,0:T(8,128)S(1)}, f32[16,16,256]{2,1,0:T(8,128)}, u32[]{:S(2)}) copy-start(f32[16,16,256]{2,1,0:T(8,128)} %param.16) | copy-start | bytes 786436
  153.7 18.7 %copy-start.18 = (f32[1,16,16,256]{3,2,1,0:T(8,128)S(1)}, f32[1,16,16,256]{3,2,1,0:T(8,128)}, u32[]{:S(2)}) copy-start(f32[1,16,16,256]{3,2,1,0:T(8,128)} %copy-done.17) | copy-start | bytes 786436
  159.3 17.9 %copy-start.9 = (f32[6,16,16,3]{3,2,1,0:T(8,128)S(1)}, f32[6,16,16,3]{3,2,1,0:T(8,128)}, u32[]{:S(2)}) copy-start(f32[6,16,16,3]{3,2,1,0:T(8,128)} %copy-done.8) | copy-start | bytes 55300
  159.3 17.9 %copy-start.11 = (f32[6,16,16,3]{3,2,1,0:T(8,128)S(1)}, f32[6,16,16,3]{3,2,1,0:T(8,128)}, u32[]{:S(2)}) copy-start(f32[6,16,16,3]{3,2,1,0:T(8,128)} %copy-done.10) | copy-start | bytes 55300
  159.3 17.9 %copy-start.14 = (f32[16,16,256]{2,1,0:T(8,128)S(1)}, f32[16,16,256]{2,1,0:T(8,128)}, u32[]{:S(2)}) copy-start(f32[16,16,256]{2,1,0:T(8,128)} %param.14) | copy-start | bytes 786436
  159.3 17.9 %copy-start.22 = (f32[6,22,3,262]{3,2,1,0:T(4,128)S(1)}, f32[6,22,3,262]{3,2,1,0:T(4,128)}, u32[]{:S(2)}) copy-start(f32[6,22,3,262]{3,2,1,0:T(4,128)} %copy-done.21) | copy-start | bytes 1245028
  159.3 17.9 %copy-start.24 = (f32[20,20,260]{2,1,0:T(8,128)S(1)}, f32[20,20,260]{2,1,0:T(8,128)}, u32[]{:S(2)}) copy-start(f32[20,20,260]{2,1,0:T(8,128)} %copy-done.23) | copy-start | bytes 1248004
  159.3 17.9 %copy-start.27 = (f32[6,3,16,262]{3,2,1,0:T(8,128)S(1)}, f32[6,3,16,262]{3,2,1,0:T(8,128)}, u32[]{:S(2)}) copy-start(f32[6,3,16,262]{3,2,1,0:T(8,128)} %copy-done.25) | copy-start | bytes 905476
  159.3 17.9 %copy-start.30 = (f32[6,3,16,262]{3,2,1,0:T(8,128)S(1)}, f32[6,3,16,262]{3,2,1,0:T(8,128)}, u32[]{:S(2)}) copy-start(f32[6,3,16,262]{3,2,1,0:T(8,128)} %copy-done.28) | copy-start | bytes 905476
  159.3 17.9 %copy-start.35 = (s32[16,16,256]{2,1,0:T(8,128)S(1)}, s32[16,16,256]{2,1,0:T(8,128)}, u32[]{:S(2)}) copy-start(s32[16,16,256]{2,1,0:T(8,128)} %param.17) | copy-start | bytes 786436
  159.4 11.0 %collective-permute-start.13 = (f32[16,1,256]{2,0,1:T(8,128)S(1)}, f32[16,1,256]{2,0,1:T(8,128)S(1)}, u32[]{:S(2)}, u32[]{:S(2)}) collective-permute-start(f32[16,1,256]{2,0,1:T(8,128)S(1)} %copy.56), channel_id=1, source_target_pairs={{0,4},{4,8},{8,12},{1,5},{5,9},{9,13},{2,6},{6,10},{10,14},{3,7},{... | collective-permute-start | bytes 49160 | tf_op jit(solution)/shard_map/ppermute | solution.py:89
  162.0 11.3 %collective-permute-start.12 = (f32[16,16,1]{2,1,0:T(8,128)S(1)}, f32[16,16,1]{2,1,0:T(8,128)S(1)}, u32[]{:S(2)}, u32[]{:S(2)}) collective-permute-start(f32[16,16,1]{2,1,0:T(8,128)S(1)} %get-tuple-element.91), channel_id=1, source_target_pairs={{0,1},{1,2},{2,3},{4,5},{5,6},{6,7},{8,9},{9,10},{10,11},{12,13},{... | collective-permute-start | bytes 3080 | tf_op jit(solution)/shard_map/ppermute | solution.py:89
  164.5 8.8 %collective-permute-start.17 = (f32[16,16,1]{2,1,0:T(8,128)S(1)}, f32[16,16,1]{2,1,0:T(8,128)S(1)}, u32[]{:S(2)}, u32[]{:S(2)}) collective-permute-start(f32[16,16,1]{2,1,0:T(8,128)S(1)} %get-tuple-element.92), channel_id=1, source_target_pairs={{1,0},{2,1},{3,2},{5,4},{6,5},{7,6},{9,8},{10,9},{11,10},{13,12},{... | collective-permute-start | bytes 3080 | tf_op jit(solution)/shard_map/ppermute | solution.py:90
  165.8 7.5 %collective-permute-start.16 = (f32[16,1,256]{2,0,1:T(8,128)S(1)}, f32[16,1,256]{2,0,1:T(8,128)S(1)}, u32[]{:S(2)}, u32[]{:S(2)}) collective-permute-start(f32[16,1,256]{2,0,1:T(8,128)S(1)} %copy.57), channel_id=1, source_target_pairs={{4,0},{8,4},{12,8},{5,1},{9,5},{13,9},{6,2},{10,6},{14,10},{7,3},{... | collective-permute-start | bytes 49160 | tf_op jit(solution)/shard_map/ppermute | solution.py:90
  167.1 6.2 %collective-permute-start.14 = (f32[1,16,256]{2,1,0:T(8,128)S(1)}, f32[1,16,256]{2,1,0:T(8,128)S(1)}, u32[]{:S(2)}, u32[]{:S(2)}) collective-permute-start(f32[1,16,256]{2,1,0:T(8,128)S(1)} %get-tuple-element.89), channel_id=1, source_target_pairs={{0,16},{16,32},{32,48},{48,64},{64,80},{80,96},{96,112},{1,17},{17... | collective-permute-start | bytes 49160 | tf_op jit(solution)/shard_map/ppermute | solution.py:89
  170.4 5.1 %collective-permute-start.15 = (f32[1,16,256]{2,1,0:T(8,128)S(1)}, f32[1,16,256]{2,1,0:T(8,128)S(1)}, u32[]{:S(2)}, u32[]{:S(2)}) collective-permute-start(f32[1,16,256]{2,1,0:T(8,128)S(1)} %get-tuple-element.90), channel_id=1, source_target_pairs={{16,0},{32,16},{48,32},{64,48},{80,64},{96,80},{112,96},{17,1},{33... | collective-permute-start | bytes 49160 | tf_op jit(solution)/shard_map/ppermute | solution.py:90
  (26 other events, 167.8 us)

commit v5 on v4

--- a/solution.py
+++ b/solution.py
@@ -62,11 +62,11 @@
 
 
 def jacobi(rhs_box, padded_cond, diagonal, storage_box, free_box):
-    guess = RELAX * rhs_box / diagonal
-    for sweep in range(1, SWEEPS):
+    def sweep(step, guess):
         image = stencil(jnp.pad(free_box * guess, 1), padded_cond, guess, storage_box, free_box)
-        guess = guess + RELAX * (rhs_box - image) / diagonal
-    return guess
+        return guess + RELAX * (rhs_box - image) / diagonal
+
+    return lax.fori_loop(0, SWEEPS, sweep, jnp.zeros_like(rhs_box))
 
 
 def project(basis, field):

time: 208 us -> 237 us (1.14)
  other arithmetic: 59 us -> 87 us
  waiting for transfers between devices: 24.7 us -> 11.4 us
  starting transfers between devices: 45.5 us -> 53.3 us
  Pallas kernels: 51.3 us -> 54.8 us
  local copies, waits for them, and re-layouts: 18 us -> 21 us
    add x2 -> x9, other arithmetic: 3.99 us -> 35.6 us  [the longest x8 33.3 us: sweep(): return guess + RELAX * (rhs_box - image) / diagonal]
    ppermute x6, waiting for transfers between devices: 17.5 us -> 5.94 us  [padded(): after = lax.ppermute(leading, axis, down)]
    mul x6 -> x8, other arithmetic: 15.3 us -> 7.31 us  [sweep(): free_box * guess]
    pallas_call x3, Pallas kernels: 51.3 us -> 54.8 us  [gather_rows(): pl.pallas_call(functools.partial(gather_kernel, sizes), out_shape=jax.Sha...]
    ppermute x6, starting transfers between devices: 9.6 us -> 12.3 us  [padded(): after = lax.ppermute(leading, axis, down)]
    sub x0 -> x1, other arithmetic: none -> 2.49 us  [shards(): rhs_box1 = rhs_box0 - alpha0 * image0_box]
    unnamed x88 -> x80, local copies, waits for them, and re-layouts: 4.55 us -> 6.22 us
  transfers between devices with their start and end apart: 18 -> 18, of which waited for: 9 -> 8; matrix products, arithmetic and copies ran while one was open for 6% -> 6% of each run, Pallas kernels for 11% -> 10%
where the time goes in v5:
time: 237 us; the launch traced here: 235 us
  other arithmetic  87 us (37%)
  Pallas kernels  54.8 us (23%)
  starting transfers between devices  53.3 us (22%)
  local copies, waits for them, and re-layouts  21 us (9%)
  waiting for transfers between devices  11.4 us (5%)
  between operations  7.08 us (3%)
    pallas_call x3, Pallas kernels, gather_rows(): pl.pallas_call(functools.partial(gather_kernel, sizes), out_shape=jax.Sha...  54.8 us
    add x8, other arithmetic, sweep(): return guess + RELAX * (rhs_box - image) / diagonal  33.3 us
    ppermute x6, starting transfers between devices, padded(): before = lax.ppermute(last, axis, up)  24.4 us
    ppermute x6, starting transfers between devices, padded(): after = lax.ppermute(leading, axis, down)  12.3 us
    ppermute x3, starting transfers between devices, faces(): lax.ppermute(lax.slice_in_dim(field, length - 1, length, axis=dim), axis,...  10.2 us
    concatenate x2, other arithmetic, padded(): value = jnp.concatenate([before, value, after], axis=dim)  7.69 us
    mul x8, other arithmetic, sweep(): free_box * guess  7.31 us
    reduce_sum x2, other arithmetic, expand(): return jnp.sum(weights[:, None, None, None] * basis, axis=0)  7.07 us
  transfers between devices with their start and end apart: 18, of which 8 were waited for; matrix products, arithmetic and copies ran while one was open for 6% of the time, Pallas kernels for 10%

profile of v5, /device:TPU:1, one launch (start us, length us, event | category | flops | bytes accessed | tf_op | source)
XLA Modules:
  0.0 235.0 jit_solution(17458435310914071715)
XLA Ops:
  9.5 4.6 %collective-permute-start = (f32[6,16,16,3]{2,1,3,0:T(8,128)S(1)}, f32[6,16,16,3]{2,1,3,0:T(8,128)S(1)}, u32[]{:S(2)}, u32[]{:S(2)}) collective-permute-start(f32[6,16,16,3]{2,1,3,0:T(8,128)S(1)} %copy.74), channel_id=1, source_target_pairs={{0,1},{1,2},{2,3},{4,5},{5,6},{6,7},{8,9},{9,10},{10,11},{12,13},{... | collective-permute-start | bytes 55304 | tf_op jit(solution)/shard_map/ppermute | solution.py:26
  17.2 3.9 %collective-permute-start.3 = (f32[6,3,16,262]{3,2,1,0:T(8,128)S(1)}, f32[6,3,16,262]{3,2,1,0:T(8,128)S(1)}, u32[]{:S(2)}, u32[]{:S(2)}) collective-permute-start(f32[6,3,16,262]{3,2,1,0:T(8,128)S(1)} %get-tuple-element.339), channel_id=1, source_target_pairs={{16,0},{32,16},{48,32},{64,48},{80,64},{96,80},{112,96},{17,1},{33... | collective-permute-start | bytes 905480 | tf_op jit(solution)/shard_map/ppermute | solution.py:27
  21.1 3.3 %collective-permute-start.2 = (f32[6,3,16,262]{3,2,1,0:T(8,128)S(1)}, f32[6,3,16,262]{3,2,1,0:T(8,128)S(1)}, u32[]{:S(2)}, u32[]{:S(2)}) collective-permute-start(f32[6,3,16,262]{3,2,1,0:T(8,128)S(1)} %get-tuple-element.338), channel_id=1, source_target_pairs={{0,16},{16,32},{32,48},{48,64},{64,80},{80,96},{96,112},{1,17},{17... | collective-permute-start | bytes 905480 | tf_op jit(solution)/shard_map/ppermute | solution.py:26
  24.5 4.0 %collective-permute-done.3 = f32[6,3,16,262]{3,2,1,0:T(8,128)S(1)} collective-permute-done((f32[6,3,16,262]{3,2,1,0:T(8,128)S(1)}, f32[6,3,16,262]{3,2,1,0:T(8,128)S(1)}, u32[]{:S(2)}, u32[]{:S(2)}) %collective-permute-start.3) | collective-permute-done | bytes 301856 | tf_op jit(solution)/shard_map/ppermute | solution.py:27
  35.5 5.1 %collective-permute-start.4 = (f32[6,22,3,262]{3,1,2,0:T(8,128)}, f32[6,22,3,262]{3,1,2,0:T(8,128)}, u32[]{:S(2)}, u32[]{:S(2)}) collective-permute-start(f32[6,22,3,262]{3,1,2,0:T(8,128)} %copy.76), channel_id=1, source_target_pairs={{0,4},{4,8},{8,12},{1,5},{5,9},{9,13},{2,6},{6,10},{10,14},{3,7},{... | collective-permute-start | bytes 1245032 | tf_op jit(solution)/shard_map/ppermute | solution.py:26
  41.6 24.0 %shard_map.77 = f32[128,1,128]{2,1,0:T(1,128)} custom-call(f32[1,1,128]{2,1,0:T(1,128)} %scatter.14.row_ref), custom_call_target="tpu_custom_call" | custom-call | tf_op jit(solution)/shard_map/pallas_call | solution.py:168
  66.7 3.5 %multiply_reduce_fusion.2 = f32[16,16,256]{2,1,0:T(8,128)} fusion(f32[16,16,16,256]{3,2,1,0:T(8,128)} %param.22, f32[16]{0:T(128)S(1)} %convolution_bitcast_fusion.1), kind=kLoop, calls=%fused_computation.66 | loop fusion | flops 2031616 | bytes 4456512 | tf_op jit(solution)/shard_map/reduce_sum | solution.py:77
  72.9 5.5 %pad_maximum_fusion = f32[6,22,22,262]{3,2,1,0:T(8,128)S(1)} fusion(f32[6,22,3,262]{3,2,1,0:T(4,128)S(1)} %copy.63, f32[6,3,16,262]{3,2,1,0:T(8,128)S(1)} %copy-done.27, f32[6,16,16,3]{3,2,1,0:T(8,128)S(1)} %copy.59, f32[1,16,16,256]{3,2,1,0:T(8,128)S(1)} %bitcast.180, f32[1,16,16,256]{3,2,1,0:T(8,128)S(1)} %fusion.89, f32[1,16,16,256]{3,2,1,0:T(8,128)S(1)} %bitcast.186, ...), kind=kLoop, calls=%fused_computation.62 | loop fusion | flops 6847632 | bytes 6086784 | tf_op jit(solution)/shard_map/concatenate | solution.py:28
  84.7 20.3 %while.30 = (s32[]{:T(128)}, f32[20,20,260]{2,1,0:T(8,128)}, f32[20,20,260]{2,1,0:T(8,128)S(1)}, f32[20,20,260]{2,1,0:T(8,128)}, f32[3,22,22,262]{3,2,1,0:T(8,12...) while((s32[]{:T(128)}, f32[20,20,260]{2,1,0:T(8,128)}, ...), condition=%wide.region_1.2_spmd.clone, body=%wide.region_0.1_spmd.clone.sunk | while | flops 3120003 | bytes 6656112 | solution.py:69
  84.8 4.0 %fusion.106 = f32[20,20,260]{2,1,0:T(8,128)} fusion(f32[20,20,260]{2,1,0:T(8,128)} %get-tuple-element.473, f32[20,20,260]{2,1,0:T(8,128)} %get-tuple-element.472, f32[20,20,260]{2,1,0:T(8,128)S(1)} %get-tuple-element.469, f32[20,20,260]{2,1,0:T(8,128)S(1)} %select_multiply_fusion.4, f32[3,22,22,262]{3,2,1,0:T(8,128)S(1)} %get-tuple-element.471, ...), kind=kLoop, calls=%fused_computation.19.clone.1 | loop fusion | flops 2912000 | bytes 5408001 | tf_op jit(solution)/shard_map/while/body/eval_jaxpr/add | solution.py:67
  90.0 4.2 %fusion.106 = f32[20,20,260]{2,1,0:T(8,128)} fusion(f32[20,20,260]{2,1,0:T(8,128)} %get-tuple-element.473, f32[20,20,260]{2,1,0:T(8,128)} %get-tuple-element.472, f32[20,20,260]{2,1,0:T(8,128)S(1)} %get-tuple-element.469, f32[20,20,260]{2,1,0:T(8,128)S(1)} %select_multiply_fusion.4, f32[3,22,22,262]{3,2,1,0:T(8,128)S(1)} %get-tuple-element.471, ...), kind=kLoop, calls=%fused_computation.19.clone.1 | loop fusion | flops 2912000 | bytes 5408001 | tf_op jit(solution)/shard_map/while/body/eval_jaxpr/add | solution.py:67
  95.4 4.2 %fusion.106 = f32[20,20,260]{2,1,0:T(8,128)} fusion(f32[20,20,260]{2,1,0:T(8,128)} %get-tuple-element.473, f32[20,20,260]{2,1,0:T(8,128)} %get-tuple-element.472, f32[20,20,260]{2,1,0:T(8,128)S(1)} %get-tuple-element.469, f32[20,20,260]{2,1,0:T(8,128)S(1)} %select_multiply_fusion.4, f32[3,22,22,262]{3,2,1,0:T(8,128)S(1)} %get-tuple-element.471, ...), kind=kLoop, calls=%fused_computation.19.clone.1 | loop fusion | flops 2912000 | bytes 5408001 | tf_op jit(solution)/shard_map/while/body/eval_jaxpr/add | solution.py:67
  100.8 4.2 %fusion.106 = f32[20,20,260]{2,1,0:T(8,128)} fusion(f32[20,20,260]{2,1,0:T(8,128)} %get-tuple-element.473, f32[20,20,260]{2,1,0:T(8,128)} %get-tuple-element.472, f32[20,20,260]{2,1,0:T(8,128)S(1)} %get-tuple-element.469, f32[20,20,260]{2,1,0:T(8,128)S(1)} %select_multiply_fusion.4, f32[3,22,22,262]{3,2,1,0:T(8,128)S(1)} %get-tuple-element.471, ...), kind=kLoop, calls=%fused_computation.19.clone.1 | loop fusion | flops 2912000 | bytes 5408001 | tf_op jit(solution)/shard_map/while/body/eval_jaxpr/add | solution.py:67
  107.7 4.7 %collective-permute-start.6 = (f32[16,16,3]{2,1,0:T(8,128)S(1)}, f32[16,16,3]{2,1,0:T(8,128)S(1)}, u32[]{:S(2)}, u32[]{:S(2)}) collective-permute-start(f32[16,16,3]{2,1,0:T(8,128)S(1)} %get-tuple-element.353), channel_id=1, source_target_pairs={{0,1},{1,2},{2,3},{4,5},{5,6},{6,7},{8,9},{9,10},{10,11},{12,13},{... | collective-permute-start | bytes 9224 | tf_op jit(solution)/shard_map/ppermute | solution.py:26
  115.6 3.1 %collective-permute-start.9 = (f32[3,16,262]{2,1,0:T(8,128)}, f32[3,16,262]{2,1,0:T(8,128)}, u32[]{:S(2)}, u32[]{:S(2)}) collective-permute-start(f32[3,16,262]{2,1,0:T(8,128)} %get-tuple-element.346), channel_id=1, source_target_pairs={{16,0},{32,16},{48,32},{64,48},{80,64},{96,80},{112,96},{17,1},{33... | collective-permute-start | bytes 150920 | tf_op jit(solution)/shard_map/ppermute | solution.py:27
  118.8 2.4 %collective-permute-start.8 = (f32[3,16,262]{2,1,0:T(8,128)}, f32[3,16,262]{2,1,0:T(8,128)}, u32[]{:S(2)}, u32[]{:S(2)}) collective-permute-start(f32[3,16,262]{2,1,0:T(8,128)} %get-tuple-element.345), channel_id=1, source_target_pairs={{0,16},{16,32},{32,48},{48,64},{64,80},{80,96},{96,112},{1,17},{17... | collective-permute-start | bytes 150920 | tf_op jit(solution)/shard_map/ppermute | solution.py:26
  125.5 4.2 %collective-permute-start.10 = (f32[22,3,262]{2,0,1:T(8,128)S(1)}, f32[22,3,262]{2,0,1:T(8,128)S(1)}, u32[]{:S(2)}, u32[]{:S(2)}) collective-permute-start(f32[22,3,262]{2,0,1:T(8,128)S(1)} %copy.78), channel_id=1, source_target_pairs={{0,4},{4,8},{8,12},{1,5},{5,9},{9,13},{2,6},{6,10},{10,14},{3,7},{... | collective-permute-start | bytes 207512 | tf_op jit(solution)/shard_map/ppermute | solution.py:26
  133.5 3.0 %fusion.52 = f32[20,20,260]{2,1,0:T(8,128)S(1)} fusion(f32[22,22,262]{2,1,0:T(8,128)S(1)} %get-tuple-element.330, f32[22,22,262]{2,1,0:T(8,128)S(1)} %get-tuple-element.329, f32[6,22,22,262]{3,2,1,0:T(8,128)S(1)} %copy-done.2, f32[22,22,262]{2,1,0:T(8,128)S(1)} %get-tuple-element.332, f32[22,22,262]{2,1,0:T(8,128)S(1)} %get-tuple-element.331), kind=kLoop, calls=%fused_computation.82 | loop fusion | flops 2392000 | bytes 7072000 | tf_op jit(solution)/shard_map/add | solution.py:54
  139.9 17.8 %shard_map.78 = f32[128,1,128]{2,1,0:T(1,128)} custom-call(f32[1,1,128]{2,1,0:T(1,128)} %copy-done.35), custom_call_target="tpu_custom_call" | custom-call | tf_op jit(solution)/shard_map/pallas_call | solution.py:168
  161.3 2.5 %multiply_subtract_fusion = f32[20,20,260]{2,1,0:T(8,128)} fusion(f32[20,20,260]{2,1,0:T(8,128)} %copy-done.24, f32[]{:T(128)S(6)} %div.21, f32[6,22,22,262]{3,2,1,0:T(8,128)} %copy-done.1), kind=kLoop, calls=%fused_computation.119 | loop fusion | flops 208000 | bytes 1248004 | tf_op jit(solution)/shard_map/sub | solution.py:239
  164.1 3.5 %multiply_reduce_fusion = f32[16,16,256]{2,1,0:T(8,128)} fusion(f32[16,16,16,256]{3,2,1,0:T(8,128)} %param.22, f32[16]{0:T(128)S(1)} %convolution_bitcast_fusion), kind=kLoop, calls=%fused_computation.64 | loop fusion | flops 2031616 | bytes 4456512 | tf_op jit(solution)/shard_map/reduce_sum | solution.py:77
  167.6 20.3 %while.31 = (s32[]{:T(128)}, f32[20,20,260]{2,1,0:T(8,128)}, f32[20,20,260]{2,1,0:T(8,128)S(1)}, f32[20,20,260]{2,1,0:T(8,128)}, f32[3,22,22,262]{3,2,1,0:T(8,12...) while((s32[]{:T(128)}, f32[20,20,260]{2,1,0:T(8,128)}, ...), condition=%wide.region_9.10_spmd.clone, body=%wide.region_8.9_spmd.clone.sunk | while | flops 3120003 | bytes 6656112 | solution.py:69
  167.7 4.0 %fusion.107 = f32[20,20,260]{2,1,0:T(8,128)} fusion(f32[20,20,260]{2,1,0:T(8,128)} %get-tuple-element.500, f32[20,20,260]{2,1,0:T(8,128)} %get-tuple-element.499, f32[20,20,260]{2,1,0:T(8,128)S(1)} %get-tuple-element.496, f32[20,20,260]{2,1,0:T(8,128)S(1)} %select_multiply_fusion.5, f32[3,22,22,262]{3,2,1,0:T(8,128)S(1)} %get-tuple-element.498, ...), kind=kLoop, calls=%fused_computation.50.clone.1 | loop fusion | flops 2912000 | bytes 5408001 | tf_op jit(solution)/shard_map/while/body/eval_jaxpr/add | solution.py:67
  172.9 4.2 %fusion.107 = f32[20,20,260]{2,1,0:T(8,128)} fusion(f32[20,20,260]{2,1,0:T(8,128)} %get-tuple-element.500, f32[20,20,260]{2,1,0:T(8,128)} %get-tuple-element.499, f32[20,20,260]{2,1,0:T(8,128)S(1)} %get-tuple-element.496, f32[20,20,260]{2,1,0:T(8,128)S(1)} %select_multiply_fusion.5, f32[3,22,22,262]{3,2,1,0:T(8,128)S(1)} %get-tuple-element.498, ...), kind=kLoop, calls=%fused_computation.50.clone.1 | loop fusion | flops 2912000 | bytes 5408001 | tf_op jit(solution)/shard_map/while/body/eval_jaxpr/add | solution.py:67
  178.3 4.2 %fusion.107 = f32[20,20,260]{2,1,0:T(8,128)} fusion(f32[20,20,260]{2,1,0:T(8,128)} %get-tuple-element.500, f32[20,20,260]{2,1,0:T(8,128)} %get-tuple-element.499, f32[20,20,260]{2,1,0:T(8,128)S(1)} %get-tuple-element.496, f32[20,20,260]{2,1,0:T(8,128)S(1)} %select_multiply_fusion.5, f32[3,22,22,262]{3,2,1,0:T(8,128)S(1)} %get-tuple-element.498, ...), kind=kLoop, calls=%fused_computation.50.clone.1 | loop fusion | flops 2912000 | bytes 5408001 | tf_op jit(solution)/shard_map/while/body/eval_jaxpr/add | solution.py:67
  183.7 4.2 %fusion.107 = f32[20,20,260]{2,1,0:T(8,128)} fusion(f32[20,20,260]{2,1,0:T(8,128)} %get-tuple-element.500, f32[20,20,260]{2,1,0:T(8,128)} %get-tuple-element.499, f32[20,20,260]{2,1,0:T(8,128)S(1)} %get-tuple-element.496, f32[20,20,260]{2,1,0:T(8,128)S(1)} %select_multiply_fusion.5, f32[3,22,22,262]{3,2,1,0:T(8,128)S(1)} %get-tuple-element.498, ...), kind=kLoop, calls=%fused_computation.50.clone.1 | loop fusion | flops 2912000 | bytes 5408001 | tf_op jit(solution)/shard_map/while/body/eval_jaxpr/add | solution.py:67
  192.5 3.9 %collective-permute-start.13 = (f32[16,1,256]{2,0,1:T(8,128)S(1)}, f32[16,1,256]{2,0,1:T(8,128)S(1)}, u32[]{:S(2)}, u32[]{:S(2)}) collective-permute-start(f32[16,1,256]{2,0,1:T(8,128)S(1)} %copy.68), channel_id=1, source_target_pairs={{0,4},{4,8},{8,12},{1,5},{5,9},{9,13},{2,6},{6,10},{10,14},{3,7},{... | collective-permute-start | bytes 49160 | tf_op jit(solution)/shard_map/ppermute | solution.py:89
  196.4 4.0 %collective-permute-start.12 = (f32[16,16,1]{2,1,0:T(8,128)S(1)}, f32[16,16,1]{2,1,0:T(8,128)S(1)}, u32[]{:S(2)}, u32[]{:S(2)}) collective-permute-start(f32[16,16,1]{2,1,0:T(8,128)S(1)} %get-tuple-element.349), channel_id=1, source_target_pairs={{0,1},{1,2},{2,3},{4,5},{5,6},{6,7},{8,9},{9,10},{10,11},{12,13},{... | collective-permute-start | bytes 3080 | tf_op jit(solution)/shard_map/ppermute | solution.py:89
  200.4 3.4 %collective-permute-start.15 = (f32[1,16,256]{2,1,0:T(8,128)S(1)}, f32[1,16,256]{2,1,0:T(8,128)S(1)}, u32[]{:S(2)}, u32[]{:S(2)}) collective-permute-start(f32[1,16,256]{2,1,0:T(8,128)S(1)} %get-tuple-element.348), channel_id=1, source_target_pairs={{16,0},{32,16},{48,32},{64,48},{80,64},{96,80},{112,96},{17,1},{33... | collective-permute-start | bytes 49160 | tf_op jit(solution)/shard_map/ppermute | solution.py:90
  203.9 2.4 %collective-permute-start.14 = (f32[1,16,256]{2,1,0:T(8,128)S(1)}, f32[1,16,256]{2,1,0:T(8,128)S(1)}, u32[]{:S(2)}, u32[]{:S(2)}) collective-permute-start(f32[1,16,256]{2,1,0:T(8,128)S(1)} %get-tuple-element.347), channel_id=1, source_target_pairs={{0,16},{16,32},{32,48},{48,64},{64,80},{80,96},{96,112},{1,17},{17... | collective-permute-start | bytes 49160 | tf_op jit(solution)/shard_map/ppermute | solution.py:89
  211.9 2.6 %maximum_bitcast_fusion.1 = f32[1,1,4]{2,1,0:T(1,128)S(1)} fusion(f32[1]{0:T(128)} %bitcast.39, f32[1]{0:T(128)} %bitcast.38, f32[1]{0:T(128)} %bitcast.37, f32[1]{0:T(128)} %bitcast.29), kind=kLoop, calls=%fused_computation.199 | loop fusion | flops 12 | bytes 32 | tf_op jit(solution)/shard_map/broadcast_in_dim;broadcast_in_dim | solution.py:167
  215.1 13.0 %shard_map.79 = f32[128,1,128]{2,1,0:T(1,128)} custom-call(f32[1,1,128]{2,1,0:T(1,128)} %scatter.19.row_ref), custom_call_target="tpu_custom_call" | custom-call | tf_op jit(solution)/shard_map/pallas_call | solution.py:168
  (164 shorter events, 70.1 us)
Async XLA Ops:
  0.6 65.9 %copy-start = (f32[16,2048]{1,0:T(8,128)S(1)}, f32[16,2048]{1,0:T(8,128)}, u32[]{:S(2)}) copy-start(f32[16,2048]{1,0:T(8,128)} %param.23) | copy-start | bytes 393220
  1.7 71.2 %copy-start.20 = (f32[1,16,16,256]{3,2,1,0:T(8,128)}, f32[1,16,16,256]{3,2,1,0:T(8,128)S(1)}, u32[]{:S(2)}) copy-start(f32[1,16,16,256]{3,2,1,0:T(8,128)S(1)} %fusion.89) | copy-start | bytes 786436
  6.4 7.7 %collective-permute-start.1 = (f32[6,16,16,3]{2,1,3,0:T(8,128)S(1)}, f32[6,16,16,3]{2,1,3,0:T(8,128)S(1)}, u32[]{:S(2)}, u32[]{:S(2)}) collective-permute-start(f32[6,16,16,3]{2,1,3,0:T(8,128)S(1)} %copy.75), channel_id=1, source_target_pairs={{1,0},{2,1},{3,2},{5,4},{6,5},{7,6},{9,8},{10,9},{11,10},{13,12},{... | collective-permute-start | bytes 55304 | tf_op jit(solution)/shard_map/ppermute | solution.py:27
  9.5 6.7 %collective-permute-start = (f32[6,16,16,3]{2,1,3,0:T(8,128)S(1)}, f32[6,16,16,3]{2,1,3,0:T(8,128)S(1)}, u32[]{:S(2)}, u32[]{:S(2)}) collective-permute-start(f32[6,16,16,3]{2,1,3,0:T(8,128)S(1)} %copy.74), channel_id=1, source_target_pairs={{0,1},{1,2},{2,3},{4,5},{5,6},{6,7},{8,9},{9,10},{10,11},{12,13},{... | collective-permute-start | bytes 55304 | tf_op jit(solution)/shard_map/ppermute | solution.py:26
  14.8 58.1 %copy-start.8 = (f32[6,16,16,3]{3,2,1,0:T(8,128)}, f32[6,16,16,3]{3,2,1,0:T(8,128)S(1)}, u32[]{:S(2)}) copy-start(f32[6,16,16,3]{3,2,1,0:T(8,128)S(1)} %copy.59) | copy-start | bytes 55300
  16.8 56.1 %copy-start.10 = (f32[6,16,16,3]{3,2,1,0:T(8,128)}, f32[6,16,16,3]{3,2,1,0:T(8,128)S(1)}, u32[]{:S(2)}) copy-start(f32[6,16,16,3]{3,2,1,0:T(8,128)S(1)} %copy.58) | copy-start | bytes 55300
  17.2 11.3 %collective-permute-start.3 = (f32[6,3,16,262]{3,2,1,0:T(8,128)S(1)}, f32[6,3,16,262]{3,2,1,0:T(8,128)S(1)}, u32[]{:S(2)}, u32[]{:S(2)}) collective-permute-start(f32[6,3,16,262]{3,2,1,0:T(8,128)S(1)} %get-tuple-element.339), channel_id=1, source_target_pairs={{16,0},{32,16},{48,32},{64,48},{80,64},{96,80},{112,96},{17,1},{33... | collective-permute-start | bytes 905480 | tf_op jit(solution)/shard_map/ppermute | solution.py:27
  21.1 8.6 %collective-permute-start.2 = (f32[6,3,16,262]{3,2,1,0:T(8,128)S(1)}, f32[6,3,16,262]{3,2,1,0:T(8,128)S(1)}, u32[]{:S(2)}, u32[]{:S(2)}) collective-permute-start(f32[6,3,16,262]{3,2,1,0:T(8,128)S(1)} %get-tuple-element.338), channel_id=1, source_target_pairs={{0,16},{16,32},{32,48},{48,64},{64,80},{80,96},{96,112},{1,17},{17... | collective-permute-start | bytes 905480 | tf_op jit(solution)/shard_map/ppermute | solution.py:26
  33.1 37.1 %collective-permute-start.5 = (f32[6,22,3,262]{3,1,2,0:T(8,128)}, f32[6,22,3,262]{3,1,2,0:T(8,128)}, u32[]{:S(2)}, u32[]{:S(2)}) collective-permute-start(f32[6,22,3,262]{3,1,2,0:T(8,128)} %copy.77), channel_id=1, source_target_pairs={{4,0},{8,4},{12,8},{5,1},{9,5},{13,9},{6,2},{10,6},{14,10},{7,3},{... | collective-permute-start | bytes 1245032 | tf_op jit(solution)/shard_map/ppermute | solution.py:27
  35.5 36.1 %collective-permute-start.4 = (f32[6,22,3,262]{3,1,2,0:T(8,128)}, f32[6,22,3,262]{3,1,2,0:T(8,128)}, u32[]{:S(2)}, u32[]{:S(2)}) collective-permute-start(f32[6,22,3,262]{3,1,2,0:T(8,128)} %copy.76), channel_id=1, source_target_pairs={{0,4},{4,8},{8,12},{1,5},{5,9},{9,13},{2,6},{6,10},{10,14},{3,7},{... | collective-permute-start | bytes 1245032 | tf_op jit(solution)/shard_map/ppermute | solution.py:26
  84.7 36.5 %copy-start.34 = (f32[128,1,128]{2,1,0:T(1,128)S(1)}, f32[128,1,128]{2,1,0:T(1,128)}, u32[]{:S(2)}) copy-start(f32[128,1,128]{2,1,0:T(1,128)} %shard_map.77) | copy-start | bytes 196612
  106.4 7.6 %collective-permute-start.7 = (f32[16,16,3]{2,1,0:T(8,128)S(1)}, f32[16,16,3]{2,1,0:T(8,128)S(1)}, u32[]{:S(2)}, u32[]{:S(2)}) collective-permute-start(f32[16,16,3]{2,1,0:T(8,128)S(1)} %get-tuple-element.354), channel_id=1, source_target_pairs={{1,0},{2,1},{3,2},{5,4},{6,5},{7,6},{9,8},{10,9},{11,10},{13,12},{... | collective-permute-start | bytes 9224 | tf_op jit(solution)/shard_map/ppermute | solution.py:27
  107.7 7.2 %collective-permute-start.6 = (f32[16,16,3]{2,1,0:T(8,128)S(1)}, f32[16,16,3]{2,1,0:T(8,128)S(1)}, u32[]{:S(2)}, u32[]{:S(2)}) collective-permute-start(f32[16,16,3]{2,1,0:T(8,128)S(1)} %get-tuple-element.353), channel_id=1, source_target_pairs={{0,1},{1,2},{2,3},{4,5},{5,6},{6,7},{8,9},{9,10},{10,11},{12,13},{... | collective-permute-start | bytes 9224 | tf_op jit(solution)/shard_map/ppermute | solution.py:26
  115.6 6.0 %collective-permute-start.9 = (f32[3,16,262]{2,1,0:T(8,128)}, f32[3,16,262]{2,1,0:T(8,128)}, u32[]{:S(2)}, u32[]{:S(2)}) collective-permute-start(f32[3,16,262]{2,1,0:T(8,128)} %get-tuple-element.346), channel_id=1, source_target_pairs={{16,0},{32,16},{48,32},{64,48},{80,64},{96,80},{112,96},{17,1},{33... | collective-permute-start | bytes 150920 | tf_op jit(solution)/shard_map/ppermute | solution.py:27
  118.8 4.1 %collective-permute-start.8 = (f32[3,16,262]{2,1,0:T(8,128)}, f32[3,16,262]{2,1,0:T(8,128)}, u32[]{:S(2)}, u32[]{:S(2)}) collective-permute-start(f32[3,16,262]{2,1,0:T(8,128)} %get-tuple-element.345), channel_id=1, source_target_pairs={{0,16},{16,32},{32,48},{48,64},{64,80},{80,96},{96,112},{1,17},{17... | collective-permute-start | bytes 150920 | tf_op jit(solution)/shard_map/ppermute | solution.py:26
  124.2 7.0 %collective-permute-start.11 = (f32[22,3,262]{2,0,1:T(8,128)S(1)}, f32[22,3,262]{2,0,1:T(8,128)S(1)}, u32[]{:S(2)}, u32[]{:S(2)}) collective-permute-start(f32[22,3,262]{2,0,1:T(8,128)S(1)} %copy.79), channel_id=1, source_target_pairs={{4,0},{8,4},{12,8},{5,1},{9,5},{13,9},{6,2},{10,6},{14,10},{7,3},{... | collective-permute-start | bytes 207512 | tf_op jit(solution)/shard_map/ppermute | solution.py:27
  125.5 6.4 %collective-permute-start.10 = (f32[22,3,262]{2,0,1:T(8,128)S(1)}, f32[22,3,262]{2,0,1:T(8,128)S(1)}, u32[]{:S(2)}, u32[]{:S(2)}) collective-permute-start(f32[22,3,262]{2,0,1:T(8,128)S(1)} %copy.78), channel_id=1, source_target_pairs={{0,4},{4,8},{8,12},{1,5},{5,9},{9,13},{2,6},{6,10},{10,14},{3,7},{... | collective-permute-start | bytes 207512 | tf_op jit(solution)/shard_map/ppermute | solution.py:26
  189.3 20.9 %copy-start.6 = (f32[3,16,16,256]{3,2,1,0:T(8,128)S(1)}, f32[3,16,16,256]{3,2,1,0:T(8,128)}, u32[]{:S(2)}) copy-start(f32[3,16,16,256]{3,2,1,0:T(8,128)} %param.19) | copy-start | bytes 2359300
  189.4 20.9 %copy-start.7 = (f32[20,20,260]{2,1,0:T(8,128)S(1)}, f32[20,20,260]{2,1,0:T(8,128)}, u32[]{:S(2)}) copy-start(f32[20,20,260]{2,1,0:T(8,128)} %get-tuple-element.507) | copy-start | bytes 1248004
  189.4 20.9 %copy-start.9 = (f32[6,16,16,3]{3,2,1,0:T(8,128)S(1)}, f32[6,16,16,3]{3,2,1,0:T(8,128)}, u32[]{:S(2)}) copy-start(f32[6,16,16,3]{3,2,1,0:T(8,128)} %copy-done.8) | copy-start | bytes 55300
  189.4 20.9 %copy-start.11 = (f32[6,16,16,3]{3,2,1,0:T(8,128)S(1)}, f32[6,16,16,3]{3,2,1,0:T(8,128)}, u32[]{:S(2)}) copy-start(f32[6,16,16,3]{3,2,1,0:T(8,128)} %copy-done.10) | copy-start | bytes 55300
  189.4 20.9 %copy-start.14 = (f32[16,16,256]{2,1,0:T(8,128)S(1)}, f32[16,16,256]{2,1,0:T(8,128)}, u32[]{:S(2)}) copy-start(f32[16,16,256]{2,1,0:T(8,128)} %copy-done.12) | copy-start | bytes 786436
  189.4 20.8 %copy-start.17 = (f32[16,16,256]{2,1,0:T(8,128)S(1)}, f32[16,16,256]{2,1,0:T(8,128)}, u32[]{:S(2)}) copy-start(f32[16,16,256]{2,1,0:T(8,128)} %param.18) | copy-start | bytes 786436
  189.4 20.8 %copy-start.19 = (f32[16,16,256]{2,1,0:T(8,128)S(1)}, f32[16,16,256]{2,1,0:T(8,128)}, u32[]{:S(2)}) copy-start(f32[16,16,256]{2,1,0:T(8,128)} %param.20) | copy-start | bytes 786436
  189.4 20.8 %copy-start.21 = (f32[1,16,16,256]{3,2,1,0:T(8,128)S(1)}, f32[1,16,16,256]{3,2,1,0:T(8,128)}, u32[]{:S(2)}) copy-start(f32[1,16,16,256]{3,2,1,0:T(8,128)} %copy-done.20) | copy-start | bytes 786436
  189.4 20.8 %copy-start.23 = (f32[6,22,3,262]{3,2,1,0:T(4,128)S(1)}, f32[6,22,3,262]{3,2,1,0:T(4,128)}, u32[]{:S(2)}) copy-start(f32[6,22,3,262]{3,2,1,0:T(4,128)} %copy-done.22) | copy-start | bytes 1245028
  189.5 14.3 %collective-permute-start.16 = (f32[16,1,256]{2,0,1:T(8,128)S(1)}, f32[16,1,256]{2,0,1:T(8,128)S(1)}, u32[]{:S(2)}, u32[]{:S(2)}) collective-permute-start(f32[16,1,256]{2,0,1:T(8,128)S(1)} %copy.69), channel_id=1, source_target_pairs={{4,0},{8,4},{12,8},{5,1},{9,5},{13,9},{6,2},{10,6},{14,10},{7,3},{... | collective-permute-start | bytes 49160 | tf_op jit(solution)/shard_map/ppermute | solution.py:90
  191.1 17.4 %collective-permute-start.17 = (f32[16,16,1]{2,1,0:T(8,128)S(1)}, f32[16,16,1]{2,1,0:T(8,128)S(1)}, u32[]{:S(2)}, u32[]{:S(2)}) collective-permute-start(f32[16,16,1]{2,1,0:T(8,128)S(1)} %get-tuple-element.350), channel_id=1, source_target_pairs={{1,0},{2,1},{3,2},{5,4},{6,5},{7,6},{9,8},{10,9},{11,10},{13,12},{... | collective-permute-start | bytes 3080 | tf_op jit(solution)/shard_map/ppermute | solution.py:90
  192.5 15.9 %collective-permute-start.13 = (f32[16,1,256]{2,0,1:T(8,128)S(1)}, f32[16,1,256]{2,0,1:T(8,128)S(1)}, u32[]{:S(2)}, u32[]{:S(2)}) collective-permute-start(f32[16,1,256]{2,0,1:T(8,128)S(1)} %copy.68), channel_id=1, source_target_pairs={{0,4},{4,8},{8,12},{1,5},{5,9},{9,13},{2,6},{6,10},{10,14},{3,7},{... | collective-permute-start | bytes 49160 | tf_op jit(solution)/shard_map/ppermute | solution.py:89
  196.4 12.1 %collective-permute-start.12 = (f32[16,16,1]{2,1,0:T(8,128)S(1)}, f32[16,16,1]{2,1,0:T(8,128)S(1)}, u32[]{:S(2)}, u32[]{:S(2)}) collective-permute-start(f32[16,16,1]{2,1,0:T(8,128)S(1)} %get-tuple-element.349), channel_id=1, source_target_pairs={{0,1},{1,2},{2,3},{4,5},{5,6},{6,7},{8,9},{9,10},{10,11},{12,13},{... | collective-permute-start | bytes 3080 | tf_op jit(solution)/shard_map/ppermute | solution.py:89
  200.4 8.1 %collective-permute-start.15 = (f32[1,16,256]{2,1,0:T(8,128)S(1)}, f32[1,16,256]{2,1,0:T(8,128)S(1)}, u32[]{:S(2)}, u32[]{:S(2)}) collective-permute-start(f32[1,16,256]{2,1,0:T(8,128)S(1)} %get-tuple-element.348), channel_id=1, source_target_pairs={{16,0},{32,16},{48,32},{64,48},{80,64},{96,80},{112,96},{17,1},{33... | collective-permute-start | bytes 49160 | tf_op jit(solution)/shard_map/ppermute | solution.py:90
  203.9 4.7 %collective-permute-start.14 = (f32[1,16,256]{2,1,0:T(8,128)S(1)}, f32[1,16,256]{2,1,0:T(8,128)S(1)}, u32[]{:S(2)}, u32[]{:S(2)}) collective-permute-start(f32[1,16,256]{2,1,0:T(8,128)S(1)} %get-tuple-element.347), channel_id=1, source_target_pairs={{0,16},{16,32},{32,48},{48,64},{64,80},{80,96},{96,112},{1,17},{17... | collective-permute-start | bytes 49160 | tf_op jit(solution)/shard_map/ppermute | solution.py:89
  (22 other events, 202.2 us)

commit v6 on v1

--- a/solution.py
+++ b/solution.py
@@ -240,8 +240,19 @@
     residual1 = rhs_box1[2:-2, 2:-2, 2:-2]
     coarse1_all = coarse0_all - alpha0 * coarse_img_all
     z1 = precondition(rhs_box1, residual1, coarse1_all)
+    bare = jnp.pad(z1, 1)
+    image_bare = stencil(free_face * bare, cond_face, z1, storage, free)
     near1 = faces(z1)
-    image_z1 = stencil(free_face * near1, cond_face, z1, storage, free)
+    halo = free_face * (near1 - bare)
+    reach = (
+        cond_face[0, 1:-1, 1:-1, 1:-1] * halo[2:, 1:-1, 1:-1]
+        + cond_face[0, :-2, 1:-1, 1:-1] * halo[:-2, 1:-1, 1:-1]
+        + cond_face[1, 1:-1, 1:-1, 1:-1] * halo[1:-1, 2:, 1:-1]
+        + cond_face[1, 1:-1, :-2, 1:-1] * halo[1:-1, :-2, 1:-1]
+        + cond_face[2, 1:-1, 1:-1, 1:-1] * halo[1:-1, 1:-1, 2:]
+        + cond_face[2, 1:-1, 1:-1, :-2] * halo[1:-1, 1:-1, :-2]
+    )
+    image_z1 = image_bare - free * reach
     local = [
         jnp.sum(residual1 * z1),
         jnp.sum(z1 * image_z1),

time: 206 us -> 209 us (1.015)
  transfers between devices with their start and end apart: 18 -> 18, of which waited for: 7 -> 8; matrix products, arithmetic and copies ran while one was open for 6% -> 6% of each run, Pallas kernels for 12% -> 12%
where the time goes in v6:
time: 209 us; the launch traced here: 207 us
  other arithmetic  59.5 us (28%)
  Pallas kernels  56.4 us (27%)
  starting transfers between devices  53.8 us (26%)
  local copies, waits for them, and re-layouts  17.8 us (9%)
  waiting for transfers between devices  11.7 us (6%)
  between operations  7.64 us (4%)
    pallas_call x3, Pallas kernels, gather_rows(): pl.pallas_call(functools.partial(gather_kernel, sizes), out_shape=jax.Sha...  56.4 us
    ppermute x6, starting transfers between devices, padded(): before = lax.ppermute(last, axis, up)  24.9 us
    mul x7, other arithmetic, jacobi(): free_box * guess  16.7 us
    ppermute x6, starting transfers between devices, padded(): after = lax.ppermute(leading, axis, down)  12.3 us
    ppermute x3, starting transfers between devices, faces(): lax.ppermute(lax.slice_in_dim(field, length - 1, length, axis=dim), axis,...  11.8 us
    concatenate x2, other arithmetic, padded(): value = jnp.concatenate([before, value, after], axis=dim)  7.68 us
    reduce_sum x2, other arithmetic, expand(): return jnp.sum(weights[:, None, None, None] * basis, axis=0)  5.87 us
    ppermute x6, waiting for transfers between devices, padded(): after = lax.ppermute(leading, axis, down)  5.64 us
  transfers between devices with their start and end apart: 18, of which 8 were waited for; matrix products, arithmetic and copies ran while one was open for 6% of the time, Pallas kernels for 12%

profile of v6, /device:TPU:1, one launch (start us, length us, event | category | flops | bytes accessed | tf_op | source)
XLA Modules:
  0.0 207.3 jit_solution(10632864741095468517)
XLA Ops:
  6.2 5.2 %collective-permute-start = (f32[6,16,16,3]{2,1,3,0:T(8,128)S(1)}, f32[6,16,16,3]{2,1,3,0:T(8,128)}, u32[]{:S(2)}, u32[]{:S(2)}) collective-permute-start(f32[6,16,16,3]{2,1,3,0:T(8,128)S(1)} %copy.62), channel_id=1, source_target_pairs={{0,1},{1,2},{2,3},{4,5},{5,6},{6,7},{8,9},{9,10},{10,11},{12,13},{... | collective-permute-start | bytes 55304 | tf_op jit(solution)/shard_map/ppermute | solution.py:26
  14.8 3.9 %collective-permute-start.3 = (f32[6,3,16,262]{3,2,1,0:T(8,128)S(1)}, f32[6,3,16,262]{3,2,1,0:T(8,128)S(1)}, u32[]{:S(2)}, u32[]{:S(2)}) collective-permute-start(f32[6,3,16,262]{3,2,1,0:T(8,128)S(1)} %get-tuple-element.84), channel_id=1, source_target_pairs={{16,0},{32,16},{48,32},{64,48},{80,64},{96,80},{112,96},{17,1},{33... | collective-permute-start | bytes 905480 | tf_op jit(solution)/shard_map/ppermute | solution.py:27
  18.7 3.3 %collective-permute-start.2 = (f32[6,3,16,262]{3,2,1,0:T(8,128)S(1)}, f32[6,3,16,262]{3,2,1,0:T(8,128)S(1)}, u32[]{:S(2)}, u32[]{:S(2)}) collective-permute-start(f32[6,3,16,262]{3,2,1,0:T(8,128)S(1)} %get-tuple-element.83), channel_id=1, source_target_pairs={{0,16},{16,32},{32,48},{48,64},{64,80},{80,96},{96,112},{1,17},{17... | collective-permute-start | bytes 905480 | tf_op jit(solution)/shard_map/ppermute | solution.py:26
  22.0 4.0 %collective-permute-done.3 = f32[6,3,16,262]{3,2,1,0:T(8,128)S(1)} collective-permute-done((f32[6,3,16,262]{3,2,1,0:T(8,128)S(1)}, f32[6,3,16,262]{3,2,1,0:T(8,128)S(1)}, u32[]{:S(2)}, u32[]{:S(2)}) %collective-permute-start.3) | collective-permute-done | bytes 301856 | tf_op jit(solution)/shard_map/ppermute | solution.py:27
  27.2 2.2 %pad_maximum_fusion.2 = f32[6,22,16,262]{3,2,1,0:T(8,128)S(1)} fusion(f32[6,3,16,262]{3,2,1,0:T(8,128)S(1)} %collective-permute-done.3, f32[6,16,16,3]{3,2,1,0:T(8,128)S(1)} %copy.47, f32[1,16,16,256]{3,2,1,0:T(8,128)S(1)} %bitcast.310, f32[1,16,16,256]{3,2,1,0:T(8,128)S(1)} %fusion.210, f32[1,16,16,256]{3,2,1,0:T(8,128)S(1)} %bitcast.315, ...), kind=kLoop, calls=%fused_computation.6 | loop fusion | flops 3873408 | bytes 4426752 | tf_op jit(solution)/shard_map/concatenate | solution.py:28
  33.0 5.0 %collective-permute-start.4 = (f32[6,22,3,262]{3,1,2,0:T(8,128)}, f32[6,22,3,262]{3,1,2,0:T(8,128)}, u32[]{:S(2)}, u32[]{:S(2)}) collective-permute-start(f32[6,22,3,262]{3,1,2,0:T(8,128)} %copy.64), channel_id=1, source_target_pairs={{0,4},{4,8},{8,12},{1,5},{5,9},{9,13},{2,6},{6,10},{10,14},{3,7},{... | collective-permute-start | bytes 1245032 | tf_op jit(solution)/shard_map/ppermute | solution.py:26
  39.1 24.0 %shard_map.77 = f32[128,1,128]{2,1,0:T(1,128)} custom-call(f32[1,1,128]{2,1,0:T(1,128)} %scatter.14.row_ref), custom_call_target="tpu_custom_call" | custom-call | tf_op jit(solution)/shard_map/pallas_call | solution.py:168
  64.2 2.8 %multiply_reduce_fusion.2 = f32[16,16,256]{2,1,0:T(8,128)S(1)} fusion(f32[16,16,16,256]{3,2,1,0:T(8,128)} %param.18, f32[16]{0:T(128)S(1)} %convolution_bitcast_fusion.1), kind=kLoop, calls=%fused_computation.4 | loop fusion | flops 2031616 | bytes 4456512 | tf_op jit(solution)/shard_map/reduce_sum | solution.py:77
  69.7 5.5 %pad_maximum_fusion = f32[6,22,22,262]{3,2,1,0:T(8,128)S(1)} fusion(f32[6,22,3,262]{3,2,1,0:T(4,128)S(1)} %copy.51, f32[6,3,16,262]{3,2,1,0:T(8,128)S(1)} %copy-done.27, f32[6,16,16,3]{3,2,1,0:T(8,128)S(1)} %copy.47, f32[1,16,16,256]{3,2,1,0:T(8,128)S(1)} %bitcast.311, f32[1,16,16,256]{3,2,1,0:T(8,128)S(1)} %fusion.210, f32[1,16,16,256]{3,2,1,0:T(8,128)S(1)} %bitcast.316, ...), kind=kLoop, calls=%fused_computation | loop fusion | flops 6847632 | bytes 6086784 | tf_op jit(solution)/shard_map/concatenate | solution.py:28
  76.9 2.4 %fusion.211 = (f32[20,20,260]{2,1,0:T(8,128)S(1)}, f32[20,20,260]{2,1,0:T(8,128)S(1)}, f32[20,20,260]{2,1,0:T(8,128)S(1)}, f32[20,20,260]{2,1,0:T(8,128)S(1)}) fusion(f32[6,22,22,262]{3,2,1,0:T(8,128)S(1)} %pad_maximum_fusion, f32[20,20,260]{2,1,0:T(8,128)S(1)} %broadcast_multiply_fusion, f32[3,20,20,260]{3,2,1,0:T(8,128)S(1)} %slice.642), kind=kLoop, calls=%fused_computation.350 | loop fusion | flops 3640000 | bytes 5824000 | tf_op jit(solution)/shard_map/mul | solution.py:67
  79.4 2.5 %fusion.217 = (f32[20,20,260]{2,1,0:T(8,128)S(1)}, f32[20,20,260]{2,1,0:T(8,128)S(1)}) fusion(f32[6,22,22,262]{3,2,1,0:T(8,128)S(1)} %pad_maximum_fusion, f32[20,20,260]{2,1,0:T(8,128)S(1)} %get-tuple-element.73, f32[20,20,260]{2,1,0:T(8,128)S(1)} %get-tuple-element.71, f32[3,20,20,260]{3,2,1,0:T(8,128)S(1)} %slice.642, f32[20,20,260]{2,1,0:T(8,128)S(1)} %get-tuple-element.72), kind=kLoop, calls=%fused_computation.370 | loop fusion | flops 3224000 | bytes 5824000 | tf_op jit(solution)/shard_map/mul | solution.py:67
  81.9 2.1 fusion.216
  87.5 4.8 %collective-permute-start.6 = (f32[16,16,3]{2,1,0:T(8,128)S(1)}, f32[16,16,3]{2,1,0:T(8,128)S(1)}, u32[]{:S(2)}, u32[]{:S(2)}) collective-permute-start(f32[16,16,3]{2,1,0:T(8,128)S(1)} %get-tuple-element.98), channel_id=1, source_target_pairs={{0,1},{1,2},{2,3},{4,5},{5,6},{6,7},{8,9},{9,10},{10,11},{12,13},{... | collective-permute-start | bytes 9224 | tf_op jit(solution)/shard_map/ppermute | solution.py:26
  96.2 3.1 %collective-permute-start.9 = (f32[3,16,262]{2,1,0:T(8,128)}, f32[3,16,262]{2,1,0:T(8,128)}, u32[]{:S(2)}, u32[]{:S(2)}) collective-permute-start(f32[3,16,262]{2,1,0:T(8,128)} %get-tuple-element.91), channel_id=1, source_target_pairs={{16,0},{32,16},{48,32},{64,48},{80,64},{96,80},{112,96},{17,1},{33... | collective-permute-start | bytes 150920 | tf_op jit(solution)/shard_map/ppermute | solution.py:27
  99.4 2.4 %collective-permute-start.8 = (f32[3,16,262]{2,1,0:T(8,128)}, f32[3,16,262]{2,1,0:T(8,128)}, u32[]{:S(2)}, u32[]{:S(2)}) collective-permute-start(f32[3,16,262]{2,1,0:T(8,128)} %get-tuple-element.90), channel_id=1, source_target_pairs={{0,16},{16,32},{32,48},{48,64},{64,80},{80,96},{96,112},{1,17},{17... | collective-permute-start | bytes 150920 | tf_op jit(solution)/shard_map/ppermute | solution.py:26
  106.4 4.0 %collective-permute-start.10 = (f32[22,3,262]{2,0,1:T(8,128)S(1)}, f32[22,3,262]{2,0,1:T(8,128)S(1)}, u32[]{:S(2)}, u32[]{:S(2)}) collective-permute-start(f32[22,3,262]{2,0,1:T(8,128)S(1)} %copy.66), channel_id=1, source_target_pairs={{0,4},{4,8},{8,12},{1,5},{5,9},{9,13},{2,6},{6,10},{10,14},{3,7},{... | collective-permute-start | bytes 207512 | tf_op jit(solution)/shard_map/ppermute | solution.py:26
  114.1 3.0 %fusion.159 = f32[20,20,260]{2,1,0:T(8,128)S(1)} fusion(f32[22,22,262]{2,1,0:T(8,128)S(1)} %get-tuple-element.66, f32[22,22,262]{2,1,0:T(8,128)S(1)} %get-tuple-element.65, f32[6,22,22,262]{3,2,1,0:T(8,128)S(1)} %copy-done.2, f32[22,22,262]{2,1,0:T(8,128)S(1)} %get-tuple-element.77, f32[22,22,262]{2,1,0:T(8,128)S(1)} %get-tuple-element.76), kind=kLoop, calls=%fused_computation.222 | loop fusion | flops 2392000 | bytes 7072000 | tf_op jit(solution)/shard_map/add | solution.py:54
  120.8 17.5 %shard_map.78 = f32[128,1,128]{2,1,0:T(1,128)} custom-call(f32[1,1,128]{2,1,0:T(1,128)} %copy-done.38), custom_call_target="tpu_custom_call" | custom-call | tf_op jit(solution)/shard_map/pallas_call | solution.py:168
  142.1 3.6 %fusion.212 = (f32[20,20,260]{2,1,0:T(8,128)}, f32[20,20,260]{2,1,0:T(8,128)}) fusion(f32[20,20,260]{2,1,0:T(8,128)} %copy-done.6, f32[20,20,260]{2,1,0:T(8,128)} %copy-done.20, f32[6,22,22,262]{3,2,1,0:T(8,128)} %copy-done.1, f32[20,20,260]{2,1,0:T(8,128)} %copy-done.24, f32[]{:T(128)S(6)} %div.37), kind=kLoop, calls=%fused_computation.351 | loop fusion | flops 624000 | bytes 2912004 | tf_op jit(solution)/shard_map/mul | solution.py:67
  146.1 3.0 %multiply_reduce_fusion = f32[16,16,256]{2,1,0:T(8,128)S(1)} fusion(f32[16,16,16,256]{3,2,1,0:T(8,128)} %param.18, f32[16]{0:T(128)S(1)} %convolution_bitcast_fusion), kind=kLoop, calls=%fused_computation.2 | loop fusion | flops 2031616 | bytes 4456512 | tf_op jit(solution)/shard_map/reduce_sum | solution.py:77
  149.1 4.0 %fusion.215 = (f32[20,20,260]{2,1,0:T(8,128)S(1)}, f32[20,20,260]{2,1,0:T(8,128)S(1)}) fusion(f32[6,22,22,262]{3,2,1,0:T(8,128)} %copy-done.1, f32[20,20,260]{2,1,0:T(8,128)S(1)} %copy-done.7, f32[20,20,260]{2,1,0:T(8,128)S(1)} %copy-done.19, f32[20,20,260]{2,1,0:T(8,128)S(1)} %copy-done.32, f32[3,20,20,260]{3,2,1,0:T(8,128)S(1)} %slice.642, ...), kind=kLoop, calls=%fused_computation.368 | loop fusion | flops 3224000 | bytes 5824000 | tf_op jit(solution)/shard_map/mul | solution.py:67
  153.2 1.8 fusion.214
  156.6 1.8 fusion.204
  161.2 2.3 %collective-permute-start.15 = (f32[1,16,256]{2,1,0:T(8,128)S(1)}, f32[1,16,256]{2,1,0:T(8,128)S(1)}, u32[]{:S(2)}, u32[]{:S(2)}) collective-permute-start(f32[1,16,256]{2,1,0:T(8,128)S(1)} %get-tuple-element.93), channel_id=1, source_target_pairs={{16,0},{32,16},{48,32},{64,48},{80,64},{96,80},{112,96},{17,1},{33... | collective-permute-start | bytes 49160 | tf_op jit(solution)/shard_map/ppermute | solution.py:90
  163.5 3.3 %collective-permute-start.14 = (f32[1,16,256]{2,1,0:T(8,128)S(1)}, f32[1,16,256]{2,1,0:T(8,128)S(1)}, u32[]{:S(2)}, u32[]{:S(2)}) collective-permute-start(f32[1,16,256]{2,1,0:T(8,128)S(1)} %get-tuple-element.92), channel_id=1, source_target_pairs={{0,16},{16,32},{32,48},{48,64},{64,80},{80,96},{96,112},{1,17},{17... | collective-permute-start | bytes 49160 | tf_op jit(solution)/shard_map/ppermute | solution.py:89
  166.8 4.0 %collective-permute-start.13 = (f32[16,1,256]{2,0,1:T(8,128)S(1)}, f32[16,1,256]{2,0,1:T(8,128)S(1)}, u32[]{:S(2)}, u32[]{:S(2)}) collective-permute-start(f32[16,1,256]{2,0,1:T(8,128)S(1)} %copy.58), channel_id=1, source_target_pairs={{0,4},{4,8},{8,12},{1,5},{5,9},{9,13},{2,6},{6,10},{10,14},{3,7},{... | collective-permute-start | bytes 49160 | tf_op jit(solution)/shard_map/ppermute | solution.py:89
  170.9 4.6 %collective-permute-start.12 = (f32[16,16,1]{2,1,0:T(8,128)S(1)}, f32[16,16,1]{2,1,0:T(8,128)S(1)}, u32[]{:S(2)}, u32[]{:S(2)}) collective-permute-start(f32[16,16,1]{2,1,0:T(8,128)S(1)} %get-tuple-element.94), channel_id=1, source_target_pairs={{0,1},{1,2},{2,3},{4,5},{5,6},{6,7},{8,9},{9,10},{10,11},{12,13},{... | collective-permute-start | bytes 3080 | tf_op jit(solution)/shard_map/ppermute | solution.py:89
  176.4 1.6 collective-permute-done.12
  178.9 2.0 multiply_reduce_fusion.7
  181.0 2.7 %maximum_bitcast_fusion.1 = f32[1,1,4]{2,1,0:T(1,128)S(1)} fusion(f32[1]{0:T(128)} %bitcast.39, f32[1]{0:T(128)} %bitcast.38, f32[1]{0:T(128)} %bitcast.37, f32[1]{0:T(128)} %bitcast.29), kind=kLoop, calls=%fused_computation.364 | loop fusion | flops 12 | bytes 32 | tf_op jit(solution)/shard_map/broadcast_in_dim;broadcast_in_dim | solution.py:167
  184.1 15.0 %shard_map.79 = f32[128,1,128]{2,1,0:T(1,128)} custom-call(f32[1,1,128]{2,1,0:T(1,128)} %scatter.19.row_ref), custom_call_target="tpu_custom_call" | custom-call | tf_op jit(solution)/shard_map/pallas_call | solution.py:168
  205.3 2.1 multiply_subtract_fusion.1
  (161 shorter events, 50.1 us)
Async XLA Ops:
  0.6 63.3 %copy-start = (f32[16,2048]{1,0:T(8,128)S(1)}, f32[16,2048]{1,0:T(8,128)}, u32[]{:S(2)}) copy-start(f32[16,2048]{1,0:T(8,128)} %param.19) | copy-start | bytes 393220
  1.7 68.0 %copy-start.15 = (f32[1,16,16,256]{3,2,1,0:T(8,128)}, f32[1,16,16,256]{3,2,1,0:T(8,128)S(1)}, u32[]{:S(2)}) copy-start(f32[1,16,16,256]{3,2,1,0:T(8,128)S(1)} %fusion.210) | copy-start | bytes 786436
  3.2 11.2 %copy-start.5 = (f32[3,16,16,256]{3,2,1,0:T(8,128)S(1)}, f32[3,16,16,256]{3,2,1,0:T(8,128)}, u32[]{:S(2)}) copy-start(f32[3,16,16,256]{3,2,1,0:T(8,128)} %param.15) | copy-start | bytes 2359300
  3.2 11.2 %copy-start.12 = (f32[16,16,256]{2,1,0:T(8,128)S(1)}, f32[16,16,256]{2,1,0:T(8,128)}, u32[]{:S(2)}) copy-start(f32[16,16,256]{2,1,0:T(8,128)} %param.14) | copy-start | bytes 786436
  3.2 11.2 %copy-start.17 = (f32[16,16,256]{2,1,0:T(8,128)S(1)}, f32[16,16,256]{2,1,0:T(8,128)}, u32[]{:S(2)}) copy-start(f32[16,16,256]{2,1,0:T(8,128)} %param.16) | copy-start | bytes 786436
  4.2 7.2 %collective-permute-start.1 = (f32[6,16,16,3]{2,1,3,0:T(8,128)S(1)}, f32[6,16,16,3]{2,1,3,0:T(8,128)S(1)}, u32[]{:S(2)}, u32[]{:S(2)}) collective-permute-start(f32[6,16,16,3]{2,1,3,0:T(8,128)S(1)} %copy.63), channel_id=1, source_target_pairs={{1,0},{2,1},{3,2},{5,4},{6,5},{7,6},{9,8},{10,9},{11,10},{13,12},{... | collective-permute-start | bytes 55304 | tf_op jit(solution)/shard_map/ppermute | solution.py:27
  6.2 6.7 %collective-permute-start = (f32[6,16,16,3]{2,1,3,0:T(8,128)S(1)}, f32[6,16,16,3]{2,1,3,0:T(8,128)}, u32[]{:S(2)}, u32[]{:S(2)}) collective-permute-start(f32[6,16,16,3]{2,1,3,0:T(8,128)S(1)} %copy.62), channel_id=1, source_target_pairs={{0,1},{1,2},{2,3},{4,5},{5,6},{6,7},{8,9},{9,10},{10,11},{12,13},{... | collective-permute-start | bytes 55304 | tf_op jit(solution)/shard_map/ppermute | solution.py:26
  12.0 57.7 %copy-start.8 = (f32[6,16,16,3]{3,2,1,0:T(8,128)}, f32[6,16,16,3]{3,2,1,0:T(8,128)S(1)}, u32[]{:S(2)}) copy-start(f32[6,16,16,3]{3,2,1,0:T(8,128)S(1)} %copy.47) | copy-start | bytes 55300
  14.4 55.3 %copy-start.10 = (f32[6,16,16,3]{3,2,1,0:T(8,128)}, f32[6,16,16,3]{3,2,1,0:T(8,128)S(1)}, u32[]{:S(2)}) copy-start(f32[6,16,16,3]{3,2,1,0:T(8,128)S(1)} %copy.46) | copy-start | bytes 55300
  14.8 11.3 %collective-permute-start.3 = (f32[6,3,16,262]{3,2,1,0:T(8,128)S(1)}, f32[6,3,16,262]{3,2,1,0:T(8,128)S(1)}, u32[]{:S(2)}, u32[]{:S(2)}) collective-permute-start(f32[6,3,16,262]{3,2,1,0:T(8,128)S(1)} %get-tuple-element.84), channel_id=1, source_target_pairs={{16,0},{32,16},{48,32},{64,48},{80,64},{96,80},{112,96},{17,1},{33... | collective-permute-start | bytes 905480 | tf_op jit(solution)/shard_map/ppermute | solution.py:27
  18.7 8.6 %collective-permute-start.2 = (f32[6,3,16,262]{3,2,1,0:T(8,128)S(1)}, f32[6,3,16,262]{3,2,1,0:T(8,128)S(1)}, u32[]{:S(2)}, u32[]{:S(2)}) collective-permute-start(f32[6,3,16,262]{3,2,1,0:T(8,128)S(1)} %get-tuple-element.83), channel_id=1, source_target_pairs={{0,16},{16,32},{32,48},{48,64},{64,80},{80,96},{96,112},{1,17},{17... | collective-permute-start | bytes 905480 | tf_op jit(solution)/shard_map/ppermute | solution.py:26
  29.4 8.6 %copy-start.3 = (f32[16,16,16,256]{3,2,1,0:T(8,128)S(1)}, f32[16,16,16,256]{3,2,1,0:T(8,128)}, u32[]{:S(2)}) copy-start(f32[16,16,16,256]{3,2,1,0:T(8,128)} %param.18) | copy-start | bytes 12582916
  30.7 36.4 %collective-permute-start.5 = (f32[6,22,3,262]{3,1,2,0:T(8,128)}, f32[6,22,3,262]{3,1,2,0:T(8,128)}, u32[]{:S(2)}, u32[]{:S(2)}) collective-permute-start(f32[6,22,3,262]{3,1,2,0:T(8,128)} %copy.65), channel_id=1, source_target_pairs={{4,0},{8,4},{12,8},{5,1},{9,5},{13,9},{6,2},{10,6},{14,10},{7,3},{... | collective-permute-start | bytes 1245032 | tf_op jit(solution)/shard_map/ppermute | solution.py:27
  33.0 35.4 %collective-permute-start.4 = (f32[6,22,3,262]{3,1,2,0:T(8,128)}, f32[6,22,3,262]{3,1,2,0:T(8,128)}, u32[]{:S(2)}, u32[]{:S(2)}) collective-permute-start(f32[6,22,3,262]{3,1,2,0:T(8,128)} %copy.64), channel_id=1, source_target_pairs={{0,4},{4,8},{8,12},{1,5},{5,9},{9,13},{2,6},{6,10},{10,14},{3,7},{... | collective-permute-start | bytes 1245032 | tf_op jit(solution)/shard_map/ppermute | solution.py:26
  75.3 8.7 %copy-start.1 = (f32[6,22,22,262]{3,2,1,0:T(8,128)}, f32[6,22,22,262]{3,2,1,0:T(8,128)S(1)}, u32[]{:S(2)}) copy-start(f32[6,22,22,262]{3,2,1,0:T(8,128)S(1)} %pad_maximum_fusion) | copy-start | bytes 9130180
  75.8 9.7 %copy-start.33 = (f32[20,20,260]{2,1,0:T(8,128)}, f32[20,20,260]{2,1,0:T(8,128)S(1)}, u32[]{:S(2)}) copy-start(f32[20,20,260]{2,1,0:T(8,128)S(1)} %get-tuple-element.78) | copy-start | bytes 1248004
  86.2 7.7 %collective-permute-start.7 = (f32[16,16,3]{2,1,0:T(8,128)S(1)}, f32[16,16,3]{2,1,0:T(8,128)S(1)}, u32[]{:S(2)}, u32[]{:S(2)}) collective-permute-start(f32[16,16,3]{2,1,0:T(8,128)S(1)} %get-tuple-element.99), channel_id=1, source_target_pairs={{1,0},{2,1},{3,2},{5,4},{6,5},{7,6},{9,8},{10,9},{11,10},{13,12},{... | collective-permute-start | bytes 9224 | tf_op jit(solution)/shard_map/ppermute | solution.py:27
  87.5 7.3 %collective-permute-start.6 = (f32[16,16,3]{2,1,0:T(8,128)S(1)}, f32[16,16,3]{2,1,0:T(8,128)S(1)}, u32[]{:S(2)}, u32[]{:S(2)}) collective-permute-start(f32[16,16,3]{2,1,0:T(8,128)S(1)} %get-tuple-element.98), channel_id=1, source_target_pairs={{0,1},{1,2},{2,3},{4,5},{5,6},{6,7},{8,9},{9,10},{10,11},{12,13},{... | collective-permute-start | bytes 9224 | tf_op jit(solution)/shard_map/ppermute | solution.py:26
  96.2 6.5 %collective-permute-start.9 = (f32[3,16,262]{2,1,0:T(8,128)}, f32[3,16,262]{2,1,0:T(8,128)}, u32[]{:S(2)}, u32[]{:S(2)}) collective-permute-start(f32[3,16,262]{2,1,0:T(8,128)} %get-tuple-element.91), channel_id=1, source_target_pairs={{16,0},{32,16},{48,32},{64,48},{80,64},{96,80},{112,96},{17,1},{33... | collective-permute-start | bytes 150920 | tf_op jit(solution)/shard_map/ppermute | solution.py:27
  99.4 4.1 %collective-permute-start.8 = (f32[3,16,262]{2,1,0:T(8,128)}, f32[3,16,262]{2,1,0:T(8,128)}, u32[]{:S(2)}, u32[]{:S(2)}) collective-permute-start(f32[3,16,262]{2,1,0:T(8,128)} %get-tuple-element.90), channel_id=1, source_target_pairs={{0,16},{16,32},{32,48},{48,64},{64,80},{80,96},{96,112},{1,17},{17... | collective-permute-start | bytes 150920 | tf_op jit(solution)/shard_map/ppermute | solution.py:26
  102.7 10.1 %copy-start.2 = (f32[6,22,22,262]{3,2,1,0:T(8,128)S(1)}, f32[6,22,22,262]{3,2,1,0:T(8,128)}, u32[]{:S(2)}) copy-start(f32[6,22,22,262]{3,2,1,0:T(8,128)} %copy-done.1) | copy-start | bytes 9130180
  102.7 10.1 %copy-start.36 = (f32[16,16,3]{2,1,0:T(8,128)S(1)}, f32[16,16,3]{2,1,0:T(8,128)}, u32[]{:S(2)}) copy-start(f32[16,16,3]{2,1,0:T(8,128)} %copy-done.35) | copy-start | bytes 9220
  105.1 6.8 %collective-permute-start.11 = (f32[22,3,262]{2,0,1:T(8,128)S(1)}, f32[22,3,262]{2,0,1:T(8,128)S(1)}, u32[]{:S(2)}, u32[]{:S(2)}) collective-permute-start(f32[22,3,262]{2,0,1:T(8,128)S(1)} %copy.67), channel_id=1, source_target_pairs={{4,0},{8,4},{12,8},{5,1},{9,5},{13,9},{6,2},{10,6},{14,10},{7,3},{... | collective-permute-start | bytes 207512 | tf_op jit(solution)/shard_map/ppermute | solution.py:27
  106.4 6.4 %collective-permute-start.10 = (f32[22,3,262]{2,0,1:T(8,128)S(1)}, f32[22,3,262]{2,0,1:T(8,128)S(1)}, u32[]{:S(2)}, u32[]{:S(2)}) collective-permute-start(f32[22,3,262]{2,0,1:T(8,128)S(1)} %copy.66), channel_id=1, source_target_pairs={{0,4},{4,8},{8,12},{1,5},{5,9},{9,13},{2,6},{6,10},{10,14},{3,7},{... | collective-permute-start | bytes 207512 | tf_op jit(solution)/shard_map/ppermute | solution.py:26
  155.0 20.4 %copy-start.16 = (f32[1,16,16,256]{3,2,1,0:T(8,128)S(1)}, f32[1,16,16,256]{3,2,1,0:T(8,128)}, u32[]{:S(2)}) copy-start(f32[1,16,16,256]{3,2,1,0:T(8,128)} %copy-done.15) | copy-start | bytes 786436
  155.0 20.4 %copy-start.18 = (f32[16,16,256]{2,1,0:T(8,128)S(1)}, f32[16,16,256]{2,1,0:T(8,128)}, u32[]{:S(2)}) copy-start(f32[16,16,256]{2,1,0:T(8,128)} %param.16) | copy-start | bytes 786436
  158.6 12.2 %collective-permute-start.16 = (f32[16,1,256]{2,0,1:T(8,128)S(1)}, f32[16,1,256]{2,0,1:T(8,128)S(1)}, u32[]{:S(2)}, u32[]{:S(2)}) collective-permute-start(f32[16,1,256]{2,0,1:T(8,128)S(1)} %copy.59), channel_id=1, source_target_pairs={{4,0},{8,4},{12,8},{5,1},{9,5},{13,9},{6,2},{10,6},{14,10},{7,3},{... | collective-permute-start | bytes 49160 | tf_op jit(solution)/shard_map/ppermute | solution.py:90
  159.9 16.5 %collective-permute-start.17 = (f32[16,16,1]{2,1,0:T(8,128)S(1)}, f32[16,16,1]{2,1,0:T(8,128)S(1)}, u32[]{:S(2)}, u32[]{:S(2)}) collective-permute-start(f32[16,16,1]{2,1,0:T(8,128)S(1)} %get-tuple-element.95), channel_id=1, source_target_pairs={{1,0},{2,1},{3,2},{5,4},{6,5},{7,6},{9,8},{10,9},{11,10},{13,12},{... | collective-permute-start | bytes 3080 | tf_op jit(solution)/shard_map/ppermute | solution.py:90
  161.2 16.9 %collective-permute-start.15 = (f32[1,16,256]{2,1,0:T(8,128)S(1)}, f32[1,16,256]{2,1,0:T(8,128)S(1)}, u32[]{:S(2)}, u32[]{:S(2)}) collective-permute-start(f32[1,16,256]{2,1,0:T(8,128)S(1)} %get-tuple-element.93), channel_id=1, source_target_pairs={{16,0},{32,16},{48,32},{64,48},{80,64},{96,80},{112,96},{17,1},{33... | collective-permute-start | bytes 49160 | tf_op jit(solution)/shard_map/ppermute | solution.py:90
  163.5 14.5 %collective-permute-start.14 = (f32[1,16,256]{2,1,0:T(8,128)S(1)}, f32[1,16,256]{2,1,0:T(8,128)S(1)}, u32[]{:S(2)}, u32[]{:S(2)}) collective-permute-start(f32[1,16,256]{2,1,0:T(8,128)S(1)} %get-tuple-element.92), channel_id=1, source_target_pairs={{0,16},{16,32},{32,48},{48,64},{64,80},{80,96},{96,112},{1,17},{17... | collective-permute-start | bytes 49160 | tf_op jit(solution)/shard_map/ppermute | solution.py:89
  166.8 9.6 %collective-permute-start.13 = (f32[16,1,256]{2,0,1:T(8,128)S(1)}, f32[16,1,256]{2,0,1:T(8,128)S(1)}, u32[]{:S(2)}, u32[]{:S(2)}) collective-permute-start(f32[16,1,256]{2,0,1:T(8,128)S(1)} %copy.58), channel_id=1, source_target_pairs={{0,4},{4,8},{8,12},{1,5},{5,9},{9,13},{2,6},{6,10},{10,14},{3,7},{... | collective-permute-start | bytes 49160 | tf_op jit(solution)/shard_map/ppermute | solution.py:89
  170.9 7.2 %collective-permute-start.12 = (f32[16,16,1]{2,1,0:T(8,128)S(1)}, f32[16,16,1]{2,1,0:T(8,128)S(1)}, u32[]{:S(2)}, u32[]{:S(2)}) collective-permute-start(f32[16,16,1]{2,1,0:T(8,128)S(1)} %get-tuple-element.94), channel_id=1, source_target_pairs={{0,1},{1,2},{2,3},{4,5},{5,6},{6,7},{8,9},{9,10},{10,11},{12,13},{... | collective-permute-start | bytes 3080 | tf_op jit(solution)/shard_map/ppermute | solution.py:89
  (27 other events, 136.3 us)

commit v7 on v1

--- a/solution.py
+++ b/solution.py
@@ -225,8 +225,10 @@
 
     residual0 = right_side
     coarse0 = project(basis, residual0)
-    coarse0_all, _ = unpack(gather_rows(pack(coarse0, [])), vecs, 0)
-    z0 = precondition(rhs_box0, residual0, coarse0_all)
+    smooth0, row0 = lax.optimization_barrier((schwarz(rhs_box0), pack(coarse0, [])))
+    coarse0_all, _ = unpack(gather_rows(row0), vecs, 0)
+    weights0 = jnp.dot(coarse_inverse, coarse0_all, precision=lax.Precision.HIGHEST)
+    z0 = smooth0 + expand(basis, weights0, residual0)
     near0 = padded(z0, (("gz", 2), ("gx", 0), ("gy", 1)), 3)
     inner = (slice(1, -1),) * 3
     image0_box = stencil(free_wide * near0, cond_wide, near0[inner], storage_wide[inner], free_wide[inner])

time: 206 us -> 212 us (1.029)
  waiting for transfers between devices: 10.1 us -> 18.9 us
  Pallas kernels: 55.8 us -> 53.6 us
    ppermute x6, waiting for transfers between devices: 5.64 us -> 13.1 us  [padded(): after = lax.ppermute(leading, axis, down)]
    add x1, other arithmetic: 2.97 us -> 5.35 us  [stencil(): return free * total + (1.0 - free) * field]
    pallas_call x3, Pallas kernels: 55.8 us -> 53.6 us  [gather_rows(): pl.pallas_call(functools.partial(gather_kernel, sizes), out_shape=jax.Sha...]
    unnamed x90 -> x92, local copies, waits for them, and re-layouts: 4.58 us -> 3.51 us
  transfers between devices with their start and end apart: 18 -> 18, of which waited for: 7 -> 9; matrix products, arithmetic and copies ran while one was open for 6% -> 4% of each run, Pallas kernels for 12% -> 0%
where the time goes in v7:
time: 212 us; the launch traced here: 211 us
  other arithmetic  60.1 us (28%)
  Pallas kernels  53.6 us (25%)
  starting transfers between devices  52.7 us (25%)
  waiting for transfers between devices  18.9 us (9%)
  local copies, waits for them, and re-layouts  17.3 us (8%)
  between operations  7.47 us (4%)
    pallas_call x3, Pallas kernels, gather_rows(): pl.pallas_call(functools.partial(gather_kernel, sizes), out_shape=jax.Sha...  53.6 us
    ppermute x6, starting transfers between devices, padded(): before = lax.ppermute(last, axis, up)  23.5 us
    mul x7, other arithmetic, jacobi(): free_box * guess  16.5 us
    ppermute x6, waiting for transfers between devices, padded(): after = lax.ppermute(leading, axis, down)  13.1 us
    ppermute x6, starting transfers between devices, padded(): after = lax.ppermute(leading, axis, down)  12.8 us
    ppermute x3, starting transfers between devices, faces(): lax.ppermute(lax.slice_in_dim(field, length - 1, length, axis=dim), axis,...  10.2 us
    concatenate x2, other arithmetic, padded(): value = jnp.concatenate([before, value, after], axis=dim)  7.86 us
    ppermute x3, starting transfers between devices, faces(): after = lax.ppermute(lax.slice_in_dim(field, 0, 1, axis=dim), axis, down)  6.27 us
  transfers between devices with their start and end apart: 18, of which 9 were waited for; matrix products, arithmetic and copies ran while one was open for 4% of the time, Pallas kernels for 0%

profile of v7, /device:TPU:1, one launch (start us, length us, event | category | flops | bytes accessed | tf_op | source)
XLA Modules:
  0.0 210.5 jit_solution(13377237582032823005)
XLA Ops:
  6.1 5.2 %collective-permute-start = (f32[6,16,16,3]{2,1,3,0:T(8,128)S(1)}, f32[6,16,16,3]{2,1,3,0:T(8,128)}, u32[]{:S(2)}, u32[]{:S(2)}) collective-permute-start(f32[6,16,16,3]{2,1,3,0:T(8,128)S(1)} %copy.62), channel_id=1, source_target_pairs={{0,1},{1,2},{2,3},{4,5},{5,6},{6,7},{8,9},{9,10},{10,11},{12,13},{... | collective-permute-start | bytes 55304 | tf_op jit(solution)/shard_map/ppermute | solution.py:26
  14.8 3.9 %collective-permute-start.3 = (f32[6,3,16,262]{3,2,1,0:T(8,128)S(1)}, f32[6,3,16,262]{3,2,1,0:T(8,128)S(1)}, u32[]{:S(2)}, u32[]{:S(2)}) collective-permute-start(f32[6,3,16,262]{3,2,1,0:T(8,128)S(1)} %get-tuple-element.86), channel_id=1, source_target_pairs={{16,0},{32,16},{48,32},{64,48},{80,64},{96,80},{112,96},{17,1},{33... | collective-permute-start | bytes 905480 | tf_op jit(solution)/shard_map/ppermute | solution.py:27
  18.6 3.3 %collective-permute-start.2 = (f32[6,3,16,262]{3,2,1,0:T(8,128)S(1)}, f32[6,3,16,262]{3,2,1,0:T(8,128)S(1)}, u32[]{:S(2)}, u32[]{:S(2)}) collective-permute-start(f32[6,3,16,262]{3,2,1,0:T(8,128)S(1)} %get-tuple-element.85), channel_id=1, source_target_pairs={{0,16},{16,32},{32,48},{48,64},{64,80},{80,96},{96,112},{1,17},{17... | collective-permute-start | bytes 905480 | tf_op jit(solution)/shard_map/ppermute | solution.py:26
  22.0 4.0 %collective-permute-done.3 = f32[6,3,16,262]{3,2,1,0:T(8,128)S(1)} collective-permute-done((f32[6,3,16,262]{3,2,1,0:T(8,128)S(1)}, f32[6,3,16,262]{3,2,1,0:T(8,128)S(1)}, u32[]{:S(2)}, u32[]{:S(2)}) %collective-permute-start.3) | collective-permute-done | bytes 301856 | tf_op jit(solution)/shard_map/ppermute | solution.py:27
  27.2 2.2 %pad_maximum_fusion.2 = f32[6,22,16,262]{3,2,1,0:T(8,128)S(1)} fusion(f32[6,3,16,262]{3,2,1,0:T(8,128)S(1)} %collective-permute-done.3, f32[6,16,16,3]{3,2,1,0:T(8,128)S(1)} %copy.47, f32[1,16,16,256]{3,2,1,0:T(8,128)S(1)} %bitcast.309, f32[1,16,16,256]{3,2,1,0:T(8,128)S(1)} %fusion.202, f32[1,16,16,256]{3,2,1,0:T(8,128)S(1)} %bitcast.314, ...), kind=kLoop, calls=%fused_computation.6 | loop fusion | flops 3873408 | bytes 4426752 | tf_op jit(solution)/shard_map/concatenate | solution.py:28
  31.4 4.2 %collective-permute-start.4 = (f32[6,22,3,262]{3,1,2,0:T(8,128)S(1)}, f32[6,22,3,262]{3,1,2,0:T(8,128)S(1)}, u32[]{:S(2)}, u32[]{:S(2)}) collective-permute-start(f32[6,22,3,262]{3,1,2,0:T(8,128)S(1)} %copy.64), channel_id=1, source_target_pairs={{0,4},{4,8},{8,12},{1,5},{5,9},{9,13},{2,6},{6,10},{10,14},{3,7},{... | collective-permute-start | bytes 1245032 | tf_op jit(solution)/shard_map/ppermute | solution.py:26
  36.7 7.7 %collective-permute-done.5 = f32[6,22,3,262]{3,1,2,0:T(8,128)S(1)} collective-permute-done((f32[6,22,3,262]{3,1,2,0:T(8,128)S(1)}, f32[6,22,3,262]{3,1,2,0:T(8,128)S(1)}, u32[]{:S(2)}, u32[]{:S(2)}) %collective-permute-start.5) | collective-permute-done | bytes 415040 | tf_op jit(solution)/shard_map/ppermute | solution.py:27
  46.5 5.7 %pad_maximum_fusion = f32[6,22,22,262]{3,2,1,0:T(8,128)S(1)} fusion(f32[6,22,3,262]{3,2,1,0:T(4,128)S(1)} %copy.51, f32[6,3,16,262]{3,2,1,0:T(8,128)S(1)} %collective-permute-done.3, f32[6,16,16,3]{3,2,1,0:T(8,128)S(1)} %copy.47, f32[1,16,16,256]{3,2,1,0:T(8,128)S(1)} %bitcast.310, f32[1,16,16,256]{3,2,1,0:T(8,128)S(1)} %fusion.202, ...), kind=kLoop, calls=%fused_computation | loop fusion | flops 6847632 | bytes 6086784 | tf_op jit(solution)/shard_map/concatenate | solution.py:28
  53.9 2.4 %fusion.203 = (f32[20,20,260]{2,1,0:T(8,128)S(1)}, f32[20,20,260]{2,1,0:T(8,128)S(1)}, f32[20,20,260]{2,1,0:T(8,128)S(1)}, f32[20,20,260]{2,1,0:T(8,128)S(1)}) fusion(f32[6,22,22,262]{3,2,1,0:T(8,128)S(1)} %pad_maximum_fusion, f32[20,20,260]{2,1,0:T(8,128)S(1)} %broadcast_multiply_fusion, f32[3,20,20,260]{3,2,1,0:T(8,128)S(1)} %slice.612), kind=kLoop, calls=%fused_computation.334 | loop fusion | flops 3640000 | bytes 5824000 | tf_op jit(solution)/shard_map/mul | solution.py:67
  56.3 2.3 %fusion.209 = (f32[20,20,260]{2,1,0:T(8,128)S(1)}, f32[20,20,260]{2,1,0:T(8,128)S(1)}) fusion(f32[6,22,22,262]{3,2,1,0:T(8,128)S(1)} %pad_maximum_fusion, f32[20,20,260]{2,1,0:T(8,128)S(1)} %get-tuple-element.77, f32[20,20,260]{2,1,0:T(8,128)S(1)} %get-tuple-element.75, f32[3,20,20,260]{3,2,1,0:T(8,128)S(1)} %slice.612, f32[20,20,260]{2,1,0:T(8,128)S(1)} %get-tuple-element.76), kind=kLoop, calls=%fused_computation.354 | loop fusion | flops 3224000 | bytes 5824000 | tf_op jit(solution)/shard_map/mul | solution.py:67
  58.6 2.1 fusion.208
  63.5 23.0 %shard_map.77 = f32[128,1,128]{2,1,0:T(1,128)} custom-call(f32[1,1,128]{2,1,0:T(1,128)} %bitcast.324), custom_call_target="tpu_custom_call" | custom-call | tf_op jit(solution)/shard_map/pallas_call | solution.py:168
  87.7 2.8 %multiply_reduce_fusion.2 = f32[16,16,256]{2,1,0:T(8,128)S(1)} fusion(f32[16,16,16,256]{3,2,1,0:T(8,128)} %param.18, f32[16]{0:T(128)S(1)} %convolution_bitcast_fusion.1), kind=kLoop, calls=%fused_computation.4 | loop fusion | flops 2031616 | bytes 4456512 | tf_op jit(solution)/shard_map/reduce_sum | solution.py:77
  92.0 4.0 %collective-permute-start.6 = (f32[16,16,3]{2,1,0:T(8,128)S(1)}, f32[16,16,3]{2,1,0:T(8,128)S(1)}, u32[]{:S(2)}, u32[]{:S(2)}) collective-permute-start(f32[16,16,3]{2,1,0:T(8,128)S(1)} %get-tuple-element.100), channel_id=1, source_target_pairs={{0,1},{1,2},{2,3},{4,5},{5,6},{6,7},{8,9},{9,10},{10,11},{12,13},{... | collective-permute-start | bytes 9224 | tf_op jit(solution)/shard_map/ppermute | solution.py:26
  98.2 3.5 %collective-permute-start.9 = (f32[3,16,262]{2,1,0:T(8,128)S(1)}, f32[3,16,262]{2,1,0:T(8,128)S(1)}, u32[]{:S(2)}, u32[]{:S(2)}) collective-permute-start(f32[3,16,262]{2,1,0:T(8,128)S(1)} %get-tuple-element.93), channel_id=1, source_target_pairs={{16,0},{32,16},{48,32},{64,48},{80,64},{96,80},{112,96},{17,1},{33... | collective-permute-start | bytes 150920 | tf_op jit(solution)/shard_map/ppermute | solution.py:27
  101.7 2.1 collective-permute-start.8
  108.0 4.6 %collective-permute-start.10 = (f32[22,3,262]{2,0,1:T(8,128)}, f32[22,3,262]{2,0,1:T(8,128)}, u32[]{:S(2)}, u32[]{:S(2)}) collective-permute-start(f32[22,3,262]{2,0,1:T(8,128)} %copy.66), channel_id=1, source_target_pairs={{0,4},{4,8},{8,12},{1,5},{5,9},{9,13},{2,6},{6,10},{10,14},{3,7},{... | collective-permute-start | bytes 207512 | tf_op jit(solution)/shard_map/ppermute | solution.py:26
  112.7 2.7 %slice_bitcast_fusion.1 = (f32[22,22,262]{2,1,0:T(8,128)}, f32[22,22,262]{2,1,0:T(8,128)}) fusion(f32[6,22,22,262]{3,2,1,0:T(8,128)} %copy-done.1), kind=kLoop, calls=%fused_computation.20 | loop fusion | bytes 2028928 | tf_op jit(solution)/shard_map/squeeze | solution.py:208
  119.9 5.3 %fusion.159 = f32[20,20,260]{2,1,0:T(8,128)S(1)} fusion(f32[22,22,262]{2,1,0:T(8,128)S(1)} %get-tuple-element.70, f32[22,22,262]{2,1,0:T(8,128)S(1)} %get-tuple-element.69, f32[6,22,22,262]{3,2,1,0:T(8,128)} %copy-done.1, f32[22,22,262]{2,1,0:T(8,128)S(1)} %copy-done.30, f32[22,22,262]{2,1,0:T(8,128)S(1)} %copy-done.29), kind=kLoop, calls=%fused_computation.220 | loop fusion | flops 2392000 | bytes 7072000 | tf_op jit(solution)/shard_map/add | solution.py:54
  128.5 16.3 %shard_map.78 = f32[128,1,128]{2,1,0:T(1,128)} custom-call(f32[1,1,128]{2,1,0:T(1,128)} %copy-done.39), custom_call_target="tpu_custom_call" | custom-call | tf_op jit(solution)/shard_map/pallas_call | solution.py:168
  148.5 3.7 %fusion.204 = (f32[20,20,260]{2,1,0:T(8,128)}, f32[20,20,260]{2,1,0:T(8,128)}) fusion(f32[20,20,260]{2,1,0:T(8,128)} %copy-done.5, f32[20,20,260]{2,1,0:T(8,128)} %copy-done.19, f32[6,22,22,262]{3,2,1,0:T(8,128)} %copy-done.1, f32[20,20,260]{2,1,0:T(8,128)} %copy-done.23, f32[]{:T(128)S(6)} %div.37), kind=kLoop, calls=%fused_computation.335 | loop fusion | flops 624000 | bytes 2912004 | tf_op jit(solution)/shard_map/mul | solution.py:67
  152.5 3.0 %multiply_reduce_fusion = f32[16,16,256]{2,1,0:T(8,128)S(1)} fusion(f32[16,16,16,256]{3,2,1,0:T(8,128)} %param.18, f32[16]{0:T(128)S(1)} %convolution_bitcast_fusion), kind=kLoop, calls=%fused_computation.2 | loop fusion | flops 2031616 | bytes 4456512 | tf_op jit(solution)/shard_map/reduce_sum | solution.py:77
  155.5 4.0 %fusion.207 = (f32[20,20,260]{2,1,0:T(8,128)S(1)}, f32[20,20,260]{2,1,0:T(8,128)S(1)}) fusion(f32[6,22,22,262]{3,2,1,0:T(8,128)} %copy-done.1, f32[20,20,260]{2,1,0:T(8,128)S(1)} %copy-done.6, f32[20,20,260]{2,1,0:T(8,128)S(1)} %copy-done.18, f32[20,20,260]{2,1,0:T(8,128)S(1)} %copy-done.31, f32[3,20,20,260]{3,2,1,0:T(8,128)S(1)} %slice.612, ...), kind=kLoop, calls=%fused_computation.352 | loop fusion | flops 3224000 | bytes 5824000 | tf_op jit(solution)/shard_map/mul | solution.py:67
  159.6 1.8 fusion.206
  163.0 1.8 fusion.197
  167.9 4.0 %collective-permute-start.13 = (f32[16,1,256]{2,0,1:T(8,128)S(1)}, f32[16,1,256]{2,0,1:T(8,128)S(1)}, u32[]{:S(2)}, u32[]{:S(2)}) collective-permute-start(f32[16,1,256]{2,0,1:T(8,128)S(1)} %copy.56), channel_id=1, source_target_pairs={{0,4},{4,8},{8,12},{1,5},{5,9},{9,13},{2,6},{6,10},{10,14},{3,7},{... | collective-permute-start | bytes 49160 | tf_op jit(solution)/shard_map/ppermute | solution.py:89
  171.9 4.0 %collective-permute-start.12 = (f32[16,16,1]{2,1,0:T(8,128)S(1)}, f32[16,16,1]{2,1,0:T(8,128)S(1)}, u32[]{:S(2)}, u32[]{:S(2)}) collective-permute-start(f32[16,16,1]{2,1,0:T(8,128)S(1)} %get-tuple-element.96), channel_id=1, source_target_pairs={{0,1},{1,2},{2,3},{4,5},{5,6},{6,7},{8,9},{9,10},{10,11},{12,13},{... | collective-permute-start | bytes 3080 | tf_op jit(solution)/shard_map/ppermute | solution.py:89
  175.9 3.4 %collective-permute-start.15 = (f32[1,16,256]{2,1,0:T(8,128)S(1)}, f32[1,16,256]{2,1,0:T(8,128)S(1)}, u32[]{:S(2)}, u32[]{:S(2)}) collective-permute-start(f32[1,16,256]{2,1,0:T(8,128)S(1)} %get-tuple-element.95), channel_id=1, source_target_pairs={{16,0},{32,16},{48,32},{64,48},{80,64},{96,80},{112,96},{17,1},{33... | collective-permute-start | bytes 49160 | tf_op jit(solution)/shard_map/ppermute | solution.py:90
  179.4 2.2 %collective-permute-start.14 = (f32[1,16,256]{2,1,0:T(8,128)S(1)}, f32[1,16,256]{2,1,0:T(8,128)S(1)}, u32[]{:S(2)}, u32[]{:S(2)}) collective-permute-start(f32[1,16,256]{2,1,0:T(8,128)S(1)} %get-tuple-element.94), channel_id=1, source_target_pairs={{0,16},{16,32},{32,48},{48,64},{64,80},{80,96},{96,112},{1,17},{17... | collective-permute-start | bytes 49160 | tf_op jit(solution)/shard_map/ppermute | solution.py:89
  185.0 2.6 %maximum_bitcast_fusion.1 = f32[1,1,4]{2,1,0:T(1,128)S(1)} fusion(f32[1]{0:T(128)} %bitcast.40, f32[1]{0:T(128)} %bitcast.39, f32[1]{0:T(128)} %bitcast.38, f32[1]{0:T(128)} %bitcast.30), kind=kLoop, calls=%fused_computation.348 | loop fusion | flops 12 | bytes 32 | tf_op jit(solution)/shard_map/broadcast_in_dim;broadcast_in_dim | solution.py:167
  188.1 14.3 %shard_map.79 = f32[128,1,128]{2,1,0:T(1,128)} custom-call(f32[1,1,128]{2,1,0:T(1,128)} %scatter.19.row_ref), custom_call_target="tpu_custom_call" | custom-call | tf_op jit(solution)/shard_map/pallas_call | solution.py:168
  208.5 2.1 multiply_subtract_fusion.1
  (164 shorter events, 48.7 us)
Async XLA Ops:
  0.6 86.8 %copy-start = (f32[16,2048]{1,0:T(8,128)S(1)}, f32[16,2048]{1,0:T(8,128)}, u32[]{:S(2)}) copy-start(f32[16,2048]{1,0:T(8,128)} %param.19) | copy-start | bytes 393220
  1.7 44.8 %copy-start.16 = (f32[1,16,16,256]{3,2,1,0:T(8,128)}, f32[1,16,16,256]{3,2,1,0:T(8,128)S(1)}, u32[]{:S(2)}) copy-start(f32[1,16,16,256]{3,2,1,0:T(8,128)S(1)} %fusion.202) | copy-start | bytes 786436
  4.2 7.2 %collective-permute-start.1 = (f32[6,16,16,3]{2,1,3,0:T(8,128)S(1)}, f32[6,16,16,3]{2,1,3,0:T(8,128)S(1)}, u32[]{:S(2)}, u32[]{:S(2)}) collective-permute-start(f32[6,16,16,3]{2,1,3,0:T(8,128)S(1)} %copy.63), channel_id=1, source_target_pairs={{1,0},{2,1},{3,2},{5,4},{6,5},{7,6},{9,8},{10,9},{11,10},{13,12},{... | collective-permute-start | bytes 55304 | tf_op jit(solution)/shard_map/ppermute | solution.py:27
  6.1 6.7 %collective-permute-start = (f32[6,16,16,3]{2,1,3,0:T(8,128)S(1)}, f32[6,16,16,3]{2,1,3,0:T(8,128)}, u32[]{:S(2)}, u32[]{:S(2)}) collective-permute-start(f32[6,16,16,3]{2,1,3,0:T(8,128)S(1)} %copy.62), channel_id=1, source_target_pairs={{0,1},{1,2},{2,3},{4,5},{5,6},{6,7},{8,9},{9,10},{10,11},{12,13},{... | collective-permute-start | bytes 55304 | tf_op jit(solution)/shard_map/ppermute | solution.py:26
  12.0 34.4 %copy-start.7 = (f32[6,16,16,3]{3,2,1,0:T(8,128)}, f32[6,16,16,3]{3,2,1,0:T(8,128)S(1)}, u32[]{:S(2)}) copy-start(f32[6,16,16,3]{3,2,1,0:T(8,128)S(1)} %copy.47) | copy-start | bytes 55300
  14.4 32.1 %copy-start.9 = (f32[6,16,16,3]{3,2,1,0:T(8,128)}, f32[6,16,16,3]{3,2,1,0:T(8,128)S(1)}, u32[]{:S(2)}) copy-start(f32[6,16,16,3]{3,2,1,0:T(8,128)S(1)} %copy.46) | copy-start | bytes 55300
  14.8 11.3 %collective-permute-start.3 = (f32[6,3,16,262]{3,2,1,0:T(8,128)S(1)}, f32[6,3,16,262]{3,2,1,0:T(8,128)S(1)}, u32[]{:S(2)}, u32[]{:S(2)}) collective-permute-start(f32[6,3,16,262]{3,2,1,0:T(8,128)S(1)} %get-tuple-element.86), channel_id=1, source_target_pairs={{16,0},{32,16},{48,32},{64,48},{80,64},{96,80},{112,96},{17,1},{33... | collective-permute-start | bytes 905480 | tf_op jit(solution)/shard_map/ppermute | solution.py:27
  18.6 8.6 %collective-permute-start.2 = (f32[6,3,16,262]{3,2,1,0:T(8,128)S(1)}, f32[6,3,16,262]{3,2,1,0:T(8,128)S(1)}, u32[]{:S(2)}, u32[]{:S(2)}) collective-permute-start(f32[6,3,16,262]{3,2,1,0:T(8,128)S(1)} %get-tuple-element.85), channel_id=1, source_target_pairs={{0,16},{16,32},{32,48},{48,64},{64,80},{80,96},{96,112},{1,17},{17... | collective-permute-start | bytes 905480 | tf_op jit(solution)/shard_map/ppermute | solution.py:26
  26.0 20.4 %copy-start.25 = (f32[6,3,16,262]{3,2,1,0:T(8,128)}, f32[6,3,16,262]{3,2,1,0:T(8,128)S(1)}, u32[]{:S(2)}) copy-start(f32[6,3,16,262]{3,2,1,0:T(8,128)S(1)} %collective-permute-done.3) | copy-start | bytes 905476
  27.2 19.3 %copy-start.27 = (f32[6,3,16,262]{3,2,1,0:T(8,128)}, f32[6,3,16,262]{3,2,1,0:T(8,128)S(1)}, u32[]{:S(2)}) copy-start(f32[6,3,16,262]{3,2,1,0:T(8,128)S(1)} %collective-permute-done.2) | copy-start | bytes 905476
  29.8 14.6 %collective-permute-start.5 = (f32[6,22,3,262]{3,1,2,0:T(8,128)S(1)}, f32[6,22,3,262]{3,1,2,0:T(8,128)S(1)}, u32[]{:S(2)}, u32[]{:S(2)}) collective-permute-start(f32[6,22,3,262]{3,1,2,0:T(8,128)S(1)} %copy.65), channel_id=1, source_target_pairs={{4,0},{8,4},{12,8},{5,1},{9,5},{13,9},{6,2},{10,6},{14,10},{7,3},{... | collective-permute-start | bytes 1245032 | tf_op jit(solution)/shard_map/ppermute | solution.py:27
  31.4 14.8 %collective-permute-start.4 = (f32[6,22,3,262]{3,1,2,0:T(8,128)S(1)}, f32[6,22,3,262]{3,1,2,0:T(8,128)S(1)}, u32[]{:S(2)}, u32[]{:S(2)}) collective-permute-start(f32[6,22,3,262]{3,1,2,0:T(8,128)S(1)} %copy.64), channel_id=1, source_target_pairs={{0,4},{4,8},{8,12},{1,5},{5,9},{9,13},{2,6},{6,10},{10,14},{3,7},{... | collective-permute-start | bytes 1245032 | tf_op jit(solution)/shard_map/ppermute | solution.py:26
  90.7 6.6 %collective-permute-start.7 = (f32[16,16,3]{2,1,0:T(8,128)S(1)}, f32[16,16,3]{2,1,0:T(8,128)S(1)}, u32[]{:S(2)}, u32[]{:S(2)}) collective-permute-start(f32[16,16,3]{2,1,0:T(8,128)S(1)} %get-tuple-element.101), channel_id=1, source_target_pairs={{1,0},{2,1},{3,2},{5,4},{6,5},{7,6},{9,8},{10,9},{11,10},{13,12},{... | collective-permute-start | bytes 9224 | tf_op jit(solution)/shard_map/ppermute | solution.py:27
  92.0 6.1 %collective-permute-start.6 = (f32[16,16,3]{2,1,0:T(8,128)S(1)}, f32[16,16,3]{2,1,0:T(8,128)S(1)}, u32[]{:S(2)}, u32[]{:S(2)}) collective-permute-start(f32[16,16,3]{2,1,0:T(8,128)S(1)} %get-tuple-element.100), channel_id=1, source_target_pairs={{0,1},{1,2},{2,3},{4,5},{5,6},{6,7},{8,9},{9,10},{10,11},{12,13},{... | collective-permute-start | bytes 9224 | tf_op jit(solution)/shard_map/ppermute | solution.py:26
  98.2 5.7 %collective-permute-start.9 = (f32[3,16,262]{2,1,0:T(8,128)S(1)}, f32[3,16,262]{2,1,0:T(8,128)S(1)}, u32[]{:S(2)}, u32[]{:S(2)}) collective-permute-start(f32[3,16,262]{2,1,0:T(8,128)S(1)} %get-tuple-element.93), channel_id=1, source_target_pairs={{16,0},{32,16},{48,32},{64,48},{80,64},{96,80},{112,96},{17,1},{33... | collective-permute-start | bytes 150920 | tf_op jit(solution)/shard_map/ppermute | solution.py:27
  101.7 3.5 %collective-permute-start.8 = (f32[3,16,262]{2,1,0:T(8,128)S(1)}, f32[3,16,262]{2,1,0:T(8,128)S(1)}, u32[]{:S(2)}, u32[]{:S(2)}) collective-permute-start(f32[3,16,262]{2,1,0:T(8,128)S(1)} %get-tuple-element.92), channel_id=1, source_target_pairs={{0,16},{16,32},{32,48},{48,64},{64,80},{80,96},{96,112},{1,17},{17... | collective-permute-start | bytes 150920 | tf_op jit(solution)/shard_map/ppermute | solution.py:26
  106.1 10.3 %collective-permute-start.11 = (f32[22,3,262]{2,0,1:T(8,128)}, f32[22,3,262]{2,0,1:T(8,128)}, u32[]{:S(2)}, u32[]{:S(2)}) collective-permute-start(f32[22,3,262]{2,0,1:T(8,128)} %copy.67), channel_id=1, source_target_pairs={{4,0},{8,4},{12,8},{5,1},{9,5},{13,9},{6,2},{10,6},{14,10},{7,3},{... | collective-permute-start | bytes 207512 | tf_op jit(solution)/shard_map/ppermute | solution.py:27
  108.0 9.4 %collective-permute-start.10 = (f32[22,3,262]{2,0,1:T(8,128)}, f32[22,3,262]{2,0,1:T(8,128)}, u32[]{:S(2)}, u32[]{:S(2)}) collective-permute-start(f32[22,3,262]{2,0,1:T(8,128)} %copy.66), channel_id=1, source_target_pairs={{0,4},{4,8},{8,12},{1,5},{5,9},{9,13},{2,6},{6,10},{10,14},{3,7},{... | collective-permute-start | bytes 207512 | tf_op jit(solution)/shard_map/ppermute | solution.py:26
  161.4 20.2 %copy-start.15 = (f32[16,16,256]{2,1,0:T(8,128)S(1)}, f32[16,16,256]{2,1,0:T(8,128)}, u32[]{:S(2)}) copy-start(f32[16,16,256]{2,1,0:T(8,128)} %param.16) | copy-start | bytes 786436
  161.4 20.2 %copy-start.17 = (f32[1,16,16,256]{3,2,1,0:T(8,128)S(1)}, f32[1,16,16,256]{3,2,1,0:T(8,128)}, u32[]{:S(2)}) copy-start(f32[1,16,16,256]{3,2,1,0:T(8,128)} %copy-done.16) | copy-start | bytes 786436
  164.9 18.3 %copy-start.8 = (f32[6,16,16,3]{3,2,1,0:T(8,128)S(1)}, f32[6,16,16,3]{3,2,1,0:T(8,128)}, u32[]{:S(2)}) copy-start(f32[6,16,16,3]{3,2,1,0:T(8,128)} %copy-done.7) | copy-start | bytes 55300
  164.9 18.3 %copy-start.10 = (f32[6,16,16,3]{3,2,1,0:T(8,128)S(1)}, f32[6,16,16,3]{3,2,1,0:T(8,128)}, u32[]{:S(2)}) copy-start(f32[6,16,16,3]{3,2,1,0:T(8,128)} %copy-done.9) | copy-start | bytes 55300
  164.9 18.3 %copy-start.13 = (f32[16,16,256]{2,1,0:T(8,128)S(1)}, f32[16,16,256]{2,1,0:T(8,128)}, u32[]{:S(2)}) copy-start(f32[16,16,256]{2,1,0:T(8,128)} %param.14) | copy-start | bytes 786436
  165.0 18.3 %copy-start.22 = (f32[6,22,3,262]{3,2,1,0:T(4,128)S(1)}, f32[6,22,3,262]{3,2,1,0:T(4,128)}, u32[]{:S(2)}) copy-start(f32[6,22,3,262]{3,2,1,0:T(4,128)} %copy-done.21) | copy-start | bytes 1245028
  165.0 18.3 %copy-start.24 = (f32[20,20,260]{2,1,0:T(8,128)S(1)}, f32[20,20,260]{2,1,0:T(8,128)}, u32[]{:S(2)}) copy-start(f32[20,20,260]{2,1,0:T(8,128)} %copy-done.23) | copy-start | bytes 1248004
  165.0 18.3 %copy-start.26 = (f32[6,3,16,262]{3,2,1,0:T(8,128)S(1)}, f32[6,3,16,262]{3,2,1,0:T(8,128)}, u32[]{:S(2)}) copy-start(f32[6,3,16,262]{3,2,1,0:T(8,128)} %copy-done.25) | copy-start | bytes 905476
  165.1 14.3 %collective-permute-start.16 = (f32[16,1,256]{2,0,1:T(8,128)S(1)}, f32[16,1,256]{2,0,1:T(8,128)S(1)}, u32[]{:S(2)}, u32[]{:S(2)}) collective-permute-start(f32[16,1,256]{2,0,1:T(8,128)S(1)} %copy.57), channel_id=1, source_target_pairs={{4,0},{8,4},{12,8},{5,1},{9,5},{13,9},{6,2},{10,6},{14,10},{7,3},{... | collective-permute-start | bytes 49160 | tf_op jit(solution)/shard_map/ppermute | solution.py:90
  166.6 15.9 %collective-permute-start.17 = (f32[16,16,1]{2,1,0:T(8,128)S(1)}, f32[16,16,1]{2,1,0:T(8,128)S(1)}, u32[]{:S(2)}, u32[]{:S(2)}) collective-permute-start(f32[16,16,1]{2,1,0:T(8,128)S(1)} %get-tuple-element.97), channel_id=1, source_target_pairs={{1,0},{2,1},{3,2},{5,4},{6,5},{7,6},{9,8},{10,9},{11,10},{13,12},{... | collective-permute-start | bytes 3080 | tf_op jit(solution)/shard_map/ppermute | solution.py:90
  167.9 14.6 %collective-permute-start.13 = (f32[16,1,256]{2,0,1:T(8,128)S(1)}, f32[16,1,256]{2,0,1:T(8,128)S(1)}, u32[]{:S(2)}, u32[]{:S(2)}) collective-permute-start(f32[16,1,256]{2,0,1:T(8,128)S(1)} %copy.56), channel_id=1, source_target_pairs={{0,4},{4,8},{8,12},{1,5},{5,9},{9,13},{2,6},{6,10},{10,14},{3,7},{... | collective-permute-start | bytes 49160 | tf_op jit(solution)/shard_map/ppermute | solution.py:89
  171.9 10.6 %collective-permute-start.12 = (f32[16,16,1]{2,1,0:T(8,128)S(1)}, f32[16,16,1]{2,1,0:T(8,128)S(1)}, u32[]{:S(2)}, u32[]{:S(2)}) collective-permute-start(f32[16,16,1]{2,1,0:T(8,128)S(1)} %get-tuple-element.96), channel_id=1, source_target_pairs={{0,1},{1,2},{2,3},{4,5},{5,6},{6,7},{8,9},{9,10},{10,11},{12,13},{... | collective-permute-start | bytes 3080 | tf_op jit(solution)/shard_map/ppermute | solution.py:89
  175.9 6.6 %collective-permute-start.15 = (f32[1,16,256]{2,1,0:T(8,128)S(1)}, f32[1,16,256]{2,1,0:T(8,128)S(1)}, u32[]{:S(2)}, u32[]{:S(2)}) collective-permute-start(f32[1,16,256]{2,1,0:T(8,128)S(1)} %get-tuple-element.95), channel_id=1, source_target_pairs={{16,0},{32,16},{48,32},{64,48},{80,64},{96,80},{112,96},{17,1},{33... | collective-permute-start | bytes 49160 | tf_op jit(solution)/shard_map/ppermute | solution.py:90
  179.4 3.2 %collective-permute-start.14 = (f32[1,16,256]{2,1,0:T(8,128)S(1)}, f32[1,16,256]{2,1,0:T(8,128)S(1)}, u32[]{:S(2)}, u32[]{:S(2)}) collective-permute-start(f32[1,16,256]{2,1,0:T(8,128)S(1)} %get-tuple-element.94), channel_id=1, source_target_pairs={{0,16},{16,32},{32,48},{48,64},{64,80},{80,96},{96,112},{1,17},{17... | collective-permute-start | bytes 49160 | tf_op jit(solution)/shard_map/ppermute | solution.py:89
  (28 other events, 175.9 us)

commit v8 on v1

--- a/solution.py
+++ b/solution.py
@@ -114,12 +114,6 @@
 
     def along_x(k):
         return (lax.rem(a + k, nx), b, c)
-
-    peers = [in_plane(k) for k in range(1, plane)] + [along_x(k) for k in range(1, nx)]
-    barrier = pltpu.get_barrier_semaphore()
-    for peer in peers:
-        pl.semaphore_signal(barrier, inc=1, device_id=peer, device_id_type=MESH_ID)
-    pl.semaphore_wait(barrier, len(peers))
 
     own = pltpu.make_async_copy(row_ref, held.at[pl.ds(me, 1)], local_sem.at[0])
     own.start()
@@ -178,7 +172,7 @@
             pltpu.SemaphoreType.DMA((sizes[0],)),
             pltpu.SemaphoreType.DMA((sizes[0],)),
         ],
-        compiler_params=pltpu.CompilerParams(collective_id=0, has_side_effects=True),
+        compiler_params=pltpu.CompilerParams(has_side_effects=True),
     )(tile)
     return rows[:, 0, :]
 

time: 206 us -> 216 us (1.049)
  Pallas kernels: 55.8 us -> 68.6 us
    pallas_call x3, Pallas kernels: 55.8 us -> 68.6 us  [gather_rows(): pl.pallas_call(functools.partial(gather_kernel, sizes), out_shape=jax.Sha...]
where the time goes in v8:
time: 216 us; the launch traced here: 215 us
  Pallas kernels  68.6 us (32%)
  other arithmetic  58.9 us (27%)
  starting transfers between devices  52.7 us (24%)
  local copies, waits for them, and re-layouts  17.5 us (8%)
  waiting for transfers between devices  9.42 us (4%)
  between operations  7.54 us (3%)
    pallas_call x3, Pallas kernels, gather_rows(): pl.pallas_call(functools.partial(gather_kernel, sizes), out_shape=jax.Sha...  68.6 us
    ppermute x6, starting transfers between devices, padded(): before = lax.ppermute(last, axis, up)  23.7 us
    mul x7, other arithmetic, jacobi(): free_box * guess  16.7 us
    ppermute x6, starting transfers between devices, padded(): after = lax.ppermute(leading, axis, down)  12.6 us
    ppermute x3, starting transfers between devices, faces(): lax.ppermute(lax.slice_in_dim(field, length - 1, length, axis=dim), axis,...  10.1 us
    concatenate x2, other arithmetic, padded(): value = jnp.concatenate([before, value, after], axis=dim)  7.68 us
    ppermute x3, starting transfers between devices, faces(): after = lax.ppermute(lax.slice_in_dim(field, 0, 1, axis=dim), axis, down)  6.27 us
    reduce_sum x2, other arithmetic, expand(): return jnp.sum(weights[:, None, None, None] * basis, axis=0)  5.87 us
  transfers between devices with their start and end apart: 18, of which 7 were waited for; matrix products, arithmetic and copies ran while one was open for 6% of the time, Pallas kernels for 12%

profile of v8, /device:TPU:1, one launch (start us, length us, event | category | flops | bytes accessed | tf_op | source)
XLA Modules:
  0.0 215.0 jit_solution(5890824846074809474)
XLA Ops:
  6.2 5.3 %collective-permute-start = (f32[6,16,16,3]{2,1,3,0:T(8,128)S(1)}, f32[6,16,16,3]{2,1,3,0:T(8,128)}, u32[]{:S(2)}, u32[]{:S(2)}) collective-permute-start(f32[6,16,16,3]{2,1,3,0:T(8,128)S(1)} %copy.62), channel_id=1, source_target_pairs={{0,1},{1,2},{2,3},{4,5},{5,6},{6,7},{8,9},{9,10},{10,11},{12,13},{... | collective-permute-start | bytes 55304 | tf_op jit(solution)/shard_map/ppermute | solution.py:26
  14.8 3.9 %collective-permute-start.3 = (f32[6,3,16,262]{3,2,1,0:T(8,128)S(1)}, f32[6,3,16,262]{3,2,1,0:T(8,128)S(1)}, u32[]{:S(2)}, u32[]{:S(2)}) collective-permute-start(f32[6,3,16,262]{3,2,1,0:T(8,128)S(1)} %get-tuple-element.82), channel_id=1, source_target_pairs={{16,0},{32,16},{48,32},{64,48},{80,64},{96,80},{112,96},{17,1},{33... | collective-permute-start | bytes 905480 | tf_op jit(solution)/shard_map/ppermute | solution.py:27
  18.7 3.3 %collective-permute-start.2 = (f32[6,3,16,262]{3,2,1,0:T(8,128)S(1)}, f32[6,3,16,262]{3,2,1,0:T(8,128)S(1)}, u32[]{:S(2)}, u32[]{:S(2)}) collective-permute-start(f32[6,3,16,262]{3,2,1,0:T(8,128)S(1)} %get-tuple-element.81), channel_id=1, source_target_pairs={{0,16},{16,32},{32,48},{48,64},{64,80},{80,96},{96,112},{1,17},{17... | collective-permute-start | bytes 905480 | tf_op jit(solution)/shard_map/ppermute | solution.py:26
  22.0 4.0 %collective-permute-done.3 = f32[6,3,16,262]{3,2,1,0:T(8,128)S(1)} collective-permute-done((f32[6,3,16,262]{3,2,1,0:T(8,128)S(1)}, f32[6,3,16,262]{3,2,1,0:T(8,128)S(1)}, u32[]{:S(2)}, u32[]{:S(2)}) %collective-permute-start.3) | collective-permute-done | bytes 301856 | tf_op jit(solution)/shard_map/ppermute | solution.py:27
  27.2 2.2 %pad_maximum_fusion.2 = f32[6,22,16,262]{3,2,1,0:T(8,128)S(1)} fusion(f32[6,3,16,262]{3,2,1,0:T(8,128)S(1)} %collective-permute-done.3, f32[6,16,16,3]{3,2,1,0:T(8,128)S(1)} %copy.47, f32[1,16,16,256]{3,2,1,0:T(8,128)S(1)} %bitcast.308, f32[1,16,16,256]{3,2,1,0:T(8,128)S(1)} %fusion.203, f32[1,16,16,256]{3,2,1,0:T(8,128)S(1)} %bitcast.313, ...), kind=kLoop, calls=%fused_computation.6 | loop fusion | flops 3873408 | bytes 4426752 | tf_op jit(solution)/shard_map/concatenate | solution.py:28
  33.0 5.0 %collective-permute-start.4 = (f32[6,22,3,262]{3,1,2,0:T(8,128)}, f32[6,22,3,262]{3,1,2,0:T(8,128)}, u32[]{:S(2)}, u32[]{:S(2)}) collective-permute-start(f32[6,22,3,262]{3,1,2,0:T(8,128)} %copy.64), channel_id=1, source_target_pairs={{0,4},{4,8},{8,12},{1,5},{5,9},{9,13},{2,6},{6,10},{10,14},{3,7},{... | collective-permute-start | bytes 1245032 | tf_op jit(solution)/shard_map/ppermute | solution.py:26
  39.1 26.1 %shard_map.77 = f32[128,1,128]{2,1,0:T(1,128)} custom-call(f32[1,1,128]{2,1,0:T(1,128)} %scatter.14.row_ref), custom_call_target="tpu_custom_call" | custom-call | tf_op jit(solution)/shard_map/pallas_call | solution.py:162
  66.3 2.8 %multiply_reduce_fusion.2 = f32[16,16,256]{2,1,0:T(8,128)S(1)} fusion(f32[16,16,16,256]{3,2,1,0:T(8,128)} %param.18, f32[16]{0:T(128)S(1)} %convolution_bitcast_fusion.1), kind=kLoop, calls=%fused_computation.4 | loop fusion | flops 2031616 | bytes 4456512 | tf_op jit(solution)/shard_map/reduce_sum | solution.py:77
  71.8 5.5 %pad_maximum_fusion = f32[6,22,22,262]{3,2,1,0:T(8,128)S(1)} fusion(f32[6,22,3,262]{3,2,1,0:T(4,128)S(1)} %copy.51, f32[6,3,16,262]{3,2,1,0:T(8,128)S(1)} %copy-done.27, f32[6,16,16,3]{3,2,1,0:T(8,128)S(1)} %copy.47, f32[1,16,16,256]{3,2,1,0:T(8,128)S(1)} %bitcast.309, f32[1,16,16,256]{3,2,1,0:T(8,128)S(1)} %fusion.203, f32[1,16,16,256]{3,2,1,0:T(8,128)S(1)} %bitcast.314, ...), kind=kLoop, calls=%fused_computation | loop fusion | flops 6847632 | bytes 6086784 | tf_op jit(solution)/shard_map/concatenate | solution.py:28
  79.0 2.4 %fusion.204 = (f32[20,20,260]{2,1,0:T(8,128)S(1)}, f32[20,20,260]{2,1,0:T(8,128)S(1)}, f32[20,20,260]{2,1,0:T(8,128)S(1)}, f32[20,20,260]{2,1,0:T(8,128)S(1)}) fusion(f32[6,22,22,262]{3,2,1,0:T(8,128)S(1)} %pad_maximum_fusion, f32[20,20,260]{2,1,0:T(8,128)S(1)} %broadcast_multiply_fusion, f32[3,20,20,260]{3,2,1,0:T(8,128)S(1)} %slice.612), kind=kLoop, calls=%fused_computation.335 | loop fusion | flops 3640000 | bytes 5824000 | tf_op jit(solution)/shard_map/mul | solution.py:67
  81.5 2.5 %fusion.210 = (f32[20,20,260]{2,1,0:T(8,128)S(1)}, f32[20,20,260]{2,1,0:T(8,128)S(1)}) fusion(f32[6,22,22,262]{3,2,1,0:T(8,128)S(1)} %pad_maximum_fusion, f32[20,20,260]{2,1,0:T(8,128)S(1)} %get-tuple-element.73, f32[20,20,260]{2,1,0:T(8,128)S(1)} %get-tuple-element.71, f32[3,20,20,260]{3,2,1,0:T(8,128)S(1)} %slice.612, f32[20,20,260]{2,1,0:T(8,128)S(1)} %get-tuple-element.72), kind=kLoop, calls=%fused_computation.355 | loop fusion | flops 3224000 | bytes 5824000 | tf_op jit(solution)/shard_map/mul | solution.py:67
  84.0 2.1 fusion.209
  86.0 1.6 fusion.79
  89.6 4.0 %collective-permute-start.6 = (f32[16,16,3]{2,1,0:T(8,128)S(1)}, f32[16,16,3]{2,1,0:T(8,128)S(1)}, u32[]{:S(2)}, u32[]{:S(2)}) collective-permute-start(f32[16,16,3]{2,1,0:T(8,128)S(1)} %get-tuple-element.96), channel_id=1, source_target_pairs={{0,1},{1,2},{2,3},{4,5},{5,6},{6,7},{8,9},{9,10},{10,11},{12,13},{... | collective-permute-start | bytes 9224 | tf_op jit(solution)/shard_map/ppermute | solution.py:26
  97.2 3.4 %collective-permute-start.9 = (f32[3,16,262]{2,1,0:T(8,128)}, f32[3,16,262]{2,1,0:T(8,128)}, u32[]{:S(2)}, u32[]{:S(2)}) collective-permute-start(f32[3,16,262]{2,1,0:T(8,128)} %get-tuple-element.89), channel_id=1, source_target_pairs={{16,0},{32,16},{48,32},{64,48},{80,64},{96,80},{112,96},{17,1},{33... | collective-permute-start | bytes 150920 | tf_op jit(solution)/shard_map/ppermute | solution.py:27
  100.6 2.1 collective-permute-start.8
  107.3 4.0 %collective-permute-start.10 = (f32[22,3,262]{2,0,1:T(8,128)S(1)}, f32[22,3,262]{2,0,1:T(8,128)S(1)}, u32[]{:S(2)}, u32[]{:S(2)}) collective-permute-start(f32[22,3,262]{2,0,1:T(8,128)S(1)} %copy.66), channel_id=1, source_target_pairs={{0,4},{4,8},{8,12},{1,5},{5,9},{9,13},{2,6},{6,10},{10,14},{3,7},{... | collective-permute-start | bytes 207512 | tf_op jit(solution)/shard_map/ppermute | solution.py:26
  114.7 3.0 %fusion.159 = f32[20,20,260]{2,1,0:T(8,128)S(1)} fusion(f32[22,22,262]{2,1,0:T(8,128)S(1)} %get-tuple-element.66, f32[22,22,262]{2,1,0:T(8,128)S(1)} %get-tuple-element.65, f32[6,22,22,262]{3,2,1,0:T(8,128)S(1)} %copy-done.2, f32[22,22,262]{2,1,0:T(8,128)S(1)} %get-tuple-element.75, f32[22,22,262]{2,1,0:T(8,128)S(1)} %get-tuple-element.74), kind=kLoop, calls=%fused_computation.220 | loop fusion | flops 2392000 | bytes 7072000 | tf_op jit(solution)/shard_map/add | solution.py:54
  121.1 23.6 %shard_map.78 = f32[128,1,128]{2,1,0:T(1,128)} custom-call(f32[1,1,128]{2,1,0:T(1,128)} %copy-done.38), custom_call_target="tpu_custom_call" | custom-call | tf_op jit(solution)/shard_map/pallas_call | solution.py:162
  148.4 3.6 %fusion.205 = (f32[20,20,260]{2,1,0:T(8,128)}, f32[20,20,260]{2,1,0:T(8,128)}) fusion(f32[20,20,260]{2,1,0:T(8,128)} %copy-done.6, f32[20,20,260]{2,1,0:T(8,128)} %copy-done.20, f32[6,22,22,262]{3,2,1,0:T(8,128)} %copy-done.1, f32[20,20,260]{2,1,0:T(8,128)} %copy-done.24, f32[]{:T(128)S(6)} %div.37), kind=kLoop, calls=%fused_computation.336 | loop fusion | flops 624000 | bytes 2912004 | tf_op jit(solution)/shard_map/mul | solution.py:67
  152.4 3.0 %multiply_reduce_fusion = f32[16,16,256]{2,1,0:T(8,128)S(1)} fusion(f32[16,16,16,256]{3,2,1,0:T(8,128)} %param.18, f32[16]{0:T(128)S(1)} %convolution_bitcast_fusion), kind=kLoop, calls=%fused_computation.2 | loop fusion | flops 2031616 | bytes 4456512 | tf_op jit(solution)/shard_map/reduce_sum | solution.py:77
  155.5 4.0 %fusion.208 = (f32[20,20,260]{2,1,0:T(8,128)S(1)}, f32[20,20,260]{2,1,0:T(8,128)S(1)}) fusion(f32[6,22,22,262]{3,2,1,0:T(8,128)} %copy-done.1, f32[20,20,260]{2,1,0:T(8,128)S(1)} %copy-done.7, f32[20,20,260]{2,1,0:T(8,128)S(1)} %copy-done.19, f32[20,20,260]{2,1,0:T(8,128)S(1)} %copy-done.32, f32[3,20,20,260]{3,2,1,0:T(8,128)S(1)} %slice.612, ...), kind=kLoop, calls=%fused_computation.353 | loop fusion | flops 3224000 | bytes 5824000 | tf_op jit(solution)/shard_map/mul | solution.py:67
  159.5 1.8 fusion.207
  163.0 1.8 fusion.197
  167.9 4.0 %collective-permute-start.13 = (f32[16,1,256]{2,0,1:T(8,128)S(1)}, f32[16,1,256]{2,0,1:T(8,128)S(1)}, u32[]{:S(2)}, u32[]{:S(2)}) collective-permute-start(f32[16,1,256]{2,0,1:T(8,128)S(1)} %copy.56), channel_id=1, source_target_pairs={{0,4},{4,8},{8,12},{1,5},{5,9},{9,13},{2,6},{6,10},{10,14},{3,7},{... | collective-permute-start | bytes 49160 | tf_op jit(solution)/shard_map/ppermute | solution.py:89
  171.9 4.0 %collective-permute-start.12 = (f32[16,16,1]{2,1,0:T(8,128)S(1)}, f32[16,16,1]{2,1,0:T(8,128)S(1)}, u32[]{:S(2)}, u32[]{:S(2)}) collective-permute-start(f32[16,16,1]{2,1,0:T(8,128)S(1)} %get-tuple-element.92), channel_id=1, source_target_pairs={{0,1},{1,2},{2,3},{4,5},{5,6},{6,7},{8,9},{9,10},{10,11},{12,13},{... | collective-permute-start | bytes 3080 | tf_op jit(solution)/shard_map/ppermute | solution.py:89
  175.9 3.4 %collective-permute-start.15 = (f32[1,16,256]{2,1,0:T(8,128)S(1)}, f32[1,16,256]{2,1,0:T(8,128)S(1)}, u32[]{:S(2)}, u32[]{:S(2)}) collective-permute-start(f32[1,16,256]{2,1,0:T(8,128)S(1)} %get-tuple-element.91), channel_id=1, source_target_pairs={{16,0},{32,16},{48,32},{64,48},{80,64},{96,80},{112,96},{17,1},{33... | collective-permute-start | bytes 49160 | tf_op jit(solution)/shard_map/ppermute | solution.py:90
  179.4 2.1 collective-permute-start.14
  183.2 1.7 multiply_reduce_fusion.7
  184.9 2.6 %maximum_bitcast_fusion.1 = f32[1,1,4]{2,1,0:T(1,128)S(1)} fusion(f32[1]{0:T(128)} %bitcast.39, f32[1]{0:T(128)} %bitcast.38, f32[1]{0:T(128)} %bitcast.37, f32[1]{0:T(128)} %bitcast.29), kind=kLoop, calls=%fused_computation.349 | loop fusion | flops 12 | bytes 32 | tf_op jit(solution)/shard_map/broadcast_in_dim;broadcast_in_dim | solution.py:161
  188.0 18.9 %shard_map.79 = f32[128,1,128]{2,1,0:T(1,128)} custom-call(f32[1,1,128]{2,1,0:T(1,128)} %scatter.19.row_ref), custom_call_target="tpu_custom_call" | custom-call | tf_op jit(solution)/shard_map/pallas_call | solution.py:162
  213.0 2.1 multiply_subtract_fusion.1
  (161 shorter events, 47.6 us)
Async XLA Ops:
  0.6 65.4 %copy-start = (f32[16,2048]{1,0:T(8,128)S(1)}, f32[16,2048]{1,0:T(8,128)}, u32[]{:S(2)}) copy-start(f32[16,2048]{1,0:T(8,128)} %param.19) | copy-start | bytes 393220
  1.7 70.1 %copy-start.17 = (f32[1,16,16,256]{3,2,1,0:T(8,128)}, f32[1,16,16,256]{3,2,1,0:T(8,128)S(1)}, u32[]{:S(2)}) copy-start(f32[1,16,16,256]{3,2,1,0:T(8,128)S(1)} %fusion.203) | copy-start | bytes 786436
  4.2 7.2 %collective-permute-start.1 = (f32[6,16,16,3]{2,1,3,0:T(8,128)S(1)}, f32[6,16,16,3]{2,1,3,0:T(8,128)S(1)}, u32[]{:S(2)}, u32[]{:S(2)}) collective-permute-start(f32[6,16,16,3]{2,1,3,0:T(8,128)S(1)} %copy.63), channel_id=1, source_target_pairs={{1,0},{2,1},{3,2},{5,4},{6,5},{7,6},{9,8},{10,9},{11,10},{13,12},{... | collective-permute-start | bytes 55304 | tf_op jit(solution)/shard_map/ppermute | solution.py:27
  6.2 6.7 %collective-permute-start = (f32[6,16,16,3]{2,1,3,0:T(8,128)S(1)}, f32[6,16,16,3]{2,1,3,0:T(8,128)}, u32[]{:S(2)}, u32[]{:S(2)}) collective-permute-start(f32[6,16,16,3]{2,1,3,0:T(8,128)S(1)} %copy.62), channel_id=1, source_target_pairs={{0,1},{1,2},{2,3},{4,5},{5,6},{6,7},{8,9},{9,10},{10,11},{12,13},{... | collective-permute-start | bytes 55304 | tf_op jit(solution)/shard_map/ppermute | solution.py:26
  12.1 59.7 %copy-start.8 = (f32[6,16,16,3]{3,2,1,0:T(8,128)}, f32[6,16,16,3]{3,2,1,0:T(8,128)S(1)}, u32[]{:S(2)}) copy-start(f32[6,16,16,3]{3,2,1,0:T(8,128)S(1)} %copy.47) | copy-start | bytes 55300
  14.4 57.4 %copy-start.10 = (f32[6,16,16,3]{3,2,1,0:T(8,128)}, f32[6,16,16,3]{3,2,1,0:T(8,128)S(1)}, u32[]{:S(2)}) copy-start(f32[6,16,16,3]{3,2,1,0:T(8,128)S(1)} %copy.46) | copy-start | bytes 55300
  14.8 11.3 %collective-permute-start.3 = (f32[6,3,16,262]{3,2,1,0:T(8,128)S(1)}, f32[6,3,16,262]{3,2,1,0:T(8,128)S(1)}, u32[]{:S(2)}, u32[]{:S(2)}) collective-permute-start(f32[6,3,16,262]{3,2,1,0:T(8,128)S(1)} %get-tuple-element.82), channel_id=1, source_target_pairs={{16,0},{32,16},{48,32},{64,48},{80,64},{96,80},{112,96},{17,1},{33... | collective-permute-start | bytes 905480 | tf_op jit(solution)/shard_map/ppermute | solution.py:27
  18.7 8.6 %collective-permute-start.2 = (f32[6,3,16,262]{3,2,1,0:T(8,128)S(1)}, f32[6,3,16,262]{3,2,1,0:T(8,128)S(1)}, u32[]{:S(2)}, u32[]{:S(2)}) collective-permute-start(f32[6,3,16,262]{3,2,1,0:T(8,128)S(1)} %get-tuple-element.81), channel_id=1, source_target_pairs={{0,16},{16,32},{32,48},{48,64},{64,80},{80,96},{96,112},{1,17},{17... | collective-permute-start | bytes 905480 | tf_op jit(solution)/shard_map/ppermute | solution.py:26
  30.6 38.5 %collective-permute-start.5 = (f32[6,22,3,262]{3,1,2,0:T(8,128)}, f32[6,22,3,262]{3,1,2,0:T(8,128)}, u32[]{:S(2)}, u32[]{:S(2)}) collective-permute-start(f32[6,22,3,262]{3,1,2,0:T(8,128)} %copy.65), channel_id=1, source_target_pairs={{4,0},{8,4},{12,8},{5,1},{9,5},{13,9},{6,2},{10,6},{14,10},{7,3},{... | collective-permute-start | bytes 1245032 | tf_op jit(solution)/shard_map/ppermute | solution.py:27
  33.0 37.5 %collective-permute-start.4 = (f32[6,22,3,262]{3,1,2,0:T(8,128)}, f32[6,22,3,262]{3,1,2,0:T(8,128)}, u32[]{:S(2)}, u32[]{:S(2)}) collective-permute-start(f32[6,22,3,262]{3,1,2,0:T(8,128)} %copy.64), channel_id=1, source_target_pairs={{0,4},{4,8},{8,12},{1,5},{5,9},{9,13},{2,6},{6,10},{10,14},{3,7},{... | collective-permute-start | bytes 1245032 | tf_op jit(solution)/shard_map/ppermute | solution.py:26
  88.3 6.6 %collective-permute-start.7 = (f32[16,16,3]{2,1,0:T(8,128)S(1)}, f32[16,16,3]{2,1,0:T(8,128)S(1)}, u32[]{:S(2)}, u32[]{:S(2)}) collective-permute-start(f32[16,16,3]{2,1,0:T(8,128)S(1)} %get-tuple-element.97), channel_id=1, source_target_pairs={{1,0},{2,1},{3,2},{5,4},{6,5},{7,6},{9,8},{10,9},{11,10},{13,12},{... | collective-permute-start | bytes 9224 | tf_op jit(solution)/shard_map/ppermute | solution.py:27
  89.6 6.1 %collective-permute-start.6 = (f32[16,16,3]{2,1,0:T(8,128)S(1)}, f32[16,16,3]{2,1,0:T(8,128)S(1)}, u32[]{:S(2)}, u32[]{:S(2)}) collective-permute-start(f32[16,16,3]{2,1,0:T(8,128)S(1)} %get-tuple-element.96), channel_id=1, source_target_pairs={{0,1},{1,2},{2,3},{4,5},{5,6},{6,7},{8,9},{9,10},{10,11},{12,13},{... | collective-permute-start | bytes 9224 | tf_op jit(solution)/shard_map/ppermute | solution.py:26
  97.2 6.5 %collective-permute-start.9 = (f32[3,16,262]{2,1,0:T(8,128)}, f32[3,16,262]{2,1,0:T(8,128)}, u32[]{:S(2)}, u32[]{:S(2)}) collective-permute-start(f32[3,16,262]{2,1,0:T(8,128)} %get-tuple-element.89), channel_id=1, source_target_pairs={{16,0},{32,16},{48,32},{64,48},{80,64},{96,80},{112,96},{17,1},{33... | collective-permute-start | bytes 150920 | tf_op jit(solution)/shard_map/ppermute | solution.py:27
  100.6 3.8 %collective-permute-start.8 = (f32[3,16,262]{2,1,0:T(8,128)}, f32[3,16,262]{2,1,0:T(8,128)}, u32[]{:S(2)}, u32[]{:S(2)}) collective-permute-start(f32[3,16,262]{2,1,0:T(8,128)} %get-tuple-element.88), channel_id=1, source_target_pairs={{0,16},{16,32},{32,48},{48,64},{64,80},{80,96},{96,112},{1,17},{17... | collective-permute-start | bytes 150920 | tf_op jit(solution)/shard_map/ppermute | solution.py:26
  106.0 6.9 %collective-permute-start.11 = (f32[22,3,262]{2,0,1:T(8,128)S(1)}, f32[22,3,262]{2,0,1:T(8,128)S(1)}, u32[]{:S(2)}, u32[]{:S(2)}) collective-permute-start(f32[22,3,262]{2,0,1:T(8,128)S(1)} %copy.67), channel_id=1, source_target_pairs={{4,0},{8,4},{12,8},{5,1},{9,5},{13,9},{6,2},{10,6},{14,10},{7,3},{... | collective-permute-start | bytes 207512 | tf_op jit(solution)/shard_map/ppermute | solution.py:27
  107.3 6.1 %collective-permute-start.10 = (f32[22,3,262]{2,0,1:T(8,128)S(1)}, f32[22,3,262]{2,0,1:T(8,128)S(1)}, u32[]{:S(2)}, u32[]{:S(2)}) collective-permute-start(f32[22,3,262]{2,0,1:T(8,128)S(1)} %copy.66), channel_id=1, source_target_pairs={{0,4},{4,8},{8,12},{1,5},{5,9},{9,13},{2,6},{6,10},{10,14},{3,7},{... | collective-permute-start | bytes 207512 | tf_op jit(solution)/shard_map/ppermute | solution.py:26
  161.4 20.1 %copy-start.16 = (f32[16,16,256]{2,1,0:T(8,128)S(1)}, f32[16,16,256]{2,1,0:T(8,128)}, u32[]{:S(2)}) copy-start(f32[16,16,256]{2,1,0:T(8,128)} %param.16) | copy-start | bytes 786436
  161.4 20.1 %copy-start.18 = (f32[1,16,16,256]{3,2,1,0:T(8,128)S(1)}, f32[1,16,16,256]{3,2,1,0:T(8,128)}, u32[]{:S(2)}) copy-start(f32[1,16,16,256]{3,2,1,0:T(8,128)} %copy-done.17) | copy-start | bytes 786436
  164.9 18.2 %copy-start.9 = (f32[6,16,16,3]{3,2,1,0:T(8,128)S(1)}, f32[6,16,16,3]{3,2,1,0:T(8,128)}, u32[]{:S(2)}) copy-start(f32[6,16,16,3]{3,2,1,0:T(8,128)} %copy-done.8) | copy-start | bytes 55300
  164.9 18.2 %copy-start.11 = (f32[6,16,16,3]{3,2,1,0:T(8,128)S(1)}, f32[6,16,16,3]{3,2,1,0:T(8,128)}, u32[]{:S(2)}) copy-start(f32[6,16,16,3]{3,2,1,0:T(8,128)} %copy-done.10) | copy-start | bytes 55300
  164.9 18.2 %copy-start.14 = (f32[16,16,256]{2,1,0:T(8,128)S(1)}, f32[16,16,256]{2,1,0:T(8,128)}, u32[]{:S(2)}) copy-start(f32[16,16,256]{2,1,0:T(8,128)} %param.14) | copy-start | bytes 786436
  164.9 18.2 %copy-start.23 = (f32[6,22,3,262]{3,2,1,0:T(4,128)S(1)}, f32[6,22,3,262]{3,2,1,0:T(4,128)}, u32[]{:S(2)}) copy-start(f32[6,22,3,262]{3,2,1,0:T(4,128)} %copy-done.22) | copy-start | bytes 1245028
  164.9 18.2 %copy-start.25 = (f32[20,20,260]{2,1,0:T(8,128)S(1)}, f32[20,20,260]{2,1,0:T(8,128)}, u32[]{:S(2)}) copy-start(f32[20,20,260]{2,1,0:T(8,128)} %copy-done.24) | copy-start | bytes 1248004
  164.9 18.2 %copy-start.28 = (f32[6,3,16,262]{3,2,1,0:T(8,128)S(1)}, f32[6,3,16,262]{3,2,1,0:T(8,128)}, u32[]{:S(2)}) copy-start(f32[6,3,16,262]{3,2,1,0:T(8,128)} %copy-done.26) | copy-start | bytes 905476
  165.0 18.2 %copy-start.31 = (f32[6,3,16,262]{3,2,1,0:T(8,128)S(1)}, f32[6,3,16,262]{3,2,1,0:T(8,128)}, u32[]{:S(2)}) copy-start(f32[6,3,16,262]{3,2,1,0:T(8,128)} %copy-done.29) | copy-start | bytes 905476
  165.0 18.2 %copy-start.37 = (s32[16,16,256]{2,1,0:T(8,128)S(1)}, s32[16,16,256]{2,1,0:T(8,128)}, u32[]{:S(2)}) copy-start(s32[16,16,256]{2,1,0:T(8,128)} %param.17) | copy-start | bytes 786436
  165.0 14.3 %collective-permute-start.16 = (f32[16,1,256]{2,0,1:T(8,128)S(1)}, f32[16,1,256]{2,0,1:T(8,128)S(1)}, u32[]{:S(2)}, u32[]{:S(2)}) collective-permute-start(f32[16,1,256]{2,0,1:T(8,128)S(1)} %copy.57), channel_id=1, source_target_pairs={{4,0},{8,4},{12,8},{5,1},{9,5},{13,9},{6,2},{10,6},{14,10},{7,3},{... | collective-permute-start | bytes 49160 | tf_op jit(solution)/shard_map/ppermute | solution.py:90
  166.6 15.8 %collective-permute-start.17 = (f32[16,16,1]{2,1,0:T(8,128)S(1)}, f32[16,16,1]{2,1,0:T(8,128)S(1)}, u32[]{:S(2)}, u32[]{:S(2)}) collective-permute-start(f32[16,16,1]{2,1,0:T(8,128)S(1)} %get-tuple-element.93), channel_id=1, source_target_pairs={{1,0},{2,1},{3,2},{5,4},{6,5},{7,6},{9,8},{10,9},{11,10},{13,12},{... | collective-permute-start | bytes 3080 | tf_op jit(solution)/shard_map/ppermute | solution.py:90
  167.9 14.5 %collective-permute-start.13 = (f32[16,1,256]{2,0,1:T(8,128)S(1)}, f32[16,1,256]{2,0,1:T(8,128)S(1)}, u32[]{:S(2)}, u32[]{:S(2)}) collective-permute-start(f32[16,1,256]{2,0,1:T(8,128)S(1)} %copy.56), channel_id=1, source_target_pairs={{0,4},{4,8},{8,12},{1,5},{5,9},{9,13},{2,6},{6,10},{10,14},{3,7},{... | collective-permute-start | bytes 49160 | tf_op jit(solution)/shard_map/ppermute | solution.py:89
  171.9 10.6 %collective-permute-start.12 = (f32[16,16,1]{2,1,0:T(8,128)S(1)}, f32[16,16,1]{2,1,0:T(8,128)S(1)}, u32[]{:S(2)}, u32[]{:S(2)}) collective-permute-start(f32[16,16,1]{2,1,0:T(8,128)S(1)} %get-tuple-element.92), channel_id=1, source_target_pairs={{0,1},{1,2},{2,3},{4,5},{5,6},{6,7},{8,9},{9,10},{10,11},{12,13},{... | collective-permute-start | bytes 3080 | tf_op jit(solution)/shard_map/ppermute | solution.py:89
  175.9 6.6 %collective-permute-start.15 = (f32[1,16,256]{2,1,0:T(8,128)S(1)}, f32[1,16,256]{2,1,0:T(8,128)S(1)}, u32[]{:S(2)}, u32[]{:S(2)}) collective-permute-start(f32[1,16,256]{2,1,0:T(8,128)S(1)} %get-tuple-element.91), channel_id=1, source_target_pairs={{16,0},{32,16},{48,32},{64,48},{80,64},{96,80},{112,96},{17,1},{33... | collective-permute-start | bytes 49160 | tf_op jit(solution)/shard_map/ppermute | solution.py:90
  179.4 3.1 %collective-permute-start.14 = (f32[1,16,256]{2,1,0:T(8,128)S(1)}, f32[1,16,256]{2,1,0:T(8,128)S(1)}, u32[]{:S(2)}, u32[]{:S(2)}) collective-permute-start(f32[1,16,256]{2,1,0:T(8,128)S(1)} %get-tuple-element.90), channel_id=1, source_target_pairs={{0,16},{16,32},{32,48},{48,64},{64,80},{80,96},{96,112},{1,17},{17... | collective-permute-start | bytes 49160 | tf_op jit(solution)/shard_map/ppermute | solution.py:89
  (27 other events, 151.7 us)

commit v9 on v1

--- a/solution.py
+++ b/solution.py
@@ -101,7 +101,7 @@
     return padded(field, (("gx", 0), ("gy", 1), ("gz", 2)), 2)
 
 
-def gather_kernel(sizes, row_ref, out_ref, held, local_sem, send1, recv1, send2, recv2):
+def gather_kernel(sizes, row_ref, held, local_sem, send1, recv1, send2, recv2):
     nx, ny, nz = sizes
     plane = ny * nz
     a = lax.axis_index("gx")
@@ -156,9 +156,6 @@
     stage(lambda k: held.at[pl.ds(x_first(k), plane)], x_first, plane, nx, along_x, send2, recv2)
     for copy in sent:
         copy.wait_send()
-    final = pltpu.make_async_copy(held, out_ref, local_sem.at[1])
-    final.start()
-    final.wait()
 
 
 def gather_rows(row):
@@ -171,8 +168,7 @@
         in_specs=[pl.BlockSpec(memory_space=pltpu.VMEM)],
         out_specs=pl.BlockSpec(memory_space=pltpu.VMEM),
         scratch_shapes=[
-            pltpu.VMEM((count, 1, LANES), jnp.float32),
-            pltpu.SemaphoreType.DMA((2,)),
+            pltpu.SemaphoreType.DMA((1,)),
             pltpu.SemaphoreType.DMA((sizes[1] * sizes[2],)),
             pltpu.SemaphoreType.DMA((sizes[1] * sizes[2],)),
             pltpu.SemaphoreType.DMA((sizes[0],)),

time: 206 us -> 205 us (level)
  no operation moved by 1% of the time
where the time goes in v9:
time: 205 us; the launch traced here: 204 us
  other arithmetic  58.9 us (29%)
  Pallas kernels  55.5 us (27%)
  starting transfers between devices  53.8 us (26%)
  local copies, waits for them, and re-layouts  17.7 us (9%)
  waiting for transfers between devices  10.1 us (5%)
  between operations  7.54 us (4%)
    pallas_call x3, Pallas kernels, gather_rows(): pl.pallas_call(functools.partial(gather_kernel, sizes), out_shape=jax.Sha...  55.5 us
    ppermute x6, starting transfers between devices, padded(): before = lax.ppermute(last, axis, up)  24.9 us
    mul x7, other arithmetic, jacobi(): free_box * guess  16.5 us
    ppermute x6, starting transfers between devices, padded(): after = lax.ppermute(leading, axis, down)  12.3 us
    ppermute x3, starting transfers between devices, faces(): lax.ppermute(lax.slice_in_dim(field, length - 1, length, axis=dim), axis,...  10.4 us
    concatenate x2, other arithmetic, padded(): value = jnp.concatenate([before, value, after], axis=dim)  7.86 us
    ppermute x3, starting transfers between devices, faces(): after = lax.ppermute(lax.slice_in_dim(field, 0, 1, axis=dim), axis, down)  6.27 us
    reduce_sum x2, other arithmetic, expand(): return jnp.sum(weights[:, None, None, None] * basis, axis=0)  5.87 us
  transfers between devices with their start and end apart: 18, of which 7 were waited for; matrix products, arithmetic and copies ran while one was open for 6% of the time, Pallas kernels for 12%

profile of v9, /device:TPU:1, one launch (start us, length us, event | category | flops | bytes accessed | tf_op | source)
XLA Modules:
  0.0 203.9 jit_solution(16038504030398982509)
XLA Ops:
  6.2 5.3 %collective-permute-start = (f32[6,16,16,3]{2,1,3,0:T(8,128)S(1)}, f32[6,16,16,3]{2,1,3,0:T(8,128)}, u32[]{:S(2)}, u32[]{:S(2)}) collective-permute-start(f32[6,16,16,3]{2,1,3,0:T(8,128)S(1)} %copy.62), channel_id=1, source_target_pairs={{0,1},{1,2},{2,3},{4,5},{5,6},{6,7},{8,9},{9,10},{10,11},{12,13},{... | collective-permute-start | bytes 55304 | tf_op jit(solution)/shard_map/ppermute | solution.py:26
  14.8 3.9 %collective-permute-start.3 = (f32[6,3,16,262]{3,2,1,0:T(8,128)S(1)}, f32[6,3,16,262]{3,2,1,0:T(8,128)S(1)}, u32[]{:S(2)}, u32[]{:S(2)}) collective-permute-start(f32[6,3,16,262]{3,2,1,0:T(8,128)S(1)} %get-tuple-element.82), channel_id=1, source_target_pairs={{16,0},{32,16},{48,32},{64,48},{80,64},{96,80},{112,96},{17,1},{33... | collective-permute-start | bytes 905480 | tf_op jit(solution)/shard_map/ppermute | solution.py:27
  18.7 3.3 %collective-permute-start.2 = (f32[6,3,16,262]{3,2,1,0:T(8,128)S(1)}, f32[6,3,16,262]{3,2,1,0:T(8,128)S(1)}, u32[]{:S(2)}, u32[]{:S(2)}) collective-permute-start(f32[6,3,16,262]{3,2,1,0:T(8,128)S(1)} %get-tuple-element.81), channel_id=1, source_target_pairs={{0,16},{16,32},{32,48},{48,64},{64,80},{80,96},{96,112},{1,17},{17... | collective-permute-start | bytes 905480 | tf_op jit(solution)/shard_map/ppermute | solution.py:26
  22.0 4.0 %collective-permute-done.3 = f32[6,3,16,262]{3,2,1,0:T(8,128)S(1)} collective-permute-done((f32[6,3,16,262]{3,2,1,0:T(8,128)S(1)}, f32[6,3,16,262]{3,2,1,0:T(8,128)S(1)}, u32[]{:S(2)}, u32[]{:S(2)}) %collective-permute-start.3) | collective-permute-done | bytes 301856 | tf_op jit(solution)/shard_map/ppermute | solution.py:27
  27.2 2.2 %pad_maximum_fusion.2 = f32[6,22,16,262]{3,2,1,0:T(8,128)S(1)} fusion(f32[6,3,16,262]{3,2,1,0:T(8,128)S(1)} %collective-permute-done.3, f32[6,16,16,3]{3,2,1,0:T(8,128)S(1)} %copy.47, f32[1,16,16,256]{3,2,1,0:T(8,128)S(1)} %bitcast.308, f32[1,16,16,256]{3,2,1,0:T(8,128)S(1)} %fusion.203, f32[1,16,16,256]{3,2,1,0:T(8,128)S(1)} %bitcast.313, ...), kind=kLoop, calls=%fused_computation.6 | loop fusion | flops 3873408 | bytes 4426752 | tf_op jit(solution)/shard_map/concatenate | solution.py:28
  33.0 5.0 %collective-permute-start.4 = (f32[6,22,3,262]{3,1,2,0:T(8,128)}, f32[6,22,3,262]{3,1,2,0:T(8,128)}, u32[]{:S(2)}, u32[]{:S(2)}) collective-permute-start(f32[6,22,3,262]{3,1,2,0:T(8,128)} %copy.64), channel_id=1, source_target_pairs={{0,4},{4,8},{8,12},{1,5},{5,9},{9,13},{2,6},{6,10},{10,14},{3,7},{... | collective-permute-start | bytes 1245032 | tf_op jit(solution)/shard_map/ppermute | solution.py:26
  39.1 23.9 %shard_map.77 = f32[128,1,128]{2,1,0:T(1,128)} custom-call(f32[1,1,128]{2,1,0:T(1,128)} %scatter.14.row_ref), custom_call_target="tpu_custom_call" | custom-call | tf_op jit(solution)/shard_map/pallas_call | solution.py:165
  64.1 2.8 %multiply_reduce_fusion.2 = f32[16,16,256]{2,1,0:T(8,128)S(1)} fusion(f32[16,16,16,256]{3,2,1,0:T(8,128)} %param.18, f32[16]{0:T(128)S(1)} %convolution_bitcast_fusion.1), kind=kLoop, calls=%fused_computation.4 | loop fusion | flops 2031616 | bytes 4456512 | tf_op jit(solution)/shard_map/reduce_sum | solution.py:77
  69.6 5.7 %pad_maximum_fusion = f32[6,22,22,262]{3,2,1,0:T(8,128)S(1)} fusion(f32[6,22,3,262]{3,2,1,0:T(4,128)S(1)} %copy.51, f32[6,3,16,262]{3,2,1,0:T(8,128)S(1)} %copy-done.27, f32[6,16,16,3]{3,2,1,0:T(8,128)S(1)} %copy.47, f32[1,16,16,256]{3,2,1,0:T(8,128)S(1)} %bitcast.309, f32[1,16,16,256]{3,2,1,0:T(8,128)S(1)} %fusion.203, f32[1,16,16,256]{3,2,1,0:T(8,128)S(1)} %bitcast.314, ...), kind=kLoop, calls=%fused_computation | loop fusion | flops 6847632 | bytes 6086784 | tf_op jit(solution)/shard_map/concatenate | solution.py:28
  77.0 2.4 %fusion.204 = (f32[20,20,260]{2,1,0:T(8,128)S(1)}, f32[20,20,260]{2,1,0:T(8,128)S(1)}, f32[20,20,260]{2,1,0:T(8,128)S(1)}, f32[20,20,260]{2,1,0:T(8,128)S(1)}) fusion(f32[6,22,22,262]{3,2,1,0:T(8,128)S(1)} %pad_maximum_fusion, f32[20,20,260]{2,1,0:T(8,128)S(1)} %broadcast_multiply_fusion, f32[3,20,20,260]{3,2,1,0:T(8,128)S(1)} %slice.612), kind=kLoop, calls=%fused_computation.335 | loop fusion | flops 3640000 | bytes 5824000 | tf_op jit(solution)/shard_map/mul | solution.py:67
  79.5 2.3 %fusion.210 = (f32[20,20,260]{2,1,0:T(8,128)S(1)}, f32[20,20,260]{2,1,0:T(8,128)S(1)}) fusion(f32[6,22,22,262]{3,2,1,0:T(8,128)S(1)} %pad_maximum_fusion, f32[20,20,260]{2,1,0:T(8,128)S(1)} %get-tuple-element.73, f32[20,20,260]{2,1,0:T(8,128)S(1)} %get-tuple-element.71, f32[3,20,20,260]{3,2,1,0:T(8,128)S(1)} %slice.612, f32[20,20,260]{2,1,0:T(8,128)S(1)} %get-tuple-element.72), kind=kLoop, calls=%fused_computation.355 | loop fusion | flops 3224000 | bytes 5824000 | tf_op jit(solution)/shard_map/mul | solution.py:67
  81.7 2.1 %fusion.209 = (f32[20,20,260]{2,1,0:T(8,128)S(1)}, f32[20,20,260]{2,1,0:T(8,128)S(1)}) fusion(f32[6,22,22,262]{3,2,1,0:T(8,128)S(1)} %pad_maximum_fusion, f32[20,20,260]{2,1,0:T(8,128)S(1)} %get-tuple-element.70, f32[20,20,260]{2,1,0:T(8,128)S(1)} %get-tuple-element.73, f32[20,20,260]{2,1,0:T(8,128)S(1)} %get-tuple-element.69, f32[3,20,20,260]{3,2,1,0:T(8,128)S(1)} %slice.612), kind=kLoop, calls=%fused_computation.354 | loop fusion | flops 2912000 | bytes 5824000 | tf_op jit(solution)/shard_map/mul | solution.py:67
  87.4 4.8 %collective-permute-start.6 = (f32[16,16,3]{2,1,0:T(8,128)S(1)}, f32[16,16,3]{2,1,0:T(8,128)S(1)}, u32[]{:S(2)}, u32[]{:S(2)}) collective-permute-start(f32[16,16,3]{2,1,0:T(8,128)S(1)} %get-tuple-element.96), channel_id=1, source_target_pairs={{0,1},{1,2},{2,3},{4,5},{5,6},{6,7},{8,9},{9,10},{10,11},{12,13},{... | collective-permute-start | bytes 9224 | tf_op jit(solution)/shard_map/ppermute | solution.py:26
  92.2 1.6 collective-permute-done.7
  96.1 3.1 %collective-permute-start.9 = (f32[3,16,262]{2,1,0:T(8,128)}, f32[3,16,262]{2,1,0:T(8,128)}, u32[]{:S(2)}, u32[]{:S(2)}) collective-permute-start(f32[3,16,262]{2,1,0:T(8,128)} %get-tuple-element.89), channel_id=1, source_target_pairs={{16,0},{32,16},{48,32},{64,48},{80,64},{96,80},{112,96},{17,1},{33... | collective-permute-start | bytes 150920 | tf_op jit(solution)/shard_map/ppermute | solution.py:27
  99.2 2.4 %collective-permute-start.8 = (f32[3,16,262]{2,1,0:T(8,128)}, f32[3,16,262]{2,1,0:T(8,128)}, u32[]{:S(2)}, u32[]{:S(2)}) collective-permute-start(f32[3,16,262]{2,1,0:T(8,128)} %get-tuple-element.88), channel_id=1, source_target_pairs={{0,16},{16,32},{32,48},{48,64},{64,80},{80,96},{96,112},{1,17},{17... | collective-permute-start | bytes 150920 | tf_op jit(solution)/shard_map/ppermute | solution.py:26
  106.2 4.0 %collective-permute-start.10 = (f32[22,3,262]{2,0,1:T(8,128)S(1)}, f32[22,3,262]{2,0,1:T(8,128)S(1)}, u32[]{:S(2)}, u32[]{:S(2)}) collective-permute-start(f32[22,3,262]{2,0,1:T(8,128)S(1)} %copy.66), channel_id=1, source_target_pairs={{0,4},{4,8},{8,12},{1,5},{5,9},{9,13},{2,6},{6,10},{10,14},{3,7},{... | collective-permute-start | bytes 207512 | tf_op jit(solution)/shard_map/ppermute | solution.py:26
  113.9 3.0 %fusion.159 = f32[20,20,260]{2,1,0:T(8,128)S(1)} fusion(f32[22,22,262]{2,1,0:T(8,128)S(1)} %get-tuple-element.66, f32[22,22,262]{2,1,0:T(8,128)S(1)} %get-tuple-element.65, f32[6,22,22,262]{3,2,1,0:T(8,128)S(1)} %copy-done.2, f32[22,22,262]{2,1,0:T(8,128)S(1)} %get-tuple-element.75, f32[22,22,262]{2,1,0:T(8,128)S(1)} %get-tuple-element.74), kind=kLoop, calls=%fused_computation.220 | loop fusion | flops 2392000 | bytes 7072000 | tf_op jit(solution)/shard_map/add | solution.py:54
  120.6 17.4 %shard_map.78 = f32[128,1,128]{2,1,0:T(1,128)} custom-call(f32[1,1,128]{2,1,0:T(1,128)} %copy-done.38), custom_call_target="tpu_custom_call" | custom-call | tf_op jit(solution)/shard_map/pallas_call | solution.py:165
  141.7 3.6 %fusion.205 = (f32[20,20,260]{2,1,0:T(8,128)}, f32[20,20,260]{2,1,0:T(8,128)}) fusion(f32[20,20,260]{2,1,0:T(8,128)} %copy-done.6, f32[20,20,260]{2,1,0:T(8,128)} %copy-done.20, f32[6,22,22,262]{3,2,1,0:T(8,128)} %copy-done.1, f32[20,20,260]{2,1,0:T(8,128)} %copy-done.24, f32[]{:T(128)S(6)} %div.37), kind=kLoop, calls=%fused_computation.336 | loop fusion | flops 624000 | bytes 2912004 | tf_op jit(solution)/shard_map/mul | solution.py:67
  145.7 3.0 %multiply_reduce_fusion = f32[16,16,256]{2,1,0:T(8,128)S(1)} fusion(f32[16,16,16,256]{3,2,1,0:T(8,128)} %param.18, f32[16]{0:T(128)S(1)} %convolution_bitcast_fusion), kind=kLoop, calls=%fused_computation.2 | loop fusion | flops 2031616 | bytes 4456512 | tf_op jit(solution)/shard_map/reduce_sum | solution.py:77
  148.8 4.0 %fusion.208 = (f32[20,20,260]{2,1,0:T(8,128)S(1)}, f32[20,20,260]{2,1,0:T(8,128)S(1)}) fusion(f32[6,22,22,262]{3,2,1,0:T(8,128)} %copy-done.1, f32[20,20,260]{2,1,0:T(8,128)S(1)} %copy-done.7, f32[20,20,260]{2,1,0:T(8,128)S(1)} %copy-done.19, f32[20,20,260]{2,1,0:T(8,128)S(1)} %copy-done.32, f32[3,20,20,260]{3,2,1,0:T(8,128)S(1)} %slice.612, ...), kind=kLoop, calls=%fused_computation.353 | loop fusion | flops 3224000 | bytes 5824000 | tf_op jit(solution)/shard_map/mul | solution.py:67
  152.8 1.8 fusion.207
  156.3 1.8 fusion.197
  161.2 4.0 %collective-permute-start.13 = (f32[16,1,256]{2,0,1:T(8,128)S(1)}, f32[16,1,256]{2,0,1:T(8,128)S(1)}, u32[]{:S(2)}, u32[]{:S(2)}) collective-permute-start(f32[16,1,256]{2,0,1:T(8,128)S(1)} %copy.56), channel_id=1, source_target_pairs={{0,4},{4,8},{8,12},{1,5},{5,9},{9,13},{2,6},{6,10},{10,14},{3,7},{... | collective-permute-start | bytes 49160 | tf_op jit(solution)/shard_map/ppermute | solution.py:89
  165.2 4.0 %collective-permute-start.12 = (f32[16,16,1]{2,1,0:T(8,128)S(1)}, f32[16,16,1]{2,1,0:T(8,128)S(1)}, u32[]{:S(2)}, u32[]{:S(2)}) collective-permute-start(f32[16,16,1]{2,1,0:T(8,128)S(1)} %get-tuple-element.92), channel_id=1, source_target_pairs={{0,1},{1,2},{2,3},{4,5},{5,6},{6,7},{8,9},{9,10},{10,11},{12,13},{... | collective-permute-start | bytes 3080 | tf_op jit(solution)/shard_map/ppermute | solution.py:89
  169.2 3.4 %collective-permute-start.15 = (f32[1,16,256]{2,1,0:T(8,128)S(1)}, f32[1,16,256]{2,1,0:T(8,128)S(1)}, u32[]{:S(2)}, u32[]{:S(2)}) collective-permute-start(f32[1,16,256]{2,1,0:T(8,128)S(1)} %get-tuple-element.91), channel_id=1, source_target_pairs={{16,0},{32,16},{48,32},{64,48},{80,64},{96,80},{112,96},{17,1},{33... | collective-permute-start | bytes 49160 | tf_op jit(solution)/shard_map/ppermute | solution.py:90
  172.6 2.4 %collective-permute-start.14 = (f32[1,16,256]{2,1,0:T(8,128)S(1)}, f32[1,16,256]{2,1,0:T(8,128)S(1)}, u32[]{:S(2)}, u32[]{:S(2)}) collective-permute-start(f32[1,16,256]{2,1,0:T(8,128)S(1)} %get-tuple-element.90), channel_id=1, source_target_pairs={{0,16},{16,32},{32,48},{48,64},{64,80},{80,96},{96,112},{1,17},{17... | collective-permute-start | bytes 49160 | tf_op jit(solution)/shard_map/ppermute | solution.py:89
  176.7 1.7 multiply_reduce_fusion.7
  178.4 2.6 %maximum_bitcast_fusion.1 = f32[1,1,4]{2,1,0:T(1,128)S(1)} fusion(f32[1]{0:T(128)} %bitcast.39, f32[1]{0:T(128)} %bitcast.38, f32[1]{0:T(128)} %bitcast.37, f32[1]{0:T(128)} %bitcast.29), kind=kLoop, calls=%fused_computation.349 | loop fusion | flops 12 | bytes 32 | tf_op jit(solution)/shard_map/broadcast_in_dim;broadcast_in_dim | solution.py:164
  181.5 14.2 %shard_map.79 = f32[128,1,128]{2,1,0:T(1,128)} custom-call(f32[1,1,128]{2,1,0:T(1,128)} %scatter.19.row_ref), custom_call_target="tpu_custom_call" | custom-call | tf_op jit(solution)/shard_map/pallas_call | solution.py:165
  201.8 2.1 %multiply_subtract_fusion.1 = (f32[16,16,256]{2,1,0:T(8,128)}, f32[16,16,256]{2,1,0:T(8,128)}) fusion(f32[16,16,256]{2,1,0:T(8,128)S(1)} %get-tuple-element.58, f32[20,20,260]{2,1,0:T(8,128)} %get-tuple-element.64, f32[]{:T(128)S(6)} %div.42, f32[]{:T(128)S(6)} %div.43, f32[20,20,260]{2,1,0:T(8,128)S(1)} %copy-done.25, f32[16,16,256]{2,1,0:T(8,128)S(1)} %fusion.197, ...), kind=kLoop, calls=%fused_computation.325 | loop fusion | flops 589824 | bytes 1835020 | tf_op jit(solution)/shard_map/sub | solution.py:254
  (161 shorter events, 48.5 us)
Async XLA Ops:
  0.6 63.3 %copy-start = (f32[16,2048]{1,0:T(8,128)S(1)}, f32[16,2048]{1,0:T(8,128)}, u32[]{:S(2)}) copy-start(f32[16,2048]{1,0:T(8,128)} %param.19) | copy-start | bytes 393220
  1.7 67.9 %copy-start.17 = (f32[1,16,16,256]{3,2,1,0:T(8,128)}, f32[1,16,16,256]{3,2,1,0:T(8,128)S(1)}, u32[]{:S(2)}) copy-start(f32[1,16,16,256]{3,2,1,0:T(8,128)S(1)} %fusion.203) | copy-start | bytes 786436
  4.2 7.2 %collective-permute-start.1 = (f32[6,16,16,3]{2,1,3,0:T(8,128)S(1)}, f32[6,16,16,3]{2,1,3,0:T(8,128)S(1)}, u32[]{:S(2)}, u32[]{:S(2)}) collective-permute-start(f32[6,16,16,3]{2,1,3,0:T(8,128)S(1)} %copy.63), channel_id=1, source_target_pairs={{1,0},{2,1},{3,2},{5,4},{6,5},{7,6},{9,8},{10,9},{11,10},{13,12},{... | collective-permute-start | bytes 55304 | tf_op jit(solution)/shard_map/ppermute | solution.py:27
  6.2 6.7 %collective-permute-start = (f32[6,16,16,3]{2,1,3,0:T(8,128)S(1)}, f32[6,16,16,3]{2,1,3,0:T(8,128)}, u32[]{:S(2)}, u32[]{:S(2)}) collective-permute-start(f32[6,16,16,3]{2,1,3,0:T(8,128)S(1)} %copy.62), channel_id=1, source_target_pairs={{0,1},{1,2},{2,3},{4,5},{5,6},{6,7},{8,9},{9,10},{10,11},{12,13},{... | collective-permute-start | bytes 55304 | tf_op jit(solution)/shard_map/ppermute | solution.py:26
  12.1 57.5 %copy-start.8 = (f32[6,16,16,3]{3,2,1,0:T(8,128)}, f32[6,16,16,3]{3,2,1,0:T(8,128)S(1)}, u32[]{:S(2)}) copy-start(f32[6,16,16,3]{3,2,1,0:T(8,128)S(1)} %copy.47) | copy-start | bytes 55300
  14.4 55.2 %copy-start.10 = (f32[6,16,16,3]{3,2,1,0:T(8,128)}, f32[6,16,16,3]{3,2,1,0:T(8,128)S(1)}, u32[]{:S(2)}) copy-start(f32[6,16,16,3]{3,2,1,0:T(8,128)S(1)} %copy.46) | copy-start | bytes 55300
  14.8 11.3 %collective-permute-start.3 = (f32[6,3,16,262]{3,2,1,0:T(8,128)S(1)}, f32[6,3,16,262]{3,2,1,0:T(8,128)S(1)}, u32[]{:S(2)}, u32[]{:S(2)}) collective-permute-start(f32[6,3,16,262]{3,2,1,0:T(8,128)S(1)} %get-tuple-element.82), channel_id=1, source_target_pairs={{16,0},{32,16},{48,32},{64,48},{80,64},{96,80},{112,96},{17,1},{33... | collective-permute-start | bytes 905480 | tf_op jit(solution)/shard_map/ppermute | solution.py:27
  18.7 8.6 %collective-permute-start.2 = (f32[6,3,16,262]{3,2,1,0:T(8,128)S(1)}, f32[6,3,16,262]{3,2,1,0:T(8,128)S(1)}, u32[]{:S(2)}, u32[]{:S(2)}) collective-permute-start(f32[6,3,16,262]{3,2,1,0:T(8,128)S(1)} %get-tuple-element.81), channel_id=1, source_target_pairs={{0,16},{16,32},{32,48},{48,64},{64,80},{80,96},{96,112},{1,17},{17... | collective-permute-start | bytes 905480 | tf_op jit(solution)/shard_map/ppermute | solution.py:26
  30.6 36.3 %collective-permute-start.5 = (f32[6,22,3,262]{3,1,2,0:T(8,128)}, f32[6,22,3,262]{3,1,2,0:T(8,128)}, u32[]{:S(2)}, u32[]{:S(2)}) collective-permute-start(f32[6,22,3,262]{3,1,2,0:T(8,128)} %copy.65), channel_id=1, source_target_pairs={{4,0},{8,4},{12,8},{5,1},{9,5},{13,9},{6,2},{10,6},{14,10},{7,3},{... | collective-permute-start | bytes 1245032 | tf_op jit(solution)/shard_map/ppermute | solution.py:27
  33.0 35.3 %collective-permute-start.4 = (f32[6,22,3,262]{3,1,2,0:T(8,128)}, f32[6,22,3,262]{3,1,2,0:T(8,128)}, u32[]{:S(2)}, u32[]{:S(2)}) collective-permute-start(f32[6,22,3,262]{3,1,2,0:T(8,128)} %copy.64), channel_id=1, source_target_pairs={{0,4},{4,8},{8,12},{1,5},{5,9},{9,13},{2,6},{6,10},{10,14},{3,7},{... | collective-permute-start | bytes 1245032 | tf_op jit(solution)/shard_map/ppermute | solution.py:26
  86.1 7.7 %collective-permute-start.7 = (f32[16,16,3]{2,1,0:T(8,128)S(1)}, f32[16,16,3]{2,1,0:T(8,128)S(1)}, u32[]{:S(2)}, u32[]{:S(2)}) collective-permute-start(f32[16,16,3]{2,1,0:T(8,128)S(1)} %get-tuple-element.97), channel_id=1, source_target_pairs={{1,0},{2,1},{3,2},{5,4},{6,5},{7,6},{9,8},{10,9},{11,10},{13,12},{... | collective-permute-start | bytes 9224 | tf_op jit(solution)/shard_map/ppermute | solution.py:27
  87.4 7.3 %collective-permute-start.6 = (f32[16,16,3]{2,1,0:T(8,128)S(1)}, f32[16,16,3]{2,1,0:T(8,128)S(1)}, u32[]{:S(2)}, u32[]{:S(2)}) collective-permute-start(f32[16,16,3]{2,1,0:T(8,128)S(1)} %get-tuple-element.96), channel_id=1, source_target_pairs={{0,1},{1,2},{2,3},{4,5},{5,6},{6,7},{8,9},{9,10},{10,11},{12,13},{... | collective-permute-start | bytes 9224 | tf_op jit(solution)/shard_map/ppermute | solution.py:26
  96.1 6.5 %collective-permute-start.9 = (f32[3,16,262]{2,1,0:T(8,128)}, f32[3,16,262]{2,1,0:T(8,128)}, u32[]{:S(2)}, u32[]{:S(2)}) collective-permute-start(f32[3,16,262]{2,1,0:T(8,128)} %get-tuple-element.89), channel_id=1, source_target_pairs={{16,0},{32,16},{48,32},{64,48},{80,64},{96,80},{112,96},{17,1},{33... | collective-permute-start | bytes 150920 | tf_op jit(solution)/shard_map/ppermute | solution.py:27
  99.2 4.1 %collective-permute-start.8 = (f32[3,16,262]{2,1,0:T(8,128)}, f32[3,16,262]{2,1,0:T(8,128)}, u32[]{:S(2)}, u32[]{:S(2)}) collective-permute-start(f32[3,16,262]{2,1,0:T(8,128)} %get-tuple-element.88), channel_id=1, source_target_pairs={{0,16},{16,32},{32,48},{48,64},{64,80},{80,96},{96,112},{1,17},{17... | collective-permute-start | bytes 150920 | tf_op jit(solution)/shard_map/ppermute | solution.py:26
  104.9 6.8 %collective-permute-start.11 = (f32[22,3,262]{2,0,1:T(8,128)S(1)}, f32[22,3,262]{2,0,1:T(8,128)S(1)}, u32[]{:S(2)}, u32[]{:S(2)}) collective-permute-start(f32[22,3,262]{2,0,1:T(8,128)S(1)} %copy.67), channel_id=1, source_target_pairs={{4,0},{8,4},{12,8},{5,1},{9,5},{13,9},{6,2},{10,6},{14,10},{7,3},{... | collective-permute-start | bytes 207512 | tf_op jit(solution)/shard_map/ppermute | solution.py:27
  106.2 6.4 %collective-permute-start.10 = (f32[22,3,262]{2,0,1:T(8,128)S(1)}, f32[22,3,262]{2,0,1:T(8,128)S(1)}, u32[]{:S(2)}, u32[]{:S(2)}) collective-permute-start(f32[22,3,262]{2,0,1:T(8,128)S(1)} %copy.66), channel_id=1, source_target_pairs={{0,4},{4,8},{8,12},{1,5},{5,9},{9,13},{2,6},{6,10},{10,14},{3,7},{... | collective-permute-start | bytes 207512 | tf_op jit(solution)/shard_map/ppermute | solution.py:26
  154.6 20.4 %copy-start.16 = (f32[16,16,256]{2,1,0:T(8,128)S(1)}, f32[16,16,256]{2,1,0:T(8,128)}, u32[]{:S(2)}) copy-start(f32[16,16,256]{2,1,0:T(8,128)} %param.16) | copy-start | bytes 786436
  154.7 20.4 %copy-start.18 = (f32[1,16,16,256]{3,2,1,0:T(8,128)S(1)}, f32[1,16,16,256]{3,2,1,0:T(8,128)}, u32[]{:S(2)}) copy-start(f32[1,16,16,256]{3,2,1,0:T(8,128)} %copy-done.17) | copy-start | bytes 786436
  158.2 18.5 %copy-start.9 = (f32[6,16,16,3]{3,2,1,0:T(8,128)S(1)}, f32[6,16,16,3]{3,2,1,0:T(8,128)}, u32[]{:S(2)}) copy-start(f32[6,16,16,3]{3,2,1,0:T(8,128)} %copy-done.8) | copy-start | bytes 55300
  158.2 18.5 %copy-start.11 = (f32[6,16,16,3]{3,2,1,0:T(8,128)S(1)}, f32[6,16,16,3]{3,2,1,0:T(8,128)}, u32[]{:S(2)}) copy-start(f32[6,16,16,3]{3,2,1,0:T(8,128)} %copy-done.10) | copy-start | bytes 55300
  158.2 18.5 %copy-start.14 = (f32[16,16,256]{2,1,0:T(8,128)S(1)}, f32[16,16,256]{2,1,0:T(8,128)}, u32[]{:S(2)}) copy-start(f32[16,16,256]{2,1,0:T(8,128)} %param.14) | copy-start | bytes 786436
  158.2 18.5 %copy-start.23 = (f32[6,22,3,262]{3,2,1,0:T(4,128)S(1)}, f32[6,22,3,262]{3,2,1,0:T(4,128)}, u32[]{:S(2)}) copy-start(f32[6,22,3,262]{3,2,1,0:T(4,128)} %copy-done.22) | copy-start | bytes 1245028
  158.2 18.5 %copy-start.25 = (f32[20,20,260]{2,1,0:T(8,128)S(1)}, f32[20,20,260]{2,1,0:T(8,128)}, u32[]{:S(2)}) copy-start(f32[20,20,260]{2,1,0:T(8,128)} %copy-done.24) | copy-start | bytes 1248004
  158.2 18.5 %copy-start.28 = (f32[6,3,16,262]{3,2,1,0:T(8,128)S(1)}, f32[6,3,16,262]{3,2,1,0:T(8,128)}, u32[]{:S(2)}) copy-start(f32[6,3,16,262]{3,2,1,0:T(8,128)} %copy-done.26) | copy-start | bytes 905476
  158.2 18.5 %copy-start.31 = (f32[6,3,16,262]{3,2,1,0:T(8,128)S(1)}, f32[6,3,16,262]{3,2,1,0:T(8,128)}, u32[]{:S(2)}) copy-start(f32[6,3,16,262]{3,2,1,0:T(8,128)} %copy-done.29) | copy-start | bytes 905476
  158.2 18.5 %copy-start.37 = (s32[16,16,256]{2,1,0:T(8,128)S(1)}, s32[16,16,256]{2,1,0:T(8,128)}, u32[]{:S(2)}) copy-start(s32[16,16,256]{2,1,0:T(8,128)} %param.17) | copy-start | bytes 786436
  158.3 14.3 %collective-permute-start.16 = (f32[16,1,256]{2,0,1:T(8,128)S(1)}, f32[16,1,256]{2,0,1:T(8,128)S(1)}, u32[]{:S(2)}, u32[]{:S(2)}) collective-permute-start(f32[16,1,256]{2,0,1:T(8,128)S(1)} %copy.57), channel_id=1, source_target_pairs={{4,0},{8,4},{12,8},{5,1},{9,5},{13,9},{6,2},{10,6},{14,10},{7,3},{... | collective-permute-start | bytes 49160 | tf_op jit(solution)/shard_map/ppermute | solution.py:90
  159.9 16.1 %collective-permute-start.17 = (f32[16,16,1]{2,1,0:T(8,128)S(1)}, f32[16,16,1]{2,1,0:T(8,128)S(1)}, u32[]{:S(2)}, u32[]{:S(2)}) collective-permute-start(f32[16,16,1]{2,1,0:T(8,128)S(1)} %get-tuple-element.93), channel_id=1, source_target_pairs={{1,0},{2,1},{3,2},{5,4},{6,5},{7,6},{9,8},{10,9},{11,10},{13,12},{... | collective-permute-start | bytes 3080 | tf_op jit(solution)/shard_map/ppermute | solution.py:90
  161.2 14.8 %collective-permute-start.13 = (f32[16,1,256]{2,0,1:T(8,128)S(1)}, f32[16,1,256]{2,0,1:T(8,128)S(1)}, u32[]{:S(2)}, u32[]{:S(2)}) collective-permute-start(f32[16,1,256]{2,0,1:T(8,128)S(1)} %copy.56), channel_id=1, source_target_pairs={{0,4},{4,8},{8,12},{1,5},{5,9},{9,13},{2,6},{6,10},{10,14},{3,7},{... | collective-permute-start | bytes 49160 | tf_op jit(solution)/shard_map/ppermute | solution.py:89
  165.2 10.8 %collective-permute-start.12 = (f32[16,16,1]{2,1,0:T(8,128)S(1)}, f32[16,16,1]{2,1,0:T(8,128)S(1)}, u32[]{:S(2)}, u32[]{:S(2)}) collective-permute-start(f32[16,16,1]{2,1,0:T(8,128)S(1)} %get-tuple-element.92), channel_id=1, source_target_pairs={{0,1},{1,2},{2,3},{4,5},{5,6},{6,7},{8,9},{9,10},{10,11},{12,13},{... | collective-permute-start | bytes 3080 | tf_op jit(solution)/shard_map/ppermute | solution.py:89
  169.2 6.8 %collective-permute-start.15 = (f32[1,16,256]{2,1,0:T(8,128)S(1)}, f32[1,16,256]{2,1,0:T(8,128)S(1)}, u32[]{:S(2)}, u32[]{:S(2)}) collective-permute-start(f32[1,16,256]{2,1,0:T(8,128)S(1)} %get-tuple-element.91), channel_id=1, source_target_pairs={{16,0},{32,16},{48,32},{64,48},{80,64},{96,80},{112,96},{17,1},{33... | collective-permute-start | bytes 49160 | tf_op jit(solution)/shard_map/ppermute | solution.py:90
  172.6 3.4 %collective-permute-start.14 = (f32[1,16,256]{2,1,0:T(8,128)S(1)}, f32[1,16,256]{2,1,0:T(8,128)S(1)}, u32[]{:S(2)}, u32[]{:S(2)}) collective-permute-start(f32[1,16,256]{2,1,0:T(8,128)S(1)} %get-tuple-element.90), channel_id=1, source_target_pairs={{0,16},{16,32},{32,48},{48,64},{64,80},{80,96},{96,112},{1,17},{17... | collective-permute-start | bytes 49160 | tf_op jit(solution)/shard_map/ppermute | solution.py:89
  (27 other events, 151.3 us)

commit v10 on v9

--- a/solution.py
+++ b/solution.py
@@ -216,7 +216,7 @@
         return jacobi(rhs_box, box_cond, box_diag, storage_box, free_box)[2:-2, 2:-2, 2:-2]
 
     def precondition(rhs_box, residual, coarse_all):
-        weights = jnp.dot(coarse_inverse, coarse_all, precision=lax.Precision.HIGHEST)
+        weights = jnp.sum(coarse_inverse * coarse_all[None], axis=1)
         return schwarz(rhs_box) + expand(basis, weights, residual)
 
     residual0 = right_side

time: 205 us -> 206 us (level)
  waiting for transfers between devices: 10.1 us -> 27 us
  starting transfers between devices: 53.8 us -> 45 us
  Pallas kernels: 55.5 us -> 51.2 us
  local copies, waits for them, and re-layouts: 17.7 us -> 15.1 us
    ppermute x6, waiting for transfers between devices: 5.64 us -> 19.5 us  [padded(): after = lax.ppermute(leading, axis, down)]
    pallas_call x3, Pallas kernels: 55.5 us -> 51.2 us  [gather_rows(): pl.pallas_call(functools.partial(gather_kernel, sizes), out_shape=jax.Sha...]
    ppermute x6, starting transfers between devices: 12.3 us -> 9 us  [padded(): after = lax.ppermute(leading, axis, down)]
    ppermute x3, waiting for transfers between devices: 0.01 us -> 2.17 us  [faces(): after = lax.ppermute(lax.slice_in_dim(field, 0, 1, axis=dim), axis, down)]
    unnamed x90 -> x76, local copies, waits for them, and re-layouts: 4.58 us -> 3.95 us
  transfers between devices with their start and end apart: 18 -> 18, of which waited for: 7 -> 10; matrix products, arithmetic and copies ran while one was open for 6% -> 5% of each run, Pallas kernels for 12% -> 11%
where the time goes in v10:
time: 206 us; the launch traced here: 205 us
  other arithmetic  59.3 us (29%)
  Pallas kernels  51.2 us (25%)
  starting transfers between devices  45 us (22%)
  waiting for transfers between devices  27 us (13%)
  local copies, waits for them, and re-layouts  15.1 us (7%)
  between operations  7.35 us (4%)
    pallas_call x3, Pallas kernels, gather_rows(): pl.pallas_call(functools.partial(gather_kernel, sizes), out_shape=jax.Sha...  51.2 us
    ppermute x6, starting transfers between devices, padded(): before = lax.ppermute(last, axis, up)  23.1 us
    ppermute x6, waiting for transfers between devices, padded(): after = lax.ppermute(leading, axis, down)  19.5 us
    mul x7, other arithmetic, jacobi(): free_box * guess  15.7 us
    ppermute x6, starting transfers between devices, padded(): after = lax.ppermute(leading, axis, down)  9 us
    ppermute x3, starting transfers between devices, faces(): lax.ppermute(lax.slice_in_dim(field, length - 1, length, axis=dim), axis,...  8.4 us
    concatenate x2, other arithmetic, padded(): value = jnp.concatenate([before, value, after], axis=dim)  7.86 us
    reduce_sum x2, other arithmetic, expand(): return jnp.sum(weights[:, None, None, None] * basis, axis=0)  5.67 us
  transfers between devices with their start and end apart: 18, of which 10 were waited for; matrix products, arithmetic and copies ran while one was open for 5% of the time, Pallas kernels for 11%

profile of v10, /device:TPU:1, one launch (start us, length us, event | category | flops | bytes accessed | tf_op | source)
XLA Modules:
  0.0 204.8 jit_solution(13446109717032393978)
XLA Ops:
  4.1 4.0 %collective-permute-start = (f32[6,16,16,3]{2,1,3,0:T(8,128)S(1)}, f32[6,16,16,3]{2,1,3,0:T(8,128)S(1)}, u32[]{:S(2)}, u32[]{:S(2)}) collective-permute-start(f32[6,16,16,3]{2,1,3,0:T(8,128)S(1)} %copy.62), channel_id=1, source_target_pairs={{0,1},{1,2},{2,3},{4,5},{5,6},{6,7},{8,9},{9,10},{10,11},{12,13},{... | collective-permute-start | bytes 55304 | tf_op jit(solution)/shard_map/ppermute | solution.py:26
  11.2 3.8 %collective-permute-done.1 = f32[6,16,16,3]{2,1,3,0:T(8,128)S(1)} collective-permute-done((f32[6,16,16,3]{2,1,3,0:T(8,128)S(1)}, f32[6,16,16,3]{2,1,3,0:T(8,128)S(1)}, u32[]{:S(2)}, u32[]{:S(2)}) %collective-permute-start.1) | collective-permute-done | bytes 18464 | tf_op jit(solution)/shard_map/ppermute | solution.py:27
  16.1 5.0 %collective-permute-start.2 = (f32[6,3,16,262]{3,2,1,0:T(8,128)S(1)}, f32[6,3,16,262]{3,2,1,0:T(8,128)S(1)}, u32[]{:S(2)}, u32[]{:S(2)}) collective-permute-start(f32[6,3,16,262]{3,2,1,0:T(8,128)S(1)} %get-tuple-element.81), channel_id=1, source_target_pairs={{0,16},{16,32},{32,48},{48,64},{64,80},{80,96},{96,112},{1,17},{17... | collective-permute-start | bytes 905480 | tf_op jit(solution)/shard_map/ppermute | solution.py:26
  23.0 3.3 %collective-permute-done.2 = f32[6,3,16,262]{3,2,1,0:T(8,128)S(1)} collective-permute-done((f32[6,3,16,262]{3,2,1,0:T(8,128)S(1)}, f32[6,3,16,262]{3,2,1,0:T(8,128)S(1)}, u32[]{:S(2)}, u32[]{:S(2)}) %collective-permute-start.2) | collective-permute-done | bytes 301856 | tf_op jit(solution)/shard_map/ppermute | solution.py:26
  26.3 4.4 %collective-permute-done.3 = f32[6,3,16,262]{3,2,1,0:T(8,128)S(1)} collective-permute-done((f32[6,3,16,262]{3,2,1,0:T(8,128)S(1)}, f32[6,3,16,262]{3,2,1,0:T(8,128)S(1)}, u32[]{:S(2)}, u32[]{:S(2)}) %collective-permute-start.3) | collective-permute-done | bytes 301856 | tf_op jit(solution)/shard_map/ppermute | solution.py:27
  30.7 2.2 %pad_maximum_fusion.2 = f32[6,22,16,262]{3,2,1,0:T(8,128)S(1)} fusion(f32[6,3,16,262]{3,2,1,0:T(8,128)S(1)} %collective-permute-done.3, f32[6,16,16,3]{3,2,1,0:T(8,128)S(1)} %copy.47, f32[1,16,16,256]{3,2,1,0:T(8,128)S(1)} %bitcast.297, f32[1,16,16,256]{3,2,1,0:T(8,128)S(1)} %fusion.203, f32[1,16,16,256]{3,2,1,0:T(8,128)S(1)} %bitcast.302, ...), kind=kLoop, calls=%fused_computation.6 | loop fusion | flops 3873408 | bytes 4426752 | tf_op jit(solution)/shard_map/concatenate | solution.py:28
  34.1 4.5 %collective-permute-start.4 = (f32[6,22,3,262]{3,1,2,0:T(8,128)}, f32[6,22,3,262]{3,1,2,0:T(8,128)}, u32[]{:S(2)}, u32[]{:S(2)}) collective-permute-start(f32[6,22,3,262]{3,1,2,0:T(8,128)} %copy.64), channel_id=1, source_target_pairs={{0,4},{4,8},{8,12},{1,5},{5,9},{9,13},{2,6},{6,10},{10,14},{3,7},{... | collective-permute-start | bytes 1245032 | tf_op jit(solution)/shard_map/ppermute | solution.py:26
  41.9 22.0 %shard_map.77 = f32[128,1,128]{2,1,0:T(1,128)} custom-call(f32[1,1,128]{2,1,0:T(1,128)} %scatter.14.row_ref), custom_call_target="tpu_custom_call" | custom-call | tf_op jit(solution)/shard_map/pallas_call | solution.py:165
  65.0 2.9 %multiply_reduce_fusion.2 = f32[16,16,256]{2,1,0:T(8,128)S(1)} fusion(f32[16,16,16,256]{3,2,1,0:T(8,128)} %param.18, f32[16]{0:T(128)S(1)} %multiply_reduce_fusion.11), kind=kLoop, calls=%fused_computation.4 | loop fusion | flops 2031616 | bytes 4456512 | tf_op jit(solution)/shard_map/reduce_sum | solution.py:77
  70.9 5.7 %pad_maximum_fusion = f32[6,22,22,262]{3,2,1,0:T(8,128)S(1)} fusion(f32[6,22,3,262]{3,2,1,0:T(4,128)S(1)} %copy.51, f32[6,3,16,262]{3,2,1,0:T(8,128)S(1)} %copy-done.26, f32[6,16,16,3]{3,2,1,0:T(8,128)S(1)} %copy.47, f32[1,16,16,256]{3,2,1,0:T(8,128)S(1)} %bitcast.298, f32[1,16,16,256]{3,2,1,0:T(8,128)S(1)} %fusion.203, f32[1,16,16,256]{3,2,1,0:T(8,128)S(1)} %bitcast.303, ...), kind=kLoop, calls=%fused_computation | loop fusion | flops 6847632 | bytes 6086784 | tf_op jit(solution)/shard_map/concatenate | solution.py:28
  78.2 2.4 %fusion.204 = (f32[20,20,260]{2,1,0:T(8,128)S(1)}, f32[20,20,260]{2,1,0:T(8,128)S(1)}, f32[20,20,260]{2,1,0:T(8,128)S(1)}, f32[20,20,260]{2,1,0:T(8,128)S(1)}) fusion(f32[6,22,22,262]{3,2,1,0:T(8,128)S(1)} %pad_maximum_fusion, f32[20,20,260]{2,1,0:T(8,128)S(1)} %broadcast_multiply_fusion, f32[3,20,20,260]{3,2,1,0:T(8,128)S(1)} %slice.612), kind=kLoop, calls=%fused_computation.333 | loop fusion | flops 3640000 | bytes 5824000 | tf_op jit(solution)/shard_map/mul | solution.py:67
  80.7 2.3 %fusion.210 = (f32[20,20,260]{2,1,0:T(8,128)S(1)}, f32[20,20,260]{2,1,0:T(8,128)S(1)}) fusion(f32[6,22,22,262]{3,2,1,0:T(8,128)S(1)} %pad_maximum_fusion, f32[20,20,260]{2,1,0:T(8,128)S(1)} %get-tuple-element.73, f32[20,20,260]{2,1,0:T(8,128)S(1)} %get-tuple-element.71, f32[3,20,20,260]{3,2,1,0:T(8,128)S(1)} %slice.612, f32[20,20,260]{2,1,0:T(8,128)S(1)} %get-tuple-element.72), kind=kLoop, calls=%fused_computation.355 | loop fusion | flops 3224000 | bytes 5824000 | tf_op jit(solution)/shard_map/mul | solution.py:67
  87.3 3.1 %collective-permute-start.6 = (f32[16,16,3]{2,1,0:T(8,128)S(1)}, f32[16,16,3]{2,1,0:T(8,128)S(1)}, u32[]{:S(2)}, u32[]{:S(2)}) collective-permute-start(f32[16,16,3]{2,1,0:T(8,128)S(1)} %get-tuple-element.96), channel_id=1, source_target_pairs={{0,1},{1,2},{2,3},{4,5},{5,6},{6,7},{8,9},{9,10},{10,11},{12,13},{... | collective-permute-start | bytes 9224 | tf_op jit(solution)/shard_map/ppermute | solution.py:26
  92.8 3.8 %collective-permute-done.7 = f32[16,16,3]{2,1,0:T(8,128)S(1)} collective-permute-done((f32[16,16,3]{2,1,0:T(8,128)S(1)}, f32[16,16,3]{2,1,0:T(8,128)S(1)}, u32[]{:S(2)}, u32[]{:S(2)}) %collective-permute-start.7) | collective-permute-done | bytes 3104 | tf_op jit(solution)/shard_map/ppermute | solution.py:27
  96.8 2.8 %collective-permute-start.8 = (f32[3,16,262]{2,1,0:T(8,128)S(1)}, f32[3,16,262]{2,1,0:T(8,128)S(1)}, u32[]{:S(2)}, u32[]{:S(2)}) collective-permute-start(f32[3,16,262]{2,1,0:T(8,128)S(1)} %get-tuple-element.88), channel_id=1, source_target_pairs={{0,16},{16,32},{32,48},{48,64},{64,80},{80,96},{96,112},{1,17},{17... | collective-permute-start | bytes 150920 | tf_op jit(solution)/shard_map/ppermute | solution.py:26
  101.6 3.7 %collective-permute-done.9 = f32[3,16,262]{2,1,0:T(8,128)S(1)} collective-permute-done((f32[3,16,262]{2,1,0:T(8,128)S(1)}, f32[3,16,262]{2,1,0:T(8,128)S(1)}, u32[]{:S(2)}, u32[]{:S(2)}) %collective-permute-start.9) | collective-permute-done | bytes 50336 | tf_op jit(solution)/shard_map/ppermute | solution.py:27
  105.5 3.7 %collective-permute-start.10 = (f32[22,3,262]{2,0,1:T(8,128)S(1)}, f32[22,3,262]{2,0,1:T(8,128)S(1)}, u32[]{:S(2)}, u32[]{:S(2)}) collective-permute-start(f32[22,3,262]{2,0,1:T(8,128)S(1)} %copy.66), channel_id=1, source_target_pairs={{0,4},{4,8},{8,12},{1,5},{5,9},{9,13},{2,6},{6,10},{10,14},{3,7},{... | collective-permute-start | bytes 207512 | tf_op jit(solution)/shard_map/ppermute | solution.py:26
  111.0 3.7 %collective-permute-done.11 = f32[22,3,262]{2,0,1:T(8,128)S(1)} collective-permute-done((f32[22,3,262]{2,0,1:T(8,128)S(1)}, f32[22,3,262]{2,0,1:T(8,128)S(1)}, u32[]{:S(2)}, u32[]{:S(2)}) %collective-permute-start.11) | collective-permute-done | bytes 69200 | tf_op jit(solution)/shard_map/ppermute | solution.py:27
  115.1 3.0 %fusion.159 = f32[20,20,260]{2,1,0:T(8,128)S(1)} fusion(f32[22,22,262]{2,1,0:T(8,128)S(1)} %get-tuple-element.66, f32[22,22,262]{2,1,0:T(8,128)S(1)} %get-tuple-element.65, f32[6,22,22,262]{3,2,1,0:T(8,128)S(1)} %pad_maximum_fusion, f32[22,22,262]{2,1,0:T(8,128)S(1)} %get-tuple-element.75, f32[22,22,262]{2,1,0:T(8,128)S(1)} %get-tuple-element.74), kind=kLoop, calls=%fused_computation.218 | loop fusion | flops 2392000 | bytes 7072000 | tf_op jit(solution)/shard_map/add | solution.py:54
  121.6 13.4 %shard_map.78 = f32[128,1,128]{2,1,0:T(1,128)} custom-call(f32[1,1,128]{2,1,0:T(1,128)} %copy-done.33), custom_call_target="tpu_custom_call" | custom-call | tf_op jit(solution)/shard_map/pallas_call | solution.py:165
  137.9 2.7 %fusion.205 = (f32[20,20,260]{2,1,0:T(8,128)S(1)}, f32[20,20,260]{2,1,0:T(8,128)S(1)}) fusion(f32[20,20,260]{2,1,0:T(8,128)} %copy-done.5, f32[20,20,260]{2,1,0:T(8,128)} %copy-done.18, f32[6,22,22,262]{3,2,1,0:T(8,128)} %copy-done, f32[20,20,260]{2,1,0:T(8,128)} %copy-done.21, f32[]{:T(128)S(6)} %div.37), kind=kLoop, calls=%fused_computation.334 | loop fusion | flops 624000 | bytes 2912004 | tf_op jit(solution)/shard_map/mul | solution.py:67
  141.4 3.3 %fusion.208 = (f32[20,20,260]{2,1,0:T(8,128)S(1)}, f32[20,20,260]{2,1,0:T(8,128)S(1)}) fusion(f32[6,22,22,262]{3,2,1,0:T(8,128)S(1)} %copy-done.1, f32[20,20,260]{2,1,0:T(8,128)} %copy-done.5, f32[20,20,260]{2,1,0:T(8,128)S(1)} %get-tuple-element.64, f32[20,20,260]{2,1,0:T(8,128)S(1)} %get-tuple-element.63, f32[3,20,20,260]{3,2,1,0:T(8,128)S(1)} %slice.612, ...), kind=kLoop, calls=%fused_computation.353 | loop fusion | flops 3224000 | bytes 5824000 | tf_op jit(solution)/shard_map/mul | solution.py:67
  144.7 2.7 %fusion.207 = (f32[20,20,260]{2,1,0:T(8,128)S(1)}, f32[20,20,260]{2,1,0:T(8,128)}) fusion(f32[6,22,22,262]{3,2,1,0:T(8,128)S(1)} %copy-done.1, f32[20,20,260]{2,1,0:T(8,128)S(1)} %get-tuple-element.62, f32[20,20,260]{2,1,0:T(8,128)S(1)} %copy-done.6, f32[20,20,260]{2,1,0:T(8,128)S(1)} %get-tuple-element.64, f32[20,20,260]{2,1,0:T(8,128)S(1)} %get-tuple-element.61, ...), kind=kLoop, calls=%fused_computation.352 | loop fusion | flops 2912000 | bytes 5824000 | tf_op jit(solution)/shard_map/mul | solution.py:67
  147.5 2.4 %fusion.145 = f32[20,20,260]{2,1,0:T(8,128)} fusion(f32[20,20,260]{2,1,0:T(8,128)S(1)} %get-tuple-element.59, f32[6,22,22,262]{3,2,1,0:T(8,128)S(1)} %copy-done.1, f32[3,20,20,260]{3,2,1,0:T(8,128)S(1)} %slice.612), kind=kLoop, calls=%fused_computation.203 | loop fusion | flops 1976000 | bytes 3744000 | tf_op jit(solution)/shard_map/add | solution.py:50
  151.9 2.8 %multiply_reduce_fusion = f32[16,16,256]{2,1,0:T(8,128)S(1)} fusion(f32[16,16,16,256]{3,2,1,0:T(8,128)} %param.18, f32[16]{0:T(128)S(1)} %multiply_reduce_fusion.10), kind=kLoop, calls=%fused_computation.2 | loop fusion | flops 2031616 | bytes 4456512 | tf_op jit(solution)/shard_map/reduce_sum | solution.py:77
  154.7 2.3 %fusion.197 = f32[16,16,256]{2,1,0:T(8,128)S(1)} fusion(f32[16,16,256]{2,1,0:T(8,128)S(1)} %multiply_reduce_fusion, f32[20,20,260]{2,1,0:T(8,128)} %fusion.145, f32[20,20,260]{2,1,0:T(8,128)} %get-tuple-element.60, f32[20,20,260]{2,1,0:T(8,128)} %copy-done.5, f32[20,20,260]{2,1,0:T(8,128)} %copy-done.29, f32[20,20,260]{2,1,0:T(8,128)} %copy-done.28, ...), kind=kLoop, calls=%fused_computation.315 | loop fusion | flops 524288 | bytes 2097152 | tf_op jit(solution)/shard_map/add | solution.py:220
  157.2 2.6 %collective-permute-start.13 = (f32[16,1,256]{2,0,1:T(8,128)S(1)}, f32[16,1,256]{2,0,1:T(8,128)S(1)}, u32[]{:S(2)}, u32[]{:S(2)}) collective-permute-start(f32[16,1,256]{2,0,1:T(8,128)S(1)} %copy.56), channel_id=1, source_target_pairs={{0,4},{4,8},{8,12},{1,5},{5,9},{9,13},{2,6},{6,10},{10,14},{3,7},{... | collective-permute-start | bytes 49160 | tf_op jit(solution)/shard_map/ppermute | solution.py:89
  159.8 2.5 %collective-permute-start.12 = (f32[16,16,1]{2,1,0:T(8,128)S(1)}, f32[16,16,1]{2,1,0:T(8,128)S(1)}, u32[]{:S(2)}, u32[]{:S(2)}) collective-permute-start(f32[16,16,1]{2,1,0:T(8,128)S(1)} %get-tuple-element.92), channel_id=1, source_target_pairs={{0,1},{1,2},{2,3},{4,5},{5,6},{6,7},{8,9},{9,10},{10,11},{12,13},{... | collective-permute-start | bytes 3080 | tf_op jit(solution)/shard_map/ppermute | solution.py:89
  165.0 3.3 %collective-permute-start.14 = (f32[1,16,256]{2,1,0:T(8,128)S(1)}, f32[1,16,256]{2,1,0:T(8,128)S(1)}, u32[]{:S(2)}, u32[]{:S(2)}) collective-permute-start(f32[1,16,256]{2,1,0:T(8,128)S(1)} %get-tuple-element.90), channel_id=1, source_target_pairs={{0,16},{16,32},{32,48},{48,64},{64,80},{80,96},{96,112},{1,17},{17... | collective-permute-start | bytes 49160 | tf_op jit(solution)/shard_map/ppermute | solution.py:89
  175.1 2.7 %multiply_reduce_fusion.7 = (f32[]{:T(128)}, f32[]{:T(128)}, f32[]{:T(128)}, f32[]{:T(128)}, f32[16,16,256]{2,1,0:T(8,128)S(1)}) fusion(f32[16,16,256]{2,1,0:T(8,128)S(1)} %fusion.197, f32[20,20,260]{2,1,0:T(8,128)S(1)} %copy-done.17, f32[20,20,260]{2,1,0:T(8,128)} %copy-done.21, f32[16,16,256]{2,1,0:T(8,128)S(1)} %fusion.201, ...), kind=kLoop, calls=%fused_computation.328 | loop fusion | flops 3211260 | bytes 9560080 | tf_op jit(solution)/shard_map/reduce_sum | solution.py:242
  177.8 2.7 %maximum_bitcast_fusion.1 = f32[1,1,4]{2,1,0:T(1,128)S(1)} fusion(f32[1]{0:T(128)} %bitcast.36, f32[1]{0:T(128)} %bitcast.35, f32[1]{0:T(128)} %bitcast.34, f32[1]{0:T(128)} %bitcast.26), kind=kLoop, calls=%fused_computation.349 | loop fusion | flops 12 | bytes 32 | tf_op jit(solution)/shard_map/broadcast_in_dim;broadcast_in_dim | solution.py:164
  181.0 15.8 %shard_map.79 = f32[128,1,128]{2,1,0:T(1,128)} custom-call(f32[1,1,128]{2,1,0:T(1,128)} %scatter.19.row_ref), custom_call_target="tpu_custom_call" | custom-call | tf_op jit(solution)/shard_map/pallas_call | solution.py:165
  (145 shorter events, 52.1 us)
Async XLA Ops:
  1.6 69.2 %copy-start.14 = (f32[1,16,16,256]{3,2,1,0:T(8,128)}, f32[1,16,16,256]{3,2,1,0:T(8,128)S(1)}, u32[]{:S(2)}) copy-start(f32[1,16,16,256]{3,2,1,0:T(8,128)S(1)} %fusion.203) | copy-start | bytes 786436
  3.1 12.6 %copy-start.4 = (f32[3,16,16,256]{3,2,1,0:T(8,128)S(1)}, f32[3,16,16,256]{3,2,1,0:T(8,128)}, u32[]{:S(2)}) copy-start(f32[3,16,16,256]{3,2,1,0:T(8,128)} %param.15) | copy-start | bytes 2359300
  4.1 6.5 %collective-permute-start = (f32[6,16,16,3]{2,1,3,0:T(8,128)S(1)}, f32[6,16,16,3]{2,1,3,0:T(8,128)S(1)}, u32[]{:S(2)}, u32[]{:S(2)}) collective-permute-start(f32[6,16,16,3]{2,1,3,0:T(8,128)S(1)} %copy.62), channel_id=1, source_target_pairs={{0,1},{1,2},{2,3},{4,5},{5,6},{6,7},{8,9},{9,10},{10,11},{12,13},{... | collective-permute-start | bytes 55304 | tf_op jit(solution)/shard_map/ppermute | solution.py:26
  8.8 6.3 %collective-permute-start.1 = (f32[6,16,16,3]{2,1,3,0:T(8,128)S(1)}, f32[6,16,16,3]{2,1,3,0:T(8,128)S(1)}, u32[]{:S(2)}, u32[]{:S(2)}) collective-permute-start(f32[6,16,16,3]{2,1,3,0:T(8,128)S(1)} %copy.63), channel_id=1, source_target_pairs={{1,0},{2,1},{3,2},{5,4},{6,5},{7,6},{9,8},{10,9},{11,10},{13,12},{... | collective-permute-start | bytes 55304 | tf_op jit(solution)/shard_map/ppermute | solution.py:27
  11.2 59.6 %copy-start.7 = (f32[6,16,16,3]{3,2,1,0:T(8,128)}, f32[6,16,16,3]{3,2,1,0:T(8,128)S(1)}, u32[]{:S(2)}) copy-start(f32[6,16,16,3]{3,2,1,0:T(8,128)S(1)} %copy.46) | copy-start | bytes 55300
  15.7 55.1 %copy-start.9 = (f32[6,16,16,3]{3,2,1,0:T(8,128)}, f32[6,16,16,3]{3,2,1,0:T(8,128)S(1)}, u32[]{:S(2)}) copy-start(f32[6,16,16,3]{3,2,1,0:T(8,128)S(1)} %copy.47) | copy-start | bytes 55300
  16.1 10.2 %collective-permute-start.2 = (f32[6,3,16,262]{3,2,1,0:T(8,128)S(1)}, f32[6,3,16,262]{3,2,1,0:T(8,128)S(1)}, u32[]{:S(2)}, u32[]{:S(2)}) collective-permute-start(f32[6,3,16,262]{3,2,1,0:T(8,128)S(1)} %get-tuple-element.81), channel_id=1, source_target_pairs={{0,16},{16,32},{32,48},{48,64},{64,80},{80,96},{96,112},{1,17},{17... | collective-permute-start | bytes 905480 | tf_op jit(solution)/shard_map/ppermute | solution.py:26
  21.1 9.6 %collective-permute-start.3 = (f32[6,3,16,262]{3,2,1,0:T(8,128)S(1)}, f32[6,3,16,262]{3,2,1,0:T(8,128)S(1)}, u32[]{:S(2)}, u32[]{:S(2)}) collective-permute-start(f32[6,3,16,262]{3,2,1,0:T(8,128)S(1)} %get-tuple-element.82), channel_id=1, source_target_pairs={{16,0},{32,16},{48,32},{64,48},{80,64},{96,80},{112,96},{17,1},{33... | collective-permute-start | bytes 905480 | tf_op jit(solution)/shard_map/ppermute | solution.py:27
  33.2 31.6 %copy-start.32 = (f32[16,2048]{1,0:T(8,128)S(1)}, f32[16,2048]{1,0:T(8,128)}, u32[]{:S(2)}) copy-start(f32[16,2048]{1,0:T(8,128)} %param.19) | copy-start | bytes 393220
  34.1 33.8 %collective-permute-start.4 = (f32[6,22,3,262]{3,1,2,0:T(8,128)}, f32[6,22,3,262]{3,1,2,0:T(8,128)}, u32[]{:S(2)}, u32[]{:S(2)}) collective-permute-start(f32[6,22,3,262]{3,1,2,0:T(8,128)} %copy.64), channel_id=1, source_target_pairs={{0,4},{4,8},{8,12},{1,5},{5,9},{9,13},{2,6},{6,10},{10,14},{3,7},{... | collective-permute-start | bytes 1245032 | tf_op jit(solution)/shard_map/ppermute | solution.py:26
  39.5 29.7 %collective-permute-start.5 = (f32[6,22,3,262]{3,1,2,0:T(8,128)}, f32[6,22,3,262]{3,1,2,0:T(8,128)}, u32[]{:S(2)}, u32[]{:S(2)}) collective-permute-start(f32[6,22,3,262]{3,1,2,0:T(8,128)} %copy.65), channel_id=1, source_target_pairs={{4,0},{8,4},{12,8},{5,1},{9,5},{13,9},{6,2},{10,6},{14,10},{7,3},{... | collective-permute-start | bytes 1245032 | tf_op jit(solution)/shard_map/ppermute | solution.py:27
  76.5 38.5 %copy-start = (f32[6,22,22,262]{3,2,1,0:T(8,128)}, f32[6,22,22,262]{3,2,1,0:T(8,128)S(1)}, u32[]{:S(2)}) copy-start(f32[6,22,22,262]{3,2,1,0:T(8,128)S(1)} %pad_maximum_fusion) | copy-start | bytes 9130180
  87.3 5.6 %collective-permute-start.6 = (f32[16,16,3]{2,1,0:T(8,128)S(1)}, f32[16,16,3]{2,1,0:T(8,128)S(1)}, u32[]{:S(2)}, u32[]{:S(2)}) collective-permute-start(f32[16,16,3]{2,1,0:T(8,128)S(1)} %get-tuple-element.96), channel_id=1, source_target_pairs={{0,1},{1,2},{2,3},{4,5},{5,6},{6,7},{8,9},{9,10},{10,11},{12,13},{... | collective-permute-start | bytes 9224 | tf_op jit(solution)/shard_map/ppermute | solution.py:26
  90.4 6.3 %collective-permute-start.7 = (f32[16,16,3]{2,1,0:T(8,128)S(1)}, f32[16,16,3]{2,1,0:T(8,128)S(1)}, u32[]{:S(2)}, u32[]{:S(2)}) collective-permute-start(f32[16,16,3]{2,1,0:T(8,128)S(1)} %get-tuple-element.97), channel_id=1, source_target_pairs={{1,0},{2,1},{3,2},{5,4},{6,5},{7,6},{9,8},{10,9},{11,10},{13,12},{... | collective-permute-start | bytes 9224 | tf_op jit(solution)/shard_map/ppermute | solution.py:27
  96.8 4.8 %collective-permute-start.8 = (f32[3,16,262]{2,1,0:T(8,128)S(1)}, f32[3,16,262]{2,1,0:T(8,128)S(1)}, u32[]{:S(2)}, u32[]{:S(2)}) collective-permute-start(f32[3,16,262]{2,1,0:T(8,128)S(1)} %get-tuple-element.88), channel_id=1, source_target_pairs={{0,16},{16,32},{32,48},{48,64},{64,80},{80,96},{96,112},{1,17},{17... | collective-permute-start | bytes 150920 | tf_op jit(solution)/shard_map/ppermute | solution.py:26
  99.6 5.7 %collective-permute-start.9 = (f32[3,16,262]{2,1,0:T(8,128)S(1)}, f32[3,16,262]{2,1,0:T(8,128)S(1)}, u32[]{:S(2)}, u32[]{:S(2)}) collective-permute-start(f32[3,16,262]{2,1,0:T(8,128)S(1)} %get-tuple-element.89), channel_id=1, source_target_pairs={{16,0},{32,16},{48,32},{64,48},{80,64},{96,80},{112,96},{17,1},{33... | collective-permute-start | bytes 150920 | tf_op jit(solution)/shard_map/ppermute | solution.py:27
  105.5 5.4 %collective-permute-start.10 = (f32[22,3,262]{2,0,1:T(8,128)S(1)}, f32[22,3,262]{2,0,1:T(8,128)S(1)}, u32[]{:S(2)}, u32[]{:S(2)}) collective-permute-start(f32[22,3,262]{2,0,1:T(8,128)S(1)} %copy.66), channel_id=1, source_target_pairs={{0,4},{4,8},{8,12},{1,5},{5,9},{9,13},{2,6},{6,10},{10,14},{3,7},{... | collective-permute-start | bytes 207512 | tf_op jit(solution)/shard_map/ppermute | solution.py:26
  109.2 5.5 %collective-permute-start.11 = (f32[22,3,262]{2,0,1:T(8,128)S(1)}, f32[22,3,262]{2,0,1:T(8,128)S(1)}, u32[]{:S(2)}, u32[]{:S(2)}) collective-permute-start(f32[22,3,262]{2,0,1:T(8,128)S(1)} %copy.67), channel_id=1, source_target_pairs={{4,0},{8,4},{12,8},{5,1},{9,5},{13,9},{6,2},{10,6},{14,10},{7,3},{... | collective-permute-start | bytes 207512 | tf_op jit(solution)/shard_map/ppermute | solution.py:27
  149.9 20.4 %copy-start.13 = (f32[16,16,256]{2,1,0:T(8,128)S(1)}, f32[16,16,256]{2,1,0:T(8,128)}, u32[]{:S(2)}) copy-start(f32[16,16,256]{2,1,0:T(8,128)} %param.16) | copy-start | bytes 786436
  149.9 20.4 %copy-start.15 = (f32[1,16,16,256]{3,2,1,0:T(8,128)S(1)}, f32[1,16,16,256]{3,2,1,0:T(8,128)}, u32[]{:S(2)}) copy-start(f32[1,16,16,256]{3,2,1,0:T(8,128)} %copy-done.14) | copy-start | bytes 786436
  157.1 17.9 %copy-start.8 = (f32[6,16,16,3]{3,2,1,0:T(8,128)S(1)}, f32[6,16,16,3]{3,2,1,0:T(8,128)}, u32[]{:S(2)}) copy-start(f32[6,16,16,3]{3,2,1,0:T(8,128)} %copy-done.7) | copy-start | bytes 55300
  157.2 17.9 %copy-start.10 = (f32[6,16,16,3]{3,2,1,0:T(8,128)S(1)}, f32[6,16,16,3]{3,2,1,0:T(8,128)}, u32[]{:S(2)}) copy-start(f32[6,16,16,3]{3,2,1,0:T(8,128)} %copy-done.9) | copy-start | bytes 55300
  157.2 17.9 %copy-start.20 = (f32[6,22,3,262]{3,2,1,0:T(4,128)S(1)}, f32[6,22,3,262]{3,2,1,0:T(4,128)}, u32[]{:S(2)}) copy-start(f32[6,22,3,262]{3,2,1,0:T(4,128)} %copy-done.19) | copy-start | bytes 1245028
  157.2 17.9 %copy-start.24 = (f32[6,3,16,262]{3,2,1,0:T(8,128)S(1)}, f32[6,3,16,262]{3,2,1,0:T(8,128)}, u32[]{:S(2)}) copy-start(f32[6,3,16,262]{3,2,1,0:T(8,128)} %copy-done.22) | copy-start | bytes 905476
  157.2 17.9 %copy-start.27 = (f32[6,3,16,262]{3,2,1,0:T(8,128)S(1)}, f32[6,3,16,262]{3,2,1,0:T(8,128)}, u32[]{:S(2)}) copy-start(f32[6,3,16,262]{3,2,1,0:T(8,128)} %copy-done.25) | copy-start | bytes 905476
  157.2 17.9 %copy-start.30 = (s32[16,16,256]{2,1,0:T(8,128)S(1)}, s32[16,16,256]{2,1,0:T(8,128)}, u32[]{:S(2)}) copy-start(s32[16,16,256]{2,1,0:T(8,128)} %param.17) | copy-start | bytes 786436
  157.2 11.0 %collective-permute-start.13 = (f32[16,1,256]{2,0,1:T(8,128)S(1)}, f32[16,1,256]{2,0,1:T(8,128)S(1)}, u32[]{:S(2)}, u32[]{:S(2)}) collective-permute-start(f32[16,1,256]{2,0,1:T(8,128)S(1)} %copy.56), channel_id=1, source_target_pairs={{0,4},{4,8},{8,12},{1,5},{5,9},{9,13},{2,6},{6,10},{10,14},{3,7},{... | collective-permute-start | bytes 49160 | tf_op jit(solution)/shard_map/ppermute | solution.py:89
  159.8 11.3 %collective-permute-start.12 = (f32[16,16,1]{2,1,0:T(8,128)S(1)}, f32[16,16,1]{2,1,0:T(8,128)S(1)}, u32[]{:S(2)}, u32[]{:S(2)}) collective-permute-start(f32[16,16,1]{2,1,0:T(8,128)S(1)} %get-tuple-element.92), channel_id=1, source_target_pairs={{0,1},{1,2},{2,3},{4,5},{5,6},{6,7},{8,9},{9,10},{10,11},{12,13},{... | collective-permute-start | bytes 3080 | tf_op jit(solution)/shard_map/ppermute | solution.py:89
  162.3 8.8 %collective-permute-start.17 = (f32[16,16,1]{2,1,0:T(8,128)S(1)}, f32[16,16,1]{2,1,0:T(8,128)S(1)}, u32[]{:S(2)}, u32[]{:S(2)}) collective-permute-start(f32[16,16,1]{2,1,0:T(8,128)S(1)} %get-tuple-element.93), channel_id=1, source_target_pairs={{1,0},{2,1},{3,2},{5,4},{6,5},{7,6},{9,8},{10,9},{11,10},{13,12},{... | collective-permute-start | bytes 3080 | tf_op jit(solution)/shard_map/ppermute | solution.py:90
  163.7 7.5 %collective-permute-start.16 = (f32[16,1,256]{2,0,1:T(8,128)S(1)}, f32[16,1,256]{2,0,1:T(8,128)S(1)}, u32[]{:S(2)}, u32[]{:S(2)}) collective-permute-start(f32[16,1,256]{2,0,1:T(8,128)S(1)} %copy.57), channel_id=1, source_target_pairs={{4,0},{8,4},{12,8},{5,1},{9,5},{13,9},{6,2},{10,6},{14,10},{7,3},{... | collective-permute-start | bytes 49160 | tf_op jit(solution)/shard_map/ppermute | solution.py:90
  165.0 6.2 %collective-permute-start.14 = (f32[1,16,256]{2,1,0:T(8,128)S(1)}, f32[1,16,256]{2,1,0:T(8,128)S(1)}, u32[]{:S(2)}, u32[]{:S(2)}) collective-permute-start(f32[1,16,256]{2,1,0:T(8,128)S(1)} %get-tuple-element.90), channel_id=1, source_target_pairs={{0,16},{16,32},{32,48},{48,64},{64,80},{80,96},{96,112},{1,17},{17... | collective-permute-start | bytes 49160 | tf_op jit(solution)/shard_map/ppermute | solution.py:89
  168.3 5.1 %collective-permute-start.15 = (f32[1,16,256]{2,1,0:T(8,128)S(1)}, f32[1,16,256]{2,1,0:T(8,128)S(1)}, u32[]{:S(2)}, u32[]{:S(2)}) collective-permute-start(f32[1,16,256]{2,1,0:T(8,128)S(1)} %get-tuple-element.91), channel_id=1, source_target_pairs={{16,0},{32,16},{48,32},{64,48},{80,64},{96,80},{112,96},{17,1},{33... | collective-permute-start | bytes 49160 | tf_op jit(solution)/shard_map/ppermute | solution.py:90
  (20 other events, 108.5 us)

commit v11 on v9

--- a/solution.py
+++ b/solution.py
@@ -62,8 +62,8 @@
 
 
 def jacobi(rhs_box, padded_cond, diagonal, storage_box, free_box):
-    guess = jnp.zeros_like(rhs_box)
-    for sweep in range(SWEEPS):
+    guess = RELAX * rhs_box / diagonal
+    for sweep in range(1, SWEEPS):
         image = stencil(jnp.pad(free_box * guess, 1), padded_cond, guess, storage_box, free_box)
         guess = guess + RELAX * (rhs_box - image) / diagonal
     return guess

time: 205 us -> 207 us (level)
  waiting for transfers between devices: 10.1 us -> 24.7 us
  starting transfers between devices: 53.8 us -> 45.5 us
  Pallas kernels: 55.5 us -> 51 us
    ppermute x6, waiting for transfers between devices: 5.64 us -> 17.5 us  [padded(): after = lax.ppermute(leading, axis, down)]
    pallas_call x3, Pallas kernels: 55.5 us -> 51 us  [gather_rows(): pl.pallas_call(functools.partial(gather_kernel, sizes), out_shape=jax.Sha...]
    ppermute x6, starting transfers between devices: 12.3 us -> 9.6 us  [padded(): after = lax.ppermute(leading, axis, down)]
    ppermute x3, waiting for transfers between devices: 0.01 us -> 2.17 us  [faces(): after = lax.ppermute(lax.slice_in_dim(field, 0, 1, axis=dim), axis, down)]
    mul x7 -> x6, other arithmetic: 16.5 us -> 15.3 us  [jacobi(): free_box * guess]
    unnamed x90 -> x88, local copies, waits for them, and re-layouts: 4.58 us -> 4.55 us
  transfers between devices with their start and end apart: 18 -> 18, of which waited for: 7 -> 9; matrix products, arithmetic and copies ran while one was open for 6% -> 6% of each run, Pallas kernels for 12% -> 11%
where the time goes in v11:
time: 207 us; the launch traced here: 206 us
  other arithmetic  59 us (29%)
  Pallas kernels  51 us (25%)
  starting transfers between devices  45.5 us (22%)
  waiting for transfers between devices  24.7 us (12%)
  local copies, waits for them, and re-layouts  18 us (9%)
  between operations  7.35 us (4%)
    pallas_call x3, Pallas kernels, gather_rows(): pl.pallas_call(functools.partial(gather_kernel, sizes), out_shape=jax.Sha...  51 us
    ppermute x6, starting transfers between devices, padded(): before = lax.ppermute(last, axis, up)  23.1 us
    ppermute x6, waiting for transfers between devices, padded(): after = lax.ppermute(leading, axis, down)  17.5 us
    mul x6, other arithmetic, jacobi(): free_box * guess  15.3 us
    ppermute x6, starting transfers between devices, padded(): after = lax.ppermute(leading, axis, down)  9.6 us
    ppermute x3, starting transfers between devices, faces(): lax.ppermute(lax.slice_in_dim(field, length - 1, length, axis=dim), axis,...  8.36 us
    concatenate x2, other arithmetic, padded(): value = jnp.concatenate([before, value, after], axis=dim)  7.86 us
    reduce_sum x2, other arithmetic, expand(): return jnp.sum(weights[:, None, None, None] * basis, axis=0)  5.73 us
  transfers between devices with their start and end apart: 18, of which 9 were waited for; matrix products, arithmetic and copies ran while one was open for 6% of the time, Pallas kernels for 11%

profile of v11, /device:TPU:1, one launch (start us, length us, event | category | flops | bytes accessed | tf_op | source)
XLA Modules:
  0.0 205.9 jit_solution(17296170192555042131)
XLA Ops:
  4.2 4.0 %collective-permute-start = (f32[6,16,16,3]{2,1,3,0:T(8,128)S(1)}, f32[6,16,16,3]{2,1,3,0:T(8,128)S(1)}, u32[]{:S(2)}, u32[]{:S(2)}) collective-permute-start(f32[6,16,16,3]{2,1,3,0:T(8,128)S(1)} %copy.62), channel_id=1, source_target_pairs={{0,1},{1,2},{2,3},{4,5},{5,6},{6,7},{8,9},{9,10},{10,11},{12,13},{... | collective-permute-start | bytes 55304 | tf_op jit(solution)/shard_map/ppermute | solution.py:26
  11.3 3.9 %collective-permute-done.1 = f32[6,16,16,3]{2,1,3,0:T(8,128)} collective-permute-done((f32[6,16,16,3]{2,1,3,0:T(8,128)S(1)}, f32[6,16,16,3]{2,1,3,0:T(8,128)}, u32[]{:S(2)}, u32[]{:S(2)}) %collective-permute-start.1) | collective-permute-done | bytes 18464 | tf_op jit(solution)/shard_map/ppermute | solution.py:27
  17.2 5.0 %collective-permute-start.2 = (f32[6,3,16,262]{3,2,1,0:T(8,128)S(1)}, f32[6,3,16,262]{3,2,1,0:T(8,128)S(1)}, u32[]{:S(2)}, u32[]{:S(2)}) collective-permute-start(f32[6,3,16,262]{3,2,1,0:T(8,128)S(1)} %get-tuple-element.80), channel_id=1, source_target_pairs={{0,16},{16,32},{32,48},{48,64},{64,80},{80,96},{96,112},{1,17},{17... | collective-permute-start | bytes 905480 | tf_op jit(solution)/shard_map/ppermute | solution.py:26
  24.1 3.3 %collective-permute-done.2 = f32[6,3,16,262]{3,2,1,0:T(8,128)S(1)} collective-permute-done((f32[6,3,16,262]{3,2,1,0:T(8,128)S(1)}, f32[6,3,16,262]{3,2,1,0:T(8,128)S(1)}, u32[]{:S(2)}, u32[]{:S(2)}) %collective-permute-start.2) | collective-permute-done | bytes 301856 | tf_op jit(solution)/shard_map/ppermute | solution.py:26
  27.4 4.4 %collective-permute-done.3 = f32[6,3,16,262]{3,2,1,0:T(8,128)S(1)} collective-permute-done((f32[6,3,16,262]{3,2,1,0:T(8,128)S(1)}, f32[6,3,16,262]{3,2,1,0:T(8,128)S(1)}, u32[]{:S(2)}, u32[]{:S(2)}) %collective-permute-start.3) | collective-permute-done | bytes 301856 | tf_op jit(solution)/shard_map/ppermute | solution.py:27
  31.8 2.2 %pad_maximum_fusion.2 = f32[6,22,16,262]{3,2,1,0:T(8,128)S(1)} fusion(f32[6,3,16,262]{3,2,1,0:T(8,128)S(1)} %collective-permute-done.3, f32[6,16,16,3]{3,2,1,0:T(8,128)S(1)} %copy.47, f32[1,16,16,256]{3,2,1,0:T(8,128)S(1)} %bitcast.282, f32[1,16,16,256]{3,2,1,0:T(8,128)S(1)} %fusion.185, f32[1,16,16,256]{3,2,1,0:T(8,128)S(1)} %bitcast.287, ...), kind=kLoop, calls=%fused_computation.6 | loop fusion | flops 3873408 | bytes 4426752 | tf_op jit(solution)/shard_map/concatenate | solution.py:28
  35.2 4.5 %collective-permute-start.4 = (f32[6,22,3,262]{3,1,2,0:T(8,128)}, f32[6,22,3,262]{3,1,2,0:T(8,128)}, u32[]{:S(2)}, u32[]{:S(2)}) collective-permute-start(f32[6,22,3,262]{3,1,2,0:T(8,128)} %copy.64), channel_id=1, source_target_pairs={{0,4},{4,8},{8,12},{1,5},{5,9},{9,13},{2,6},{6,10},{10,14},{3,7},{... | collective-permute-start | bytes 1245032 | tf_op jit(solution)/shard_map/ppermute | solution.py:26
  42.9 22.0 %shard_map.77 = f32[128,1,128]{2,1,0:T(1,128)} custom-call(f32[1,1,128]{2,1,0:T(1,128)} %scatter.14.row_ref), custom_call_target="tpu_custom_call" | custom-call | tf_op jit(solution)/shard_map/pallas_call | solution.py:165
  66.1 2.8 %multiply_reduce_fusion.2 = f32[16,16,256]{2,1,0:T(8,128)S(1)} fusion(f32[16,16,16,256]{3,2,1,0:T(8,128)} %param.18, f32[16]{0:T(128)S(1)} %convolution_bitcast_fusion.1), kind=kLoop, calls=%fused_computation.4 | loop fusion | flops 2031616 | bytes 4456512 | tf_op jit(solution)/shard_map/reduce_sum | solution.py:77
  71.9 5.7 %pad_maximum_fusion = f32[6,22,22,262]{3,2,1,0:T(8,128)S(1)} fusion(f32[6,22,3,262]{3,2,1,0:T(4,128)S(1)} %copy.51, f32[6,3,16,262]{3,2,1,0:T(8,128)S(1)} %copy-done.29, f32[6,16,16,3]{3,2,1,0:T(8,128)S(1)} %copy.47, f32[1,16,16,256]{3,2,1,0:T(8,128)S(1)} %bitcast.283, f32[1,16,16,256]{3,2,1,0:T(8,128)S(1)} %fusion.185, f32[1,16,16,256]{3,2,1,0:T(8,128)S(1)} %bitcast.288, ...), kind=kLoop, calls=%fused_computation | loop fusion | flops 6847632 | bytes 6086784 | tf_op jit(solution)/shard_map/concatenate | solution.py:28
  87.0 3.1 %collective-permute-start.6 = (f32[16,16,3]{2,1,0:T(8,128)S(1)}, f32[16,16,3]{2,1,0:T(8,128)S(1)}, u32[]{:S(2)}, u32[]{:S(2)}) collective-permute-start(f32[16,16,3]{2,1,0:T(8,128)S(1)} %get-tuple-element.95), channel_id=1, source_target_pairs={{0,1},{1,2},{2,3},{4,5},{5,6},{6,7},{8,9},{9,10},{10,11},{12,13},{... | collective-permute-start | bytes 9224 | tf_op jit(solution)/shard_map/ppermute | solution.py:26
  92.6 3.8 %collective-permute-done.7 = f32[16,16,3]{2,1,0:T(8,128)S(1)} collective-permute-done((f32[16,16,3]{2,1,0:T(8,128)S(1)}, f32[16,16,3]{2,1,0:T(8,128)S(1)}, u32[]{:S(2)}, u32[]{:S(2)}) %collective-permute-start.7) | collective-permute-done | bytes 3104 | tf_op jit(solution)/shard_map/ppermute | solution.py:27
  97.8 2.8 %collective-permute-start.8 = (f32[3,16,262]{2,1,0:T(8,128)}, f32[3,16,262]{2,1,0:T(8,128)}, u32[]{:S(2)}, u32[]{:S(2)}) collective-permute-start(f32[3,16,262]{2,1,0:T(8,128)} %get-tuple-element.87), channel_id=1, source_target_pairs={{0,16},{16,32},{32,48},{48,64},{64,80},{80,96},{96,112},{1,17},{17... | collective-permute-start | bytes 150920 | tf_op jit(solution)/shard_map/ppermute | solution.py:26
  100.7 2.5 %collective-permute-start.9 = (f32[3,16,262]{2,1,0:T(8,128)}, f32[3,16,262]{2,1,0:T(8,128)}, u32[]{:S(2)}, u32[]{:S(2)}) collective-permute-start(f32[3,16,262]{2,1,0:T(8,128)} %get-tuple-element.88), channel_id=1, source_target_pairs={{16,0},{32,16},{48,32},{64,48},{80,64},{96,80},{112,96},{17,1},{33... | collective-permute-start | bytes 150920 | tf_op jit(solution)/shard_map/ppermute | solution.py:27
  104.2 2.5 %collective-permute-done.9 = f32[3,16,262]{2,1,0:T(8,128)} collective-permute-done((f32[3,16,262]{2,1,0:T(8,128)}, f32[3,16,262]{2,1,0:T(8,128)}, u32[]{:S(2)}, u32[]{:S(2)}) %collective-permute-start.9) | collective-permute-done | bytes 50336 | tf_op jit(solution)/shard_map/ppermute | solution.py:27
  107.8 3.7 %collective-permute-start.10 = (f32[22,3,262]{2,0,1:T(8,128)S(1)}, f32[22,3,262]{2,0,1:T(8,128)S(1)}, u32[]{:S(2)}, u32[]{:S(2)}) collective-permute-start(f32[22,3,262]{2,0,1:T(8,128)S(1)} %copy.66), channel_id=1, source_target_pairs={{0,4},{4,8},{8,12},{1,5},{5,9},{9,13},{2,6},{6,10},{10,14},{3,7},{... | collective-permute-start | bytes 207512 | tf_op jit(solution)/shard_map/ppermute | solution.py:26
  114.4 2.9 %collective-permute-done.11 = f32[22,3,262]{2,0,1:T(8,128)S(1)} collective-permute-done((f32[22,3,262]{2,0,1:T(8,128)S(1)}, f32[22,3,262]{2,0,1:T(8,128)S(1)}, u32[]{:S(2)}, u32[]{:S(2)}) %collective-permute-start.11) | collective-permute-done | bytes 69200 | tf_op jit(solution)/shard_map/ppermute | solution.py:27
  118.6 3.0 %fusion.139 = f32[20,20,260]{2,1,0:T(8,128)S(1)} fusion(f32[22,22,262]{2,1,0:T(8,128)S(1)} %get-tuple-element.66, f32[22,22,262]{2,1,0:T(8,128)S(1)} %get-tuple-element.65, f32[6,22,22,262]{3,2,1,0:T(8,128)S(1)} %copy-done.2, f32[22,22,262]{2,1,0:T(8,128)S(1)} %get-tuple-element.74, f32[22,22,262]{2,1,0:T(8,128)S(1)} %get-tuple-element.73), kind=kLoop, calls=%fused_computation.194 | loop fusion | flops 2392000 | bytes 7072000 | tf_op jit(solution)/shard_map/add | solution.py:54
  125.1 13.4 %shard_map.78 = f32[128,1,128]{2,1,0:T(1,128)} custom-call(f32[1,1,128]{2,1,0:T(1,128)} %copy-done.37), custom_call_target="tpu_custom_call" | custom-call | tf_op jit(solution)/shard_map/pallas_call | solution.py:165
  141.4 2.5 %fusion.156 = (f32[20,20,260]{2,1,0:T(8,128)S(1)}, f32[20,20,260]{2,1,0:T(8,128)S(1)}) fusion(f32[20,20,260]{2,1,0:T(8,128)} %copy-done.6, f32[6,22,22,262]{3,2,1,0:T(8,128)} %copy-done.1, f32[20,20,260]{2,1,0:T(8,128)} %copy-done.23, f32[]{:T(128)S(6)} %div.37), kind=kLoop, calls=%fused_computation.239 | loop fusion | flops 520000 | bytes 2496004 | tf_op jit(solution)/shard_map/mul | solution.py:67
  144.0 4.4 %fusion.188 = (f32[20,20,260]{2,1,0:T(8,128)S(1)}, f32[20,20,260]{2,1,0:T(8,128)S(1)}) fusion(f32[6,22,22,262]{3,2,1,0:T(8,128)} %copy-done.1, f32[20,20,260]{2,1,0:T(8,128)} %copy-done.6, f32[20,20,260]{2,1,0:T(8,128)S(1)} %get-tuple-element.64, f32[20,20,260]{2,1,0:T(8,128)S(1)} %get-tuple-element.63, f32[3,20,20,260]{3,2,1,0:T(8,128)S(1)} %slice.568), kind=kLoop, calls=%fused_computation.326 | loop fusion | flops 3120000 | bytes 5408000 | tf_op jit(solution)/shard_map/mul | solution.py:67
  148.4 2.7 %fusion.187 = (f32[20,20,260]{2,1,0:T(8,128)S(1)}, f32[20,20,260]{2,1,0:T(8,128)}) fusion(f32[6,22,22,262]{3,2,1,0:T(8,128)S(1)} %bitcast.279, f32[20,20,260]{2,1,0:T(8,128)S(1)} %get-tuple-element.62, f32[20,20,260]{2,1,0:T(8,128)S(1)} %copy-done.7, f32[20,20,260]{2,1,0:T(8,128)S(1)} %get-tuple-element.64, f32[20,20,260]{2,1,0:T(8,128)S(1)} %get-tuple-element.61, ...), kind=kLoop, calls=%fused_computation.325 | loop fusion | flops 2912000 | bytes 5824000 | tf_op jit(solution)/shard_map/mul | solution.py:67
  151.1 2.4 %fusion.125 = f32[20,20,260]{2,1,0:T(8,128)} fusion(f32[20,20,260]{2,1,0:T(8,128)S(1)} %get-tuple-element.59, f32[6,22,22,262]{3,2,1,0:T(8,128)S(1)} %bitcast.279, f32[3,20,20,260]{3,2,1,0:T(8,128)S(1)} %slice.568), kind=kLoop, calls=%fused_computation.179 | loop fusion | flops 1976000 | bytes 3744000 | tf_op jit(solution)/shard_map/add | solution.py:50
  153.8 2.9 %multiply_reduce_fusion = f32[16,16,256]{2,1,0:T(8,128)S(1)} fusion(f32[16,16,16,256]{3,2,1,0:T(8,128)} %param.18, f32[16]{0:T(128)S(1)} %convolution_bitcast_fusion), kind=kLoop, calls=%fused_computation.2 | loop fusion | flops 2031616 | bytes 4456512 | tf_op jit(solution)/shard_map/reduce_sum | solution.py:77
  156.7 2.3 %fusion.179 = f32[16,16,256]{2,1,0:T(8,128)S(1)} fusion(f32[16,16,256]{2,1,0:T(8,128)S(1)} %multiply_reduce_fusion, f32[20,20,260]{2,1,0:T(8,128)} %fusion.125, f32[20,20,260]{2,1,0:T(8,128)} %get-tuple-element.60, f32[20,20,260]{2,1,0:T(8,128)} %copy-done.6, f32[20,20,260]{2,1,0:T(8,128)} %copy-done.32, f32[20,20,260]{2,1,0:T(8,128)} %copy-done.31, ...), kind=kLoop, calls=%fused_computation.292 | loop fusion | flops 524288 | bytes 2097152 | tf_op jit(solution)/shard_map/add | solution.py:220
  159.2 2.6 %collective-permute-start.13 = (f32[16,1,256]{2,0,1:T(8,128)S(1)}, f32[16,1,256]{2,0,1:T(8,128)S(1)}, u32[]{:S(2)}, u32[]{:S(2)}) collective-permute-start(f32[16,1,256]{2,0,1:T(8,128)S(1)} %copy.56), channel_id=1, source_target_pairs={{0,4},{4,8},{8,12},{1,5},{5,9},{9,13},{2,6},{6,10},{10,14},{3,7},{... | collective-permute-start | bytes 49160 | tf_op jit(solution)/shard_map/ppermute | solution.py:89
  161.8 2.5 %collective-permute-start.12 = (f32[16,16,1]{2,1,0:T(8,128)S(1)}, f32[16,16,1]{2,1,0:T(8,128)S(1)}, u32[]{:S(2)}, u32[]{:S(2)}) collective-permute-start(f32[16,16,1]{2,1,0:T(8,128)S(1)} %get-tuple-element.91), channel_id=1, source_target_pairs={{0,1},{1,2},{2,3},{4,5},{5,6},{6,7},{8,9},{9,10},{10,11},{12,13},{... | collective-permute-start | bytes 3080 | tf_op jit(solution)/shard_map/ppermute | solution.py:89
  166.9 3.3 %collective-permute-start.14 = (f32[1,16,256]{2,1,0:T(8,128)S(1)}, f32[1,16,256]{2,1,0:T(8,128)S(1)}, u32[]{:S(2)}, u32[]{:S(2)}) collective-permute-start(f32[1,16,256]{2,1,0:T(8,128)S(1)} %get-tuple-element.89), channel_id=1, source_target_pairs={{0,16},{16,32},{32,48},{48,64},{64,80},{80,96},{96,112},{1,17},{17... | collective-permute-start | bytes 49160 | tf_op jit(solution)/shard_map/ppermute | solution.py:89
  173.1 2.2 %collective-permute-done.15 = f32[1,16,256]{2,1,0:T(8,128)S(1)} collective-permute-done((f32[1,16,256]{2,1,0:T(8,128)S(1)}, f32[1,16,256]{2,1,0:T(8,128)S(1)}, u32[]{:S(2)}, u32[]{:S(2)}) %collective-permute-start.15) | collective-permute-done | bytes 16416 | tf_op jit(solution)/shard_map/ppermute | solution.py:90
  177.0 2.3 %multiply_reduce_fusion.7 = (f32[]{:T(128)}, f32[]{:T(128)}, f32[]{:T(128)}, f32[]{:T(128)}, f32[16,16,256]{2,1,0:T(8,128)}) fusion(f32[16,16,256]{2,1,0:T(8,128)S(1)} %fusion.179, f32[20,20,260]{2,1,0:T(8,128)S(1)} %copy-done.20, f32[20,20,260]{2,1,0:T(8,128)S(1)} %copy-done.24, f32[16,16,256]{2,1,0:T(8,128)S(1)} %fusion.183, ...), kind=kLoop, calls=%fused_computation.305 | loop fusion | flops 3211260 | bytes 9560080 | tf_op jit(solution)/shard_map/reduce_sum | solution.py:242
  179.3 2.5 %maximum_bitcast_fusion.1 = f32[1,1,4]{2,1,0:T(1,128)S(1)} fusion(f32[1]{0:T(128)} %bitcast.39, f32[1]{0:T(128)} %bitcast.38, f32[1]{0:T(128)} %bitcast.37, f32[1]{0:T(128)} %bitcast.29), kind=kLoop, calls=%fused_computation.322 | loop fusion | flops 12 | bytes 32 | tf_op jit(solution)/shard_map/broadcast_in_dim;broadcast_in_dim | solution.py:164
  182.4 15.7 %shard_map.79 = f32[128,1,128]{2,1,0:T(1,128)} custom-call(f32[1,1,128]{2,1,0:T(1,128)} %scatter.19.row_ref), custom_call_target="tpu_custom_call" | custom-call | tf_op jit(solution)/shard_map/pallas_call | solution.py:165
  (158 shorter events, 54.9 us)
Async XLA Ops:
  0.6 65.3 %copy-start = (f32[16,2048]{1,0:T(8,128)S(1)}, f32[16,2048]{1,0:T(8,128)}, u32[]{:S(2)}) copy-start(f32[16,2048]{1,0:T(8,128)} %param.19) | copy-start | bytes 393220
  1.7 70.2 %copy-start.17 = (f32[1,16,16,256]{3,2,1,0:T(8,128)}, f32[1,16,16,256]{3,2,1,0:T(8,128)S(1)}, u32[]{:S(2)}) copy-start(f32[1,16,16,256]{3,2,1,0:T(8,128)S(1)} %fusion.185) | copy-start | bytes 786436
  4.2 6.5 %collective-permute-start = (f32[6,16,16,3]{2,1,3,0:T(8,128)S(1)}, f32[6,16,16,3]{2,1,3,0:T(8,128)S(1)}, u32[]{:S(2)}, u32[]{:S(2)}) collective-permute-start(f32[6,16,16,3]{2,1,3,0:T(8,128)S(1)} %copy.62), channel_id=1, source_target_pairs={{0,1},{1,2},{2,3},{4,5},{5,6},{6,7},{8,9},{9,10},{10,11},{12,13},{... | collective-permute-start | bytes 55304 | tf_op jit(solution)/shard_map/ppermute | solution.py:26
  8.8 6.4 %collective-permute-start.1 = (f32[6,16,16,3]{2,1,3,0:T(8,128)S(1)}, f32[6,16,16,3]{2,1,3,0:T(8,128)}, u32[]{:S(2)}, u32[]{:S(2)}) collective-permute-start(f32[6,16,16,3]{2,1,3,0:T(8,128)S(1)} %copy.63), channel_id=1, source_target_pairs={{1,0},{2,1},{3,2},{5,4},{6,5},{7,6},{9,8},{10,9},{11,10},{13,12},{... | collective-permute-start | bytes 55304 | tf_op jit(solution)/shard_map/ppermute | solution.py:27
  11.3 60.6 %copy-start.8 = (f32[6,16,16,3]{3,2,1,0:T(8,128)}, f32[6,16,16,3]{3,2,1,0:T(8,128)S(1)}, u32[]{:S(2)}) copy-start(f32[6,16,16,3]{3,2,1,0:T(8,128)S(1)} %copy.46) | copy-start | bytes 55300
  16.8 55.1 %copy-start.10 = (f32[6,16,16,3]{3,2,1,0:T(8,128)}, f32[6,16,16,3]{3,2,1,0:T(8,128)S(1)}, u32[]{:S(2)}) copy-start(f32[6,16,16,3]{3,2,1,0:T(8,128)S(1)} %copy.47) | copy-start | bytes 55300
  17.2 10.2 %collective-permute-start.2 = (f32[6,3,16,262]{3,2,1,0:T(8,128)S(1)}, f32[6,3,16,262]{3,2,1,0:T(8,128)S(1)}, u32[]{:S(2)}, u32[]{:S(2)}) collective-permute-start(f32[6,3,16,262]{3,2,1,0:T(8,128)S(1)} %get-tuple-element.80), channel_id=1, source_target_pairs={{0,16},{16,32},{32,48},{48,64},{64,80},{80,96},{96,112},{1,17},{17... | collective-permute-start | bytes 905480 | tf_op jit(solution)/shard_map/ppermute | solution.py:26
  22.1 9.6 %collective-permute-start.3 = (f32[6,3,16,262]{3,2,1,0:T(8,128)S(1)}, f32[6,3,16,262]{3,2,1,0:T(8,128)S(1)}, u32[]{:S(2)}, u32[]{:S(2)}) collective-permute-start(f32[6,3,16,262]{3,2,1,0:T(8,128)S(1)} %get-tuple-element.81), channel_id=1, source_target_pairs={{16,0},{32,16},{48,32},{64,48},{80,64},{96,80},{112,96},{17,1},{33... | collective-permute-start | bytes 905480 | tf_op jit(solution)/shard_map/ppermute | solution.py:27
  35.2 33.8 %collective-permute-start.4 = (f32[6,22,3,262]{3,1,2,0:T(8,128)}, f32[6,22,3,262]{3,1,2,0:T(8,128)}, u32[]{:S(2)}, u32[]{:S(2)}) collective-permute-start(f32[6,22,3,262]{3,1,2,0:T(8,128)} %copy.64), channel_id=1, source_target_pairs={{0,4},{4,8},{8,12},{1,5},{5,9},{9,13},{2,6},{6,10},{10,14},{3,7},{... | collective-permute-start | bytes 1245032 | tf_op jit(solution)/shard_map/ppermute | solution.py:26
  40.6 29.7 %collective-permute-start.5 = (f32[6,22,3,262]{3,1,2,0:T(8,128)}, f32[6,22,3,262]{3,1,2,0:T(8,128)}, u32[]{:S(2)}, u32[]{:S(2)}) collective-permute-start(f32[6,22,3,262]{3,1,2,0:T(8,128)} %copy.65), channel_id=1, source_target_pairs={{4,0},{8,4},{12,8},{5,1},{9,5},{13,9},{6,2},{10,6},{14,10},{7,3},{... | collective-permute-start | bytes 1245032 | tf_op jit(solution)/shard_map/ppermute | solution.py:27
  87.0 5.6 %collective-permute-start.6 = (f32[16,16,3]{2,1,0:T(8,128)S(1)}, f32[16,16,3]{2,1,0:T(8,128)S(1)}, u32[]{:S(2)}, u32[]{:S(2)}) collective-permute-start(f32[16,16,3]{2,1,0:T(8,128)S(1)} %get-tuple-element.95), channel_id=1, source_target_pairs={{0,1},{1,2},{2,3},{4,5},{5,6},{6,7},{8,9},{9,10},{10,11},{12,13},{... | collective-permute-start | bytes 9224 | tf_op jit(solution)/shard_map/ppermute | solution.py:26
  90.1 6.3 %collective-permute-start.7 = (f32[16,16,3]{2,1,0:T(8,128)S(1)}, f32[16,16,3]{2,1,0:T(8,128)S(1)}, u32[]{:S(2)}, u32[]{:S(2)}) collective-permute-start(f32[16,16,3]{2,1,0:T(8,128)S(1)} %get-tuple-element.96), channel_id=1, source_target_pairs={{1,0},{2,1},{3,2},{5,4},{6,5},{7,6},{9,8},{10,9},{11,10},{13,12},{... | collective-permute-start | bytes 9224 | tf_op jit(solution)/shard_map/ppermute | solution.py:27
  97.8 6.3 %collective-permute-start.8 = (f32[3,16,262]{2,1,0:T(8,128)}, f32[3,16,262]{2,1,0:T(8,128)}, u32[]{:S(2)}, u32[]{:S(2)}) collective-permute-start(f32[3,16,262]{2,1,0:T(8,128)} %get-tuple-element.87), channel_id=1, source_target_pairs={{0,16},{16,32},{32,48},{48,64},{64,80},{80,96},{96,112},{1,17},{17... | collective-permute-start | bytes 150920 | tf_op jit(solution)/shard_map/ppermute | solution.py:26
  100.7 6.0 %collective-permute-start.9 = (f32[3,16,262]{2,1,0:T(8,128)}, f32[3,16,262]{2,1,0:T(8,128)}, u32[]{:S(2)}, u32[]{:S(2)}) collective-permute-start(f32[3,16,262]{2,1,0:T(8,128)} %get-tuple-element.88), channel_id=1, source_target_pairs={{16,0},{32,16},{48,32},{64,48},{80,64},{96,80},{112,96},{17,1},{33... | collective-permute-start | bytes 150920 | tf_op jit(solution)/shard_map/ppermute | solution.py:27
  107.8 6.5 %collective-permute-start.10 = (f32[22,3,262]{2,0,1:T(8,128)S(1)}, f32[22,3,262]{2,0,1:T(8,128)S(1)}, u32[]{:S(2)}, u32[]{:S(2)}) collective-permute-start(f32[22,3,262]{2,0,1:T(8,128)S(1)} %copy.66), channel_id=1, source_target_pairs={{0,4},{4,8},{8,12},{1,5},{5,9},{9,13},{2,6},{6,10},{10,14},{3,7},{... | collective-permute-start | bytes 207512 | tf_op jit(solution)/shard_map/ppermute | solution.py:26
  111.6 5.7 %collective-permute-start.11 = (f32[22,3,262]{2,0,1:T(8,128)S(1)}, f32[22,3,262]{2,0,1:T(8,128)S(1)}, u32[]{:S(2)}, u32[]{:S(2)}) collective-permute-start(f32[22,3,262]{2,0,1:T(8,128)S(1)} %copy.67), channel_id=1, source_target_pairs={{4,0},{8,4},{12,8},{5,1},{9,5},{13,9},{6,2},{10,6},{14,10},{7,3},{... | collective-permute-start | bytes 207512 | tf_op jit(solution)/shard_map/ppermute | solution.py:27
  153.5 18.7 %copy-start.16 = (f32[16,16,256]{2,1,0:T(8,128)S(1)}, f32[16,16,256]{2,1,0:T(8,128)}, u32[]{:S(2)}) copy-start(f32[16,16,256]{2,1,0:T(8,128)} %param.16) | copy-start | bytes 786436
  153.5 18.7 %copy-start.18 = (f32[1,16,16,256]{3,2,1,0:T(8,128)S(1)}, f32[1,16,16,256]{3,2,1,0:T(8,128)}, u32[]{:S(2)}) copy-start(f32[1,16,16,256]{3,2,1,0:T(8,128)} %copy-done.17) | copy-start | bytes 786436
  159.1 17.9 %copy-start.9 = (f32[6,16,16,3]{3,2,1,0:T(8,128)S(1)}, f32[6,16,16,3]{3,2,1,0:T(8,128)}, u32[]{:S(2)}) copy-start(f32[6,16,16,3]{3,2,1,0:T(8,128)} %copy-done.8) | copy-start | bytes 55300
  159.1 17.9 %copy-start.11 = (f32[6,16,16,3]{3,2,1,0:T(8,128)S(1)}, f32[6,16,16,3]{3,2,1,0:T(8,128)}, u32[]{:S(2)}) copy-start(f32[6,16,16,3]{3,2,1,0:T(8,128)} %copy-done.10) | copy-start | bytes 55300
  159.1 17.9 %copy-start.14 = (f32[16,16,256]{2,1,0:T(8,128)S(1)}, f32[16,16,256]{2,1,0:T(8,128)}, u32[]{:S(2)}) copy-start(f32[16,16,256]{2,1,0:T(8,128)} %param.14) | copy-start | bytes 786436
  159.1 17.9 %copy-start.22 = (f32[6,22,3,262]{3,2,1,0:T(4,128)S(1)}, f32[6,22,3,262]{3,2,1,0:T(4,128)}, u32[]{:S(2)}) copy-start(f32[6,22,3,262]{3,2,1,0:T(4,128)} %copy-done.21) | copy-start | bytes 1245028
  159.1 17.9 %copy-start.24 = (f32[20,20,260]{2,1,0:T(8,128)S(1)}, f32[20,20,260]{2,1,0:T(8,128)}, u32[]{:S(2)}) copy-start(f32[20,20,260]{2,1,0:T(8,128)} %copy-done.23) | copy-start | bytes 1248004
  159.1 17.9 %copy-start.27 = (f32[6,3,16,262]{3,2,1,0:T(8,128)S(1)}, f32[6,3,16,262]{3,2,1,0:T(8,128)}, u32[]{:S(2)}) copy-start(f32[6,3,16,262]{3,2,1,0:T(8,128)} %copy-done.25) | copy-start | bytes 905476
  159.2 17.9 %copy-start.30 = (f32[6,3,16,262]{3,2,1,0:T(8,128)S(1)}, f32[6,3,16,262]{3,2,1,0:T(8,128)}, u32[]{:S(2)}) copy-start(f32[6,3,16,262]{3,2,1,0:T(8,128)} %copy-done.28) | copy-start | bytes 905476
  159.2 17.9 %copy-start.35 = (s32[16,16,256]{2,1,0:T(8,128)S(1)}, s32[16,16,256]{2,1,0:T(8,128)}, u32[]{:S(2)}) copy-start(s32[16,16,256]{2,1,0:T(8,128)} %param.17) | copy-start | bytes 786436
  159.2 11.0 %collective-permute-start.13 = (f32[16,1,256]{2,0,1:T(8,128)S(1)}, f32[16,1,256]{2,0,1:T(8,128)S(1)}, u32[]{:S(2)}, u32[]{:S(2)}) collective-permute-start(f32[16,1,256]{2,0,1:T(8,128)S(1)} %copy.56), channel_id=1, source_target_pairs={{0,4},{4,8},{8,12},{1,5},{5,9},{9,13},{2,6},{6,10},{10,14},{3,7},{... | collective-permute-start | bytes 49160 | tf_op jit(solution)/shard_map/ppermute | solution.py:89
  161.8 11.3 %collective-permute-start.12 = (f32[16,16,1]{2,1,0:T(8,128)S(1)}, f32[16,16,1]{2,1,0:T(8,128)S(1)}, u32[]{:S(2)}, u32[]{:S(2)}) collective-permute-start(f32[16,16,1]{2,1,0:T(8,128)S(1)} %get-tuple-element.91), channel_id=1, source_target_pairs={{0,1},{1,2},{2,3},{4,5},{5,6},{6,7},{8,9},{9,10},{10,11},{12,13},{... | collective-permute-start | bytes 3080 | tf_op jit(solution)/shard_map/ppermute | solution.py:89
  164.3 8.8 %collective-permute-start.17 = (f32[16,16,1]{2,1,0:T(8,128)S(1)}, f32[16,16,1]{2,1,0:T(8,128)S(1)}, u32[]{:S(2)}, u32[]{:S(2)}) collective-permute-start(f32[16,16,1]{2,1,0:T(8,128)S(1)} %get-tuple-element.92), channel_id=1, source_target_pairs={{1,0},{2,1},{3,2},{5,4},{6,5},{7,6},{9,8},{10,9},{11,10},{13,12},{... | collective-permute-start | bytes 3080 | tf_op jit(solution)/shard_map/ppermute | solution.py:90
  165.6 7.5 %collective-permute-start.16 = (f32[16,1,256]{2,0,1:T(8,128)S(1)}, f32[16,1,256]{2,0,1:T(8,128)S(1)}, u32[]{:S(2)}, u32[]{:S(2)}) collective-permute-start(f32[16,1,256]{2,0,1:T(8,128)S(1)} %copy.57), channel_id=1, source_target_pairs={{4,0},{8,4},{12,8},{5,1},{9,5},{13,9},{6,2},{10,6},{14,10},{7,3},{... | collective-permute-start | bytes 49160 | tf_op jit(solution)/shard_map/ppermute | solution.py:90
  166.9 6.2 %collective-permute-start.14 = (f32[1,16,256]{2,1,0:T(8,128)S(1)}, f32[1,16,256]{2,1,0:T(8,128)S(1)}, u32[]{:S(2)}, u32[]{:S(2)}) collective-permute-start(f32[1,16,256]{2,1,0:T(8,128)S(1)} %get-tuple-element.89), channel_id=1, source_target_pairs={{0,16},{16,32},{32,48},{48,64},{64,80},{80,96},{96,112},{1,17},{17... | collective-permute-start | bytes 49160 | tf_op jit(solution)/shard_map/ppermute | solution.py:89
  170.2 5.1 %collective-permute-start.15 = (f32[1,16,256]{2,1,0:T(8,128)S(1)}, f32[1,16,256]{2,1,0:T(8,128)S(1)}, u32[]{:S(2)}, u32[]{:S(2)}) collective-permute-start(f32[1,16,256]{2,1,0:T(8,128)S(1)} %get-tuple-element.90), channel_id=1, source_target_pairs={{16,0},{32,16},{48,32},{64,48},{80,64},{96,80},{112,96},{17,1},{33... | collective-permute-start | bytes 49160 | tf_op jit(solution)/shard_map/ppermute | solution.py:90
  (26 other events, 167.8 us)

commit v12 on v9

--- a/solution.py
+++ b/solution.py
@@ -198,19 +198,20 @@
     vecs = basis.shape[0]
     sides = (("gx", 0), ("gy", 1), ("gz", 2))
     free = 1.0 - dirichlet.astype(jnp.float32)
-    stacked = jnp.concatenate([conductance, storage[None], free[None], right_side[None]], axis=0)
+    signed = jnp.where(dirichlet == 0, storage, -storage)
+    stacked = jnp.concatenate([conductance, signed[None], right_side[None]], axis=0)
     wide = padded(stacked, (("gz", 3), ("gx", 1), ("gy", 2)), 3)
     cond_wide = wide[:3]
-    free_wide = wide[4]
-    storage_wide = wide[3]
+    free_wide = (wide[3] > 0).astype(jnp.float32)
+    storage_wide = jnp.abs(wide[3])
     cond_box = wide[:3, 1:-1, 1:-1, 1:-1]
-    storage_box = wide[3, 1:-1, 1:-1, 1:-1]
-    free_box = wide[4, 1:-1, 1:-1, 1:-1]
-    rhs_box0 = wide[5, 1:-1, 1:-1, 1:-1]
+    storage_box = storage_wide[1:-1, 1:-1, 1:-1]
+    free_box = free_wide[1:-1, 1:-1, 1:-1]
+    rhs_box0 = wide[4, 1:-1, 1:-1, 1:-1]
     box_cond = pad_cond(cond_box)
     box_diag = diagonal_of(box_cond, storage_box, free_box)
     cond_face = wide[:3, 2:-2, 2:-2, 2:-2]
-    free_face = wide[4, 2:-2, 2:-2, 2:-2]
+    free_face = free_wide[2:-2, 2:-2, 2:-2]
 
     def schwarz(rhs_box):
         return jacobi(rhs_box, box_cond, box_diag, storage_box, free_box)[2:-2, 2:-2, 2:-2]

time: 205 us -> 207 us (level)
  waiting for transfers between devices: 10.1 us -> 33 us
  starting transfers between devices: 53.8 us -> 43.9 us
  Pallas kernels: 55.5 us -> 47.6 us
  local copies, waits for them, and re-layouts: 17.7 us -> 15.2 us
    ppermute x6, waiting for transfers between devices: 5.64 us -> 17.4 us  [padded(): after = lax.ppermute(leading, axis, down)]
    pallas_call x3, Pallas kernels: 55.5 us -> 47.6 us  [gather_rows(): pl.pallas_call(functools.partial(gather_kernel, sizes), out_shape=jax.Sha...]
    ppermute x6, waiting for transfers between devices: 4.4 us -> 9.72 us  [padded(): before = lax.ppermute(last, axis, up)]
    ppermute x3, waiting for transfers between devices: 0.01 us -> 4.09 us  [faces(): after = lax.ppermute(lax.slice_in_dim(field, 0, 1, axis=dim), axis, down)]
    concatenate x2 -> x1, other arithmetic: 7.86 us -> 4.03 us  [padded(): value = jnp.concatenate([before, value, after], axis=dim)]
    ppermute x3, starting transfers between devices: 10.4 us -> 6.92 us  [faces(): lax.ppermute(lax.slice_in_dim(field, length - 1, length, axis=dim), axis,...]
    ppermute x6, starting transfers between devices: 12.3 us -> 9.4 us  [padded(): after = lax.ppermute(leading, axis, down)]
    add x1, other arithmetic: 2.97 us -> 5.55 us  [stencil(): return free * total + (1.0 - free) * field]
  transfers between devices with their start and end apart: 18 -> 18, of which waited for: 7 -> 9; matrix products, arithmetic and copies ran while one was open for 6% -> 4% of each run, Pallas kernels for 12% -> 8%
where the time goes in v12:
time: 207 us; the launch traced here: 206 us
  other arithmetic  59 us (29%)
  Pallas kernels  47.6 us (23%)
  starting transfers between devices  43.9 us (21%)
  waiting for transfers between devices  33 us (16%)
  local copies, waits for them, and re-layouts  15.2 us (7%)
  between operations  7.15 us (3%)
    pallas_call x3, Pallas kernels, gather_rows(): pl.pallas_call(functools.partial(gather_kernel, sizes), out_shape=jax.Sha...  47.6 us
    ppermute x6, starting transfers between devices, padded(): before = lax.ppermute(last, axis, up)  22.7 us
    ppermute x6, waiting for transfers between devices, padded(): after = lax.ppermute(leading, axis, down)  17.4 us
    mul x7, other arithmetic, jacobi(): free_box * guess  15.9 us
    ppermute x6, waiting for transfers between devices, padded(): before = lax.ppermute(last, axis, up)  9.72 us
    ppermute x6, starting transfers between devices, padded(): after = lax.ppermute(leading, axis, down)  9.4 us
    ppermute x3, starting transfers between devices, faces(): lax.ppermute(lax.slice_in_dim(field, length - 1, length, axis=dim), axis,...  6.92 us
    add x1, other arithmetic, stencil(): return free * total + (1.0 - free) * field  5.55 us
  transfers between devices with their start and end apart: 18, of which 9 were waited for; matrix products, arithmetic and copies ran while one was open for 4% of the time, Pallas kernels for 8%

profile of v12, /device:TPU:1, one launch (start us, length us, event | category | flops | bytes accessed | tf_op | source)
XLA Modules:
  0.0 206.3 jit_solution(16294860059536067703)
XLA Ops:
  6.0 4.0 %collective-permute-start = (f32[5,16,16,3]{2,1,3,0:T(8,128)S(1)}, f32[5,16,16,3]{2,1,3,0:T(8,128)S(1)}, u32[]{:S(2)}, u32[]{:S(2)}) collective-permute-start(f32[5,16,16,3]{2,1,3,0:T(8,128)S(1)} %copy.65), channel_id=1, source_target_pairs={{0,1},{1,2},{2,3},{4,5},{5,6},{6,7},{8,9},{9,10},{10,11},{12,13},{... | collective-permute-start | bytes 46088 | tf_op jit(solution)/shard_map/ppermute | solution.py:26
  12.4 3.8 %collective-permute-done.1 = f32[5,16,16,3]{2,1,3,0:T(8,128)S(1)} collective-permute-done((f32[5,16,16,3]{2,1,3,0:T(8,128)S(1)}, f32[5,16,16,3]{2,1,3,0:T(8,128)S(1)}, u32[]{:S(2)}, u32[]{:S(2)}) %collective-permute-start.1) | collective-permute-done | bytes 15392 | tf_op jit(solution)/shard_map/ppermute | solution.py:27
  17.9 5.2 %collective-permute-start.2 = (f32[5,3,16,262]{3,2,1,0:T(8,128)}, f32[5,3,16,262]{3,2,1,0:T(8,128)S(1)}, u32[]{:S(2)}, u32[]{:S(2)}) collective-permute-start(f32[5,3,16,262]{3,2,1,0:T(8,128)} %get-tuple-element.78), channel_id=1, source_target_pairs={{0,16},{16,32},{32,48},{48,64},{64,80},{80,96},{96,112},{1,17},{17... | collective-permute-start | bytes 754568 | tf_op jit(solution)/shard_map/ppermute | solution.py:26
  25.0 2.6 %multiply_reduce_fusion.3 = f32[16]{0:T(128)S(1)} fusion(f32[16,16,16,256]{3,2,1,0:T(8,128)} %param.18, f32[16,16,256]{2,1,0:T(8,128)S(1)} %copy-done.15), kind=kLoop, calls=%fused_computation.3 | loop fusion | flops 2097136 | bytes 4456512 | tf_op jit(solution)/shard_map/reduce_sum | solution.py:73
  28.2 17.0 %shard_map.77 = f32[128,1,128]{2,1,0:T(1,128)} custom-call(f32[1,1,128]{2,1,0:T(1,128)} %scatter.14.row_ref), custom_call_target="tpu_custom_call" | custom-call | tf_op jit(solution)/shard_map/pallas_call | solution.py:165
  47.0 2.4 %collective-permute-start.4 = (f32[5,22,3,262]{3,1,2,0:T(8,128)S(1)}, f32[5,22,3,262]{3,1,2,0:T(8,128)S(1)}, u32[]{:S(2)}, u32[]{:S(2)}) collective-permute-start(f32[5,22,3,262]{3,1,2,0:T(8,128)S(1)} %copy.67), channel_id=1, source_target_pairs={{0,4},{4,8},{8,12},{1,5},{5,9},{9,13},{2,6},{6,10},{10,14},{3,7},{... | collective-permute-start | bytes 1037528 | tf_op jit(solution)/shard_map/ppermute | solution.py:26
  51.7 9.1 %collective-permute-done.4 = f32[5,22,3,262]{3,1,2,0:T(8,128)S(1)} collective-permute-done((f32[5,22,3,262]{3,1,2,0:T(8,128)S(1)}, f32[5,22,3,262]{3,1,2,0:T(8,128)S(1)}, u32[]{:S(2)}, u32[]{:S(2)}) %collective-permute-start.4) | collective-permute-done | bytes 345872 | tf_op jit(solution)/shard_map/ppermute | solution.py:26
  61.0 3.7 %collective-permute-done.5 = f32[5,22,3,262]{3,1,2,0:T(8,128)S(1)} collective-permute-done((f32[5,22,3,262]{3,1,2,0:T(8,128)S(1)}, f32[5,22,3,262]{3,1,2,0:T(8,128)S(1)}, u32[]{:S(2)}, u32[]{:S(2)}) %collective-permute-start.5) | collective-permute-done | bytes 345872 | tf_op jit(solution)/shard_map/ppermute | solution.py:27
  64.9 4.0 %pad_maximum_fusion = f32[5,22,22,262]{3,2,1,0:T(8,128)S(1)} fusion(f32[5,22,3,262]{3,2,1,0:T(4,128)S(1)} %copy.54, f32[5,3,16,262]{3,2,1,0:T(8,128)S(1)} %collective-permute-done.3, f32[5,16,16,3]{3,2,1,0:T(8,128)S(1)} %copy.50, f32[1,16,16,256]{3,2,1,0:T(8,128)S(1)} %bitcast.239, f32[1,16,16,256]{3,2,1,0:T(8,128)S(1)} %fusion.175, ...), kind=kLoop, calls=%fused_computation.4 | loop fusion | flops 5072320 | bytes 5072320 | tf_op jit(solution)/shard_map/concatenate | solution.py:28
  71.6 2.4 %fusion.210 = (f32[20,20,260]{2,1,0:T(8,128)S(1)}, f32[20,20,260]{2,1,0:T(8,128)S(1)}, f32[20,20,260]{2,1,0:T(8,128)S(1)}) fusion(f32[5,22,22,262]{3,2,1,0:T(8,128)S(1)} %pad_maximum_fusion, f32[22,22,262]{2,1,0:T(8,128)S(1)} %get-tuple-element.74, f32[20,20,260]{2,1,0:T(8,128)S(1)} %broadcast_multiply_fusion, f32[3,20,20,260]{3,2,1,0:T(8,128)S(1)} %slice.598, ...), kind=kLoop, calls=%fused_computation.337 | loop fusion | flops 3640000 | bytes 5408000 | tf_op jit(solution)/shard_map/mul | solution.py:67
  74.1 2.3 %slice_multiply_fusion.7 = (f32[20,20,260]{2,1,0:T(8,128)S(1)}, f32[20,20,260]{2,1,0:T(8,128)S(1)}, f32[20,20,260]{2,1,0:T(8,128)S(1)}, f32[20,20,260]{2,1,0:T(8,128)S(1)}) fusion(f32[22,22,262]{2,1,0:T(8,128)S(1)} %get-tuple-element.74, f32[20,20,260]{2,1,0:T(8,128)S(1)} %get-tuple-element.73, f32[20,20,260]{2,1,0:T(8,128)S(1)} %get-tuple-element.71, ...), kind=kLoop, calls=%fused_computation.356 | loop fusion | flops 3224000 | bytes 6656000 | tf_op jit(solution)/shard_map/mul | solution.py:67
  80.9 2.5 %collective-permute-start.6 = (f32[16,16,3]{2,1,0:T(8,128)S(1)}, f32[16,16,3]{2,1,0:T(8,128)S(1)}, u32[]{:S(2)}, u32[]{:S(2)}) collective-permute-start(f32[16,16,3]{2,1,0:T(8,128)S(1)} %get-tuple-element.95), channel_id=1, source_target_pairs={{0,1},{1,2},{2,3},{4,5},{5,6},{6,7},{8,9},{9,10},{10,11},{12,13},{... | collective-permute-start | bytes 9224 | tf_op jit(solution)/shard_map/ppermute | solution.py:26
  85.4 3.8 %collective-permute-done.7 = f32[16,16,3]{2,1,0:T(8,128)S(1)} collective-permute-done((f32[16,16,3]{2,1,0:T(8,128)S(1)}, f32[16,16,3]{2,1,0:T(8,128)S(1)}, u32[]{:S(2)}, u32[]{:S(2)}) %collective-permute-start.7) | collective-permute-done | bytes 3104 | tf_op jit(solution)/shard_map/ppermute | solution.py:27
  89.3 5.0 %collective-permute-start.8 = (f32[3,16,262]{2,1,0:T(8,128)S(1)}, f32[3,16,262]{2,1,0:T(8,128)S(1)}, u32[]{:S(2)}, u32[]{:S(2)}) collective-permute-start(f32[3,16,262]{2,1,0:T(8,128)S(1)} %get-tuple-element.87), channel_id=1, source_target_pairs={{0,16},{16,32},{32,48},{48,64},{64,80},{80,96},{96,112},{1,17},{17... | collective-permute-start | bytes 150920 | tf_op jit(solution)/shard_map/ppermute | solution.py:26
  96.2 3.7 %collective-permute-done.9 = f32[3,16,262]{2,1,0:T(8,128)S(1)} collective-permute-done((f32[3,16,262]{2,1,0:T(8,128)S(1)}, f32[3,16,262]{2,1,0:T(8,128)S(1)}, u32[]{:S(2)}, u32[]{:S(2)}) %collective-permute-start.9) | collective-permute-done | bytes 50336 | tf_op jit(solution)/shard_map/ppermute | solution.py:27
  100.8 3.7 %collective-permute-start.10 = (f32[22,3,262]{2,0,1:T(8,128)}, f32[22,3,262]{2,0,1:T(8,128)}, u32[]{:S(2)}, u32[]{:S(2)}) collective-permute-start(f32[22,3,262]{2,0,1:T(8,128)} %copy.69), channel_id=1, source_target_pairs={{0,4},{4,8},{8,12},{1,5},{5,9},{9,13},{2,6},{6,10},{10,14},{3,7},{... | collective-permute-start | bytes 207512 | tf_op jit(solution)/shard_map/ppermute | solution.py:26
  108.5 2.4 %collective-permute-done.11 = f32[22,3,262]{2,0,1:T(8,128)} collective-permute-done((f32[22,3,262]{2,0,1:T(8,128)}, f32[22,3,262]{2,0,1:T(8,128)}, u32[]{:S(2)}, u32[]{:S(2)}) %collective-permute-start.11) | collective-permute-done | bytes 69200 | tf_op jit(solution)/shard_map/ppermute | solution.py:27
  113.3 5.5 %fusion.159 = f32[20,20,260]{2,1,0:T(8,128)S(1)} fusion(f32[22,22,262]{2,1,0:T(8,128)S(1)} %get-tuple-element.66, f32[22,22,262]{2,1,0:T(8,128)S(1)} %get-tuple-element.65, f32[5,22,22,262]{3,2,1,0:T(8,128)} %copy-done.1, f32[22,22,262]{2,1,0:T(8,128)} %copy-done.5, f32[22,22,262]{2,1,0:T(8,128)S(1)} %get-tuple-element.74), kind=kLoop, calls=%fused_computation.222 | loop fusion | flops 2392000 | bytes 7072000 | tf_op jit(solution)/shard_map/add | solution.py:54
  122.3 14.7 %shard_map.78 = f32[128,1,128]{2,1,0:T(1,128)} custom-call(f32[1,1,128]{2,1,0:T(1,128)} %copy-done.37), custom_call_target="tpu_custom_call" | custom-call | tf_op jit(solution)/shard_map/pallas_call | solution.py:165
  139.8 2.5 %fusion.211 = (f32[20,20,260]{2,1,0:T(8,128)S(1)}, f32[20,20,260]{2,1,0:T(8,128)S(1)}) fusion(f32[20,20,260]{2,1,0:T(8,128)} %copy-done.7, f32[20,20,260]{2,1,0:T(8,128)} %copy-done.19, f32[22,22,262]{2,1,0:T(8,128)S(1)} %get-tuple-element.74, f32[20,20,260]{2,1,0:T(8,128)} %copy-done.22, f32[]{:T(128)S(6)} %div.37, f32[5,22,22,262]{3,2,1,0:T(8,128)} %copy-done.1), kind=kLoop, calls=%fused_computation.338 | loop fusion | flops 624000 | bytes 2912004 | tf_op jit(solution)/shard_map/mul | solution.py:67
  143.0 3.4 %slice_multiply_fusion.5 = (f32[20,20,260]{2,1,0:T(8,128)S(1)}, f32[20,20,260]{2,1,0:T(8,128)S(1)}) fusion(f32[22,22,262]{2,1,0:T(8,128)S(1)} %get-tuple-element.74, f32[20,20,260]{2,1,0:T(8,128)} %copy-done.7, f32[20,20,260]{2,1,0:T(8,128)S(1)} %get-tuple-element.64, f32[20,20,260]{2,1,0:T(8,128)S(1)} %get-tuple-element.63, ...), kind=kLoop, calls=%fused_computation.354 | loop fusion | flops 3224000 | bytes 5824000 | tf_op jit(solution)/shard_map/mul | solution.py:67
  146.5 2.8 %slice_multiply_fusion.4 = (f32[20,20,260]{2,1,0:T(8,128)S(1)}, f32[20,20,260]{2,1,0:T(8,128)}) fusion(f32[22,22,262]{2,1,0:T(8,128)S(1)} %get-tuple-element.74, f32[20,20,260]{2,1,0:T(8,128)S(1)} %get-tuple-element.62, f32[20,20,260]{2,1,0:T(8,128)S(1)} %copy-done.8, f32[20,20,260]{2,1,0:T(8,128)S(1)} %get-tuple-element.64, ...), kind=kLoop, calls=%fused_computation.353 | loop fusion | flops 2912000 | bytes 5824000 | tf_op jit(solution)/shard_map/mul | solution.py:67
  149.3 2.5 %fusion.145 = f32[20,20,260]{2,1,0:T(8,128)} fusion(f32[20,20,260]{2,1,0:T(8,128)S(1)} %get-tuple-element.59, f32[5,22,22,262]{3,2,1,0:T(8,128)S(1)} %copy-done.2, f32[22,22,262]{2,1,0:T(8,128)S(1)} %copy-done.6, f32[3,20,20,260]{3,2,1,0:T(8,128)S(1)} %slice.598), kind=kLoop, calls=%fused_computation.207 | loop fusion | flops 1976000 | bytes 3744000 | tf_op jit(solution)/shard_map/add | solution.py:50
  152.2 3.0 %multiply_reduce_fusion = f32[16,16,256]{2,1,0:T(8,128)S(1)} fusion(f32[16,16,16,256]{3,2,1,0:T(8,128)} %param.18, f32[16]{0:T(128)S(1)} %convolution_bitcast_fusion), kind=kLoop, calls=%fused_computation | loop fusion | flops 2031616 | bytes 4456512 | tf_op jit(solution)/shard_map/reduce_sum | solution.py:77
  155.2 2.5 %fusion.204 = f32[16,16,256]{2,1,0:T(8,128)S(1)} fusion(f32[16,16,256]{2,1,0:T(8,128)S(1)} %multiply_reduce_fusion, f32[20,20,260]{2,1,0:T(8,128)} %fusion.145, f32[20,20,260]{2,1,0:T(8,128)} %get-tuple-element.60, f32[20,20,260]{2,1,0:T(8,128)} %copy-done.7, f32[20,20,260]{2,1,0:T(8,128)} %copy-done.30, f32[20,20,260]{2,1,0:T(8,128)} %copy-done.29, ...), kind=kLoop, calls=%fused_computation.321 | loop fusion | flops 524288 | bytes 2097152 | tf_op jit(solution)/shard_map/add | solution.py:221
  157.7 2.4 %collective-permute-start.13 = (f32[16,1,256]{2,0,1:T(8,128)S(1)}, f32[16,1,256]{2,0,1:T(8,128)S(1)}, u32[]{:S(2)}, u32[]{:S(2)}) collective-permute-start(f32[16,1,256]{2,0,1:T(8,128)S(1)} %copy.59), channel_id=1, source_target_pairs={{0,4},{4,8},{8,12},{1,5},{5,9},{9,13},{2,6},{6,10},{10,14},{3,7},{... | collective-permute-start | bytes 49160 | tf_op jit(solution)/shard_map/ppermute | solution.py:89
  163.5 2.3 %collective-permute-start.15 = (f32[1,16,256]{2,1,0:T(8,128)S(1)}, f32[1,16,256]{2,1,0:T(8,128)S(1)}, u32[]{:S(2)}, u32[]{:S(2)}) collective-permute-start(f32[1,16,256]{2,1,0:T(8,128)S(1)} %get-tuple-element.90), channel_id=1, source_target_pairs={{16,0},{32,16},{48,32},{64,48},{80,64},{96,80},{112,96},{17,1},{33... | collective-permute-start | bytes 49160 | tf_op jit(solution)/shard_map/ppermute | solution.py:90
  165.9 2.5 %collective-permute-start.12 = (f32[16,16,1]{2,1,0:T(8,128)S(1)}, f32[16,16,1]{2,1,0:T(8,128)S(1)}, u32[]{:S(2)}, u32[]{:S(2)}) collective-permute-start(f32[16,16,1]{2,1,0:T(8,128)S(1)} %get-tuple-element.91), channel_id=1, source_target_pairs={{0,1},{1,2},{2,3},{4,5},{5,6},{6,7},{8,9},{9,10},{10,11},{12,13},{... | collective-permute-start | bytes 3080 | tf_op jit(solution)/shard_map/ppermute | solution.py:89
  171.6 4.1 %collective-permute-done.17 = f32[16,16,1]{2,1,0:T(8,128)S(1)} collective-permute-done((f32[16,16,1]{2,1,0:T(8,128)S(1)}, f32[16,16,1]{2,1,0:T(8,128)S(1)}, u32[]{:S(2)}, u32[]{:S(2)}) %collective-permute-start.17) | collective-permute-done | bytes 1056 | tf_op jit(solution)/shard_map/ppermute | solution.py:90
  176.5 2.8 %multiply_reduce_fusion.7 = (f32[]{:T(128)}, f32[]{:T(128)}, f32[]{:T(128)}, f32[]{:T(128)}, f32[16,16,256]{2,1,0:T(8,128)S(1)}) fusion(f32[16,16,256]{2,1,0:T(8,128)S(1)} %fusion.204, f32[20,20,260]{2,1,0:T(8,128)} %copy-done.18, f32[20,20,260]{2,1,0:T(8,128)} %copy-done.22, f32[16,16,256]{2,1,0:T(8,128)S(1)} %fusion.208, f32[18,18,258]{2,1,0:T(8,128)S(1)} %fusion.173, ...), kind=kLoop, calls=%fused_computation.334 | loop fusion | flops 3145724 | bytes 8491024 | tf_op jit(solution)/shard_map/reduce_sum | solution.py:243
  179.2 2.5 %maximum_bitcast_fusion.1 = f32[1,1,4]{2,1,0:T(1,128)S(1)} fusion(f32[1]{0:T(128)} %bitcast.35, f32[1]{0:T(128)} %bitcast.34, f32[1]{0:T(128)} %bitcast.33, f32[1]{0:T(128)} %bitcast.26), kind=kLoop, calls=%fused_computation.351 | loop fusion | flops 12 | bytes 32 | tf_op jit(solution)/shard_map/broadcast_in_dim;broadcast_in_dim | solution.py:164
  182.3 15.9 %shard_map.79 = f32[128,1,128]{2,1,0:T(1,128)} custom-call(f32[1,1,128]{2,1,0:T(1,128)} %scatter.19.row_ref), custom_call_target="tpu_custom_call" | custom-call | tf_op jit(solution)/shard_map/pallas_call | solution.py:165
  (153 shorter events, 52.2 us)
Async XLA Ops:
  0.6 50.2 %copy-start = (f32[16,2048]{1,0:T(8,128)S(1)}, f32[16,2048]{1,0:T(8,128)}, u32[]{:S(2)}) copy-start(f32[16,2048]{1,0:T(8,128)} %param.19) | copy-start | bytes 393220
  1.8 63.1 %copy-start.20 = (f32[1,16,16,256]{3,2,1,0:T(8,128)}, f32[1,16,16,256]{3,2,1,0:T(8,128)S(1)}, u32[]{:S(2)}) copy-start(f32[1,16,16,256]{3,2,1,0:T(8,128)S(1)} %fusion.175) | copy-start | bytes 786436
  6.0 5.8 %collective-permute-start = (f32[5,16,16,3]{2,1,3,0:T(8,128)S(1)}, f32[5,16,16,3]{2,1,3,0:T(8,128)S(1)}, u32[]{:S(2)}, u32[]{:S(2)}) collective-permute-start(f32[5,16,16,3]{2,1,3,0:T(8,128)S(1)} %copy.65), channel_id=1, source_target_pairs={{0,1},{1,2},{2,3},{4,5},{5,6},{6,7},{8,9},{9,10},{10,11},{12,13},{... | collective-permute-start | bytes 46088 | tf_op jit(solution)/shard_map/ppermute | solution.py:26
  10.5 5.6 %collective-permute-start.1 = (f32[5,16,16,3]{2,1,3,0:T(8,128)S(1)}, f32[5,16,16,3]{2,1,3,0:T(8,128)S(1)}, u32[]{:S(2)}, u32[]{:S(2)}) collective-permute-start(f32[5,16,16,3]{2,1,3,0:T(8,128)S(1)} %copy.66), channel_id=1, source_target_pairs={{1,0},{2,1},{3,2},{5,4},{6,5},{7,6},{9,8},{10,9},{11,10},{13,12},{... | collective-permute-start | bytes 46088 | tf_op jit(solution)/shard_map/ppermute | solution.py:27
  12.4 52.5 %copy-start.11 = (f32[5,16,16,3]{3,2,1,0:T(8,128)}, f32[5,16,16,3]{3,2,1,0:T(8,128)S(1)}, u32[]{:S(2)}) copy-start(f32[5,16,16,3]{3,2,1,0:T(8,128)S(1)} %copy.49) | copy-start | bytes 46084
  16.7 48.2 %copy-start.13 = (f32[5,16,16,3]{3,2,1,0:T(8,128)}, f32[5,16,16,3]{3,2,1,0:T(8,128)S(1)}, u32[]{:S(2)}) copy-start(f32[5,16,16,3]{3,2,1,0:T(8,128)S(1)} %copy.50) | copy-start | bytes 46084
  17.9 28.2 %collective-permute-start.2 = (f32[5,3,16,262]{3,2,1,0:T(8,128)}, f32[5,3,16,262]{3,2,1,0:T(8,128)S(1)}, u32[]{:S(2)}, u32[]{:S(2)}) collective-permute-start(f32[5,3,16,262]{3,2,1,0:T(8,128)} %get-tuple-element.78), channel_id=1, source_target_pairs={{0,16},{16,32},{32,48},{48,64},{64,80},{80,96},{96,112},{1,17},{17... | collective-permute-start | bytes 754568 | tf_op jit(solution)/shard_map/ppermute | solution.py:26
  23.1 23.0 %collective-permute-start.3 = (f32[5,3,16,262]{3,2,1,0:T(8,128)}, f32[5,3,16,262]{3,2,1,0:T(8,128)S(1)}, u32[]{:S(2)}, u32[]{:S(2)}) collective-permute-start(f32[5,3,16,262]{3,2,1,0:T(8,128)} %get-tuple-element.79), channel_id=1, source_target_pairs={{16,0},{32,16},{48,32},{64,48},{80,64},{96,80},{112,96},{17,1},{33... | collective-permute-start | bytes 754568 | tf_op jit(solution)/shard_map/ppermute | solution.py:27
  47.0 13.8 %collective-permute-start.4 = (f32[5,22,3,262]{3,1,2,0:T(8,128)S(1)}, f32[5,22,3,262]{3,1,2,0:T(8,128)S(1)}, u32[]{:S(2)}, u32[]{:S(2)}) collective-permute-start(f32[5,22,3,262]{3,1,2,0:T(8,128)S(1)} %copy.67), channel_id=1, source_target_pairs={{0,4},{4,8},{8,12},{1,5},{5,9},{9,13},{2,6},{6,10},{10,14},{3,7},{... | collective-permute-start | bytes 1037528 | tf_op jit(solution)/shard_map/ppermute | solution.py:26
  49.4 15.3 %collective-permute-start.5 = (f32[5,22,3,262]{3,1,2,0:T(8,128)S(1)}, f32[5,22,3,262]{3,1,2,0:T(8,128)S(1)}, u32[]{:S(2)}, u32[]{:S(2)}) collective-permute-start(f32[5,22,3,262]{3,1,2,0:T(8,128)S(1)} %copy.68), channel_id=1, source_target_pairs={{4,0},{8,4},{12,8},{5,1},{9,5},{13,9},{6,2},{10,6},{14,10},{7,3},{... | collective-permute-start | bytes 1037528 | tf_op jit(solution)/shard_map/ppermute | solution.py:27
  80.9 4.4 %collective-permute-start.6 = (f32[16,16,3]{2,1,0:T(8,128)S(1)}, f32[16,16,3]{2,1,0:T(8,128)S(1)}, u32[]{:S(2)}, u32[]{:S(2)}) collective-permute-start(f32[16,16,3]{2,1,0:T(8,128)S(1)} %get-tuple-element.95), channel_id=1, source_target_pairs={{0,1},{1,2},{2,3},{4,5},{5,6},{6,7},{8,9},{9,10},{10,11},{12,13},{... | collective-permute-start | bytes 9224 | tf_op jit(solution)/shard_map/ppermute | solution.py:26
  83.4 5.7 %collective-permute-start.7 = (f32[16,16,3]{2,1,0:T(8,128)S(1)}, f32[16,16,3]{2,1,0:T(8,128)S(1)}, u32[]{:S(2)}, u32[]{:S(2)}) collective-permute-start(f32[16,16,3]{2,1,0:T(8,128)S(1)} %get-tuple-element.96), channel_id=1, source_target_pairs={{1,0},{2,1},{3,2},{5,4},{6,5},{7,6},{9,8},{10,9},{11,10},{13,12},{... | collective-permute-start | bytes 9224 | tf_op jit(solution)/shard_map/ppermute | solution.py:27
  89.3 6.9 %collective-permute-start.8 = (f32[3,16,262]{2,1,0:T(8,128)S(1)}, f32[3,16,262]{2,1,0:T(8,128)S(1)}, u32[]{:S(2)}, u32[]{:S(2)}) collective-permute-start(f32[3,16,262]{2,1,0:T(8,128)S(1)} %get-tuple-element.87), channel_id=1, source_target_pairs={{0,16},{16,32},{32,48},{48,64},{64,80},{80,96},{96,112},{1,17},{17... | collective-permute-start | bytes 150920 | tf_op jit(solution)/shard_map/ppermute | solution.py:26
  94.3 5.7 %collective-permute-start.9 = (f32[3,16,262]{2,1,0:T(8,128)S(1)}, f32[3,16,262]{2,1,0:T(8,128)S(1)}, u32[]{:S(2)}, u32[]{:S(2)}) collective-permute-start(f32[3,16,262]{2,1,0:T(8,128)S(1)} %get-tuple-element.88), channel_id=1, source_target_pairs={{16,0},{32,16},{48,32},{64,48},{80,64},{96,80},{112,96},{17,1},{33... | collective-permute-start | bytes 150920 | tf_op jit(solution)/shard_map/ppermute | solution.py:27
  100.8 6.8 %collective-permute-start.10 = (f32[22,3,262]{2,0,1:T(8,128)}, f32[22,3,262]{2,0,1:T(8,128)}, u32[]{:S(2)}, u32[]{:S(2)}) collective-permute-start(f32[22,3,262]{2,0,1:T(8,128)} %copy.69), channel_id=1, source_target_pairs={{0,4},{4,8},{8,12},{1,5},{5,9},{9,13},{2,6},{6,10},{10,14},{3,7},{... | collective-permute-start | bytes 207512 | tf_op jit(solution)/shard_map/ppermute | solution.py:26
  105.2 5.8 %collective-permute-start.11 = (f32[22,3,262]{2,0,1:T(8,128)}, f32[22,3,262]{2,0,1:T(8,128)}, u32[]{:S(2)}, u32[]{:S(2)}) collective-permute-start(f32[22,3,262]{2,0,1:T(8,128)} %copy.70), channel_id=1, source_target_pairs={{4,0},{8,4},{12,8},{5,1},{9,5},{13,9},{6,2},{10,6},{14,10},{7,3},{... | collective-permute-start | bytes 207512 | tf_op jit(solution)/shard_map/ppermute | solution.py:27
  152.1 24.3 %copy-start.10 = (f32[3,16,16,256]{3,2,1,0:T(8,128)S(1)}, f32[3,16,16,256]{3,2,1,0:T(8,128)}, u32[]{:S(2)}) copy-start(f32[3,16,16,256]{3,2,1,0:T(8,128)} %param.15) | copy-start | bytes 2359300
  152.1 24.3 %copy-start.12 = (f32[5,16,16,3]{3,2,1,0:T(8,128)S(1)}, f32[5,16,16,3]{3,2,1,0:T(8,128)}, u32[]{:S(2)}) copy-start(f32[5,16,16,3]{3,2,1,0:T(8,128)} %copy-done.11) | copy-start | bytes 46084
  152.1 24.3 %copy-start.14 = (f32[5,16,16,3]{3,2,1,0:T(8,128)S(1)}, f32[5,16,16,3]{3,2,1,0:T(8,128)}, u32[]{:S(2)}) copy-start(f32[5,16,16,3]{3,2,1,0:T(8,128)} %copy-done.13) | copy-start | bytes 46084
  152.2 24.3 %copy-start.17 = (f32[16,16,256]{2,1,0:T(8,128)S(1)}, f32[16,16,256]{2,1,0:T(8,128)}, u32[]{:S(2)}) copy-start(f32[16,16,256]{2,1,0:T(8,128)} %param.14) | copy-start | bytes 786436
  152.2 24.3 %copy-start.21 = (f32[1,16,16,256]{3,2,1,0:T(8,128)S(1)}, f32[1,16,16,256]{3,2,1,0:T(8,128)}, u32[]{:S(2)}) copy-start(f32[1,16,16,256]{3,2,1,0:T(8,128)} %copy-done.20) | copy-start | bytes 786436
  152.2 24.3 %copy-start.24 = (f32[5,22,3,262]{3,2,1,0:T(4,128)S(1)}, f32[5,22,3,262]{3,2,1,0:T(4,128)}, u32[]{:S(2)}) copy-start(f32[5,22,3,262]{3,2,1,0:T(4,128)} %copy-done.23) | copy-start | bytes 1037524
  152.2 24.3 %copy-start.26 = (f32[5,3,16,262]{3,2,1,0:T(8,128)S(1)}, f32[5,3,16,262]{3,2,1,0:T(8,128)}, u32[]{:S(2)}) copy-start(f32[5,3,16,262]{3,2,1,0:T(8,128)} %copy-done.25) | copy-start | bytes 754564
  152.2 24.3 %copy-start.28 = (f32[5,3,16,262]{3,2,1,0:T(8,128)S(1)}, f32[5,3,16,262]{3,2,1,0:T(8,128)}, u32[]{:S(2)}) copy-start(f32[5,3,16,262]{3,2,1,0:T(8,128)} %copy-done.27) | copy-start | bytes 754564
  152.2 24.3 %copy-start.32 = (f32[16,16,256]{2,1,0:T(8,128)S(1)}, f32[16,16,256]{2,1,0:T(8,128)}, u32[]{:S(2)}) copy-start(f32[16,16,256]{2,1,0:T(8,128)} %param.16) | copy-start | bytes 786436
  152.2 24.3 %copy-start.33 = (s32[16,16,256]{2,1,0:T(8,128)S(1)}, s32[16,16,256]{2,1,0:T(8,128)}, u32[]{:S(2)}) copy-start(s32[16,16,256]{2,1,0:T(8,128)} %param.17) | copy-start | bytes 786436
  157.7 10.7 %collective-permute-start.13 = (f32[16,1,256]{2,0,1:T(8,128)S(1)}, f32[16,1,256]{2,0,1:T(8,128)S(1)}, u32[]{:S(2)}, u32[]{:S(2)}) collective-permute-start(f32[16,1,256]{2,0,1:T(8,128)S(1)} %copy.59), channel_id=1, source_target_pairs={{0,4},{4,8},{8,12},{1,5},{5,9},{9,13},{2,6},{6,10},{10,14},{3,7},{... | collective-permute-start | bytes 49160 | tf_op jit(solution)/shard_map/ppermute | solution.py:89
  160.2 9.6 %collective-permute-start.16 = (f32[16,1,256]{2,0,1:T(8,128)S(1)}, f32[16,1,256]{2,0,1:T(8,128)S(1)}, u32[]{:S(2)}, u32[]{:S(2)}) collective-permute-start(f32[16,1,256]{2,0,1:T(8,128)S(1)} %copy.60), channel_id=1, source_target_pairs={{4,0},{8,4},{12,8},{5,1},{9,5},{13,9},{6,2},{10,6},{14,10},{7,3},{... | collective-permute-start | bytes 49160 | tf_op jit(solution)/shard_map/ppermute | solution.py:90
  161.5 14.2 %collective-permute-start.14 = (f32[1,16,256]{2,1,0:T(8,128)S(1)}, f32[1,16,256]{2,1,0:T(8,128)S(1)}, u32[]{:S(2)}, u32[]{:S(2)}) collective-permute-start(f32[1,16,256]{2,1,0:T(8,128)S(1)} %get-tuple-element.89), channel_id=1, source_target_pairs={{0,16},{16,32},{32,48},{48,64},{64,80},{80,96},{96,112},{1,17},{17... | collective-permute-start | bytes 49160 | tf_op jit(solution)/shard_map/ppermute | solution.py:89
  163.5 12.3 %collective-permute-start.15 = (f32[1,16,256]{2,1,0:T(8,128)S(1)}, f32[1,16,256]{2,1,0:T(8,128)S(1)}, u32[]{:S(2)}, u32[]{:S(2)}) collective-permute-start(f32[1,16,256]{2,1,0:T(8,128)S(1)} %get-tuple-element.90), channel_id=1, source_target_pairs={{16,0},{32,16},{48,32},{64,48},{80,64},{96,80},{112,96},{17,1},{33... | collective-permute-start | bytes 49160 | tf_op jit(solution)/shard_map/ppermute | solution.py:90
  165.9 5.7 %collective-permute-start.12 = (f32[16,16,1]{2,1,0:T(8,128)S(1)}, f32[16,16,1]{2,1,0:T(8,128)S(1)}, u32[]{:S(2)}, u32[]{:S(2)}) collective-permute-start(f32[16,16,1]{2,1,0:T(8,128)S(1)} %get-tuple-element.91), channel_id=1, source_target_pairs={{0,1},{1,2},{2,3},{4,5},{5,6},{6,7},{8,9},{9,10},{10,11},{12,13},{... | collective-permute-start | bytes 3080 | tf_op jit(solution)/shard_map/ppermute | solution.py:89
  168.4 7.3 %collective-permute-start.17 = (f32[16,16,1]{2,1,0:T(8,128)S(1)}, f32[16,16,1]{2,1,0:T(8,128)S(1)}, u32[]{:S(2)}, u32[]{:S(2)}) collective-permute-start(f32[16,16,1]{2,1,0:T(8,128)S(1)} %get-tuple-element.92), channel_id=1, source_target_pairs={{1,0},{2,1},{3,2},{5,4},{6,5},{7,6},{9,8},{10,9},{11,10},{13,12},{... | collective-permute-start | bytes 3080 | tf_op jit(solution)/shard_map/ppermute | solution.py:90
  (24 other events, 171.8 us)
